TPU v7x, 32 devices: a whole 2x2x4 slice. The times are simulated.
32 devices in a mesh: dp: 4 (over y, x), seq: 8 (over z, core).
Axes of the slice: x: 2, y: 2, z: 4, core: 2. Of those that a mesh axis runs over, the one named last changes fastest.
Arguments:
- inputs: bfloat16 [4, 4096, 1024], P('dp', 'seq'), may hold values from -6 to 6
- skip_input: bfloat16 [4, 4096, 1024], P('dp', 'seq'), may hold values from -6 to 6
- time_embed: bfloat16 [4, 1024], P('dp'), may hold values from -6 to 6
- segment_ids: int32 [4, 4096], P('dp'), may hold values from 0 to 2, as said below
- span_start: int32 [4, 3], P('dp'), may hold values from 0 to 768, as said below
- span_length: int32 [4, 3], P('dp'), may hold values from 359 to 2560, as said below
- cotangent: bfloat16 [4, 4096, 1024], P('dp', 'seq'), may hold values from -6 to 6
- skip_weight: bfloat16 [2048, 1024], P('dp', 'seq'), may hold values from -0.125 to 0.125
- ada_weight: bfloat16 [1024, 4096], P('dp', 'seq'), may hold values from -0.09375 to 0.09375
- qkv_weight: bfloat16 [1024, 3072], P('dp', 'seq'), may hold values from -0.1875 to 0.1875
- out_weight: bfloat16 [1024, 1024], P('dp', 'seq'), may hold values from -1 to 1
- up_weight: bfloat16 [1024, 4096], P('dp', 'seq'), may hold values from -0.1875 to 0.1875
- down_weight: bfloat16 [4096, 1024], P('dp', 'seq'), may hold values from -0.09375 to 0.09375
Outputs:
- layer_output: bfloat16 [4, 4096, 1024], P('dp', 'seq')
- grad_inputs: float32 [4, 4096, 1024], P('dp', 'seq')
- grad_skip: float32 [4, 4096, 1024], P('dp', 'seq')
- grad_skip_weight: float32 [2048, 1024], P('dp', 'seq')
- grad_ada_weight: float32 [1024, 4096], P('dp', 'seq')
- grad_qkv_weight: float32 [1024, 3072], P('dp', 'seq')
- grad_out_weight: float32 [1024, 1024], P('dp', 'seq')
- grad_up_weight: float32 [1024, 4096], P('dp', 'seq')
- grad_down_weight: float32 [4096, 1024], P('dp', 'seq')
Inputs may be any that keep to these rules, and one draw needn't show every extreme that they name: `segment_ids`: each row holds 3 utterances in order, ids never falling; each utterance has 512 to 2560 frames. `span_start`: the span of each utterance lies inside it and covers 70 to 100 percent of its frames. `span_length`: see span_start.
All inputs are finite; a program needn't handle non-finite values.
Results may differ from a plain program's by a relative error of at most 0.022.
Values may be sent and summed in bfloat16 or wider, within the bound.
No kernel may reach another device: no remote copies, remote signals or barrier semaphores. Data moves between devices by JAX's collectives and lax.ppermute only.
A program may use at most 512 MiB of HBM per device.

v0:
```python
from functools import partial
import math

import jax
import jax.numpy as jnp
from jax import lax
from jax.sharding import PartitionSpec as P

H = 16
HD = 64
UTT = 3
HG = 8


epsilon = 1e-06
masked_score = -1e30


def ada_norm(stream, scale_part, shift_part):
    inverse = lax.rsqrt(jnp.mean(stream * stream, axis=-1, keepdims=True) + epsilon)
    return stream * inverse * (1.0 + scale_part) + shift_part


def rotate(tensor, cosine, sine_part):
    half_width = tensor.shape[-1] // 2
    lower_half = tensor[..., :half_width]
    upper_half = tensor[..., half_width:]
    cos_wide = cosine[..., None, :]
    sin_wide = sine_part[..., None, :]
    return jnp.concatenate(
        [
            lower_half * cos_wide - upper_half * sin_wide,
            lower_half * sin_wide + upper_half * cos_wide,
        ],
        axis=-1,
    )


def rotary_tables(position, half_width):
    frequency = jnp.exp(-math.log(10000.0) * jnp.arange(half_width, dtype=jnp.float32) / half_width)
    angles = position.astype(jnp.float32)[..., None] * frequency
    return (jnp.cos(angles), jnp.sin(angles))


def gather_weights(skip_tile, ada_tile, qkv_tile, out_tile, up_tile, down_tile):
    row_full = (
        lax.all_gather(skip_tile, "dp", axis=0, tiled=True),
        lax.all_gather(ada_tile, "dp", axis=0, tiled=True),
        lax.all_gather(qkv_tile, "dp", axis=0, tiled=True),
        lax.all_gather(out_tile, "dp", axis=0, tiled=True),
        lax.all_gather(up_tile, "dp", axis=0, tiled=True),
        lax.all_gather(down_tile, "dp", axis=0, tiled=True),
    )
    return (
        lax.all_gather(row_full[0], "seq", axis=1, tiled=True),
        lax.all_gather(row_full[1], "seq", axis=1, tiled=True),
        lax.all_gather(row_full[2], "seq", axis=1, tiled=True),
        lax.all_gather(row_full[3], "seq", axis=1, tiled=True),
        lax.all_gather(row_full[4], "seq", axis=1, tiled=True),
        lax.all_gather(row_full[5], "seq", axis=1, tiled=True),
    )


def group_scores(query_part, key_part, allowed, factor):
    scores = (
        jnp.einsum("qhd,khd->hqk", query_part, key_part, preferred_element_type=jnp.float32)
        * factor
    )
    return jnp.where(allowed[None], scores, masked_score)


def attend_row(queries, key_rows, value_rows, segment_local, segment_full):
    factor = queries.shape[2] ** (-0.5)
    allowed = segment_local[:, None] == segment_full[None, :]
    outputs = []
    totals = []
    for head_start in range(0, H, HG):
        head_end = head_start + HG
        scores = group_scores(
            queries[:, head_start:head_end], key_rows[:, head_start:head_end], allowed, factor
        )
        log_total = jax.nn.logsumexp(scores, axis=-1)
        weights = jnp.exp(scores - log_total[..., None]).astype(jnp.bfloat16)
        outputs.append(
            jnp.einsum(
                "hqk,khd->qhd",
                weights,
                value_rows[:, head_start:head_end],
                preferred_element_type=jnp.float32,
            )
        )
        totals.append(log_total)
    return (jnp.concatenate(outputs, axis=1), jnp.concatenate(totals, axis=0))


def attend_back(
    queries, key_rows, value_rows, segment_local, segment_full, log_total, grad_attended, row_dot
):
    factor = queries.shape[2] ** (-0.5)
    allowed = segment_local[:, None] == segment_full[None, :]
    query_grads = []
    key_grads = []
    value_grads = []
    for head_start in range(0, H, HG):
        head_end = head_start + HG
        key_part = key_rows[:, head_start:head_end]
        query_part = queries[:, head_start:head_end]
        grad_part = grad_attended[:, head_start:head_end]
        scores = group_scores(query_part, key_part, allowed, factor)
        weights = jnp.exp(scores - log_total[head_start:head_end][..., None])
        weights_low = weights.astype(jnp.bfloat16)
        value_grads.append(
            jnp.einsum("hqk,qhd->khd", weights_low, grad_part, preferred_element_type=jnp.float32)
        )
        grad_weights = jnp.einsum(
            "qhd,khd->hqk",
            grad_part,
            value_rows[:, head_start:head_end],
            preferred_element_type=jnp.float32,
        )
        grad_scores = (weights * (grad_weights - row_dot[head_start:head_end][..., None])).astype(
            jnp.bfloat16
        )
        query_grads.append(
            jnp.einsum("hqk,khd->qhd", grad_scores, key_part, preferred_element_type=jnp.float32)
            * factor
        )
        key_grads.append(
            jnp.einsum("hqk,qhd->khd", grad_scores, query_part, preferred_element_type=jnp.float32)
            * factor
        )
    return (
        jnp.concatenate(query_grads, axis=1),
        jnp.concatenate(key_grads, axis=1),
        jnp.concatenate(value_grads, axis=1),
    )


def local(
    inputs,
    skip_input,
    time_embed,
    segment_ids,
    span_start,
    span_length,
    cotangent,
    skip_weight,
    ada_weight,
    qkv_weight,
    out_weight,
    up_weight,
    down_weight,
):
    row_count = inputs.shape[0]
    frames = inputs.shape[1]
    model_width = inputs.shape[2]
    row_length = segment_ids.shape[1]
    frame_base = lax.axis_index("seq") * frames
    utterance = jnp.arange(UTT, dtype=jnp.int32)
    member = (segment_ids[:, :, None] == utterance[None, None, :]).astype(jnp.int32)
    counts = jnp.sum(member, axis=1)
    firsts = jnp.cumsum(counts, axis=1) - counts
    local_member = lax.dynamic_slice_in_dim(member, frame_base, frames, 1)
    local_segments = lax.dynamic_slice_in_dim(segment_ids, frame_base, frames, 1)
    local_frames = frame_base + jnp.arange(frames, dtype=jnp.int32)
    position = local_frames[None, :] - jnp.sum(local_member * firsts[:, None, :], axis=2)
    span_begin = jnp.sum(local_member * span_start[:, None, :], axis=2)
    span_end = span_begin + jnp.sum(local_member * span_length[:, None, :], axis=2)
    inside = jnp.logical_and(position >= span_begin, position < span_end)
    cosine, sine_part = rotary_tables(position, HD // 2)
    skip_full, ada_full, qkv_full, out_full, up_full, down_full = gather_weights(
        skip_weight, ada_weight, qkv_weight, out_weight, up_weight, down_weight
    )
    joined = jnp.concatenate([inputs, skip_input], axis=-1)
    stream = jnp.einsum("rfc,cd->rfd", joined, skip_full, preferred_element_type=jnp.float32)
    modulation = jnp.dot(time_embed, ada_full, preferred_element_type=jnp.float32)[:, None, :]
    scale_one = modulation[..., :model_width]
    shift_one = modulation[..., model_width : 2 * model_width]
    scale_two = modulation[..., 2 * model_width : 3 * model_width]
    shift_two = modulation[..., 3 * model_width :]
    normed_one = ada_norm(stream, scale_one, shift_one).astype(jnp.bfloat16)
    projected = jnp.einsum("rfd,de->rfe", normed_one, qkv_full, preferred_element_type=jnp.float32)
    queries = rotate(
        projected[..., :model_width].reshape(row_count, frames, H, HD), cosine, sine_part
    ).astype(jnp.bfloat16)
    key_rotated = rotate(
        projected[..., model_width : 2 * model_width].reshape(row_count, frames, H, HD),
        cosine,
        sine_part,
    )
    key_local = key_rotated.reshape(row_count, frames, model_width).astype(jnp.bfloat16)
    value_local = projected[..., 2 * model_width :].astype(jnp.bfloat16)
    key_all, value_all = (
        lax.all_gather(key_local, "seq", axis=1, tiled=True),
        lax.all_gather(value_local, "seq", axis=1, tiled=True),
    )

    def forward_row(row_items):
        query_row, key_row, value_row, local_row, full_row = row_items
        return attend_row(
            query_row,
            key_row.reshape(row_length, H, HD),
            value_row.reshape(row_length, H, HD),
            local_row,
            full_row,
        )

    attended, log_total = lax.map(
        forward_row, (queries, key_all, value_all, local_segments, segment_ids)
    )
    attended = attended.reshape(row_count, frames, model_width)
    attended_low = attended.astype(jnp.bfloat16)
    middle = stream + jnp.einsum(
        "rfe,ed->rfd", attended_low, out_full, preferred_element_type=jnp.float32
    )
    normed_two = ada_norm(middle, scale_two, shift_two).astype(jnp.bfloat16)
    up_proj = jnp.einsum("rfd,di->rfi", normed_two, up_full, preferred_element_type=jnp.float32)
    hidden = jax.nn.gelu(up_proj, approximate=True).astype(jnp.bfloat16)
    down_proj = jnp.einsum("rfi,id->rfd", hidden, down_full, preferred_element_type=jnp.float32)
    layer_output = (middle + down_proj).astype(jnp.bfloat16)
    skip_full, ada_full, qkv_full, out_full, up_full, down_full = gather_weights(
        skip_weight, ada_weight, qkv_weight, out_weight, up_weight, down_weight
    )
    grad_out = cotangent.astype(jnp.float32) * inside[..., None].astype(jnp.float32)
    grad_low = grad_out.astype(jnp.bfloat16)
    grad_hidden = jnp.einsum("rfd,id->rfi", grad_low, down_full, preferred_element_type=jnp.float32)
    _, gelu_pull = jax.vjp(partial(jax.nn.gelu, approximate=True), up_proj)
    grad_up_act = gelu_pull(grad_hidden)[0].astype(jnp.bfloat16)
    grad_normed_two = jnp.einsum(
        "rfi,di->rfd", grad_up_act, up_full, preferred_element_type=jnp.float32
    )
    _, norm_pull_two = jax.vjp(ada_norm, middle, scale_two, shift_two)
    grad_middle_norm, grad_scale_two, grad_shift_two = norm_pull_two(grad_normed_two)
    grad_middle = grad_out + grad_middle_norm
    grad_middle_low = grad_middle.astype(jnp.bfloat16)
    grad_attended = jnp.einsum(
        "rfd,ed->rfe", grad_middle_low, out_full, preferred_element_type=jnp.float32
    ).astype(jnp.bfloat16)
    row_dot = jnp.sum(
        (grad_attended.astype(jnp.float32) * attended).reshape(row_count, frames, H, HD), axis=-1
    )
    row_dot = jnp.swapaxes(row_dot, 1, 2)
    grad_heads = grad_attended.reshape(row_count, frames, H, HD)

    def backward_row(row_items):
        query_row, key_row, value_row, local_row, full_row, total_row, grad_row, dot_row = row_items
        return attend_back(
            query_row,
            key_row.reshape(row_length, H, HD),
            value_row.reshape(row_length, H, HD),
            local_row,
            full_row,
            total_row,
            grad_row,
            dot_row,
        )

    grad_queries, grad_keys, grad_values = lax.map(
        backward_row,
        (queries, key_all, value_all, local_segments, segment_ids, log_total, grad_heads, row_dot),
    )
    key_share, value_share = (
        lax.psum_scatter(
            grad_keys.reshape(row_count, row_length, model_width).astype(jnp.bfloat16),
            "seq",
            scatter_dimension=1,
            tiled=True,
        ).astype(jnp.float32),
        lax.psum_scatter(
            grad_values.reshape(row_count, row_length, model_width).astype(jnp.bfloat16),
            "seq",
            scatter_dimension=1,
            tiled=True,
        ).astype(jnp.float32),
    )
    _, rotate_pull = jax.vjp(
        partial(rotate, cosine=cosine, sine_part=sine_part),
        jnp.zeros((row_count, frames, H, HD), jnp.float32),
    )
    grad_query_raw = rotate_pull(grad_queries)[0].reshape(row_count, frames, model_width)
    grad_key_raw = rotate_pull(key_share.reshape(row_count, frames, H, HD))[0].reshape(
        row_count, frames, model_width
    )
    grad_projected = jnp.concatenate([grad_query_raw, grad_key_raw, value_share], axis=-1).astype(
        jnp.bfloat16
    )
    grad_normed_one = jnp.einsum(
        "rfe,de->rfd", grad_projected, qkv_full, preferred_element_type=jnp.float32
    )
    _, norm_pull_one = jax.vjp(ada_norm, stream, scale_one, shift_one)
    grad_stream_norm, grad_scale_one, grad_shift_one = norm_pull_one(grad_normed_one)
    grad_stream = (grad_middle + grad_stream_norm).astype(jnp.bfloat16)
    grad_joined = jnp.einsum(
        "rfd,cd->rfc", grad_stream, skip_full, preferred_element_type=jnp.float32
    )
    grad_modulation = jnp.concatenate(
        [grad_scale_one, grad_shift_one, grad_scale_two, grad_shift_two], axis=-1
    )[:, 0, :]
    grad_down = jnp.einsum("rfi,rfd->id", hidden, grad_low, preferred_element_type=jnp.float32)
    grad_up = jnp.einsum("rfd,rfi->di", normed_two, grad_up_act, preferred_element_type=jnp.float32)
    grad_attn_out = jnp.einsum(
        "rfe,rfd->ed", attended_low, grad_middle_low, preferred_element_type=jnp.float32
    )
    grad_qkv = jnp.einsum(
        "rfd,rfe->de", normed_one, grad_projected, preferred_element_type=jnp.float32
    )
    grad_skip_w = jnp.einsum("rfc,rfd->cd", joined, grad_stream, preferred_element_type=jnp.float32)
    grad_ada = jnp.einsum(
        "rd,re->de",
        time_embed.astype(jnp.float32),
        grad_modulation,
        precision=lax.Precision.HIGHEST,
    )
    column_parts = (
        lax.psum_scatter(
            grad_skip_w.astype(jnp.bfloat16), "seq", scatter_dimension=1, tiled=True
        ).astype(jnp.float32),
        lax.psum_scatter(
            grad_ada.astype(jnp.bfloat16), "seq", scatter_dimension=1, tiled=True
        ).astype(jnp.float32),
        lax.psum_scatter(
            grad_qkv.astype(jnp.bfloat16), "seq", scatter_dimension=1, tiled=True
        ).astype(jnp.float32),
        lax.psum_scatter(
            grad_attn_out.astype(jnp.bfloat16), "seq", scatter_dimension=1, tiled=True
        ).astype(jnp.float32),
        lax.psum_scatter(
            grad_up.astype(jnp.bfloat16), "seq", scatter_dimension=1, tiled=True
        ).astype(jnp.float32),
        lax.psum_scatter(
            grad_down.astype(jnp.bfloat16), "seq", scatter_dimension=1, tiled=True
        ).astype(jnp.float32),
    )
    weight_tiles = (
        lax.psum_scatter(
            column_parts[0].astype(jnp.bfloat16), "dp", scatter_dimension=0, tiled=True
        ).astype(jnp.float32),
        lax.psum_scatter(
            column_parts[1].astype(jnp.bfloat16), "dp", scatter_dimension=0, tiled=True
        ).astype(jnp.float32),
        lax.psum_scatter(
            column_parts[2].astype(jnp.bfloat16), "dp", scatter_dimension=0, tiled=True
        ).astype(jnp.float32),
        lax.psum_scatter(
            column_parts[3].astype(jnp.bfloat16), "dp", scatter_dimension=0, tiled=True
        ).astype(jnp.float32),
        lax.psum_scatter(
            column_parts[4].astype(jnp.bfloat16), "dp", scatter_dimension=0, tiled=True
        ).astype(jnp.float32),
        lax.psum_scatter(
            column_parts[5].astype(jnp.bfloat16), "dp", scatter_dimension=0, tiled=True
        ).astype(jnp.float32),
    )
    skip_tile, ada_tile, qkv_tile, out_tile, up_tile, down_tile = weight_tiles
    return (
        layer_output,
        grad_joined[..., :model_width],
        grad_joined[..., model_width:],
        skip_tile,
        ada_tile,
        qkv_tile,
        out_tile,
        up_tile,
        down_tile,
    )


def solution(mesh):
    in_specs = (
        P("dp", "seq", None),
        P("dp", "seq", None),
        P("dp", None),
        P("dp", None),
        P("dp", None),
        P("dp", None),
        P("dp", "seq", None),
        P("dp", "seq"),
        P("dp", "seq"),
        P("dp", "seq"),
        P("dp", "seq"),
        P("dp", "seq"),
        P("dp", "seq"),
    )
    out_specs = (
        P("dp", "seq", None),
        P("dp", "seq", None),
        P("dp", "seq", None),
        P("dp", "seq"),
        P("dp", "seq"),
        P("dp", "seq"),
        P("dp", "seq"),
        P("dp", "seq"),
        P("dp", "seq"),
    )
    return jax.shard_map(local, mesh=mesh, in_specs=in_specs, out_specs=out_specs, check_vma=False)
```

profile of v0, /device:TPU:0, one launch (start us, length us, event | category | flops | bytes accessed | tf_op | source)
XLA Modules:
  0.0 1585.7 jit_solution(13002443196707940408)
XLA Ops:
  8.0 13.1 all_gather.52
  21.2 18.1 %all-gather.14.cloned.1.call-done = bf16[1024,512]{1,0:T(8,128)(2,1)} async-done(((bf16[256,512]{1,0:T(8,128)(2,1)}), bf16[1024,512]{1,0:T(8,128)(2,1)}) %all-gather.14.cloned.1.call-update) | async-done | bytes 1048592 | tf_op jit(solution)/shard_map/all_gather | solution.py:48
  39.3 12.7 all_gather.56
  54.2 34.5 %all-gather.12.cloned.1.call-done = bf16[2048,1024]{1,0:T(8,128)(2,1)} async-done(((bf16[2048,128]{1,0:T(8,128)(2,1)}), bf16[2048,1024]{1,0:T(8,128)(2,1)}) %all-gather.12.cloned.1.call-update) | async-done | bytes 4194320 | tf_op jit(solution)/shard_map/all_gather | solution.py:55
  88.7 5.3 multiply_reduce_fusion.5
  94.5 76.1 %all-gather.16.cloned.1.call-done = bf16[1024,4096]{1,0:T(8,128)(2,1)} async-done(((bf16[1024,512]{1,0:T(8,128)(2,1)}), bf16[1024,4096]{1,0:T(8,128)(2,1)}) %all-gather.16.cloned.1.call-update) | async-done | bytes 8388624 | tf_op jit(solution)/shard_map/all_gather | solution.py:56
  170.6 4.6 convolution_bitcast_fusion.1
  175.8 59.4 %all-gather.18.cloned.1.call-done = bf16[1024,3072]{1,0:T(8,128)(2,1)} async-done(((bf16[1024,384]{1,0:T(8,128)(2,1)}), bf16[1024,3072]{1,0:T(8,128)(2,1)}) %all-gather.18.cloned.1.call-update) | async-done | bytes 6291472 | tf_op jit(solution)/shard_map/all_gather | solution.py:57
  235.2 5.7 convolution_bitcast_fusion
  240.9 3.0 fusion.80
  253.0 2.9 slice.170
  256.0 10.4 all_gather.60
  269.0 22.6 %all-gather.30.cloned.1.call-done = bf16[4096,128]{1,0:T(8,128)(2,1)} async-done(((bf16[1024,128]{1,0:T(8,128)(2,1)}), bf16[4096,128]{1,0:T(8,128)(2,1)}) %all-gather.30.cloned.1.call-update) | async-done | bytes 1048592 | tf_op jit(solution)/shard_map/all_gather | solution.py:52
  292.2 83.7 %all-gather.22.cloned.1.call-done = bf16[1,4096,1024]{1,2,0:T(8,128)(2,1)} async-done(((bf16[1,512,1024]{1,2,0:T(8,128)(2,1)}), bf16[1,4096,1024]{1,2,0:T(8,128)(2,1)}) %all-gather.22.cloned.1.call-update) | async-done | bytes 8388624 | tf_op jit(solution)/shard_map/all_gather | solution.py:194
  375.9 28.5 %fusion.82 = (f32[8,512]{1,0:T(8,128)S(1)}, f32[8,512,4096]{2,1,0:T(8,128)}) fusion(bf16[4096,16,64]{0,2,1:T(8,128)(2,1)} %bitcast.203, bf16[512,16,32]{0,2,1:T(8,128)(2,1)S(1)} %get-tuple-element.89, bf16[512,16,32]{0,2,1:T(8,128)(2,1)S(1)} %get-tuple-element.88, pred[512,4096]{1,0:T(8,128)(4,1)S(1)} %broadcast_compare_fusion), kind=kOutput, calls=%fused_computation.147 | convolution fusion | flops 2199908352 | bytes 74465280 | tf_op jit(solution)/shard_map/while/body/eval_jaxpr/qhd,khd->hqk/dot_general | solution.py:66
  404.4 27.4 %fusion.83 = (f32[8,512]{1,0:T(8,128)S(1)}, f32[8,512,4096]{2,1,0:T(8,128)}) fusion(bf16[4096,16,64]{0,2,1:T(8,128)(2,1)} %bitcast.204, bf16[512,16,32]{0,2,1:T(8,128)(2,1)S(1)} %get-tuple-element.89, bf16[512,16,32]{0,2,1:T(8,128)(2,1)S(1)} %get-tuple-element.88, pred[512,4096]{1,0:T(8,128)(4,1)S(1)} %broadcast_compare_fusion), kind=kOutput, calls=%fused_computation.148 | convolution fusion | flops 2199908352 | bytes 74465280 | tf_op jit(solution)/shard_map/while/body/eval_jaxpr/qhd,khd->hqk/dot_general | solution.py:66
  431.8 21.4 %exponential_reduce_fusion = f32[8,512]{1,0:T(8,128)S(1)} fusion(f32[8,512,4096]{2,1,0:T(8,128)} %get-tuple-element.107, f32[8,512]{1,0:T(8,128)S(1)} %is-finite_select_fusion), kind=kLoop, calls=%fused_computation.3 | loop fusion | flops 33550336 | bytes 67141632 | tf_op jit(solution)/shard_map/while/body/eval_jaxpr/reduce_sum | solution.py:82
  453.3 5.4 all-gather.20.cloned.1.call-done
  458.7 11.6 copy.43
  470.3 24.8 %fusion.46 = f32[512,8,64]{0,2,1:T(8,128)S(1)} fusion(bf16[4096,16,64]{0,2,1:T(8,128)(2,1)} %bitcast.153, f32[8,512,4096]{2,1,0:T(8,128)} %get-tuple-element.107, f32[8,512]{1,0:T(8,128)S(1)} %log_add_fusion), kind=kOutput, calls=%fused_computation.80 | convolution fusion | flops 2181038080 | bytes 76562432 | tf_op jit(solution)/shard_map/while/body/eval_jaxpr/hqk,khd->qhd/dot_general | solution.py:85
  495.1 23.3 %exponential_reduce_fusion.1 = f32[8,512]{1,0:T(8,128)S(1)} fusion(f32[8,512,4096]{2,1,0:T(8,128)} %get-tuple-element.109, f32[8,512]{1,0:T(8,128)S(1)} %is-finite_select_fusion.1), kind=kLoop, calls=%fused_computation.6 | loop fusion | flops 33550336 | bytes 67141632 | tf_op jit(solution)/shard_map/while/body/eval_jaxpr/reduce_sum | solution.py:82
  518.4 26.2 %fusion.43 = f32[512,8,64]{0,2,1:T(8,128)} fusion(bf16[4096,16,64]{0,2,1:T(8,128)(2,1)} %bitcast.154, f32[8,512,4096]{2,1,0:T(8,128)} %get-tuple-element.109, f32[8,512]{1,0:T(8,128)S(1)} %log_add_fusion.1), kind=kOutput, calls=%fused_computation.79 | convolution fusion | flops 2181038080 | bytes 76562432 | tf_op jit(solution)/shard_map/while/body/eval_jaxpr/hqk,khd->qhd/dot_general | solution.py:85
  548.0 4.9 multiply_reduce_fusion.4
  552.9 4.7 fusion.118
  557.6 4.9 fusion.120
  562.5 9.8 all-gather.28.cloned.1.call-done
  572.3 10.3 fusion.77
  582.6 72.3 %all-gather.32.cloned.1.call-done = bf16[4096,1024]{1,0:T(8,128)(2,1)} async-done(((bf16[4096,128]{1,0:T(8,128)(2,1)}), bf16[4096,1024]{1,0:T(8,128)(2,1)}) %all-gather.32.cloned.1.call-update) | async-done | bytes 8388624 | tf_op jit(solution)/shard_map/all_gather | solution.py:60
  655.0 12.9 fusion.16
  667.9 5.4 multiply_reduce_fusion
  681.0 38.8 %multiply_convert_fusion = bf16[8,512,4096]{2,1,0:T(8,128)(2,1)} fusion(f32[8,512,4096]{2,1,0:T(8,128)} %get-tuple-element.107, bf16[512,16,64]{0,2,1:T(8,128)(2,1)S(1)} %bitcast.168, f32[8,512]{1,0:T(8,128)S(1)} %get-tuple-element.97, f32[8,512]{1,0:T(8,128)S(1)} %log_add_fusion, bf16[4096,8,64]{0,2,1:T(8,128)(2,1)} %fusion.118), kind=kOutput, calls=%fused_computation | convolution fusion | flops 2214592512 | bytes 105938944 | tf_op jit(solution)/shard_map/while/body/eval_jaxpr/qhd,khd->hqk/dot_general | solution.py:115
  719.8 14.5 fusion.31
  734.4 39.1 %multiply_convert_fusion.1 = bf16[8,512,4096]{2,1,0:T(8,128)(2,1)} fusion(f32[8,512,4096]{2,1,0:T(8,128)} %get-tuple-element.109, bf16[512,16,64]{0,2,1:T(8,128)(2,1)S(1)} %bitcast.169, f32[8,512]{1,0:T(8,128)S(1)} %get-tuple-element.96, f32[8,512]{1,0:T(8,128)S(1)} %copy-done.33, bf16[4096,8,64]{0,2,1:T(8,128)(2,1)} %fusion.120), kind=kOutput, calls=%fused_computation.1 | convolution fusion | flops 2214592512 | bytes 105938944 | tf_op jit(solution)/shard_map/while/body/eval_jaxpr/qhd,khd->hqk/dot_general | solution.py:115
  773.5 14.5 fusion.30
  788.0 7.5 pad_maximum_fusion
  795.6 26.6 %fusion.24 = bf16[4096,8,64]{0,2,1:T(8,128)(2,1)} fusion(bf16[512,16,64]{0,2,1:T(8,128)(2,1)S(1)} %bitcast.170, f32[8,512,4096]{2,1,0:T(8,128)} %get-tuple-element.107, f32[8,512]{1,0:T(8,128)S(1)} %log_add_fusion), kind=kOutput, calls=%fused_computation.35 | convolution fusion | flops 2183135232 | bytes 72368128 | tf_op jit(solution)/shard_map/while/body/eval_jaxpr/hqk,qhd->khd/dot_general | solution.py:113
  822.1 26.0 %fusion.27 = bf16[4096,8,64]{0,2,1:T(8,128)(2,1)} fusion(bf16[512,16,64]{0,2,1:T(8,128)(2,1)S(1)} %bitcast.171, f32[8,512,4096]{2,1,0:T(8,128)} %get-tuple-element.109, f32[8,512]{1,0:T(8,128)S(1)} %copy-done.33), kind=kOutput, calls=%fused_computation.36 | convolution fusion | flops 2183135232 | bytes 72368128 | tf_op jit(solution)/shard_map/while/body/eval_jaxpr/hqk,qhd->khd/dot_general | solution.py:113
  848.2 7.6 pad_maximum_fusion.1
  860.9 4.0 copy.53
  865.0 10.3 convolution_convert_fusion
  875.4 11.3 copy.55
  888.2 9.5 convolution_convert_fusion.1
  898.0 17.3 %fusion.49 = f32[512,8,64]{0,2,1:T(8,128)S(1)} fusion(bf16[4096,16,64]{0,2,1:T(8,128)(2,1)} %bitcast.205, bf16[8,512,4096]{2,1,0:T(8,128)(2,1)} %multiply_convert_fusion), kind=kOutput, calls=%fused_computation.82 | convolution fusion | flops 2147745792 | bytes 42991616 | tf_op jit(solution)/shard_map/while/body/eval_jaxpr/hqk,khd->qhd/dot_general | solution.py:125
  915.4 17.6 %fusion.50 = f32[512,8,64]{0,2,1:T(8,128)} fusion(bf16[4096,16,64]{0,2,1:T(8,128)(2,1)} %bitcast.206, bf16[8,512,4096]{2,1,0:T(8,128)(2,1)} %multiply_convert_fusion.1), kind=kOutput, calls=%fused_computation.84 | convolution fusion | flops 2147745792 | bytes 42991616 | tf_op jit(solution)/shard_map/while/body/eval_jaxpr/hqk,khd->qhd/dot_general | solution.py:125
  938.4 35.4 %reduce-scatter.25.cloned.1.call-done = bf16[1,512,1024]{1,2,0:T(8,128)(2,1)} async-done(((bf16[1,4096,1024]{1,2,0:T(8,128)(2,1)}), bf16[1,512,1024]{1,2,0:T(8,128)(2,1)}) %reduce-scatter.25.cloned.1.call-update) | async-done | bytes 1048592 | tf_op jit(solution)/shard_map/reduce_scatter | solution.py:269
  973.8 7.4 multiply_reduce_fusion.1
  982.8 4.4 convolution_convert_fusion.3
  987.2 6.8 copy.49
  994.6 8.3 convolution_convert_fusion.2
  1002.9 8.7 copy.51
  1012.3 5.5 fusion.17
  1019.8 80.7 %reduce-scatter.49.cloned.1.call-done = bf16[128,4096]{1,0:T(8,128)(2,1)} async-done(((bf16[1024,4096]{1,0:T(8,128)(2,1)}), bf16[128,4096]{1,0:T(8,128)(2,1)}) %reduce-scatter.49.cloned.1.call-update) | async-done | bytes 1048592
  1103.0 87.7 %reduce-scatter.37.cloned.1.call-done = bf16[1024,512]{1,0:T(8,128)(2,1)} async-done(((bf16[1024,4096]{1,0:T(8,128)(2,1)}), bf16[1024,512]{1,0:T(8,128)(2,1)}) %reduce-scatter.37.cloned.1.call-update) | async-done | bytes 1048592 | tf_op jit(solution)/shard_map/reduce_scatter | solution.py:327
  1190.7 50.4 %reduce-scatter.43.cloned.1.call-done = bf16[128,2048]{1,0:T(8,128)(2,1)} async-done(((bf16[1024,2048]{1,0:T(8,128)(2,1)}), bf16[128,2048]{1,0:T(8,128)(2,1)}) %reduce-scatter.43.cloned.1.call-update) | async-done | bytes 524304
  1243.3 68.0 %reduce-scatter.45.cloned.1.call-done = bf16[384,1024]{1,0:T(8,128)(2,1)} async-done(((bf16[3072,1024]{1,0:T(8,128)(2,1)}), bf16[384,1024]{1,0:T(8,128)(2,1)}) %reduce-scatter.45.cloned.1.call-update) | async-done | bytes 786448
  1314.0 87.6 %reduce-scatter.29.cloned.1.call-done = bf16[1024,512]{1,0:T(8,128)(2,1)} async-done(((bf16[1024,4096]{1,0:T(8,128)(2,1)}), bf16[1024,512]{1,0:T(8,128)(2,1)}) %reduce-scatter.29.cloned.1.call-update) | async-done | bytes 1048592 | tf_op jit(solution)/shard_map/reduce_scatter | solution.py:318
  1401.7 11.9 fusion.42
  1413.6 13.7 reduce-scatter.35.cloned.1.call-done
  1428.8 4.6 convolution_bitcast_fusion.2
  1435.9 22.3 %reduce-scatter.41.cloned.1.call-done = bf16[1024,128]{1,0:T(8,128)(2,1)} async-done(((bf16[4096,128]{1,0:T(8,128)(2,1)}), bf16[1024,128]{1,0:T(8,128)(2,1)}) %reduce-scatter.41.cloned.1.call-update) | async-done | bytes 262160 | tf_op jit(solution)/shard_map/reduce_scatter | solution.py:350
  1460.0 28.9 %reduce-scatter.39.cloned.1.call-done = bf16[256,512]{1,0:T(8,128)(2,1)} async-done(((bf16[1024,512]{1,0:T(8,128)(2,1)}), bf16[256,512]{1,0:T(8,128)(2,1)}) %reduce-scatter.39.cloned.1.call-update) | async-done | bytes 262160 | tf_op jit(solution)/shard_map/reduce_scatter | solution.py:347
  1490.7 26.6 %reduce-scatter.27.cloned.1.call-done = bf16[512,128]{1,0:T(8,128)(2,1)} async-done(((bf16[2048,128]{1,0:T(8,128)(2,1)}), bf16[512,128]{1,0:T(8,128)(2,1)}) %reduce-scatter.27.cloned.1.call-update) | async-done | bytes 131088 | tf_op jit(solution)/shard_map/reduce_scatter | solution.py:335
  1518.9 27.3 %reduce-scatter.33.cloned.1.call-done = bf16[256,384]{1,0:T(8,128)(2,1)} async-done(((bf16[1024,384]{1,0:T(8,128)(2,1)}), bf16[256,384]{1,0:T(8,128)(2,1)}) %reduce-scatter.33.cloned.1.call-update) | async-done | bytes 196624 | tf_op jit(solution)/shard_map/reduce_scatter | solution.py:341
  1547.9 28.9 %reduce-scatter.31.cloned.1.call-done = bf16[256,512]{1,0:T(8,128)(2,1)} async-done(((bf16[1024,512]{1,0:T(8,128)(2,1)}), bf16[256,512]{1,0:T(8,128)(2,1)}) %reduce-scatter.31.cloned.1.call-update) | async-done | bytes 262160 | tf_op jit(solution)/shard_map/reduce_scatter | solution.py:338
  (214 shorter events, 64.9 us)
Async XLA Ops:
  7.2 46.1 %copy-start.24 = (s32[1,4096]{1,0:T(1,128)S(1)}, s32[1,4096]{1,0:T(1,128)}, u32[]{:S(2)}) copy-start(s32[1,4096]{1,0:T(1,128)} %param.16) | copy-start | bytes 49156
  7.2 46.5 %copy-start.48 = (s32[1,3]{1,0:T(1,128)S(1)}, s32[1,3]{1,0:T(1,128)}, u32[]{:S(2)}) copy-start(s32[1,3]{1,0:T(1,128)} %param.18) | copy-start | bytes 40
  7.2 46.5 %copy-start.49 = (s32[1,3]{1,0:T(1,128)S(1)}, s32[1,3]{1,0:T(1,128)}, u32[]{:S(2)}) copy-start(s32[1,3]{1,0:T(1,128)} %param.17) | copy-start | bytes 40
  7.2 32.0 %all-gather.14.cloned.1.call-start = ((), (), s32[]{:S(2)}) async-start(), calls=%async_computation.15 | async-start | bytes 1310720 | tf_op jit(solution)/shard_map/all_gather | solution.py:48
  7.9 80.7 %all-gather.12.cloned.1.call-start = ((), (), s32[]{:S(2)}) async-start(), calls=%async_computation.14 | async-start | bytes 4718592 | tf_op jit(solution)/shard_map/all_gather | solution.py:55
  21.1 149.5 %all-gather.16.cloned.1.call-start = ((), (), s32[]{:S(2)}) async-start(), calls=%async_computation.16 | async-start | bytes 9437184 | tf_op jit(solution)/shard_map/all_gather | solution.py:56
  39.3 195.9 %all-gather.18.cloned.1.call-start = ((), (), s32[]{:S(2)}) async-start(), calls=%async_computation.17 | async-start | bytes 7077888 | tf_op jit(solution)/shard_map/all_gather | solution.py:57
  52.1 214.4 %all-gather.26.cloned.1.call-start = ((), (), s32[]{:S(2)}) async-start(), calls=%async_computation.21 | async-start | bytes 1310720 | tf_op jit(solution)/shard_map/all_gather | solution.py:51
  52.7 239.0 %all-gather.30.cloned.1.call-start = ((), (), s32[]{:S(2)}) async-start(), calls=%async_computation.23 | async-start | bytes 1310720 | tf_op jit(solution)/shard_map/all_gather | solution.py:52
  53.2 322.7 %all-gather.22.cloned.1.call-start = ((), (), s32[]{:S(2)}) async-start(), calls=%async_computation.19 | async-start | bytes 9437184 | tf_op jit(solution)/shard_map/all_gather | solution.py:194
  54.1 195.6 %copy-start.16 = (f32[512,32]{0,1:T(8,128)}, f32[512,32]{0,1:T(8,128)S(1)}, u32[]{:S(2)}) copy-start(f32[512,32]{0,1:T(8,128)S(1)} %get-tuple-element.102) | copy-start | bytes 196612
  54.1 195.6 %copy-start.18 = (f32[512,32]{0,1:T(8,128)}, f32[512,32]{0,1:T(8,128)S(1)}, u32[]{:S(2)}) copy-start(f32[512,32]{0,1:T(8,128)S(1)} %get-tuple-element.103) | copy-start | bytes 196612
  54.2 116.5 %copy-start.26 = (bf16[1,1024]{1,0:T(2,128)(2,1)S(1)}, bf16[1,1024]{1,0:T(2,128)(2,1)}, u32[]{:S(2)}) copy-start(bf16[1,1024]{1,0:T(2,128)(2,1)} %param.15) | copy-start | bytes 6148
  93.9 141.3 %copy-start.10 = (f32[512,1024]{1,0:T(8,128)}, f32[512,1024]{1,0:T(8,128)S(1)}, u32[]{:S(2)}) copy-start(f32[512,1024]{1,0:T(8,128)S(1)} %get-tuple-element.105) | copy-start | bytes 6291460
  94.5 140.7 %copy-start.36 = (f32[512]{0:T(512)}, f32[512]{0:T(512)S(1)}, u32[]{:S(2)}) copy-start(f32[512]{0:T(512)S(1)} %fusion.70) | copy-start | bytes 6148
  175.8 65.1 %copy-start.30 = (f32[1,1,1024]{2,1,0:T(1,128)}, f32[1,1,1024]{2,1,0:T(1,128)S(1)}, u32[]{:S(2)}) copy-start(f32[1,1,1024]{2,1,0:T(1,128)S(1)} %get-tuple-element.101) | copy-start | bytes 12292
  175.8 65.1 %copy-start.42 = (f32[1,1,1024]{2,1,0:T(1,128)}, f32[1,1,1024]{2,1,0:T(1,128)S(1)}, u32[]{:S(2)}) copy-start(f32[1,1,1024]{2,1,0:T(1,128)S(1)} %get-tuple-element.100) | copy-start | bytes 12292
  240.9 4.0 copy-start.4
  251.9 152.5 %copy-start.20 = (bf16[512,16,32]{0,2,1:T(8,128)(2,1)}, bf16[512,16,32]{0,2,1:T(8,128)(2,1)S(1)}, u32[]{:S(2)}) copy-start(bf16[512,16,32]{0,2,1:T(8,128)(2,1)S(1)} %get-tuple-element.88) | copy-start | bytes 1572868
  251.9 152.5 %copy-start.22 = (bf16[512,16,32]{0,2,1:T(8,128)(2,1)}, bf16[512,16,32]{0,2,1:T(8,128)(2,1)S(1)}, u32[]{:S(2)}) copy-start(bf16[512,16,32]{0,2,1:T(8,128)(2,1)S(1)} %get-tuple-element.89) | copy-start | bytes 1572868
  251.9 4.1 copy-start.25
  253.0 205.7 %all-gather.20.cloned.1.call-start = ((), (), s32[]{:S(2)}) async-start(), calls=%async_computation.18 | async-start | bytes 9437184 | tf_op jit(solution)/shard_map/all_gather | solution.py:195
  256.0 292.0 %all-gather.24.cloned.1.call-start = ((), (), s32[]{:S(2)}) async-start(), calls=%async_computation.20 | async-start | bytes 2359296 | tf_op jit(solution)/shard_map/all_gather | solution.py:58
  266.4 305.9 %all-gather.28.cloned.1.call-start = ((), (), s32[]{:S(2)}) async-start(), calls=%async_computation.22 | async-start | bytes 9437184 | tf_op jit(solution)/shard_map/all_gather | solution.py:59
  267.0 387.9 %all-gather.32.cloned.1.call-start = ((), (), s32[]{:S(2)}) async-start(), calls=%async_computation.24 | async-start | bytes 9437184 | tf_op jit(solution)/shard_map/all_gather | solution.py:60
  291.7 642.9 %reduce-scatter.23.cloned.1.call-start = ((), (), s32[]{:S(2)}) async-start(), calls=%async_computation.25 | async-start | bytes 9437184 | tf_op jit(solution)/shard_map/reduce_scatter | solution.py:263
  495.1 49.5 %copy-start.5 = (f32[512,8,64]{0,2,1:T(8,128)}, f32[512,8,64]{0,2,1:T(8,128)S(1)}, u32[]{:S(2)}) copy-start(f32[512,8,64]{0,2,1:T(8,128)S(1)} %fusion.46) | copy-start | bytes 3145732
  518.4 26.2 %copy-start.32 = (f32[8,512]{1,0:T(8,128)}, f32[8,512]{1,0:T(8,128)S(1)}, u32[]{:S(2)}) copy-start(f32[8,512]{1,0:T(8,128)S(1)} %log_add_fusion.1) | copy-start | bytes 49156
  552.9 120.4 %copy-start.38 = (f32[512]{0:T(512)}, f32[512]{0:T(512)S(1)}, u32[]{:S(2)}) copy-start(f32[512]{0:T(512)S(1)} %fusion.72) | copy-start | bytes 6148
  557.6 14.7 copy-start.7
  557.6 14.7 copy-start.28
  557.6 14.7 copy-start.44
  572.3 82.6 %copy-start.13 = (bf16[1,512,1024]{2,1,0:T(8,128)(2,1)S(1)}, bf16[1,512,1024]{2,1,0:T(8,128)(2,1)}, u32[]{:S(2)}) copy-start(bf16[1,512,1024]{2,1,0:T(8,128)(2,1)} %param.19) | copy-start | bytes 3145732
  572.3 82.6 %copy-start.34 = (f32[512]{0:T(512)S(1)}, f32[512]{0:T(512)}, u32[]{:S(2)}) copy-start(f32[512]{0:T(512)} %fusion.69) | copy-start | bytes 6148
  655.0 12.9 copy-start.50
  667.9 5.4 copy-start.53
  675.5 2.7 copy-start
  681.0 38.8 %copy-start.21 = (bf16[512,16,32]{0,2,1:T(8,128)(2,1)S(1)}, bf16[512,16,32]{0,2,1:T(8,128)(2,1)}, u32[]{:S(2)}) copy-start(bf16[512,16,32]{0,2,1:T(8,128)(2,1)} %copy-done.20) | copy-start | bytes 1572868
  681.0 38.8 %copy-start.23 = (bf16[512,16,32]{0,2,1:T(8,128)(2,1)S(1)}, bf16[512,16,32]{0,2,1:T(8,128)(2,1)}, u32[]{:S(2)}) copy-start(bf16[512,16,32]{0,2,1:T(8,128)(2,1)} %copy-done.22) | copy-start | bytes 1572868
  719.8 14.5 copy-start.33
  795.5 178.3 %reduce-scatter.25.cloned.1.call-start = ((), (), s32[]{:S(2)}) async-start(), calls=%async_computation.26 | async-start | bytes 9437184 | tf_op jit(solution)/shard_map/reduce_scatter | solution.py:269
  855.8 162.2 %reduce-scatter.47.cloned.1.call-start = ((), (), s32[]{:S(2)}) async-start(), calls=%async_computation.37 | async-start | bytes 2359296
  860.9 4.1 copy-start.14
  860.9 4.1 copy-start.35
  865.0 235.6 %reduce-scatter.49.cloned.1.call-start = ((), (), s32[]{:S(2)}) async-start(), calls=%async_computation.38 | async-start | bytes 9437184
  886.7 304.0 %reduce-scatter.37.cloned.1.call-start = ((), (), s32[]{:S(2)}) async-start(), calls=%async_computation.32 | async-start | bytes 9437184 | tf_op jit(solution)/shard_map/reduce_scatter | solution.py:327
  897.8 343.4 %reduce-scatter.43.cloned.1.call-start = ((), (), s32[]{:S(2)}) async-start(), calls=%async_computation.35 | async-start | bytes 4718592
  933.0 3.1 copy-start.17
  933.0 3.1 copy-start.19
  937.0 36.8 %copy-start.11 = (f32[512,1024]{1,0:T(8,128)S(1)}, f32[512,1024]{1,0:T(8,128)}, u32[]{:S(2)}) copy-start(f32[512,1024]{1,0:T(8,128)} %copy-done.10) | copy-start | bytes 6291460
  937.0 36.8 %copy-start.31 = (f32[1,1,1024]{2,1,0:T(1,128)S(1)}, f32[1,1,1024]{2,1,0:T(1,128)}, u32[]{:S(2)}) copy-start(f32[1,1,1024]{2,1,0:T(1,128)} %copy-done.30) | copy-start | bytes 12292
  937.1 36.7 %copy-start.37 = (f32[512]{0:T(512)S(1)}, f32[512]{0:T(512)}, u32[]{:S(2)}) copy-start(f32[512]{0:T(512)} %copy-done.36) | copy-start | bytes 6148
  938.4 42.9 %copy-start.15 = (bf16[1,512,16,64]{1,3,2,0:T(8,128)(2,1)}, bf16[1,512,16,64]{1,3,2,0:T(8,128)(2,1)S(1)}, u32[]{:S(2)}) copy-start(bf16[1,512,16,64]{1,3,2,0:T(8,128)(2,1)S(1)} %get-tuple-element.116) | copy-start | bytes 3145732
  973.8 7.5 copy-start.41
  973.8 7.5 copy-start.2
  993.9 317.4 %reduce-scatter.45.cloned.1.call-start = ((), (), s32[]{:S(2)}) async-start(), calls=%async_computation.36 | async-start | bytes 7077888
  1011.6 390.0 %reduce-scatter.29.cloned.1.call-start = ((), (), s32[]{:S(2)}) async-start(), calls=%async_computation.28 | async-start | bytes 9437184 | tf_op jit(solution)/shard_map/reduce_scatter | solution.py:318
  1017.9 409.4 %reduce-scatter.35.cloned.1.call-start = ((), (), s32[]{:S(2)}) async-start(), calls=%async_computation.31 | async-start | bytes 327680 | tf_op jit(solution)/shard_map/reduce_scatter | solution.py:344
  1019.8 438.4 %reduce-scatter.41.cloned.1.call-start = ((), (), s32[]{:S(2)}) async-start(), calls=%async_computation.34 | async-start | bytes 1310720 | tf_op jit(solution)/shard_map/reduce_scatter | solution.py:350
  1100.5 301.2 %copy-start.9 = (f32[512,1024]{1,0:T(8,128)S(1)}, f32[512,1024]{1,0:T(8,128)}, u32[]{:S(2)}) copy-start(f32[512,1024]{1,0:T(8,128)} %get-tuple-element.111) | copy-start | bytes 6291460
  1103.0 385.9 %reduce-scatter.39.cloned.1.call-start = ((), (), s32[]{:S(2)}) async-start(), calls=%async_computation.33 | async-start | bytes 1310720 | tf_op jit(solution)/shard_map/reduce_scatter | solution.py:347
  1190.7 326.6 %reduce-scatter.27.cloned.1.call-start = ((), (), s32[]{:S(2)}) async-start(), calls=%async_computation.27 | async-start | bytes 655360 | tf_op jit(solution)/shard_map/reduce_scatter | solution.py:335
  1243.2 302.9 %reduce-scatter.33.cloned.1.call-start = ((), (), s32[]{:S(2)}) async-start(), calls=%async_computation.30 | async-start | bytes 983040 | tf_op jit(solution)/shard_map/reduce_scatter | solution.py:341
  1313.7 263.2 %reduce-scatter.31.cloned.1.call-start = ((), (), s32[]{:S(2)}) async-start(), calls=%async_computation.29 | async-start | bytes 1310720 | tf_op jit(solution)/shard_map/reduce_scatter | solution.py:338
  (15 other events, 20.1 us)
Sparse Core Ops, SparseCore 0:
  9.9 29.3 all-gather.13
  40.8 47.7 all-gather.11
  90.3 80.2 all-gather.15
  172.1 63.0 all-gather.17
  236.9 25.7 all-gather.25
  264.3 27.2 all-gather.29
  293.8 82.0 all-gather.21
  378.1 80.5 all-gather.19
  460.3 29.3 all-gather.23
  491.2 81.1 all-gather.27
  573.9 81.0 all-gather.31
  795.6 87.8 reduce-scatter.22
  885.8 87.9 reduce-scatter.24
  975.9 34.1 reduce-scatter.46
  1012.3 88.1 reduce-scatter.48
  1102.7 87.9 reduce-scatter.36
  1192.8 48.3 reduce-scatter.42
  1243.3 67.9 reduce-scatter.44
  1313.6 87.9 reduce-scatter.28
  1404.8 22.4 reduce-scatter.34
  1430.4 27.7 reduce-scatter.40
  1461.1 27.7 reduce-scatter.38
  1492.5 24.7 reduce-scatter.26
  1520.1 26.0 reduce-scatter.32
  1549.1 27.7 reduce-scatter.30
where the time goes:
time: 1590 us
  waiting for transfers between devices  942 us (59%)
  matrix products  412 us (26%)
  other arithmetic  91.7 us (6%)
  local copies, waits for them, and re-layouts  86.1 us (5%)
  blocking collectives  36.2 us (2%)
    unnamed x29, waiting for transfers between devices  202 us
    reduce_scatter x1, waiting for transfers between devices, local(): lax.psum_scatter(grad_up.astype(jnp.bfloat16), 'seq', scatter_dimension=1...  87.7 us
    reduce_scatter x1, waiting for transfers between devices, local(): lax.psum_scatter(grad_ada.astype(jnp.bfloat16), 'seq', scatter_dimension=...  87.6 us
    all_gather x1, waiting for transfers between devices, local(): lax.all_gather(key_local, 'seq', axis=1, tiled=True)  83.7 us
    dot_general x2, matrix products, attend_back(): jnp.einsum('qhd,khd->hqk', grad_part, value_rows[:, head_start:head_end],...  77.9 us
    all_gather x1, waiting for transfers between devices, gather_weights(): lax.all_gather(row_full[1], 'seq', axis=1, tiled=True)  76.1 us
    all_gather x1, waiting for transfers between devices, gather_weights(): lax.all_gather(row_full[5], 'seq', axis=1, tiled=True)  72.3 us
    all_gather x1, waiting for transfers between devices, gather_weights(): lax.all_gather(row_full[2], 'seq', axis=1, tiled=True)  59.4 us
  transfers between devices with their start and end apart: 25, of which 21 were waited for; matrix products, arithmetic and copies ran while one was open for 28% of the time, Pallas kernels for 0%

commit v1 on v0

--- a/solution.py
+++ b/solution.py
@@ -4,6 +4,8 @@
 import jax
 import jax.numpy as jnp
 from jax import lax
+from jax.experimental import pallas as pl
+from jax.experimental.pallas import tpu as pltpu
 from jax.sharding import PartitionSpec as P
 
 H = 16
@@ -136,7 +138,7 @@
     )
 
 
-def local(
+def local_general(
     inputs,
     skip_input,
     time_embed,
@@ -365,6 +367,445 @@
     )
 
 
+LOG2E = 1.4426950408889634
+SCALE = HD**-0.5
+PAIR = 2 * HD
+
+
+def dot_nn(a, b):
+    return lax.dot_general(a, b, (((1,), (0,)), ((), ())), preferred_element_type=jnp.float32)
+
+
+def dot_nt(a, b):
+    return lax.dot_general(a, b, (((1,), (1,)), ((), ())), preferred_element_type=jnp.float32)
+
+
+def dot_tn(a, b):
+    return lax.dot_general(a, b, (((0,), (0,)), ((), ())), preferred_element_type=jnp.float32)
+
+
+def segment_of(index, ends_ref):
+    return (index >= ends_ref[0]).astype(jnp.int32) + (index >= ends_ref[1]).astype(jnp.int32)
+
+
+def segment_span(ends_ref, first, last, length):
+    end_a, end_b = ends_ref[0], ends_ref[1]
+    low = jnp.where(first < end_a, 0, jnp.where(first < end_b, end_a, end_b))
+    high = jnp.where(last < end_a, end_a, jnp.where(last < end_b, end_b, length))
+    return low, high
+
+
+def key_blocks(ends_ref, start, size, length):
+    low, high = segment_span(ends_ref, start, start + size - 1, length)
+    low_last, _ = segment_span(ends_ref, start + size - 1, start, length)
+    first = low // size
+    last = (high + size - 1) // size
+    whole_first = jnp.where(low == low_last, (low + size - 1) // size, last)
+    whole_first = jnp.minimum(whole_first, last)
+    whole_last = jnp.where(low == low_last, jnp.maximum(high // size, whole_first), last)
+    return first, whole_first, whole_last, last
+
+
+def turn(pair, cosine, sine_part):
+    half = HD // 2
+    rows = []
+    for head in range(2):
+        lower = pair[head * HD : head * HD + half]
+        upper = pair[head * HD + half : (head + 1) * HD]
+        rows += [lower * cosine - upper * sine_part, lower * sine_part + upper * cosine]
+    return jnp.concatenate(rows, axis=0)
+
+
+def project_kernel(normed_ref, weight_ref, cos_ref, sin_ref, qt_ref, kt_ref, vt_ref, k_ref, v_ref):
+    projected = dot_nt(weight_ref[...], normed_ref[0])
+    cosine, sine_part = cos_ref[...], sin_ref[...]
+    queries = turn(projected[:PAIR], cosine, sine_part).astype(jnp.bfloat16)
+    keys = turn(projected[PAIR : 2 * PAIR], cosine, sine_part)
+    values = projected[2 * PAIR :]
+    qt_ref[0] = (queries.astype(jnp.float32) * SCALE).astype(jnp.bfloat16)
+    kt_ref[...] = keys.astype(jnp.bfloat16)
+    vt_ref[...] = values.astype(jnp.bfloat16)
+    k_ref[...] = keys.T.astype(jnp.bfloat16)
+    v_ref[...] = values.T.astype(jnp.bfloat16)
+
+
+def project_pair(normed_all, weight_rows, cos_all, sin_all):
+    chunks, frames, width = normed_all.shape
+    length = chunks * frames
+    return pl.pallas_call(
+        project_kernel,
+        grid=(chunks,),
+        in_specs=[
+            pl.BlockSpec((1, frames, width), lambda i: (i, 0, 0)),
+            pl.BlockSpec((3 * PAIR, width), lambda i: (0, 0)),
+            pl.BlockSpec((HD // 2, frames), lambda i: (0, i)),
+            pl.BlockSpec((HD // 2, frames), lambda i: (0, i)),
+        ],
+        out_specs=[
+            pl.BlockSpec((1, PAIR, frames), lambda i: (i, 0, 0)),
+            pl.BlockSpec((PAIR, frames), lambda i: (0, i)),
+            pl.BlockSpec((PAIR, frames), lambda i: (0, i)),
+            pl.BlockSpec((frames, PAIR), lambda i: (i, 0)),
+            pl.BlockSpec((frames, PAIR), lambda i: (i, 0)),
+        ],
+        out_shape=[
+            jax.ShapeDtypeStruct((chunks, PAIR, frames), jnp.bfloat16),
+            jax.ShapeDtypeStruct((PAIR, length), jnp.bfloat16),
+            jax.ShapeDtypeStruct((PAIR, length), jnp.bfloat16),
+            jax.ShapeDtypeStruct((length, PAIR), jnp.bfloat16),
+            jax.ShapeDtypeStruct((length, PAIR), jnp.bfloat16),
+        ],
+        compiler_params=pltpu.CompilerParams(vmem_limit_bytes=32 << 20),
+        cost_estimate=pl.CostEstimate(
+            flops=6 * length * width * PAIR, bytes_accessed=2 * length * (width + 5 * PAIR), transcendentals=0
+        ),
+        name="project_pair",
+    )(normed_all, weight_rows, cos_all, sin_all)
+
+
+def split_heads(block):
+    row = lax.broadcasted_iota(jnp.int32, block.shape, 0)
+    zero = jnp.zeros((), block.dtype)
+    return jnp.where(row < HD, block, zero), jnp.where(row < HD, zero, block)
+
+
+def attend_kernel(ends_ref, qt_ref, k_ref, vt_ref, low_ref, full_ref, total_ref, acc_ref, top_ref, *, size, length):
+    start = pl.program_id(0) * size
+    queries = split_heads(qt_ref[0])
+    query_segment = segment_of(start + lax.broadcasted_iota(jnp.int32, (1, size), 1), ends_ref)
+    first, whole_first, whole_last, last = key_blocks(ends_ref, start, size, length)
+    acc_ref[...] = jnp.zeros_like(acc_ref)
+    top_ref[...] = jnp.full_like(top_ref, masked_score)
+    ones = jnp.ones((16, size), jnp.bfloat16)
+
+    def step(masked):
+        def run(block, carry):
+            offset = pl.multiple_of(block * size, size)
+            keys = k_ref[pl.ds(offset, size), :]
+            scores = [dot_nn(keys, queries[head]) for head in range(2)]
+            if masked:
+                key_segment = segment_of(offset + lax.broadcasted_iota(jnp.int32, (size, 1), 0), ends_ref)
+                same = key_segment == query_segment
+                scores = [jnp.where(same, part, masked_score) for part in scores]
+            old = [top_ref[head] for head in range(2)]
+            new = [jnp.maximum(old[head], jnp.max(scores[head], axis=0, keepdims=True) * LOG2E) for head in range(2)]
+            weights = [jnp.exp2(scores[head] * LOG2E - new[head]).astype(jnp.bfloat16) for head in range(2)]
+            for head in range(2):
+                values = jnp.concatenate([vt_ref[pl.ds(head * HD, HD), pl.ds(offset, size)], ones], axis=0)
+                acc_ref[head] = acc_ref[head] * jnp.exp2(old[head] - new[head]) + dot_nn(values, weights[head])
+                top_ref[head] = new[head]
+            return carry
+
+        return run
+
+    lax.fori_loop(first, whole_first, step(True), 0)
+    lax.fori_loop(whole_first, whole_last, step(False), 0)
+    lax.fori_loop(whole_last, last, step(True), 0)
+    for head in range(2):
+        total = acc_ref[head, HD : HD + 1, :]
+        attended = acc_ref[head, :HD, :] / total
+        full_ref[0, head * HD : (head + 1) * HD, :] = attended
+        low_ref[0, head * HD : (head + 1) * HD, :] = attended.astype(jnp.bfloat16)
+        total_ref[0, head : head + 1, :] = jnp.log(total) * LOG2E + top_ref[head]
+
+
+def attend_pair(ends, qt, k, vt):
+    chunks, _, size = qt.shape
+    length = k.shape[0]
+    chunk = pl.BlockSpec((1, PAIR, size), lambda i, ends: (i, 0, 0))
+    return pl.pallas_call(
+        partial(attend_kernel, size=size, length=length),
+        grid_spec=pltpu.PrefetchScalarGridSpec(
+            num_scalar_prefetch=1,
+            grid=(chunks,),
+            in_specs=[
+                chunk,
+                pl.BlockSpec((length, PAIR), lambda i, ends: (0, 0)),
+                pl.BlockSpec((PAIR, length), lambda i, ends: (0, 0)),
+            ],
+            out_specs=[chunk, chunk, pl.BlockSpec((1, 2, size), lambda i, ends: (i, 0, 0))],
+            scratch_shapes=[pltpu.VMEM((2, HD + 16, size), jnp.float32), pltpu.VMEM((2, 1, size), jnp.float32)],
+        ),
+        out_shape=[
+            jax.ShapeDtypeStruct((chunks, PAIR, size), jnp.bfloat16),
+            jax.ShapeDtypeStruct((chunks, PAIR, size), jnp.float32),
+            jax.ShapeDtypeStruct((chunks, 2, size), jnp.float32),
+        ],
+        compiler_params=pltpu.CompilerParams(vmem_limit_bytes=32 << 20),
+        cost_estimate=pl.CostEstimate(
+            flops=8 * length * length * HD, bytes_accessed=14 * length * PAIR, transcendentals=length * length
+        ),
+        name="attend_pair",
+    )(ends, qt, k, vt)
+
+
+def attend_back_kernel(
+    ends_ref, qt_ref, gt_ref, full_ref, total_ref, k_ref, v_ref, kt_ref, cos_ref, sin_ref, out_ref,
+    dk_ref, dv_ref, dq_ref, *, size, length, chunks,
+):
+    index = pl.program_id(0)
+    start = index * size
+
+    @pl.when(index == 0)
+    def _():
+        dk_ref[...] = jnp.zeros_like(dk_ref)
+        dv_ref[...] = jnp.zeros_like(dv_ref)
+
+    queries = split_heads(qt_ref[0])
+    grads = split_heads(gt_ref[0])
+    product = gt_ref[0].astype(jnp.float32) * full_ref[0]
+    row_dot = [jnp.sum(product[head * HD : (head + 1) * HD], axis=0, keepdims=True) for head in range(2)]
+    query_segment = segment_of(start + lax.broadcasted_iota(jnp.int32, (1, size), 1), ends_ref)
+    first, whole_first, whole_last, last = key_blocks(ends_ref, start, size, length)
+    dq_ref[...] = jnp.zeros_like(dq_ref)
+    part = size // 2
+
+    def step(masked):
+        def run(block, carry):
+            for piece in range(2):
+                offset = pl.multiple_of(block * size + piece * part, part)
+                rows = pl.ds(offset, part)
+                keys, values = k_ref[rows, :], v_ref[rows, :]
+                for head in range(2):
+                    scores = dot_nn(keys, queries[head])
+                    if masked:
+                        key_segment = segment_of(offset + lax.broadcasted_iota(jnp.int32, (part, 1), 0), ends_ref)
+                        scores = jnp.where(key_segment == query_segment, scores, masked_score)
+                    weights = jnp.exp2(scores * LOG2E - total_ref[0, head : head + 1, :])
+                    grad_weights = dot_nn(values, grads[head])
+                    grad_scores = (weights * (grad_weights - row_dot[head])).astype(jnp.bfloat16)
+                    dv_ref[rows, :] += dot_nt(weights.astype(jnp.bfloat16), grads[head])
+                    dk_ref[rows, :] += dot_nt(grad_scores, queries[head])
+                    dq_ref[head * HD : (head + 1) * HD, :] += dot_nn(
+                        kt_ref[head * HD : (head + 1) * HD, rows], grad_scores
+                    )
+            return carry
+
+        return run
+
+    lax.fori_loop(first, whole_first, step(True), 0)
+    lax.fori_loop(whole_first, whole_last, step(False), 0)
+    lax.fori_loop(whole_last, last, step(True), 0)
+    own = pl.ds(pl.multiple_of(start, size), size)
+    out_ref[index, :PAIR, :] = turn(dq_ref[...] * SCALE, cos_ref[:, own], -sin_ref[:, own]).astype(jnp.bfloat16)
+
+    @pl.when(index == chunks - 1)
+    def _():
+        for chunk in range(chunks):
+            rows = pl.ds(chunk * size, size)
+            turned = turn(dk_ref[rows, :].T, cos_ref[:, rows], -sin_ref[:, rows])
+            out_ref[chunk, PAIR : 2 * PAIR, :] = turned.astype(jnp.bfloat16)
+            out_ref[chunk, 2 * PAIR :, :] = dv_ref[rows, :].T.astype(jnp.bfloat16)
+
+
+def attend_pair_back(ends, qt, gt, full, total, k, v, kt, cos_all, sin_all):
+    chunks, _, size = qt.shape
+    length = k.shape[0]
+    chunk = pl.BlockSpec((1, PAIR, size), lambda i, ends: (i, 0, 0))
+
+    def whole(shape):
+        return pl.BlockSpec(shape, lambda i, ends: (0,) * len(shape))
+
+    return pl.pallas_call(
+        partial(attend_back_kernel, size=size, length=length, chunks=chunks),
+        grid_spec=pltpu.PrefetchScalarGridSpec(
+            num_scalar_prefetch=1,
+            grid=(chunks,),
+            in_specs=[
+                chunk, chunk, chunk, pl.BlockSpec((1, 2, size), lambda i, ends: (i, 0, 0)),
+                whole((length, PAIR)), whole((length, PAIR)), whole((PAIR, length)),
+                whole((HD // 2, length)), whole((HD // 2, length)),
+            ],
+            out_specs=whole((chunks, 3 * PAIR, size)),
+            scratch_shapes=[
+                pltpu.VMEM((length, PAIR), jnp.float32),
+                pltpu.VMEM((length, PAIR), jnp.float32),
+                pltpu.VMEM((PAIR, size), jnp.float32),
+            ],
+        ),
+        out_shape=jax.ShapeDtypeStruct((chunks, 3 * PAIR, size), jnp.bfloat16),
+        compiler_params=pltpu.CompilerParams(vmem_limit_bytes=40 << 20),
+        cost_estimate=pl.CostEstimate(
+            flops=20 * length * length * HD, bytes_accessed=30 * length * PAIR, transcendentals=length * length
+        ),
+        name="attend_pair_back",
+    )(ends, qt, gt, full, total, k, v, kt, cos_all, sin_all)
+
+
+def pair_routes(count):
+    routes = [[(source, (3 * source + piece) % count) for source in range(count)] for piece in range(3)]
+    slots = [[0] * 3 for _ in range(count)]
+    for piece in range(3):
+        for source, target in routes[piece]:
+            slots[target][piece] = (3 * source + piece) // count
+    return routes, slots
+
+
+def own_pair_columns(tile, count):
+    routes, slots = pair_routes(count)
+    width = tile.shape[1] // 3
+    got = [lax.ppermute(tile[:, p * width : (p + 1) * width], "seq", routes[p]) for p in range(3)]
+    slot_of = jnp.asarray(slots, jnp.int32)[lax.axis_index("seq")]
+    columns = []
+    for slot in range(3):
+        columns.append(
+            jnp.where(slot_of[0] == slot, got[0], jnp.where(slot_of[1] == slot, got[1], got[2]))
+        )
+    return jnp.concatenate(columns, axis=1)
+
+
+def stored_columns(pair_tile, count):
+    routes, slots = pair_routes(count)
+    width = pair_tile.shape[1] // 3
+    slot_of = jnp.asarray(slots, jnp.int32)[lax.axis_index("seq")]
+    parts = [pair_tile[:, s * width : (s + 1) * width] for s in range(3)]
+    back = []
+    for piece in range(3):
+        slot = slot_of[piece]
+        chosen = jnp.where(slot == 0, parts[0], jnp.where(slot == 1, parts[1], parts[2]))
+        back.append(lax.ppermute(chosen, "seq", [(target, source) for source, target in routes[piece]]))
+    return jnp.concatenate(back, axis=1)
+
+
+def gather_tiles(tile):
+    rows, columns = tile.shape
+    dp, seq = lax.axis_size("dp"), lax.axis_size("seq")
+    pieces = lax.all_gather(tile, ("dp", "seq"), axis=0).reshape(dp, seq, rows, columns)
+    return jnp.swapaxes(pieces, 1, 2).reshape(dp * rows, seq * columns)
+
+
+def scatter_sum(partial_sum):
+    rows, columns = partial_sum.shape
+    dp, seq = lax.axis_size("dp"), lax.axis_size("seq")
+    over_seq = lax.psum_scatter(
+        partial_sum.astype(jnp.bfloat16), "seq", scatter_dimension=1, tiled=True
+    ).astype(jnp.float32)
+    return lax.psum_scatter(
+        over_seq.astype(jnp.bfloat16), "dp", scatter_dimension=0, tiled=True
+    ).astype(jnp.float32)
+
+
+def norm_back(grad, stream, inverse, scale_part):
+    unit = stream * inverse
+    lifted = grad * (1.0 + scale_part)
+    grad_stream = inverse * (lifted - unit * jnp.mean(lifted * unit, axis=-1, keepdims=True))
+    return grad_stream, jnp.sum(grad * unit, axis=0), jnp.sum(grad, axis=0)
+
+
+def local_paired(
+    inputs, skip_input, time_embed, segment_ids, span_start, span_length, cotangent,
+    skip_weight, ada_weight, qkv_weight, out_weight, up_weight, down_weight,
+):
+    seq = lax.axis_size("seq")
+    dp = lax.axis_size("dp")
+    frames, width = inputs.shape[1], inputs.shape[2]
+    length = segment_ids.shape[1]
+    segments = segment_ids[0]
+    end_a = jnp.sum((segments < 1).astype(jnp.int32))
+    end_b = jnp.sum((segments < 2).astype(jnp.int32))
+    ends = jnp.stack([end_a, end_b])
+    firsts = jnp.where(segments == 0, 0, jnp.where(segments == 1, end_a, end_b))
+    position = jnp.arange(length, dtype=jnp.int32) - firsts
+    half = HD // 2
+    frequency = jnp.exp(-math.log(10000.0) * jnp.arange(half, dtype=jnp.float32) / half)
+    angles = frequency[:, None] * position.astype(jnp.float32)[None, :]
+    cos_all, sin_all = jnp.cos(angles), jnp.sin(angles)
+    base = lax.axis_index("seq") * frames
+    local_segments = lax.dynamic_slice_in_dim(segments, base, frames, 0)
+    local_position = lax.dynamic_slice_in_dim(position, base, frames, 0)
+    starts, lengths = span_start[0], span_length[0]
+
+    def pick(table):
+        return jnp.where(local_segments == 0, table[0], jnp.where(local_segments == 1, table[1], table[2]))
+
+    span_begin = pick(starts)
+    inside = jnp.logical_and(local_position >= span_begin, local_position < span_begin + pick(lengths))
+    embed_all = lax.all_gather(time_embed, "dp", axis=0, tiled=True)
+    embed_rows = width // dp
+    embed_part = lax.dynamic_slice_in_dim(embed_all, lax.axis_index("dp") * embed_rows, embed_rows, 1)
+    modulation_part = jnp.dot(embed_part, ada_weight, preferred_element_type=jnp.float32)
+    modulation_part = lax.psum_scatter(modulation_part, "dp", scatter_dimension=0, tiled=True)
+    modulation = lax.all_gather(modulation_part, "seq", axis=1, tiled=True)
+    scale_one = modulation[:, :width]
+    shift_one = modulation[:, width : 2 * width]
+    scale_two = modulation[:, 2 * width : 3 * width]
+    shift_two = modulation[:, 3 * width :]
+
+    skip_full = gather_tiles(skip_weight)
+    pair_tile = own_pair_columns(qkv_weight, seq)
+    pair_weight = lax.all_gather(pair_tile, "dp", axis=0, tiled=True)
+    joined = jnp.concatenate([inputs[0], skip_input[0]], axis=-1)
+    stream = dot_nn(joined, skip_full)
+    inverse_one = lax.rsqrt(jnp.mean(stream * stream, axis=-1, keepdims=True) + epsilon)
+    normed_one = (stream * inverse_one * (1.0 + scale_one) + shift_one).astype(jnp.bfloat16)
+    normed_all = lax.all_gather(normed_one, "seq", axis=0)
+    qt, kt, vt, keys, values = project_pair(normed_all, pair_weight.T, cos_all, sin_all)
+    attended_pair, attended_wide, total = attend_pair(ends, qt, keys, vt)
+    attended = lax.all_to_all(attended_pair, "seq", 0, 0).reshape(width, frames)
+    out_full = gather_tiles(out_weight)
+    up_full = gather_tiles(up_weight)
+    down_full = gather_tiles(down_weight)
+    middle = stream + dot_tn(attended, out_full)
+    inverse_two = lax.rsqrt(jnp.mean(middle * middle, axis=-1, keepdims=True) + epsilon)
+    normed_two = (middle * inverse_two * (1.0 + scale_two) + shift_two).astype(jnp.bfloat16)
+    up_proj = dot_nn(normed_two, up_full)
+    hidden = jax.nn.gelu(up_proj, approximate=True).astype(jnp.bfloat16)
+    layer_output = (middle + dot_nn(hidden, down_full)).astype(jnp.bfloat16)
+
+    grad_out = cotangent[0].astype(jnp.float32) * inside[:, None].astype(jnp.float32)
+    grad_low = grad_out.astype(jnp.bfloat16)
+    grad_hidden = dot_nt(grad_low, down_full)
+    _, gelu_pull = jax.vjp(partial(jax.nn.gelu, approximate=True), up_proj)
+    grad_up_act = gelu_pull(grad_hidden)[0].astype(jnp.bfloat16)
+    grad_normed_two = dot_nt(grad_up_act, up_full)
+    grad_middle_norm, grad_scale_two, grad_shift_two = norm_back(grad_normed_two, middle, inverse_two, scale_two)
+    grad_middle = grad_out + grad_middle_norm
+    grad_middle_low = grad_middle.astype(jnp.bfloat16)
+    grad_attended = dot_nt(out_full, grad_middle_low).astype(jnp.bfloat16)
+    grad_pair = lax.all_to_all(grad_attended.reshape(seq, PAIR, frames), "seq", 0, 0)
+    down_tile = scatter_sum(dot_tn(hidden, grad_low))
+    up_tile = scatter_sum(dot_tn(normed_two, grad_up_act))
+    out_tile = scatter_sum(dot_nn(attended, grad_middle_low))
+
+    grad_projected = attend_pair_back(ends, qt, grad_pair, attended_wide, total, keys, values, kt, cos_all, sin_all)
+    grad_local = lax.all_to_all(grad_projected, "seq", 0, 0)
+    pair_all = lax.all_gather(pair_tile, ("dp", "seq"), axis=0).reshape(dp, seq, width // dp, 3 * PAIR)
+    pair_all = pair_all.transpose(0, 2, 1, 3).reshape(width, 3 * width)
+    grad_normed_one = lax.dot_general(
+        grad_local.reshape(3 * width, frames), pair_all, (((0,), (1,)), ((), ())),
+        preferred_element_type=jnp.float32,
+    )
+    grad_pair_weight = jnp.einsum(
+        "icf,ifd->cd", grad_projected, normed_all, preferred_element_type=jnp.float32
+    )
+    grad_pair_tile = lax.psum_scatter(
+        grad_pair_weight.astype(jnp.bfloat16), "dp", scatter_dimension=1, tiled=True
+    )
+    qkv_tile = stored_columns(grad_pair_tile.T, seq).astype(jnp.float32)
+    grad_stream_norm, grad_scale_one, grad_shift_one = norm_back(grad_normed_one, stream, inverse_one, scale_one)
+    grad_stream = (grad_middle + grad_stream_norm).astype(jnp.bfloat16)
+    grad_joined = dot_nt(grad_stream, skip_full)
+    skip_tile = scatter_sum(dot_tn(joined, grad_stream))
+    grad_modulation = jnp.concatenate([grad_scale_one, grad_shift_one, grad_scale_two, grad_shift_two])
+    grad_modulation = lax.psum_scatter(grad_modulation, "seq", scatter_dimension=0, tiled=True)
+    grad_modulation = lax.all_gather(grad_modulation[None], "dp", axis=0, tiled=True)
+    ada_tile = lax.dot_general(
+        embed_part.astype(jnp.float32), grad_modulation, (((0,), (0,)), ((), ())),
+        precision=lax.Precision.HIGHEST,
+    )
+    return (
+        layer_output[None],
+        grad_joined[None, :, :width],
+        grad_joined[None, :, width:],
+        skip_tile,
+        ada_tile,
+        qkv_tile,
+        out_tile,
+        up_tile,
+        down_tile,
+    )
+
+
 def solution(mesh):
     in_specs = (
         P("dp", "seq", None),
@@ -392,4 +833,7 @@
         P("dp", "seq"),
         P("dp", "seq"),
     )
-    return jax.shard_map(local, mesh=mesh, in_specs=in_specs, out_specs=out_specs, check_vma=False)
+    seq_size = mesh.shape["seq"]
+    paired = H == 2 * seq_size and seq_size % 3 != 0
+    body = local_paired if paired else local_general
+    return jax.shard_map(body, mesh=mesh, in_specs=in_specs, out_specs=out_specs, check_vma=False)

time: 1590 us -> 1050 us (0.66)
  waiting for transfers between devices: 942 us -> 549 us
  matrix products: 412 us -> 103 us
  Pallas kernels: 0 us -> 85.6 us
  blocking collectives: 36.2 us -> 118 us
  other arithmetic: 91.7 us -> 20.1 us
  local copies, waits for them, and re-layouts: 86.1 us -> 125 us
  starting transfers between devices: 2.22 us -> 20.8 us
    dot_general x28 -> x16, matrix products: 412 us -> 103 us  [the longest x4 28.5 us: dot_nn(): lax.dot_general(a, b, (((1,), (0,)), ((), ())), preferred_element_type=jn...]
    reduce_scatter x10 -> x6, waiting for transfers between devices: 358 us -> 162 us  [the longest x1 88 us: scatter_sum(): lax.psum_scatter(partial_sum.astype(jnp.bfloat16), 'seq', scatter_dimensi...]
    all_gather x11 -> x6, waiting for transfers between devices: 382 us -> 229 us  [the longest x4 184 us: gather_tiles(): lax.all_gather(tile, ('dp', 'seq'), axis=0).reshape(dp, seq, rows, columns)]
    unnamed x29 -> x18, waiting for transfers between devices: 202 us -> 97.7 us
    pallas_call x0 -> x3, Pallas kernels: none -> 85.6 us  [the longest x1 45.5 us: attend_pair_back(): pl.pallas_call(partial(attend_back_kernel, size=size, length=length, chun...]
    all_to_all x0 -> x2, waiting for transfers between devices: none -> 59.7 us  [the longest x1 59.7 us: local_paired(): grad_local = lax.all_to_all(grad_projected, 'seq', 0, 0)]
    reduce_sum x5 -> x1, other arithmetic: 45.3 us -> 0.68 us  [local_paired(): end_a = jnp.sum((segments < 1).astype(jnp.int32))]
    reshape x1 -> x5, local copies, waits for them, and re-layouts: 1.84 us -> 43.3 us  [the longest x4 33.2 us: gather_tiles(): lax.all_gather(tile, ('dp', 'seq'), axis=0).reshape(dp, seq, rows, columns)]
  transfers between devices with their start and end apart: 25 -> 23, of which waited for: 21 -> 13; matrix products, arithmetic and copies ran while one was open for 28% -> 21% of each run, Pallas kernels for 0% -> 8%
where the time goes in v1:
time: 1050 us; the launch traced here: 1040 us
  waiting for transfers between devices  549 us (52%)
  local copies, waits for them, and re-layouts  125 us (12%)
  blocking collectives  118 us (11%)
  matrix products  103 us (10%)
  Pallas kernels  85.6 us (8%)
  starting transfers between devices  20.8 us (2%)
  between operations  20.6 us (2%)
  other arithmetic  20.1 us (2%)
    all_gather x4, waiting for transfers between devices, gather_tiles(): lax.all_gather(tile, ('dp', 'seq'), axis=0).reshape(dp, seq, rows, columns)  184 us
    unnamed x18, waiting for transfers between devices  97.7 us
    reduce_scatter x1, waiting for transfers between devices, scatter_sum(): lax.psum_scatter(partial_sum.astype(jnp.bfloat16), 'seq', scatter_dimensi...  88 us
    unnamed x101, local copies, waits for them, and re-layouts  74.6 us
    all_to_all x1, waiting for transfers between devices, local_paired(): grad_local = lax.all_to_all(grad_projected, 'seq', 0, 0)  59.7 us
    reduce_scatter x4, waiting for transfers between devices, scatter_sum(): lax.psum_scatter(over_seq.astype(jnp.bfloat16), 'dp', scatter_dimension=0...  49.3 us
    pallas_call x1, Pallas kernels, attend_pair_back(): pl.pallas_call(partial(attend_back_kernel, size=size, length=length, chun...  45.5 us
    all_gather x1, waiting for transfers between devices, local_paired(): normed_all = lax.all_gather(normed_one, 'seq', axis=0)  45.2 us
  transfers between devices with their start and end apart: 23, of which 13 were waited for; matrix products, arithmetic and copies ran while one was open for 21% of the time, Pallas kernels for 8%

profile of v1, /device:TPU:0, one launch (start us, length us, event | category | flops | bytes accessed | tf_op | source)
XLA Modules:
  0.0 1042.1 jit_solution(7341781277521748396)
XLA Ops:
  9.2 9.7 all-gather.7
  19.7 9.2 all-reduce
  29.6 12.8 %all_gather.51 = f32[1,4096]{1,0:T(1,128)S(1)} all-gather(f32[1,512]{1,0:T(1,128)S(1)} %constant_dynamic-slice_fusion.2), channel_id=1, replica_groups=mesh['dp'=4,'seq'=8] {'seq'}, dimensions={1}, use_global_device_ids=true | all-gather | bytes 18432 | tf_op jit(solution)/shard_map/all_gather | solution.py:728
  42.4 33.5 %all-gather.16.cloned.1.call-done = bf16[16384,128]{1,0:T(8,128)(2,1)} async-done(((bf16[512,128]{1,0:T(8,128)(2,1)}), bf16[16384,128]{1,0:T(8,128)(2,1)}) %all-gather.16.cloned.1.call-update) | async-done | bytes 4194320 | tf_op jit(solution)/shard_map/all_gather | solution.py:673
  76.0 5.0 copy.39
  81.0 2.4 multiply_reduce_fusion.5
  88.9 2.7 collective-permute-start.1
  91.7 3.7 collective-permute-start.2
  102.7 1.9 multiply_sine_fusion
  106.0 16.2 %all_gather.54 = bf16[1024,384]{0,1:T(8,128)(2,1)S(1)} all-gather(bf16[256,384]{0,1:T(8,128)(2,1)S(1)} %pad_maximum_fusion.3), channel_id=1, replica_groups=mesh['dp'=4,'seq'=8] {'dp'}, dimensions={0}, use_global_device_ids=true | all-gather | bytes 983040 | tf_op jit(solution)/shard_map/all_gather | solution.py:736
  122.2 45.2 %all-gather.18.cloned.1.call-done = bf16[4096,1024]{1,0:T(8,128)(2,1)} async-done(((bf16[512,1024]{1,0:T(8,128)(2,1)}), bf16[4096,1024]{1,0:T(8,128)(2,1)}) %all-gather.18.cloned.1.call-update) | async-done | bytes 8388624 | tf_op jit(solution)/shard_map/all_gather | solution.py:741
  167.4 3.4 copy-done.2
  170.8 6.1 project_pair.1
  177.0 34.0 %attend_pair.1 = (bf16[8,128,512]{2,1,0:T(8,128)(2,1)}, f32[8,128,512]{2,1,0:T(8,128)S(1)}, f32[8,2,512]{2,1,0:T(2,128)S(1)}) custom-call(s32[2]{0:T(128)S(1)} %pad_add_fusion.ends_ref, bf16[8,128,512]{2,1,0:T(8,128)(2,1)S(1)} %get-tuple-element.17.qt_ref, bf16[4096,128]{1,0:T(8,128)(2,1)S(1)} %get-tuple-element.18.k_ref, ...), custom_call_target="tpu_custom_call" | custom-call | flops 8589934592 | bytes 7340032 | tf_op jit(solution)/shard_map/attend_pair/pallas_call | solution.py:516
  212.4 3.6 all-to-all-start
  217.2 3.8 compare_select_fusion.4
  221.0 5.7 all-gather.20.cloned.1.call-done
  226.8 4.3 copy.43
  231.0 78.2 %all-gather.24.cloned.1.call-done = bf16[32768,128]{1,0:T(8,128)(2,1)} async-done(((bf16[1024,128]{1,0:T(8,128)(2,1)}), bf16[32768,128]{1,0:T(8,128)(2,1)}) %all-gather.24.cloned.1.call-update) | async-done | bytes 8388624 | tf_op jit(solution)/shard_map/all_gather | solution.py:673
  309.3 12.1 %copy.45 = bf16[4,8,1024,128]{3,1,2,0:T(8,128)(2,1)} copy(bf16[4,8,1024,128]{3,2,1,0:T(8,128)(2,1)} %bitcast.154) | data formatting | bytes 16777216 | tf_op jit(solution)/shard_map/reshape | solution.py:673
  321.4 66.8 %all-gather.22.cloned.1.call-done = bf16[8192,512]{1,0:T(8,128)(2,1)} async-done(((bf16[256,512]{1,0:T(8,128)(2,1)}), bf16[8192,512]{1,0:T(8,128)(2,1)}) %all-gather.22.cloned.1.call-update) | async-done | bytes 8388624 | tf_op jit(solution)/shard_map/all_gather | solution.py:673
  388.1 11.9 %copy.44 = bf16[4,8,256,512]{3,1,2,0:T(8,128)(2,1)} copy(bf16[4,8,256,512]{3,2,1,0:T(8,128)(2,1)} %bitcast.155) | data formatting | bytes 16777216 | tf_op jit(solution)/shard_map/reshape | solution.py:673
  400.0 12.2 %copy.62 = bf16[128,8,8,512]{3,1,2,0:T(8,128)(2,1)} copy(bf16[128,8,8,512]{3,2,1,0:T(8,128)(2,1)} %bitcast.146) | data formatting | bytes 16777216
  412.2 4.0 multiply_reduce_fusion.4
  416.3 11.3 %fusion.66 = f32[512,4096]{1,0:T(8,128)} fusion(bf16[1024,4096]{1,0:T(8,128)(2,1)} %bitcast.156, f32[512,1024]{1,0:T(8,128)S(1)} %get-tuple-element.93, f32[1024]{0:T(1024)S(1)} %bitcast.190, f32[1024]{0:T(1024)S(1)} %bitcast.181, f32[512]{0:T(512)S(1)} %add_rsqrt_fusion), kind=kOutput, calls=%fused_computation.108 | convolution fusion | flops 4297064448 | bytes 18884608 | tf_op jit(solution)/shard_map/dot_general | solution.py:376
  427.6 12.7 %fusion.6 = bf16[512,4096]{1,0:T(8,128)(2,1)} fusion(f32[512,4096]{1,0:T(8,128)} %fusion.66, bf16[512,8,8,128]{3,2,1,0:T(8,128)(2,1)S(1)} %bitcast.153, bf16[1,512,1024]{2,1,0:T(8,128)(2,1)S(1)} %copy-done.21, f32[512]{0:T(512)S(1)} %fusion.61), kind=kOutput, calls=%fused_computation.8 | convolution fusion | flops 4338483200 | bytes 22022144 | tf_op jit(solution)/shard_map/dot_general | solution.py:380
  440.3 7.9 multiply_reduce_fusion
  450.2 2.3 fusion.39
  454.0 33.8 %all_to_all.15.gt_ref = bf16[8,128,512]{2,1,0:T(8,128)(2,1)S(1)} all-to-all(bf16[8,128,512]{2,1,0:T(8,128)(2,1)S(1)} %bitcast.166), channel_id=1, replica_groups=mesh['dp'=4,'seq'=8] {'seq'}, dimensions={0} | all-to-all | bytes 2097152 | tf_op jit(solution)/shard_map/all_to_all | solution.py:765
  491.5 1.6 copy-done.10
  493.1 45.5 %attend_pair_back.1 = bf16[8,384,512]{2,1,0:T(8,128)(2,1)} custom-call(s32[2]{0:T(128)S(1)} %pad_add_fusion.ends_ref, bf16[8,128,512]{2,1,0:T(8,128)(2,1)S(1)} %get-tuple-element.17.qt_ref, bf16[8,128,512]{2,1,0:T(8,128)(2,1)S(1)} %all_to_all.15.gt_ref, f32[8,128,512]{2,1,0:T(8,128)S(1)} %copy-done.10, f32[8,2,512]{2,1,0:T(2,128)S(1)} %get-tuple-element.22.total_ref, ...), custom_call_target="tpu_custom_call" | custom-call | flops 21474836480 | bytes 15728640 | tf_op jit(solution)/shard_map/attend_pair_back/pallas_call | solution.py:609
  538.6 4.7 all-to-all-start.2
  543.4 2.6 convolution_convert_fusion.3
  545.9 3.9 copy.51
  550.0 7.6 copy.64
  557.6 10.1 copy.47
  567.7 7.2 copy.65
  574.8 59.7 %all-to-all-done.2 = bf16[8,384,512]{2,1,0:T(8,128)(2,1)} async-done(((bf16[8,384,512]{2,1,0:T(8,128)(2,1)}), bf16[8,384,512]{2,1,0:T(8,128)(2,1)}, u32[]{:S(2)}, u32[]{:S(2)}) %all-to-all-start.2) | async-done | bytes 3145760 | tf_op jit(solution)/shard_map/all_to_all | solution.py:771
  634.5 9.0 multiply_reduce_fusion.1
  645.1 4.5 convolution_convert_fusion.2
  649.6 6.5 copy.49
  657.6 9.1 convolution_convert_fusion.1
  667.0 8.8 bitcast_convert_fusion
  675.9 10.4 convolution_convert_fusion
  686.2 11.4 %copy.53 = bf16[4096,1024]{0,1:T(8,128)(2,1)} copy(bf16[4096,1024]{1,0:T(8,128)(2,1)} %convolution_convert_fusion) | data formatting | bytes 16777216
  697.7 1.8 copy.52
  699.6 8.7 reduce-scatter.28.cloned.1.call-done
  708.3 2.0 copy.50
  710.4 88.0 %reduce-scatter.22.cloned.1.call-done = bf16[1024,512]{1,0:T(8,128)(2,1)} async-done(((bf16[1024,4096]{1,0:T(8,128)(2,1)}), bf16[1024,512]{1,0:T(8,128)(2,1)}) %reduce-scatter.22.cloned.1.call-update) | async-done | bytes 1048592 | tf_op jit(solution)/shard_map/reduce_scatter | solution.py:680
  801.0 25.2 %reduce-scatter.18.cloned.1.call-done = bf16[384,256]{1,0:T(8,128)(2,1)} async-done(((bf16[384,1024]{1,0:T(8,128)(2,1)}), bf16[384,256]{1,0:T(8,128)(2,1)}) %reduce-scatter.18.cloned.1.call-update) | async-done | bytes 196624 | tf_op jit(solution)/shard_map/reduce_scatter | solution.py:781
  827.1 3.4 collective-permute-start.5
  831.8 86.3 %reduce-scatter.32.cloned.1.call-done = bf16[128,4096]{1,0:T(8,128)(2,1)} async-done(((bf16[1024,4096]{1,0:T(8,128)(2,1)}), bf16[128,4096]{1,0:T(8,128)(2,1)}) %reduce-scatter.32.cloned.1.call-update) | async-done | bytes 1048592
  918.1 2.3 copy.54
  920.4 12.3 %fusion.42 = bf16[1,512,1024]{2,1,0:T(8,128)(2,1)} fusion(f32[512,1024]{1,0:T(8,128)S(1)} %copy-done.18, bf16[512,8,8,128]{3,2,1,0:T(8,128)(2,1)} %bitcast.150, f32[512,4096]{1,0:T(8,128)} %fusion.66), kind=kOutput, calls=%fused_computation.55 | convolution fusion | flops 4314890240 | bytes 19922944 | tf_op jit(solution)/shard_map/dot_general | solution.py:376
  933.7 10.2 reduce-scatter.20.cloned.1.call-done
  946.1 28.0 %all-reduce.1 = f32[4096]{0:T(1024)S(1)} all-reduce(f32[4096]{0:T(1024)S(1)} %pad_maximum_fusion.4), channel_id=12, replica_groups=mesh['dp'=4,'seq'=8] {'seq'}, use_global_device_ids=true, to_apply=%region_13.14.clone | all-reduce | flops 4096 | bytes 32768
  974.2 8.4 all-gather.8
  983.8 4.6 fusion.13
  988.5 2.6 slice_bitcast_fusion
  991.1 1.6 convert_element_type.118
  992.7 10.1 reduce-scatter.24.cloned.1.call-done
  1002.8 1.8 convert_element_type.124
  1004.6 28.9 %reduce-scatter.26.cloned.1.call-done = bf16[1024,128]{1,0:T(8,128)(2,1)} async-done(((bf16[4096,128]{1,0:T(8,128)(2,1)}), bf16[1024,128]{1,0:T(8,128)(2,1)}) %reduce-scatter.26.cloned.1.call-update) | async-done | bytes 262160 | tf_op jit(solution)/shard_map/reduce_scatter | solution.py:683
  1033.6 1.8 convert_element_type.127
  (163 shorter events, 34.7 us)
Async XLA Ops:
  7.2 12.4 %copy-start = (bf16[256,512]{1,0:T(8,128)(2,1)S(1)}, bf16[256,512]{1,0:T(8,128)(2,1)}, u32[]{:S(2)}) copy-start(bf16[256,512]{1,0:T(8,128)(2,1)} %param.23) | copy-start | bytes 786436
  7.2 68.8 %all-gather.16.cloned.1.call-start = ((), (), s32[]{:S(2)}) async-start(), calls=%async_computation.18 | async-start | bytes 4325376 | tf_op jit(solution)/shard_map/all_gather | solution.py:673
  7.9 159.5 %all-gather.18.cloned.1.call-start = ((), (), s32[]{:S(2)}) async-start(), calls=%async_computation.19 | async-start | bytes 9437184 | tf_op jit(solution)/shard_map/all_gather | solution.py:741
  75.9 5.1 copy-start.33
  75.9 5.1 copy-start.35
  81.0 2.4 copy-start.15
  83.4 1.3 copy-start.13
  83.5 4.5 copy-start.27
  83.5 17.2 %copy-start.28 = (s32[1,4096]{1,0:T(1,128)S(1)}, s32[1,4096]{1,0:T(1,128)}, u32[]{:S(2)}) copy-start(s32[1,4096]{1,0:T(1,128)} %param.18) | copy-start | bytes 49156
  86.1 140.7 %all-gather.20.cloned.1.call-start = ((), (), s32[]{:S(2)}) async-start(), calls=%async_computation.20 | async-start | bytes 2162688 | tf_op jit(solution)/shard_map/all_gather | solution.py:673
  86.8 222.5 %all-gather.24.cloned.1.call-start = ((), (), s32[]{:S(2)}) async-start(), calls=%async_computation.22 | async-start | bytes 8650752 | tf_op jit(solution)/shard_map/all_gather | solution.py:673
  87.4 300.7 %all-gather.22.cloned.1.call-start = ((), (), s32[]{:S(2)}) async-start(), calls=%async_computation.21 | async-start | bytes 8650752 | tf_op jit(solution)/shard_map/all_gather | solution.py:673
  88.1 17.8 %collective-permute-start = (bf16[256,128]{0,1:T(8,128)(2,1)S(1)}, bf16[256,128]{0,1:T(8,128)(2,1)S(1)}, u32[]{:S(2)}, u32[]{:S(2)}) collective-permute-start(bf16[256,128]{0,1:T(8,128)(2,1)S(1)} %copy.57), channel_id=1, source_target_pairs={{0,0},{1,3},{2,6},{3,1},{4,4},{5,7},{6,2},{7,5},{8,8},{9,11},{10,1... | collective-permute-start | bytes 196616 | tf_op jit(solution)/shard_map/ppermute | solution.py:647
  88.9 17.0 %collective-permute-start.1 = (bf16[256,128]{0,1:T(8,128)(2,1)S(1)}, bf16[256,128]{0,1:T(8,128)(2,1)S(1)}, u32[]{:S(2)}, u32[]{:S(2)}) collective-permute-start(bf16[256,128]{0,1:T(8,128)(2,1)S(1)} %copy.58), channel_id=1, source_target_pairs={{0,1},{1,4},{2,7},{3,2},{4,5},{5,0},{6,3},{7,6},{8,9},{9,12},{10,1... | collective-permute-start | bytes 196616 | tf_op jit(solution)/shard_map/ppermute | solution.py:647
  91.7 14.2 %collective-permute-start.2 = (bf16[256,128]{0,1:T(8,128)(2,1)S(1)}, bf16[256,128]{0,1:T(8,128)(2,1)S(1)}, u32[]{:S(2)}, u32[]{:S(2)}) collective-permute-start(bf16[256,128]{0,1:T(8,128)(2,1)S(1)} %copy.59), channel_id=1, source_target_pairs={{0,2},{1,5},{2,0},{3,3},{4,6},{5,1},{6,4},{7,7},{8,10},{9,13},{10,... | collective-permute-start | bytes 196616 | tf_op jit(solution)/shard_map/ppermute | solution.py:647
  106.0 70.9 %copy-start.20 = (bf16[256,384]{0,1:T(8,128)(2,1)}, bf16[256,384]{0,1:T(8,128)(2,1)S(1)}, u32[]{:S(2)}) copy-start(bf16[256,384]{0,1:T(8,128)(2,1)S(1)} %pad_maximum_fusion.3) | copy-start | bytes 589828
  167.4 3.4 copy-start.2
  176.9 34.1 %copy-start.3 = (bf16[128,4096]{1,0:T(8,128)(2,1)}, bf16[128,4096]{1,0:T(8,128)(2,1)S(1)}, u32[]{:S(2)}) copy-start(bf16[128,4096]{1,0:T(8,128)(2,1)S(1)} %get-tuple-element.24.kt_ref) | copy-start | bytes 3145732
  176.9 34.0 %copy-start.5 = (bf16[4096,128]{1,0:T(8,128)(2,1)}, bf16[4096,128]{1,0:T(8,128)(2,1)S(1)}, u32[]{:S(2)}) copy-start(bf16[4096,128]{1,0:T(8,128)(2,1)S(1)} %get-tuple-element.18.k_ref) | copy-start | bytes 3145732
  176.9 34.0 %copy-start.7 = (bf16[4096,128]{1,0:T(8,128)(2,1)}, bf16[4096,128]{1,0:T(8,128)(2,1)S(1)}, u32[]{:S(2)}) copy-start(bf16[4096,128]{1,0:T(8,128)(2,1)S(1)} %get-tuple-element.23.v_ref) | copy-start | bytes 3145732
  176.9 39.0 %copy-start.31 = (s32[1,3]{1,0:T(1,128)S(1)}, s32[1,3]{1,0:T(1,128)}, u32[]{:S(2)}) copy-start(s32[1,3]{1,0:T(1,128)} %param.20) | copy-start | bytes 40
  177.0 39.6 %copy-start.32 = (s32[1,3]{1,0:T(1,128)S(1)}, s32[1,3]{1,0:T(1,128)}, u32[]{:S(2)}) copy-start(s32[1,3]{1,0:T(1,128)} %param.19) | copy-start | bytes 40
  211.0 1.4 copy-start.9
  212.4 199.9 %all-to-all-start = ((bf16[8,128,512]{2,1,0:T(8,128)(2,1)}), bf16[8,128,512]{2,1,0:T(8,128)(2,1)S(1)}, u32[]{:S(2)}, u32[]{:S(2)}) async-start(bf16[8,128,512]{2,1,0:T(8,128)(2,1)} %get-tuple-element.20), calls=%async_computation | async-start | bytes 2097152 | tf_op jit(solution)/shard_map/all_to_all | solution.py:744
  215.9 334.0 %all-gather.26.cloned.1.call-start = ((), (), s32[]{:S(2)}) async-start(), calls=%async_computation.23 | async-start | bytes 6488064 | tf_op jit(solution)/shard_map/all_gather | solution.py:772
  412.2 4.0 copy-start.23
  412.2 15.3 %slice-start = ((s8[8388608]{0:T(1024)(128)(4,1)}), s8[4194304]{0:T(1024)(128)(4,1)S(1)}, s32[]{:S(2)}) async-start(s8[8388608]{0:T(1024)(128)(4,1)} %bitcast.151), calls=%async_computation.27 | async-start | bytes 8388608
  416.2 11.3 %copy-start.16 = (f32[512,1024]{1,0:T(8,128)}, f32[512,1024]{1,0:T(8,128)S(1)}, u32[]{:S(2)}) copy-start(f32[512,1024]{1,0:T(8,128)S(1)} %get-tuple-element.93) | copy-start | bytes 6291460
  416.3 11.3 %slice-start.1 = ((s8[8388608]{0:T(1024)(128)(4,1)}), s8[4194304]{0:T(1024)(128)(4,1)S(1)}, s32[]{:S(2)}) async-start(s8[8388608]{0:T(1024)(128)(4,1)} %bitcast.151), calls=%async_computation.28 | async-start | bytes 8388608
  416.3 11.3 %copy-start.21 = (bf16[1,512,1024]{2,1,0:T(8,128)(2,1)S(1)}, bf16[1,512,1024]{2,1,0:T(8,128)(2,1)}, u32[]{:S(2)}) copy-start(bf16[1,512,1024]{2,1,0:T(8,128)(2,1)} %param.21) | copy-start | bytes 3145732
  416.3 24.0 %slice-start.2 = ((s8[8388608]{0:T(1024)(128)(4,1)}), s8[4194304]{0:T(1024)(128)(4,1)S(1)}, s32[]{:S(2)}) async-start(s8[8388608]{0:T(1024)(128)(4,1)} %bitcast.157), calls=%async_computation.29 | async-start | bytes 8388608
  427.6 12.7 %slice-start.3 = ((s8[8388608]{0:T(1024)(128)(4,1)}), s8[4194304]{0:T(1024)(128)(4,1)S(1)}, s32[]{:S(2)}) async-start(s8[8388608]{0:T(1024)(128)(4,1)} %bitcast.157), calls=%async_computation.30 | async-start | bytes 8388608
  440.3 7.9 copy-start.17
  448.2 2.1 copy-start.19
  448.9 1.3 copy-start.11
  487.8 1.2 copy-start.4
  489.0 1.2 copy-start.6
  490.3 1.2 copy-start.8
  491.5 1.6 copy-start.10
  538.6 4.8 copy-start.12
  538.6 4.8 copy-start.24
  538.6 95.9 %all-to-all-start.2 = ((bf16[8,384,512]{2,1,0:T(8,128)(2,1)}), bf16[8,384,512]{2,1,0:T(8,128)(2,1)}, u32[]{:S(2)}, u32[]{:S(2)}) async-start(bf16[8,384,512]{2,1,0:T(8,128)(2,1)} %attend_pair_back.1), calls=%async_computation.2 | async-start | bytes 6291456 | tf_op jit(solution)/shard_map/all_to_all | solution.py:771
  543.3 154.4 %reduce-scatter.30.cloned.1.call-start = ((), (), s32[]{:S(2)}) async-start(), calls=%async_computation.25 | async-start | bytes 2359296
  549.9 158.4 %reduce-scatter.28.cloned.1.call-start = ((), (), s32[]{:S(2)}) async-start(), calls=%async_computation.24 | async-start | bytes 4718592
  634.5 9.0 copy-start.14
  643.5 1.6 copy-start.34
  643.5 1.6 copy-start.36
  644.1 1.0 copy-start.25
  656.1 1.6 copy-start.18
  656.1 142.3 %reduce-scatter.22.cloned.1.call-start = ((), (), s32[]{:S(2)}) async-start(), calls=%async_computation.15 | async-start | bytes 9437184 | tf_op jit(solution)/shard_map/reduce_scatter | solution.py:680
  666.8 9.1 copy-start.22
  666.8 159.4 %reduce-scatter.18.cloned.1.call-start = ((), (), s32[]{:S(2)}) async-start(), calls=%async_computation.13 | async-start | bytes 983040 | tf_op jit(solution)/shard_map/reduce_scatter | solution.py:781
  675.8 242.3 %reduce-scatter.32.cloned.1.call-start = ((), (), s32[]{:S(2)}) async-start(), calls=%async_computation.26 | async-start | bytes 9437184
  697.6 102.1 %copy-start.37 = (u32[32]{0:T(128)S(1)}, u32[32]{0:T(128)}, u32[]{:S(2)}) copy-start(u32[32]{0:T(128)} %constant.90) | copy-start | bytes 388
  697.6 246.3 %reduce-scatter.20.cloned.1.call-start = ((), (), s32[]{:S(2)}) async-start(), calls=%async_computation.14 | async-start | bytes 327680 | tf_op jit(solution)/shard_map/reduce_scatter | solution.py:683
  699.5 291.5 %reduce-scatter.16.cloned.1.call-start = ((), (), s32[]{:S(2)}) async-start(), calls=%async_computation.12 | async-start | bytes 655360 | tf_op jit(solution)/shard_map/reduce_scatter | solution.py:683
  710.4 292.5 %reduce-scatter.24.cloned.1.call-start = ((), (), s32[]{:S(2)}) async-start(), calls=%async_computation.16 | async-start | bytes 1310720 | tf_op jit(solution)/shard_map/reduce_scatter | solution.py:683
  798.4 235.2 %reduce-scatter.26.cloned.1.call-start = ((), (), s32[]{:S(2)}) async-start(), calls=%async_computation.17 | async-start | bytes 1310720 | tf_op jit(solution)/shard_map/reduce_scatter | solution.py:683
  827.1 105.6 %collective-permute-start.5 = (bf16[256,128]{0,1:T(8,128)(2,1)S(1)}, bf16[256,128]{0,1:T(8,128)(2,1)S(1)}, u32[]{:S(2)}, u32[]{:S(2)}) collective-permute-start(bf16[256,128]{0,1:T(8,128)(2,1)S(1)} %get-tuple-element.66), channel_id=1, source_target_pairs={{2,0},{5,1},{0,2},{3,3},{6,4},{1,5},{4,6},{7,7},{10,8},{13,9},{8,1... | collective-permute-start | bytes 196616 | tf_op jit(solution)/shard_map/ppermute | solution.py:666
  830.5 102.2 %collective-permute-start.4 = (bf16[256,128]{0,1:T(8,128)(2,1)S(1)}, bf16[256,128]{0,1:T(8,128)(2,1)S(1)}, u32[]{:S(2)}, u32[]{:S(2)}) collective-permute-start(bf16[256,128]{0,1:T(8,128)(2,1)S(1)} %get-tuple-element.65), channel_id=1, source_target_pairs={{1,0},{4,1},{7,2},{2,3},{5,4},{0,5},{3,6},{6,7},{9,8},{12,9},{15,1... | collective-permute-start | bytes 196616 | tf_op jit(solution)/shard_map/ppermute | solution.py:666
  831.1 101.6 %collective-permute-start.3 = (bf16[256,128]{0,1:T(8,128)(2,1)S(1)}, bf16[256,128]{0,1:T(8,128)(2,1)S(1)}, u32[]{:S(2)}, u32[]{:S(2)}) collective-permute-start(bf16[256,128]{0,1:T(8,128)(2,1)S(1)} %get-tuple-element.64), channel_id=1, source_target_pairs={{0,0},{3,1},{6,2},{1,3},{4,4},{7,5},{2,6},{5,7},{8,8},{11,9},{14,1... | collective-permute-start | bytes 196616 | tf_op jit(solution)/shard_map/ppermute | solution.py:666
  920.4 62.2 %copy-start.30 = (bf16[4,1,256]{2,1,0:T(2,128)(2,1)S(1)}, bf16[4,1,256]{2,1,0:T(2,128)(2,1)}, u32[]{:S(2)}) copy-start(bf16[4,1,256]{2,1,0:T(2,128)(2,1)} %copy-done.29) | copy-start | bytes 6148
  920.4 63.4 %copy-start.26 = (bf16[512,1024]{1,0:T(8,128)(2,1)S(1)}, bf16[512,1024]{1,0:T(8,128)(2,1)}, u32[]{:S(2)}) copy-start(bf16[512,1024]{1,0:T(8,128)(2,1)} %copy-done.25) | copy-start | bytes 3145732
  983.8 51.5 %copy-start.1 = (bf16[256,512]{1,0:T(8,128)(2,1)S(1)}, bf16[256,512]{1,0:T(8,128)(2,1)}, u32[]{:S(2)}) copy-start(bf16[256,512]{1,0:T(8,128)(2,1)} %param.23) | copy-start | bytes 786436
  (1 other events, 0.6 us)
Sparse Core Ops, SparseCore 0:
  11.0 64.8 all-gather.15
  86.2 81.1 all-gather.17
  170.4 56.3 all-gather.19
  229.6 79.6 all-gather.23
  312.1 75.9 all-gather.21
  391.4 89.5 all-gather.25
  550.0 63.2 reduce-scatter.29
  656.2 52.0 reduce-scatter.27
  710.6 87.7 reduce-scatter.21
  801.7 24.4 reduce-scatter.17
  828.5 89.5 reduce-scatter.31
  921.3 22.5 reduce-scatter.19
  947.5 24.7 reduce-scatter.15
  975.1 27.6 reduce-scatter.23
  1005.8 27.7 reduce-scatter.25

commit v2 on v1

--- a/solution.py
+++ b/solution.py
@@ -667,29 +667,426 @@
     return jnp.concatenate(back, axis=1)
 
 
-def gather_tiles(tile):
-    rows, columns = tile.shape
-    dp, seq = lax.axis_size("dp"), lax.axis_size("seq")
-    pieces = lax.all_gather(tile, ("dp", "seq"), axis=0).reshape(dp, seq, rows, columns)
-    return jnp.swapaxes(pieces, 1, 2).reshape(dp * rows, seq * columns)
-
-
-def scatter_sum(partial_sum):
-    rows, columns = partial_sum.shape
-    dp, seq = lax.axis_size("dp"), lax.axis_size("seq")
-    over_seq = lax.psum_scatter(
-        partial_sum.astype(jnp.bfloat16), "seq", scatter_dimension=1, tiled=True
-    ).astype(jnp.float32)
-    return lax.psum_scatter(
-        over_seq.astype(jnp.bfloat16), "dp", scatter_dimension=0, tiled=True
-    ).astype(jnp.float32)
-
-
-def norm_back(grad, stream, inverse, scale_part):
+def chip_routes(dp, seq):
+    chips = seq // 2
+
+    def flat(move):
+        return [(d * seq + s, move(d, s)) for d in range(dp) for s in range(seq)]
+
+    def along_z(step):
+        return flat(lambda d, s: d * seq + 2 * ((s // 2 + step) % chips) + s % 2)
+
+    return {
+        "x": flat(lambda d, s: (d ^ 1) * seq + s),
+        "y": flat(lambda d, s: (d ^ 2) * seq + s),
+        "xy": flat(lambda d, s: (d ^ 3) * seq + s),
+        "core": flat(lambda d, s: d * seq + (s ^ 1)),
+        "z": [along_z(step) for step in range(1, chips)],
+    }
+
+
+def send(value, route):
+    return lax.ppermute(value, ("dp", "seq"), route)
+
+
+def gather_column(tile, routes):
+    return jnp.stack([tile] + [send(tile, route) for route in routes["z"]])
+
+
+def gather_near(column, route):
+    return jnp.stack([column, send(column, route)])
+
+
+GELU_C = math.sqrt(2.0 / math.pi)
+
+
+def gelu_parts(value):
+    square = value * value
+    slope = jnp.tanh(GELU_C * value * (1.0 + 0.044715 * square))
+    low = 0.5 * (1.0 + slope)
+    derivative = low + 0.5 * value * (1.0 - slope * slope) * (GELU_C * (1.0 + 3 * 0.044715 * square))
+    return value * low, derivative
+
+
+def lanes(parts):
+    return jnp.concatenate(parts, axis=1)
+
+
+def middle_kernel(
+    place_ref, att_ref, stream_ref, low_ref, scale_ref, shift_ref, out_w_ref,
+    up_0, up_1, up_2, up_3, down_0, down_1, down_2, down_3,
+    layer_ref, hidden_ref, grad_up_ref, grad_mid_ref, grad_low_ref, grad_att_ref, sums_ref, turned_ref,
+    up_w, down_w, normed_ref, middle_ref, out_acc, grad_acc, up_sem, down_sem, *, dp, seq,
+):
+    dp_at, chip_at, core_at = place_ref[0], place_ref[1], place_ref[2]
+    chips = seq // 2
+    up_rows, up_cols = up_0.shape[2], up_0.shape[3]
+    down_rows, down_cols = down_0.shape[2], down_0.shape[3]
+
+    def copies():
+        made = []
+        for name, pieces, masks, sems in (
+            ("up", (up_0, up_1, up_2, up_3), (1, 2), up_sem),
+            ("down", (down_0, down_1, down_2, down_3), (2, 1), down_sem),
+        ):
+            for part in range(4):
+                core = core_at if part < 2 else 1 - core_at
+                for step in range(2):
+                    mask = (masks[1] if part % 2 else 0) ^ (masks[0] if step else 0)
+                    row = jnp.bitwise_xor(dp_at, mask)
+                    for back in range(chips):
+                        block = 2 * lax.rem(chip_at + chips - back, chips) + core
+                        if name == "up":
+                            target = up_w.at[block, pl.ds(pl.multiple_of(row * up_rows, up_rows), up_rows), :]
+                        else:
+                            target = down_w.at[
+                                pl.ds(pl.multiple_of(row * down_rows, down_rows), down_rows),
+                                pl.ds(pl.multiple_of(block * down_cols, down_cols), down_cols),
+                            ]
+                        made.append(
+                            pltpu.make_async_copy(
+                                pieces[part].at[step, back], target, sems.at[(part * 2 + step) * chips + back]
+                            )
+                        )
+        return made
+
+    for copy in copies():
+        copy.start()
+    width = stream_ref.shape[1]
+    tile_rows = width // dp
+    middle_ref[...] = stream_ref[...]
+    for row in range(dp):
+        weight = lanes([out_w_ref[row * seq + s] for s in range(seq)])
+        middle_ref[...] += dot_tn(att_ref[row * tile_rows : (row + 1) * tile_rows, :], weight)
+    middle = middle_ref[...]
+    inverse = lax.rsqrt(jnp.mean(middle * middle, axis=-1, keepdims=True) + epsilon)
+    normed = middle * inverse * (1.0 + scale_ref[...]) + shift_ref[...]
+    normed_ref[...] = normed.astype(jnp.bfloat16)
+    turned_ref[...] = normed.T.astype(jnp.bfloat16)
+    for copy in copies():
+        copy.wait()
+    out_acc[...] = jnp.zeros_like(out_acc)
+    grad_acc[...] = jnp.zeros_like(grad_acc)
+
+    @pl.loop(0, seq)
+    def _(block):
+        rows = pl.ds(pl.multiple_of(block * up_cols, up_cols), up_cols)
+        up_weight, down_weight = up_w[block], down_w[rows, :]
+        value, derivative = gelu_parts(dot_nn(normed_ref[...], up_weight))
+        hidden = value.astype(jnp.bfloat16)
+        hidden_ref[:, rows] = hidden
+        out_acc[...] += dot_nn(hidden, down_weight)
+        grad_up = (dot_nt(low_ref[...], down_weight) * derivative).astype(jnp.bfloat16)
+        grad_up_ref[:, rows] = grad_up
+        grad_acc[...] += dot_nt(grad_up, up_weight)
+
+    middle = middle_ref[...]
+    layer_ref[...] = (middle + out_acc[...]).astype(jnp.bfloat16)
+    inverse = lax.rsqrt(jnp.mean(middle * middle, axis=-1, keepdims=True) + epsilon)
+    unit = middle * inverse
+    grad = grad_acc[...]
+    lifted = grad * (1.0 + scale_ref[...])
+    sums_ref[0:1, :] = jnp.sum(grad * unit, axis=0, keepdims=True)
+    sums_ref[1:2, :] = jnp.sum(grad, axis=0, keepdims=True)
+    grad_mid = low_ref[...].astype(jnp.float32) + inverse * (
+        lifted - unit * jnp.mean(lifted * unit, axis=-1, keepdims=True)
+    )
+    grad_mid_ref[...] = grad_mid
+    grad_low_ref[...] = grad_mid.astype(jnp.bfloat16)
+    for row in range(dp):
+        weight = lanes([out_w_ref[row * seq + s] for s in range(seq)])
+        grad_att_ref[row * tile_rows : (row + 1) * tile_rows, :] = dot_nt(weight, grad_low_ref[...]).astype(
+            jnp.bfloat16
+        )
+
+
+def middle_block(place, attended, stream, grad_low, scale, shift, out_tiles, up_pieces, down_pieces, dp, seq):
+    frames, width = stream.shape
+    hidden = up_pieces[0].shape[3] * seq
+    whole = pl.BlockSpec(memory_space=pltpu.VMEM)
+    anywhere = pl.BlockSpec(memory_space=pl.ANY)
+    low, wide = jnp.bfloat16, jnp.float32
+    return pl.pallas_call(
+        partial(middle_kernel, dp=dp, seq=seq),
+        in_specs=[pl.BlockSpec(memory_space=pltpu.SMEM)] + [whole] * 6 + [anywhere] * 8,
+        out_specs=[whole] * 8,
+        out_shape=[
+            jax.ShapeDtypeStruct((frames, width), low),
+            jax.ShapeDtypeStruct((frames, hidden), low),
+            jax.ShapeDtypeStruct((frames, hidden), low),
+            jax.ShapeDtypeStruct((frames, width), wide),
+            jax.ShapeDtypeStruct((frames, width), low),
+            jax.ShapeDtypeStruct((width, frames), low),
+            jax.ShapeDtypeStruct((2, width), wide),
+            jax.ShapeDtypeStruct((width, frames), low),
+        ],
+        scratch_shapes=[
+            pltpu.VMEM((seq, width, hidden // seq), low),
+            pltpu.VMEM((hidden, width), low),
+            pltpu.VMEM((frames, width), low),
+            pltpu.VMEM((frames, width), wide),
+            pltpu.VMEM((frames, width), wide),
+            pltpu.VMEM((frames, width), wide),
+            pltpu.SemaphoreType.DMA((dp * seq,)),
+            pltpu.SemaphoreType.DMA((dp * seq,)),
+        ],
+        compiler_params=pltpu.CompilerParams(vmem_limit_bytes=58 << 20),
+        cost_estimate=pl.CostEstimate(
+            flops=8 * frames * width * hidden + 4 * frames * width * width,
+            bytes_accessed=4 * hidden * width + 24 * frames * width,
+            transcendentals=frames * hidden,
+        ),
+        name="middle_block",
+    )(place, attended, stream, grad_low, scale, shift, out_tiles, *up_pieces, *down_pieces)
+
+
+def entry_kernel(main_ref, side_ref, weight_ref, scale_ref, shift_ref, stream_ref, normed_ref, *, dp, seq):
+    row = pl.program_id(0)
+
+    @pl.when(row == 0)
+    def _():
+        stream_ref[...] = jnp.zeros_like(stream_ref)
+
+    operand = jnp.where(row < dp // 2, main_ref[...], side_ref[...])
+    stream_ref[...] += dot_nn(operand, lanes([weight_ref[s] for s in range(seq)]))
+
+    @pl.when(row == dp - 1)
+    def _():
+        stream = stream_ref[...]
+        inverse = lax.rsqrt(jnp.mean(stream * stream, axis=-1, keepdims=True) + epsilon)
+        normed_ref[...] = (stream * inverse * (1.0 + scale_ref[...]) + shift_ref[...]).astype(jnp.bfloat16)
+
+
+def entry_block(main, side, skip_tiles, scale, shift, dp, seq):
+    frames, width = main.shape
+    rows, columns = skip_tiles.shape[1:]
+    fixed = pl.BlockSpec((1, width), lambda i: (0, 0))
+    return pl.pallas_call(
+        partial(entry_kernel, dp=dp, seq=seq),
+        grid=(dp,),
+        in_specs=[
+            pl.BlockSpec((frames, rows), lambda i: (0, jnp.minimum(i, dp // 2 - 1))),
+            pl.BlockSpec((frames, rows), lambda i: (0, jnp.maximum(i - dp // 2, 0))),
+            pl.BlockSpec((seq, rows, columns), lambda i: (i, 0, 0)),
+            fixed,
+            fixed,
+        ],
+        out_specs=[pl.BlockSpec((frames, width), lambda i: (0, 0))] * 2,
+        out_shape=[
+            jax.ShapeDtypeStruct((frames, width), jnp.float32),
+            jax.ShapeDtypeStruct((frames, width), jnp.bfloat16),
+        ],
+        compiler_params=pltpu.CompilerParams(vmem_limit_bytes=32 << 20),
+        cost_estimate=pl.CostEstimate(
+            flops=4 * frames * width * width, bytes_accessed=14 * frames * width, transcendentals=0
+        ),
+        name="entry_block",
+    )(main, side, skip_tiles, scale, shift)
+
+
+def exit_kernel(
+    projected_ref, pair_ref, stream_ref, grad_mid_ref, scale_ref, grad_ref, turned_ref, sums_ref, normed_ref,
+    *, dp, seq,
+):
+    rows = pair_ref.shape[1]
+    for row in range(dp):
+        weight = lanes([pair_ref[row * seq + s] for s in range(seq)])
+        normed_ref[:, row * rows : (row + 1) * rows] = dot_nn(weight, projected_ref[...]).T
+    grad, stream = normed_ref[...], stream_ref[...]
+    inverse = lax.rsqrt(jnp.mean(stream * stream, axis=-1, keepdims=True) + epsilon)
     unit = stream * inverse
-    lifted = grad * (1.0 + scale_part)
-    grad_stream = inverse * (lifted - unit * jnp.mean(lifted * unit, axis=-1, keepdims=True))
-    return grad_stream, jnp.sum(grad * unit, axis=0), jnp.sum(grad, axis=0)
+    lifted = grad * (1.0 + scale_ref[...])
+    sums_ref[0:1, :] = jnp.sum(grad * unit, axis=0, keepdims=True)
+    sums_ref[1:2, :] = jnp.sum(grad, axis=0, keepdims=True)
+    grad_stream = grad_mid_ref[...] + inverse * (lifted - unit * jnp.mean(lifted * unit, axis=-1, keepdims=True))
+    grad_ref[...] = grad_stream.astype(jnp.bfloat16)
+    turned_ref[...] = grad_stream.T.astype(jnp.bfloat16)
+
+
+def exit_block(projected, pair_tiles, stream, grad_mid, scale, dp, seq):
+    frames, width = stream.shape
+    whole = pl.BlockSpec(memory_space=pltpu.VMEM)
+    return pl.pallas_call(
+        partial(exit_kernel, dp=dp, seq=seq),
+        in_specs=[whole] * 5,
+        out_specs=[whole] * 3,
+        out_shape=[
+            jax.ShapeDtypeStruct((frames, width), jnp.bfloat16),
+            jax.ShapeDtypeStruct((width, frames), jnp.bfloat16),
+            jax.ShapeDtypeStruct((2, width), jnp.float32),
+        ],
+        scratch_shapes=[pltpu.VMEM((frames, width), jnp.float32)],
+        compiler_params=pltpu.CompilerParams(vmem_limit_bytes=40 << 20),
+        cost_estimate=pl.CostEstimate(
+            flops=6 * frames * width * width, bytes_accessed=18 * frames * width + 6 * width * width, transcendentals=0
+        ),
+        name="exit_block",
+    )(projected, pair_tiles, stream, grad_mid, scale)
+
+
+def joined_kernel(grad_ref, weight_ref, main_ref, side_ref, *, dp, seq):
+    row = pl.program_id(0)
+    grad = dot_nt(grad_ref[...], lanes([weight_ref[s] for s in range(seq)]))
+
+    @pl.when(row < dp // 2)
+    def _():
+        main_ref[...] = grad
+
+    @pl.when(row >= dp // 2)
+    def _():
+        side_ref[...] = grad
+
+
+def joined_grads(grad_stream, skip_tiles, dp, seq):
+    frames, width = grad_stream.shape
+    rows, columns = skip_tiles.shape[1:]
+    out = jax.ShapeDtypeStruct((frames, width), jnp.float32)
+    return pl.pallas_call(
+        partial(joined_kernel, dp=dp, seq=seq),
+        grid=(dp,),
+        in_specs=[
+            pl.BlockSpec((frames, width), lambda i: (0, 0)),
+            pl.BlockSpec((seq, rows, columns), lambda i: (i, 0, 0)),
+        ],
+        out_specs=[
+            pl.BlockSpec((frames, rows), lambda i: (0, jnp.minimum(i, dp // 2 - 1))),
+            pl.BlockSpec((frames, rows), lambda i: (0, jnp.maximum(i - dp // 2, 0))),
+        ],
+        out_shape=[out, out],
+        compiler_params=pltpu.CompilerParams(vmem_limit_bytes=32 << 20),
+        cost_estimate=pl.CostEstimate(
+            flops=4 * frames * width * width, bytes_accessed=14 * frames * width, transcendentals=0
+        ),
+        name="joined_grads",
+    )(grad_stream, skip_tiles)
+
+
+def blocks_kernel(place_ref, left_ref, right_ref, *refs, kind, masks, other, chips):
+    chip_at, core_at = place_ref[1], place_ref[2]
+    core = 1 - core_at if other else core_at
+    step = pl.program_id(0)
+    out_refs = refs if other else refs[1:]
+    block = out_refs[0].shape[2] if kind == "turned" else out_refs[0].shape[3]
+    starts = [(2 * lax.rem(chip_at + ahead, chips) + core) * block for ahead in range(chips)]
+    starts = [pl.multiple_of(start, block) for start in starts]
+    if kind == "turned":
+        left = jnp.concatenate([left_ref[pl.ds(start, block), :] for start in starts], axis=0)
+        product = dot_nn(left, right_ref[...])
+        parts = [product[ahead * block : (ahead + 1) * block] for ahead in range(chips)]
+    else:
+        right = lanes([right_ref[:, pl.ds(start, block)] for start in starts])
+        product = dot_nn(left_ref[...], right)
+        parts = [product[:, ahead * block : (ahead + 1) * block] for ahead in range(chips)]
+    if other:
+        for ahead in range(chips):
+            out_refs[0][0, ahead] = parts[ahead].astype(jnp.bfloat16)
+        return
+    parts = [parts[ahead] + refs[0][0, ahead].astype(jnp.float32) for ahead in range(chips)]
+
+    @pl.when(step < 2)
+    def _():
+        for ahead in range(chips):
+            out_refs[0][0, ahead] = parts[ahead].astype(jnp.bfloat16)
+
+    @pl.when(step >= 2)
+    def _():
+        for ahead in range(chips):
+            out_refs[1][0, ahead] = parts[ahead].astype(jnp.bfloat16)
+
+
+def grad_blocks(place, left, right, kind, masks, seq, arrived=None, part=(0, 1)):
+    first, second = masks
+    chips, dp = seq // 2, 4
+    depth = left.shape[1]
+
+    def owner(i, place):
+        return jnp.bitwise_xor(place[0], (i % 2) * second + (i // 2) * first)
+
+    if kind == "turned":
+        columns = right.shape[1] // (dp * part[1])
+        shape = (left.shape[0] // seq, columns)
+        left_spec = pl.BlockSpec(left.shape, lambda i, place: (0, 0))
+        right_spec = pl.BlockSpec((depth, columns), lambda i, place: (0, owner(i, place) * part[1] + part[0]))
+    else:
+        shape = (left.shape[0] // dp, right.shape[1] // seq)
+        left_spec = pl.BlockSpec((shape[0], depth), lambda i, place: (owner(i, place), 0))
+        right_spec = pl.BlockSpec(right.shape, lambda i, place: (0, 0))
+    other = arrived is None
+    one = (1, chips) + shape
+    if other:
+        specs, count = [pl.BlockSpec(one, lambda i, place: (i, 0, 0, 0))], 4
+        extra, operands = [], (left, right)
+    else:
+        specs = [
+            pl.BlockSpec(one, lambda i, place: (jnp.minimum(i, 1), 0, 0, 0)),
+            pl.BlockSpec(one, lambda i, place: (jnp.maximum(i - 2, 0), 0, 0, 0)),
+        ]
+        count = 2
+        extra, operands = [pl.BlockSpec(one, lambda i, place: (i, 0, 0, 0))], (left, right, arrived)
+    return pl.pallas_call(
+        partial(blocks_kernel, kind=kind, masks=masks, other=other, chips=chips),
+        grid_spec=pltpu.PrefetchScalarGridSpec(
+            num_scalar_prefetch=1, grid=(4,), in_specs=[left_spec, right_spec] + extra, out_specs=specs
+        ),
+        out_shape=[jax.ShapeDtypeStruct((count, chips) + shape, jnp.bfloat16)] * len(specs),
+        compiler_params=pltpu.CompilerParams(vmem_limit_bytes=40 << 20),
+        cost_estimate=pl.CostEstimate(
+            flops=2 * dp * chips * shape[0] * shape[1] * depth,
+            bytes_accessed=2 * dp * chips * shape[0] * shape[1] * (1 if other else 2) + 2 * left.size + 2 * right.size,
+            transcendentals=0,
+        ),
+        name="grad_blocks",
+    )(place, *operands)
+
+
+AXIS_MASK = {"x": 1, "y": 2}
+
+
+def wide(value):
+    return value.astype(jnp.float32)
+
+
+def scatter_first(place, left, right, kind, routes, seq, first, second, part=(0, 1)):
+    masks = (AXIS_MASK[first], AXIS_MASK[second])
+    (outgoing,) = grad_blocks(place, left, right, kind, masks, seq, None, part)
+    arrived = send(outgoing, routes["core"])
+    keep, away = grad_blocks(place, left, right, kind, masks, seq, arrived, part)
+    return keep, send(away, routes[first])
+
+
+def scatter_second(state, routes, second):
+    keep, arrived = state
+    back = send((wide(keep[1]) + wide(arrived[1])).astype(jnp.bfloat16), routes[second])
+    return wide(keep[0]) + wide(arrived[0]), back
+
+
+def scatter_last(state, routes):
+    total = state[0] + wide(state[1])
+    low = total.astype(jnp.bfloat16)
+    got = [send(low[ahead + 1], route) for ahead, route in enumerate(routes["z"])]
+    result = total[0]
+    for piece in got:
+        result = result + wide(piece)
+    return result
+
+
+def dp_sum(value, routes, dp):
+    at = lax.axis_index("dp")
+    result = wide(lax.dynamic_index_in_dim(value, at, 0, keepdims=False))
+    for mask, route in ((1, routes["x"]), (2, routes["y"]), (3, routes["xy"])):
+        piece = lax.dynamic_index_in_dim(value, jnp.bitwise_xor(at, mask), 0, keepdims=False)
+        result = result + wide(send(piece, route))
+    return result
+
+
+def dp_gather(tile, routes, dp):
+    at = lax.axis_index("dp")
+    rows = tile.shape[0]
+    full = jnp.zeros((dp * rows, tile.shape[1]), tile.dtype)
+    full = lax.dynamic_update_slice_in_dim(full, tile, at * rows, 0)
+    for mask, route in ((1, routes["x"]), (2, routes["y"]), (3, routes["xy"])):
+        full = lax.dynamic_update_slice_in_dim(full, send(tile, route), jnp.bitwise_xor(at, mask) * rows, 0)
+    return full
 
 
 def local_paired(
@@ -720,6 +1117,12 @@
 
     span_begin = pick(starts)
     inside = jnp.logical_and(local_position >= span_begin, local_position < span_begin + pick(lengths))
+    grad_low = jnp.where(inside[:, None], cotangent[0], jnp.zeros((), jnp.bfloat16))
+    routes = chip_routes(dp, seq)
+    seq_at = lax.axis_index("seq")
+    place = jnp.stack([lax.axis_index("dp"), seq_at // 2, seq_at % 2]).astype(jnp.int32)
+    up_column = gather_column(up_weight, routes)
+    down_column = gather_column(down_weight, routes)
     embed_all = lax.all_gather(time_embed, "dp", axis=0, tiled=True)
     embed_rows = width // dp
     embed_part = lax.dynamic_slice_in_dim(embed_all, lax.axis_index("dp") * embed_rows, embed_rows, 1)
@@ -731,62 +1134,64 @@
     scale_two = modulation[:, 2 * width : 3 * width]
     shift_two = modulation[:, 3 * width :]
 
-    skip_full = gather_tiles(skip_weight)
+    skip_tiles = lax.all_gather(skip_weight, ("dp", "seq"), axis=0)
     pair_tile = own_pair_columns(qkv_weight, seq)
-    pair_weight = lax.all_gather(pair_tile, "dp", axis=0, tiled=True)
-    joined = jnp.concatenate([inputs[0], skip_input[0]], axis=-1)
-    stream = dot_nn(joined, skip_full)
-    inverse_one = lax.rsqrt(jnp.mean(stream * stream, axis=-1, keepdims=True) + epsilon)
-    normed_one = (stream * inverse_one * (1.0 + scale_one) + shift_one).astype(jnp.bfloat16)
+    pair_weight = dp_gather(pair_tile, routes, dp)
+    skip_tiles, up_column, down_column, pair_weight, cos_all, sin_all, ends, grad_low, place = lax.optimization_barrier(
+        (skip_tiles, up_column, down_column, pair_weight.T, cos_all, sin_all, ends, grad_low, place)
+    )
+    stream, normed_one = entry_block(inputs[0], skip_input[0], skip_tiles, scale_one, shift_one, dp, seq)
     normed_all = lax.all_gather(normed_one, "seq", axis=0)
-    qt, kt, vt, keys, values = project_pair(normed_all, pair_weight.T, cos_all, sin_all)
+    up_near = gather_near(up_column, routes["x"])
+    down_near = gather_near(down_column, routes["y"])
+    up_far, down_far = send(up_near, routes["y"]), send(down_near, routes["x"])
+    up_near_core, down_near_core = send(up_near, routes["core"]), send(down_near, routes["core"])
+    normed_all, up_far, down_far, up_near_core, down_near_core = lax.optimization_barrier(
+        (normed_all, up_far, down_far, up_near_core, down_near_core)
+    )
+    up_pieces = (up_near, up_far, up_near_core, send(up_far, routes["core"]))
+    down_pieces = (down_near, down_far, down_near_core, send(down_far, routes["core"]))
+    qt, kt, vt, keys, values = project_pair(normed_all, pair_weight, cos_all, sin_all)
     attended_pair, attended_wide, total = attend_pair(ends, qt, keys, vt)
     attended = lax.all_to_all(attended_pair, "seq", 0, 0).reshape(width, frames)
-    out_full = gather_tiles(out_weight)
-    up_full = gather_tiles(up_weight)
-    down_full = gather_tiles(down_weight)
-    middle = stream + dot_tn(attended, out_full)
-    inverse_two = lax.rsqrt(jnp.mean(middle * middle, axis=-1, keepdims=True) + epsilon)
-    normed_two = (middle * inverse_two * (1.0 + scale_two) + shift_two).astype(jnp.bfloat16)
-    up_proj = dot_nn(normed_two, up_full)
-    hidden = jax.nn.gelu(up_proj, approximate=True).astype(jnp.bfloat16)
-    layer_output = (middle + dot_nn(hidden, down_full)).astype(jnp.bfloat16)
-
-    grad_out = cotangent[0].astype(jnp.float32) * inside[:, None].astype(jnp.float32)
-    grad_low = grad_out.astype(jnp.bfloat16)
-    grad_hidden = dot_nt(grad_low, down_full)
-    _, gelu_pull = jax.vjp(partial(jax.nn.gelu, approximate=True), up_proj)
-    grad_up_act = gelu_pull(grad_hidden)[0].astype(jnp.bfloat16)
-    grad_normed_two = dot_nt(grad_up_act, up_full)
-    grad_middle_norm, grad_scale_two, grad_shift_two = norm_back(grad_normed_two, middle, inverse_two, scale_two)
-    grad_middle = grad_out + grad_middle_norm
-    grad_middle_low = grad_middle.astype(jnp.bfloat16)
-    grad_attended = dot_nt(out_full, grad_middle_low).astype(jnp.bfloat16)
+    out_tiles = lax.all_gather(out_weight, ("dp", "seq"), axis=0)
+    (
+        layer_output, hidden, grad_up_act, grad_middle, grad_middle_low, grad_attended, sums_two, normed_two_turned,
+    ) = middle_block(
+        place, attended, stream, grad_low, scale_two, shift_two, out_tiles, up_pieces, down_pieces, dp, seq
+    )
     grad_pair = lax.all_to_all(grad_attended.reshape(seq, PAIR, frames), "seq", 0, 0)
-    down_tile = scatter_sum(dot_tn(hidden, grad_low))
-    up_tile = scatter_sum(dot_tn(normed_two, grad_up_act))
-    out_tile = scatter_sum(dot_nn(attended, grad_middle_low))
+    down_sum = scatter_first(place, grad_low.T, hidden, "turned", routes, seq, "x", "y")
+    up_sum = scatter_first(place, normed_two_turned, grad_up_act, "plain", routes, seq, "y", "x")
+    out_sum = scatter_first(place, attended, grad_middle_low, "plain", routes, seq, "x", "y")
 
     grad_projected = attend_pair_back(ends, qt, grad_pair, attended_wide, total, keys, values, kt, cos_all, sin_all)
     grad_local = lax.all_to_all(grad_projected, "seq", 0, 0)
-    pair_all = lax.all_gather(pair_tile, ("dp", "seq"), axis=0).reshape(dp, seq, width // dp, 3 * PAIR)
-    pair_all = pair_all.transpose(0, 2, 1, 3).reshape(width, 3 * width)
-    grad_normed_one = lax.dot_general(
-        grad_local.reshape(3 * width, frames), pair_all, (((0,), (1,)), ((), ())),
-        preferred_element_type=jnp.float32,
-    )
+    pair_all = lax.all_gather(pair_tile, ("dp", "seq"), axis=0)
+    down_sum = scatter_second(down_sum, routes, "y")
+    up_sum = scatter_second(up_sum, routes, "x")
+    out_sum = scatter_second(out_sum, routes, "y")
     grad_pair_weight = jnp.einsum(
         "icf,ifd->cd", grad_projected, normed_all, preferred_element_type=jnp.float32
-    )
-    grad_pair_tile = lax.psum_scatter(
-        grad_pair_weight.astype(jnp.bfloat16), "dp", scatter_dimension=1, tiled=True
-    )
-    qkv_tile = stored_columns(grad_pair_tile.T, seq).astype(jnp.float32)
-    grad_stream_norm, grad_scale_one, grad_shift_one = norm_back(grad_normed_one, stream, inverse_one, scale_one)
-    grad_stream = (grad_middle + grad_stream_norm).astype(jnp.bfloat16)
-    grad_joined = dot_nt(grad_stream, skip_full)
-    skip_tile = scatter_sum(dot_tn(joined, grad_stream))
-    grad_modulation = jnp.concatenate([grad_scale_one, grad_shift_one, grad_scale_two, grad_shift_two])
+    ).astype(jnp.bfloat16)
+    grad_stream, grad_stream_turned, sums_one = exit_block(
+        grad_local.reshape(3 * width, frames), pair_all, stream, grad_middle, scale_one, dp, seq
+    )
+    joined = jnp.concatenate([inputs[0], skip_input[0]], axis=-1)
+    skip_sums = [
+        scatter_first(place, grad_stream_turned, joined, "turned", routes, seq, first, second, (part, 2))
+        for part, (first, second) in enumerate((("x", "y"), ("y", "x")))
+    ]
+    grad_main, grad_side = joined_grads(grad_stream, skip_tiles, dp, seq)
+    sums_one, grad_main, grad_pair_weight = lax.optimization_barrier((sums_one, grad_main, grad_pair_weight))
+    skip_sums = [scatter_second(skip_sums[0], routes, "y"), scatter_second(skip_sums[1], routes, "x")]
+    skip_tile = jnp.concatenate([scatter_last(part, routes) for part in skip_sums], axis=1).T
+    down_tile = scatter_last(down_sum, routes).T
+    up_tile = scatter_last(up_sum, routes)
+    out_tile = scatter_last(out_sum, routes)
+    grad_pair_tile = dp_sum(grad_pair_weight.T.reshape(dp, width // dp, 3 * PAIR), routes, dp)
+    qkv_tile = stored_columns(grad_pair_tile.astype(jnp.bfloat16), seq).astype(jnp.float32)
+    grad_modulation = jnp.concatenate([sums_one[0], sums_one[1], sums_two[0], sums_two[1]])
     grad_modulation = lax.psum_scatter(grad_modulation, "seq", scatter_dimension=0, tiled=True)
     grad_modulation = lax.all_gather(grad_modulation[None], "dp", axis=0, tiled=True)
     ada_tile = lax.dot_general(
@@ -795,8 +1200,8 @@
     )
     return (
         layer_output[None],
-        grad_joined[None, :, :width],
-        grad_joined[None, :, width:],
+        grad_main[None],
+        grad_side[None],
         skip_tile,
         ada_tile,
         qkv_tile,
@@ -834,6 +1239,6 @@
         P("dp", "seq"),
     )
     seq_size = mesh.shape["seq"]
-    paired = H == 2 * seq_size and seq_size % 3 != 0
+    paired = H == 2 * seq_size and seq_size % 3 != 0 and mesh.shape["dp"] == 4
     body = local_paired if paired else local_general
     return jax.shard_map(body, mesh=mesh, in_specs=in_specs, out_specs=out_specs, check_vma=False)

time: 1050 us -> 687 us (0.65)
  waiting for transfers between devices: 549 us -> 195 us
  matrix products: 103 us -> 8.25 us
  Pallas kernels: 85.6 us -> 174 us
  starting transfers between devices: 20.8 us -> 108 us
  local copies, waits for them, and re-layouts: 125 us -> 62.5 us
  blocking collectives: 118 us -> 63.7 us
  other arithmetic: 20.1 us -> 43.9 us
    all_gather x5 -> x3, waiting for transfers between devices: 184 us -> 8.38 us  [the longest x1 8.36 us: local_paired(): out_tiles = lax.all_gather(out_weight, ('dp', 'seq'), axis=0)]
    reduce_scatter x6 -> x0, waiting for transfers between devices: 162 us -> none  [the longest x1 88 us: scatter_sum(): lax.psum_scatter(partial_sum.astype(jnp.bfloat16), 'seq', scatter_dimensi...]
    ppermute x0 -> x50, waiting for transfers between devices: none -> 128 us  [send(): return lax.ppermute(value, ('dp', 'seq'), route)]
    unnamed x18 -> x4, waiting for transfers between devices: 97.7 us -> 1.39 us
    dot_general x13 -> x0, matrix products: 92.9 us -> none  [the longest x4 28.5 us: dot_nn(): lax.dot_general(a, b, (((1,), (0,)), ((), ())), preferred_element_type=jn...]
    pallas_call x0 -> x14, Pallas kernels: none -> 90.1 us  [the longest x10 39 us: grad_blocks(): pl.pallas_call(partial(blocks_kernel, kind=kind, masks=masks, other=other...]
    ppermute x0 -> x50, starting transfers between devices: none -> 84.4 us  [send(): return lax.ppermute(value, ('dp', 'seq'), route)]
    all_to_all x1, waiting for transfers between devices: 59.7 us -> 0.01 us  [local_paired(): grad_local = lax.all_to_all(grad_projected, 'seq', 0, 0)]
  transfers between devices with their start and end apart: 23 -> 63, of which waited for: 13 -> 22; matrix products, arithmetic and copies ran while one was open for 21% -> 13% of each run, Pallas kernels for 8% -> 25%
where the time goes in v2:
time: 687 us; the launch traced here: 677 us
  waiting for transfers between devices  195 us (28%)
  Pallas kernels  174 us (25%)
  starting transfers between devices  108 us (16%)
  blocking collectives  63.7 us (9%)
  local copies, waits for them, and re-layouts  62.5 us (9%)
  other arithmetic  43.9 us (6%)
  between operations  21 us (3%)
  matrix products  8.25 us (1%)
    ppermute x50, waiting for transfers between devices, send(): return lax.ppermute(value, ('dp', 'seq'), route)  128 us
    ppermute x50, starting transfers between devices, send(): return lax.ppermute(value, ('dp', 'seq'), route)  84.4 us
    pallas_call x1, Pallas kernels, attend_pair_back(): pl.pallas_call(partial(attend_back_kernel, size=size, length=length, chun...  43.9 us
    pallas_call x10, Pallas kernels, grad_blocks(): pl.pallas_call(partial(blocks_kernel, kind=kind, masks=masks, other=other...  39 us
    unnamed x140, local copies, waits for them, and re-layouts  36.9 us
    unnamed x2, blocking collectives  35.1 us
    pallas_call x1, Pallas kernels, attend_pair(): pl.pallas_call(partial(attend_kernel, size=size, length=length), grid_spe...  34 us
    pallas_call x1, Pallas kernels, middle_block(): pl.pallas_call(partial(middle_kernel, dp=dp, seq=seq), in_specs=[pl.Block...  33.6 us
  transfers between devices with their start and end apart: 63, of which 22 were waited for; matrix products, arithmetic and copies ran while one was open for 13% of the time, Pallas kernels for 25%

profile of v2, /device:TPU:0, one launch (start us, length us, event | category | flops | bytes accessed | tf_op | source)
XLA Modules:
  0.0 676.9 jit_solution(7549621843296587749)
XLA Ops:
  8.0 3.1 collective-permute-start
  11.1 2.6 collective-permute-start.1
  16.3 4.5 collective-permute-start.8
  22.9 8.2 %all-gather.5 = bf16[4,1,1024]{2,1,0:T(2,128)(2,1)S(1)} all-gather(bf16[1,1,1024]{2,1,0:T(2,128)(2,1)S(1)} %bitcast.222), channel_id=1, replica_groups=mesh['dp'=4,'seq'=8] {'dp'}, dimensions={0}, use_global_device_ids=true | all-gather | bytes 10240 | tf_op jit(solution)/shard_map/all_gather | solution.py:1126
  31.2 9.1 %all-reduce = f32[4,512]{1,0:T(4,128)S(1)} all-reduce(f32[4,512]{1,0:T(4,128)S(1)} %fusion.30), channel_id=7, replica_groups=mesh['dp'=4,'seq'=8] {'dp'}, use_global_device_ids=true, to_apply=%region_2.3.clone | all-reduce | flops 2048 | bytes 16384
  41.0 12.7 %all_gather.36 = f32[1,4096]{1,0:T(1,128)S(1)} all-gather(f32[1,512]{1,0:T(1,128)S(1)} %constant_dynamic-slice_fusion.7), channel_id=1, replica_groups=mesh['dp'=4,'seq'=8] {'seq'}, dimensions={1}, use_global_device_ids=true | all-gather | bytes 18432 | tf_op jit(solution)/shard_map/all_gather | solution.py:1131
  55.6 3.9 compare_select_fusion.4
  62.3 2.8 multiply_sine_fusion
  77.6 5.3 collective-permute-done.10
  83.8 3.0 collective-permute-start.5
  88.5 2.4 pad_maximum_fusion.3
  90.8 3.4 collective-permute-done.3
  94.2 8.2 %collective-permute-done.4 = bf16[1024,128]{1,0:T(8,128)(2,1)S(1)} collective-permute-done((bf16[1024,128]{1,0:T(8,128)(2,1)}, bf16[1024,128]{1,0:T(8,128)(2,1)S(1)}, u32[]{:S(2)}, u32[]{:S(2)}) %collective-permute-start.4) | collective-permute-done | bytes 262176 | tf_op jit(solution)/shard_map/ppermute | solution.py:689
  106.7 4.6 entry_block.1
  113.4 2.8 collective-permute-start.14
  117.7 20.8 %collective-permute-done.14 = bf16[4,1024,128]{2,1,0:T(8,128)(2,1)S(1)} collective-permute-done((bf16[4,1024,128]{2,1,0:T(8,128)(2,1)}, bf16[4,1024,128]{2,1,0:T(8,128)(2,1)S(1)}, u32[]{:S(2)}, u32[]{:S(2)}) %collective-permute-start.14) | collective-permute-done | bytes 1048608 | tf_op jit(solution)/shard_map/ppermute | solution.py:689
  138.5 2.9 pad_maximum_fusion.1.down_0
  145.7 41.8 %collective-permute-done.15.down_1 = bf16[2,4,1024,128]{3,2,1,0:T(8,128)(2,1)} collective-permute-done((bf16[2,4,1024,128]{3,2,1,0:T(8,128)(2,1)}, bf16[2,4,1024,128]{3,2,1,0:T(8,128)(2,1)}, u32[]{:S(2)}, u32[]{:S(2)}) %collective-permute-start.15) | collective-permute-done | bytes 2097184 | tf_op jit(solution)/shard_map/ppermute | solution.py:689
  187.5 4.8 collective-permute-done.13.up_1
  192.3 6.9 %all-gather.14.cloned.1.call-done = bf16[4096,1024]{1,0:T(8,128)(2,1)} async-done(((bf16[512,1024]{1,0:T(8,128)(2,1)}), bf16[4096,1024]{1,0:T(8,128)(2,1)}) %all-gather.14.cloned.1.call-update) | async-done | bytes 8388624 | tf_op jit(solution)/shard_map/all_gather | solution.py:1144
  199.8 3.4 copy-done.34
  203.2 6.1 project_pair.1
  209.3 34.0 %attend_pair.1 = (bf16[8,128,512]{2,1,0:T(8,128)(2,1)}, f32[8,128,512]{2,1,0:T(8,128)S(1)}, f32[8,2,512]{2,1,0:T(2,128)S(1)}) custom-call(s32[2]{0:T(128)S(1)} %pad_add_fusion.ends_ref, bf16[8,128,512]{2,1,0:T(8,128)(2,1)S(1)} %get-tuple-element.69.qt_ref, bf16[4096,128]{1,0:T(8,128)(2,1)S(1)} %get-tuple-element.70.k_ref, ...), custom_call_target="tpu_custom_call" | custom-call | flops 8589934592 | bytes 7340032 | tf_op jit(solution)/shard_map/attend_pair/pallas_call | solution.py:516
  244.7 3.7 all-to-all-start
  249.8 8.4 %all-gather.16.cloned.1.call-done = bf16[8192,128]{1,0:T(8,128)(2,1)} async-done(((bf16[256,128]{1,0:T(8,128)(2,1)}), bf16[8192,128]{1,0:T(8,128)(2,1)}) %all-gather.16.cloned.1.call-update) | async-done | bytes 2097168 | tf_op jit(solution)/shard_map/all_gather | solution.py:1157
  258.1 19.7 %all-to-all-done = bf16[8,128,512]{2,1,0:T(8,128)(2,1)S(1)} async-done(((bf16[8,128,512]{2,1,0:T(8,128)(2,1)}), bf16[8,128,512]{2,1,0:T(8,128)(2,1)S(1)}, u32[]{:S(2)}, u32[]{:S(2)}) %all-to-all-start) | async-done | bytes 1048608 | tf_op jit(solution)/shard_map/all_to_all | solution.py:1156
  278.8 33.6 %middle_block.1 = (bf16[512,1024]{1,0:T(8,128)(2,1)}, bf16[512,4096]{1,0:T(8,128)(2,1)}, bf16[512,4096]{1,0:T(8,128)(2,1)}, f32[512,1024]{1,0:T(8,128)}, bf16[51...) custom-call(s32[3]{0:T(128)} %pad_add_fusion.1.place_ref, ...), custom_call_target="tpu_custom_call" | custom-call | flops 19327352832 | bytes 29360128 | tf_op jit(solution)/shard_map/middle_block/pallas_call | solution.py:809
  312.4 3.8 all-to-all-start.1
  316.2 2.3 copy-done.4
  318.5 4.9 grad_blocks.18
  323.8 4.7 grad_blocks.16
  328.7 31.0 %all-to-all-done.1.gt_ref = bf16[8,128,512]{2,1,0:T(8,128)(2,1)S(1)} async-done(((bf16[8,128,512]{2,1,0:T(8,128)(2,1)}), bf16[8,128,512]{2,1,0:T(8,128)(2,1)S(1)}, u32[]{:S(2)}, u32[]{:S(2)}) %all-to-all-start.1) | async-done | bytes 1048608 | tf_op jit(solution)/shard_map/all_to_all | solution.py:1163
  366.2 43.9 %attend_pair_back.1 = bf16[8,384,512]{2,1,0:T(8,128)(2,1)S(1)} custom-call(s32[2]{0:T(128)S(1)} %pad_add_fusion.ends_ref, bf16[8,128,512]{2,1,0:T(8,128)(2,1)S(1)} %copy-done.38, bf16[8,128,512]{2,1,0:T(8,128)(2,1)S(1)} %all-to-all-done.1.gt_ref, f32[8,128,512]{2,1,0:T(8,128)S(1)} %copy-done.46, f32[8,2,512]{2,1,0:T(2,128)S(1)} %get-tuple-element.82.total_ref, ...), custom_call_target="tpu_custom_call" | custom-call | flops 21474836480 | bytes 15728640 | tf_op jit(solution)/shard_map/attend_pair_back/pallas_call | solution.py:609
  411.9 4.6 all-to-all-start.2
  419.0 2.3 collective-permute-done.38.refs_0_
  421.3 2.9 grad_blocks.15
  425.1 6.3 collective-permute-start.39
  435.6 8.6 %copy.52 = bf16[8192,384]{1,0:T(8,128)(2,1)} copy(bf16[8192,384]{0,1:T(8,128)(2,1)} %all-gather.18.cloned.1.call-done) | data formatting | bytes 12582912 | tf_op jit(solution)/shard_map/all_gather | solution.py:1170
  447.6 2.2 copy-done.5
  449.8 5.8 grad_blocks.19
  456.5 6.1 grad_blocks.17
  466.5 2.4 collective-permute-start.42
  470.6 6.9 %bitcast_convert_fusion = bf16[384,1024]{1,0:T(8,128)(2,1)} fusion(bf16[8,384,512]{2,1,0:T(8,128)(2,1)S(1)} %copy-done.12, bf16[8,512,1024]{2,1,0:T(8,128)(2,1)} %bitcast.191), kind=kOutput, calls=%fused_computation.7 | convolution fusion | flops 3221618688 | bytes 12320768 | tf_op jit(solution)/shard_map/icf,ifd->cd/dot_general | solution.py:1174
  477.5 15.1 %collective-permute-done.42 = bf16[256,128]{1,0:T(8,128)(2,1)S(1)} collective-permute-done((bf16[256,128]{1,0:T(8,128)(2,1)S(1)}, bf16[256,128]{1,0:T(8,128)(2,1)S(1)}, u32[]{:S(2)}, u32[]{:S(2)}) %collective-permute-start.42) | collective-permute-done | bytes 65568 | tf_op jit(solution)/shard_map/ppermute | solution.py:689
  493.3 9.8 %collective-permute-done.51 = bf16[2,4,128,1024]{3,2,1,0:T(8,128)(2,1)} collective-permute-done((bf16[2,4,128,1024]{3,2,1,0:T(8,128)(2,1)S(1)}, bf16[2,4,128,1024]{3,2,1,0:T(8,128)(2,1)}, u32[]{:S(2)}, u32[]{:S(2)}) %collective-permute-start.51) | collective-permute-done | bytes 2097184 | tf_op jit(solution)/shard_map/ppermute | solution.py:689
  503.1 2.6 fusion.1
  506.6 4.6 collective-permute-done.45
  516.8 8.2 %exit_block.1 = (bf16[512,1024]{1,0:T(8,128)(2,1)S(1)}, bf16[1024,512]{1,0:T(8,128)(2,1)S(1)}, f32[2,1024]{1,0:T(2,128)S(1)}) custom-call(bf16[3072,512]{1,0:T(8,128)(2,1)} %bitcast.44.projected_ref, bf16[32,256,384]{2,1,0:T(8,128)(2,1)} %bitcast.195, f32[512,1024]{1,0:T(8,128)S(1)} %copy-done.14, f32[512,1024]{1,0:T(8,128)S(1)} %copy-done.15, ...), custom_call_target="tpu_custom_call" | custom-call | flops 3221225472 | bytes 15728640 | tf_op jit(solution)/shard_map/exit_block/pallas_call | solution.py:909
  525.0 4.8 joined_grads.1
  529.8 2.3 copy.53
  543.7 26.0 %all-reduce.1 = f32[4096]{0:T(1024)S(1)} all-reduce(f32[4096]{0:T(1024)S(1)} %pad_maximum_fusion.6), channel_id=8, replica_groups=mesh['dp'=4,'seq'=8] {'seq'}, use_global_device_ids=true, to_apply=%region_3.4.clone | all-reduce | flops 4096 | bytes 32768
  569.8 7.7 %all-gather.6 = f32[4,1,512]{2,1,0:T(1,128)S(1)} all-gather(f32[1,1,512]{2,1,0:T(1,128)S(1)} %bitcast.219), channel_id=6, replica_groups=mesh['dp'=4,'seq'=8] {'dp'}, dimensions={0}, use_global_device_ids=true | all-gather | bytes 10240 | tf_op jit(solution)/shard_map/all_gather | solution.py:1196
  579.5 3.0 grad_blocks.12
  583.8 3.8 fusion.35
  587.9 3.1 fusion.36
  593.0 5.1 collective-permute-start.37
  599.0 2.8 grad_blocks.11
  602.7 2.8 collective-permute-start.54
  612.4 4.4 grad_blocks.13
  616.8 2.7 collective-permute-start.48
  620.7 14.8 %collective-permute-start.49 = (bf16[256,512]{1,0:T(8,128)(2,1)S(1)}, bf16[256,512]{1,0:T(8,128)(2,1)S(1)}, u32[]{:S(2)}, u32[]{:S(2)}) collective-permute-start(bf16[256,512]{1,0:T(8,128)(2,1)S(1)} %copy-done.52), channel_id=1, source_target_pairs={{0,6},{1,7},{2,0},{3,1},{4,2},{5,3},{6,4},{7,5},{8,14},{9,15},{10,... | collective-permute-start | bytes 786440 | tf_op jit(solution)/shard_map/ppermute | solution.py:689
  648.8 9.0 %collective-permute-start.23 = (bf16[128,256]{1,0:T(8,128)(2,1)S(1)}, bf16[128,256]{1,0:T(8,128)(2,1)S(1)}, u32[]{:S(2)}, u32[]{:S(2)}) collective-permute-start(bf16[128,256]{1,0:T(8,128)(2,1)S(1)} %get-tuple-element.163), channel_id=1, source_target_pairs={{0,2},{1,3},{2,4},{3,5},{4,6},{5,7},{6,0},{7,1},{8,10},{9,11},{10,... | collective-permute-start | bytes 196616 | tf_op jit(solution)/shard_map/ppermute | solution.py:689
  657.8 2.4 collective-permute-start.25
  660.4 2.5 collective-permute-start.30
  (292 shorter events, 117.2 us)
Async XLA Ops:
  7.2 97.2 %all-gather.12.cloned.1.call-start = ((), (), s32[]{:S(2)}) async-start(), calls=%async_computation.3 | async-start | bytes 4325376 | tf_op jit(solution)/shard_map/all_gather | solution.py:1137
  8.0 191.3 %all-gather.14.cloned.1.call-start = ((), (), s32[]{:S(2)}) async-start(), calls=%async_computation.4 | async-start | bytes 9437184 | tf_op jit(solution)/shard_map/all_gather | solution.py:1144
  8.0 75.8 %collective-permute-start = (bf16[256,512]{1,0:T(8,128)(2,1)}, bf16[256,512]{1,0:T(8,128)(2,1)S(1)}, u32[]{:S(2)}, u32[]{:S(2)}) collective-permute-start(bf16[256,512]{1,0:T(8,128)(2,1)} %param.26), channel_id=1, source_target_pairs={{0,2},{1,3},{2,4},{3,5},{4,6},{5,7},{6,0},{7,1},{8,10},{9,11},{10,... | collective-permute-start | bytes 786440 | tf_op jit(solution)/shard_map/ppermute | solution.py:689
  11.1 76.7 %collective-permute-start.1 = (bf16[256,512]{1,0:T(8,128)(2,1)}, bf16[256,512]{1,0:T(8,128)(2,1)S(1)}, u32[]{:S(2)}, u32[]{:S(2)}) collective-permute-start(bf16[256,512]{1,0:T(8,128)(2,1)} %param.26), channel_id=1, source_target_pairs={{0,4},{1,5},{2,6},{3,7},{4,0},{5,1},{6,2},{7,3},{8,12},{9,13},{10,... | collective-permute-start | bytes 786440 | tf_op jit(solution)/shard_map/ppermute | solution.py:689
  14.7 54.9 %collective-permute-start.6 = (bf16[256,128]{0,1:T(8,128)(2,1)S(1)}, bf16[256,128]{0,1:T(8,128)(2,1)S(1)}, u32[]{:S(2)}, u32[]{:S(2)}) collective-permute-start(bf16[256,128]{0,1:T(8,128)(2,1)S(1)} %copy.63), channel_id=1, source_target_pairs={{0,0},{1,3},{2,6},{3,1},{4,4},{5,7},{6,2},{7,5},{8,8},{9,11},{10,1... | collective-permute-start | bytes 196616 | tf_op jit(solution)/shard_map/ppermute | solution.py:647
  15.5 54.1 %collective-permute-start.7 = (bf16[256,128]{0,1:T(8,128)(2,1)S(1)}, bf16[256,128]{0,1:T(8,128)(2,1)S(1)}, u32[]{:S(2)}, u32[]{:S(2)}) collective-permute-start(bf16[256,128]{0,1:T(8,128)(2,1)S(1)} %copy.64), channel_id=1, source_target_pairs={{0,1},{1,4},{2,7},{3,2},{4,5},{5,0},{6,3},{7,6},{8,9},{9,12},{10,1... | collective-permute-start | bytes 196616 | tf_op jit(solution)/shard_map/ppermute | solution.py:647
  16.3 53.4 %collective-permute-start.8 = (bf16[256,128]{0,1:T(8,128)(2,1)S(1)}, bf16[256,128]{0,1:T(8,128)(2,1)S(1)}, u32[]{:S(2)}, u32[]{:S(2)}) collective-permute-start(bf16[256,128]{0,1:T(8,128)(2,1)S(1)} %copy.65), channel_id=1, source_target_pairs={{0,2},{1,5},{2,0},{3,3},{4,6},{5,1},{6,4},{7,7},{8,10},{9,13},{10,... | collective-permute-start | bytes 196616 | tf_op jit(solution)/shard_map/ppermute | solution.py:647
  69.8 7.8 %collective-permute-start.9 = (bf16[256,384]{0,1:T(8,128)(2,1)S(1)}, bf16[256,384]{0,1:T(8,128)(2,1)S(1)}, u32[]{:S(2)}, u32[]{:S(2)}) collective-permute-start(bf16[256,384]{0,1:T(8,128)(2,1)S(1)} %get-tuple-element.172), channel_id=1, source_target_pairs={{0,8},{1,9},{2,10},{3,11},{4,12},{5,13},{6,14},{7,15},{8,0},{9,1},... | collective-permute-start | bytes 589832 | tf_op jit(solution)/shard_map/ppermute | solution.py:689
  71.8 11.1 %collective-permute-start.10 = (bf16[256,384]{0,1:T(8,128)(2,1)S(1)}, bf16[256,384]{0,1:T(8,128)(2,1)S(1)}, u32[]{:S(2)}, u32[]{:S(2)}) collective-permute-start(bf16[256,384]{0,1:T(8,128)(2,1)S(1)} %get-tuple-element.172), channel_id=1, source_target_pairs={{0,16},{1,17},{2,18},{3,19},{4,20},{5,21},{6,22},{7,23},{8,24},{9,... | collective-permute-start | bytes 589832 | tf_op jit(solution)/shard_map/ppermute | solution.py:689
  73.2 9.7 %collective-permute-start.11 = (bf16[256,384]{0,1:T(8,128)(2,1)S(1)}, bf16[256,384]{0,1:T(8,128)(2,1)S(1)}, u32[]{:S(2)}, u32[]{:S(2)}) collective-permute-start(bf16[256,384]{0,1:T(8,128)(2,1)S(1)} %get-tuple-element.172), channel_id=1, source_target_pairs={{0,24},{1,25},{2,26},{3,27},{4,28},{5,29},{6,30},{7,31},{8,16},{9,... | collective-permute-start | bytes 589832 | tf_op jit(solution)/shard_map/ppermute | solution.py:689
  77.6 10.2 %collective-permute-start.2 = (bf16[256,512]{1,0:T(8,128)(2,1)S(1)}, bf16[256,512]{1,0:T(8,128)(2,1)S(1)}, u32[]{:S(2)}, u32[]{:S(2)}) collective-permute-start(bf16[256,512]{1,0:T(8,128)(2,1)S(1)} %copy-done.54), channel_id=1, source_target_pairs={{0,6},{1,7},{2,0},{3,1},{4,2},{5,3},{6,4},{7,5},{8,14},{9,15},{10,... | collective-permute-start | bytes 786440 | tf_op jit(solution)/shard_map/ppermute | solution.py:689
  82.9 11.3 %collective-permute-start.3 = (bf16[1024,128]{1,0:T(8,128)(2,1)}, bf16[1024,128]{1,0:T(8,128)(2,1)S(1)}, u32[]{:S(2)}, u32[]{:S(2)}) collective-permute-start(bf16[1024,128]{1,0:T(8,128)(2,1)} %param.27), channel_id=1, source_target_pairs={{0,2},{1,3},{2,4},{3,5},{4,6},{5,7},{6,0},{7,1},{8,10},{9,11},{10,... | collective-permute-start | bytes 786440 | tf_op jit(solution)/shard_map/ppermute | solution.py:689
  82.9 19.5 %collective-permute-start.4 = (bf16[1024,128]{1,0:T(8,128)(2,1)}, bf16[1024,128]{1,0:T(8,128)(2,1)S(1)}, u32[]{:S(2)}, u32[]{:S(2)}) collective-permute-start(bf16[1024,128]{1,0:T(8,128)(2,1)} %param.27), channel_id=1, source_target_pairs={{0,4},{1,5},{2,6},{3,7},{4,0},{5,1},{6,2},{7,3},{8,12},{9,13},{10,... | collective-permute-start | bytes 786440 | tf_op jit(solution)/shard_map/ppermute | solution.py:689
  83.8 18.6 %collective-permute-start.5 = (bf16[1024,128]{1,0:T(8,128)(2,1)}, bf16[1024,128]{1,0:T(8,128)(2,1)S(1)}, u32[]{:S(2)}, u32[]{:S(2)}) collective-permute-start(bf16[1024,128]{1,0:T(8,128)(2,1)} %param.27), channel_id=1, source_target_pairs={{0,6},{1,7},{2,0},{3,1},{4,2},{5,3},{6,4},{7,5},{8,14},{9,15},{10,... | collective-permute-start | bytes 786440 | tf_op jit(solution)/shard_map/ppermute | solution.py:689
  112.6 145.5 %all-gather.16.cloned.1.call-start = ((), (), s32[]{:S(2)}) async-start(), calls=%async_computation.5 | async-start | bytes 2162688 | tf_op jit(solution)/shard_map/all_gather | solution.py:1157
  113.4 322.2 %all-gather.18.cloned.1.call-start = ((), (), s32[]{:S(2)}) async-start(), calls=%async_computation.6 | async-start | bytes 6488064 | tf_op jit(solution)/shard_map/all_gather | solution.py:1170
  113.4 25.1 %collective-permute-start.14 = (bf16[4,1024,128]{2,1,0:T(8,128)(2,1)}, bf16[4,1024,128]{2,1,0:T(8,128)(2,1)S(1)}, u32[]{:S(2)}, u32[]{:S(2)}) collective-permute-start(bf16[4,1024,128]{2,1,0:T(8,128)(2,1)} %pad_maximum_fusion.4), channel_id=1, source_target_pairs={{0,16},{1,17},{2,18},{3,19},{4,20},{5,21},{6,22},{7,23},{8,24},{9,... | collective-permute-start | bytes 3145736 | tf_op jit(solution)/shard_map/ppermute | solution.py:689
  116.2 26.3 %collective-permute-start.12 = (bf16[4,256,512]{2,1,0:T(8,128)(2,1)}, bf16[4,256,512]{2,1,0:T(8,128)(2,1)S(1)}, u32[]{:S(2)}, u32[]{:S(2)}) collective-permute-start(bf16[4,256,512]{2,1,0:T(8,128)(2,1)} %pad_maximum_fusion.3), channel_id=1, source_target_pairs={{0,8},{1,9},{2,10},{3,11},{4,12},{5,13},{6,14},{7,15},{8,0},{9,1},... | collective-permute-start | bytes 3145736 | tf_op jit(solution)/shard_map/ppermute | solution.py:689
  141.4 46.1 %collective-permute-start.15 = (bf16[2,4,1024,128]{3,2,1,0:T(8,128)(2,1)}, bf16[2,4,1024,128]{3,2,1,0:T(8,128)(2,1)}, u32[]{:S(2)}, u32[]{:S(2)}) collective-permute-start(bf16[2,4,1024,128]{3,2,1,0:T(8,128)(2,1)} %pad_maximum_fusion.1.down_0), channel_id=1, source_target_pairs={{0,8},{1,9},{2,10},{3,11},{4,12},{5,13},{6,14},{7,15},{8,0},{9,1},... | collective-permute-start | bytes 6291464 | tf_op jit(solution)/shard_map/ppermute | solution.py:689
  142.4 45.1 %collective-permute-start.17 = (bf16[2,4,1024,128]{3,2,1,0:T(8,128)(2,1)}, bf16[2,4,1024,128]{3,2,1,0:T(8,128)(2,1)}, u32[]{:S(2)}, u32[]{:S(2)}) collective-permute-start(bf16[2,4,1024,128]{3,2,1,0:T(8,128)(2,1)} %pad_maximum_fusion.1.down_0), channel_id=1, source_target_pairs={{0,1},{1,0},{2,3},{3,2},{4,5},{5,4},{6,7},{7,6},{8,9},{9,8},{10,11... | collective-permute-start | bytes 6291464 | tf_op jit(solution)/shard_map/ppermute | solution.py:689
  142.4 57.3 %copy-start.23 = (bf16[1024,384]{0,1:T(8,128)(2,1)S(1)}, bf16[1024,384]{0,1:T(8,128)(2,1)}, u32[]{:S(2)}) copy-start(bf16[1024,384]{0,1:T(8,128)(2,1)} %copy-done.22) | copy-start | bytes 2359300
  144.0 48.3 %collective-permute-start.13 = (bf16[2,4,256,512]{3,2,1,0:T(8,128)(2,1)}, bf16[2,4,256,512]{3,2,1,0:T(8,128)(2,1)}, u32[]{:S(2)}, u32[]{:S(2)}) collective-permute-start(bf16[2,4,256,512]{3,2,1,0:T(8,128)(2,1)} %pad_maximum_fusion.up_0), channel_id=1, source_target_pairs={{0,16},{1,17},{2,18},{3,19},{4,20},{5,21},{6,22},{7,23},{8,24},{9,... | collective-permute-start | bytes 6291464 | tf_op jit(solution)/shard_map/ppermute | solution.py:689
  145.4 46.9 %collective-permute-start.16 = (bf16[2,4,256,512]{3,2,1,0:T(8,128)(2,1)}, bf16[2,4,256,512]{3,2,1,0:T(8,128)(2,1)}, u32[]{:S(2)}, u32[]{:S(2)}) collective-permute-start(bf16[2,4,256,512]{3,2,1,0:T(8,128)(2,1)} %pad_maximum_fusion.up_0), channel_id=1, source_target_pairs={{0,1},{1,0},{2,3},{3,2},{4,5},{5,4},{6,7},{7,6},{8,9},{9,8},{10,11... | collective-permute-start | bytes 6291464 | tf_op jit(solution)/shard_map/ppermute | solution.py:689
  199.3 78.5 %collective-permute-start.18 = (bf16[2,4,256,512]{3,2,1,0:T(8,128)(2,1)}, bf16[2,4,256,512]{3,2,1,0:T(8,128)(2,1)}, u32[]{:S(2)}, u32[]{:S(2)}) collective-permute-start(bf16[2,4,256,512]{3,2,1,0:T(8,128)(2,1)} %collective-permute-done.13.up_1), channel_id=1, source_target_pairs={{0,1},{1,0},{2,3},{3,2},{4,5},{5,4},{6,7},{7,6},{8,9},{9,8},{10,11... | collective-permute-start | bytes 6291464 | tf_op jit(solution)/shard_map/ppermute | solution.py:689
  199.5 78.3 %collective-permute-start.19 = (bf16[2,4,1024,128]{3,2,1,0:T(8,128)(2,1)}, bf16[2,4,1024,128]{3,2,1,0:T(8,128)(2,1)}, u32[]{:S(2)}, u32[]{:S(2)}) collective-permute-start(bf16[2,4,1024,128]{3,2,1,0:T(8,128)(2,1)} %collective-permute-done.15.down_1), channel_id=1, source_target_pairs={{0,1},{1,0},{2,3},{3,2},{4,5},{5,4},{6,7},{7,6},{8,9},{9,8},{10,11... | collective-permute-start | bytes 6291464 | tf_op jit(solution)/shard_map/ppermute | solution.py:689
  244.7 33.1 %all-to-all-start = ((bf16[8,128,512]{2,1,0:T(8,128)(2,1)}), bf16[8,128,512]{2,1,0:T(8,128)(2,1)S(1)}, u32[]{:S(2)}, u32[]{:S(2)}) async-start(bf16[8,128,512]{2,1,0:T(8,128)(2,1)} %get-tuple-element.72), calls=%async_computation | async-start | bytes 2097152 | tf_op jit(solution)/shard_map/all_to_all | solution.py:1156
  312.4 47.3 %all-to-all-start.1 = ((bf16[8,128,512]{2,1,0:T(8,128)(2,1)}), bf16[8,128,512]{2,1,0:T(8,128)(2,1)S(1)}, u32[]{:S(2)}, u32[]{:S(2)}) async-start(bf16[8,128,512]{2,1,0:T(8,128)(2,1)} %bitcast.199), calls=%async_computation.1 | async-start | bytes 2097152 | tf_op jit(solution)/shard_map/all_to_all | solution.py:1163
  323.4 124.2 %collective-permute-start.50 = (bf16[4,4,128,1024]{3,2,1,0:T(8,128)(2,1)}, bf16[4,4,128,1024]{3,2,1,0:T(8,128)(2,1)}, u32[]{:S(2)}, u32[]{:S(2)}) collective-permute-start(bf16[4,4,128,1024]{3,2,1,0:T(8,128)(2,1)} %grad_blocks.18), channel_id=1, source_target_pairs={{0,1},{1,0},{2,3},{3,2},{4,5},{5,4},{6,7},{7,6},{8,9},{9,8},{10,11... | collective-permute-start | bytes 12582920 | tf_op jit(solution)/shard_map/ppermute | solution.py:689
  328.6 127.9 %collective-permute-start.44 = (bf16[4,4,256,512]{3,2,1,0:T(8,128)(2,1)}, bf16[4,4,256,512]{3,2,1,0:T(8,128)(2,1)}, u32[]{:S(2)}, u32[]{:S(2)}) collective-permute-start(bf16[4,4,256,512]{3,2,1,0:T(8,128)(2,1)} %grad_blocks.16), channel_id=1, source_target_pairs={{0,1},{1,0},{2,3},{3,2},{4,5},{5,4},{6,7},{7,6},{8,9},{9,8},{10,11... | collective-permute-start | bytes 12582920 | tf_op jit(solution)/shard_map/ppermute | solution.py:689
  411.9 101.8 %all-to-all-start.2 = ((bf16[8,384,512]{2,1,0:T(8,128)(2,1)}), bf16[8,384,512]{2,1,0:T(8,128)(2,1)}, u32[]{:S(2)}, u32[]{:S(2)}) async-start(bf16[8,384,512]{2,1,0:T(8,128)(2,1)} %copy-done.11), calls=%async_computation.2 | async-start | bytes 6291456 | tf_op jit(solution)/shard_map/all_to_all | solution.py:1169
  418.6 2.7 collective-permute-start.38
  425.1 19.2 %collective-permute-start.39 = (bf16[2,4,256,128]{3,2,1,0:T(8,128)(2,1)}, bf16[2,4,256,128]{3,2,1,0:T(8,128)(2,1)}, u32[]{:S(2)}, u32[]{:S(2)}) collective-permute-start(bf16[2,4,256,128]{3,2,1,0:T(8,128)(2,1)} %get-tuple-element.101), channel_id=1, source_target_pairs={{0,8},{1,9},{2,10},{3,11},{4,12},{5,13},{6,14},{7,15},{8,0},{9,1},... | collective-permute-start | bytes 1572872 | tf_op jit(solution)/shard_map/ppermute | solution.py:689
  446.1 17.4 %collective-permute-start.40 = (bf16[4,256,128]{2,1,0:T(8,128)(2,1)}, bf16[4,256,128]{2,1,0:T(8,128)(2,1)}, u32[]{:S(2)}, u32[]{:S(2)}) collective-permute-start(bf16[4,256,128]{2,1,0:T(8,128)(2,1)} %fusion.14), channel_id=1, source_target_pairs={{0,16},{1,17},{2,18},{3,19},{4,20},{5,21},{6,22},{7,23},{8,24},{9,... | collective-permute-start | bytes 786440 | tf_op jit(solution)/shard_map/ppermute | solution.py:689
  455.7 47.4 %collective-permute-start.51 = (bf16[2,4,128,1024]{3,2,1,0:T(8,128)(2,1)S(1)}, bf16[2,4,128,1024]{3,2,1,0:T(8,128)(2,1)}, u32[]{:S(2)}, u32[]{:S(2)}) collective-permute-start(bf16[2,4,128,1024]{3,2,1,0:T(8,128)(2,1)S(1)} %get-tuple-element.108), channel_id=1, source_target_pairs={{0,8},{1,9},{2,10},{3,11},{4,12},{5,13},{6,14},{7,15},{8,0},{9,1},... | collective-permute-start | bytes 6291464 | tf_op jit(solution)/shard_map/ppermute | solution.py:689
  462.6 48.6 %collective-permute-start.45 = (bf16[2,4,256,512]{3,2,1,0:T(8,128)(2,1)S(1)}, bf16[2,4,256,512]{3,2,1,0:T(8,128)(2,1)S(1)}, u32[]{:S(2)}, u32[]{:S(2)}) collective-permute-start(bf16[2,4,256,512]{3,2,1,0:T(8,128)(2,1)S(1)} %get-tuple-element.105), channel_id=1, source_target_pairs={{0,16},{1,17},{2,18},{3,19},{4,20},{5,21},{6,22},{7,23},{8,24},{9,... | collective-permute-start | bytes 6291464 | tf_op jit(solution)/shard_map/ppermute | solution.py:689
  464.6 12.8 %collective-permute-start.41 = (bf16[256,128]{1,0:T(8,128)(2,1)S(1)}, bf16[256,128]{1,0:T(8,128)(2,1)S(1)}, u32[]{:S(2)}, u32[]{:S(2)}) collective-permute-start(bf16[256,128]{1,0:T(8,128)(2,1)S(1)} %get-tuple-element.160), channel_id=1, source_target_pairs={{0,2},{1,3},{2,4},{3,5},{4,6},{5,7},{6,0},{7,1},{8,10},{9,11},{10,... | collective-permute-start | bytes 196616 | tf_op jit(solution)/shard_map/ppermute | solution.py:689
  466.5 26.1 %collective-permute-start.42 = (bf16[256,128]{1,0:T(8,128)(2,1)S(1)}, bf16[256,128]{1,0:T(8,128)(2,1)S(1)}, u32[]{:S(2)}, u32[]{:S(2)}) collective-permute-start(bf16[256,128]{1,0:T(8,128)(2,1)S(1)} %get-tuple-element.162), channel_id=1, source_target_pairs={{0,4},{1,5},{2,6},{3,7},{4,0},{5,1},{6,2},{7,3},{8,12},{9,13},{10,... | collective-permute-start | bytes 196616 | tf_op jit(solution)/shard_map/ppermute | solution.py:689
  468.9 23.7 %collective-permute-start.43 = (bf16[256,128]{1,0:T(8,128)(2,1)S(1)}, bf16[256,128]{1,0:T(8,128)(2,1)S(1)}, u32[]{:S(2)}, u32[]{:S(2)}) collective-permute-start(bf16[256,128]{1,0:T(8,128)(2,1)S(1)} %get-tuple-element.161), channel_id=1, source_target_pairs={{0,6},{1,7},{2,0},{3,1},{4,2},{5,3},{6,4},{7,5},{8,14},{9,15},{10,... | collective-permute-start | bytes 196616 | tf_op jit(solution)/shard_map/ppermute | solution.py:689
  505.7 78.0 %collective-permute-start.52 = (bf16[4,128,1024]{2,1,0:T(8,128)(2,1)}, bf16[4,128,1024]{2,1,0:T(8,128)(2,1)}, u32[]{:S(2)}, u32[]{:S(2)}) collective-permute-start(bf16[4,128,1024]{2,1,0:T(8,128)(2,1)} %fusion.1), channel_id=1, source_target_pairs={{0,16},{1,17},{2,18},{3,19},{4,20},{5,21},{6,22},{7,23},{8,24},{9,... | collective-permute-start | bytes 3145736 | tf_op jit(solution)/shard_map/ppermute | solution.py:689
  512.8 74.7 %collective-permute-start.46 = (bf16[4,256,512]{2,1,0:T(8,128)(2,1)}, bf16[4,256,512]{2,1,0:T(8,128)(2,1)}, u32[]{:S(2)}, u32[]{:S(2)}) collective-permute-start(bf16[4,256,512]{2,1,0:T(8,128)(2,1)} %fusion), channel_id=1, source_target_pairs={{0,8},{1,9},{2,10},{3,11},{4,12},{5,13},{6,14},{7,15},{8,0},{9,1},... | collective-permute-start | bytes 3145736 | tf_op jit(solution)/shard_map/ppermute | solution.py:689
  535.8 55.2 %collective-permute-start.32 = (bf16[256,384]{0,1:T(8,128)(2,1)}, bf16[256,384]{0,1:T(8,128)(2,1)}, u32[]{:S(2)}, u32[]{:S(2)}) collective-permute-start(bf16[256,384]{0,1:T(8,128)(2,1)} %bitcast.210), channel_id=1, source_target_pairs={{0,8},{1,9},{2,10},{3,11},{4,12},{5,13},{6,14},{7,15},{8,0},{9,1},... | collective-permute-start | bytes 589832 | tf_op jit(solution)/shard_map/ppermute | solution.py:689
  538.8 52.2 %collective-permute-start.33 = (bf16[256,384]{0,1:T(8,128)(2,1)}, bf16[256,384]{0,1:T(8,128)(2,1)}, u32[]{:S(2)}, u32[]{:S(2)}) collective-permute-start(bf16[256,384]{0,1:T(8,128)(2,1)} %bitcast.211), channel_id=1, source_target_pairs={{0,16},{1,17},{2,18},{3,19},{4,20},{5,21},{6,22},{7,23},{8,24},{9,... | collective-permute-start | bytes 589832 | tf_op jit(solution)/shard_map/ppermute | solution.py:689
  541.4 49.7 %collective-permute-start.34 = (bf16[256,384]{0,1:T(8,128)(2,1)}, bf16[256,384]{0,1:T(8,128)(2,1)}, u32[]{:S(2)}, u32[]{:S(2)}) collective-permute-start(bf16[256,384]{0,1:T(8,128)(2,1)} %bitcast.212), channel_id=1, source_target_pairs={{0,24},{1,25},{2,26},{3,27},{4,28},{5,29},{6,30},{7,31},{8,16},{9,... | collective-permute-start | bytes 589832 | tf_op jit(solution)/shard_map/ppermute | solution.py:689
  583.8 15.3 %collective-permute-start.20 = (bf16[4,4,128,256]{3,2,1,0:T(8,128)(2,1)S(1)}, bf16[4,4,128,256]{3,2,1,0:T(8,128)(2,1)S(1)}, u32[]{:S(2)}, u32[]{:S(2)}) collective-permute-start(bf16[4,4,128,256]{3,2,1,0:T(8,128)(2,1)S(1)} %grad_blocks.10), channel_id=1, source_target_pairs={{0,1},{1,0},{2,3},{3,2},{4,5},{5,4},{6,7},{7,6},{8,9},{9,8},{10,11... | collective-permute-start | bytes 3145736 | tf_op jit(solution)/shard_map/ppermute | solution.py:689
  587.5 23.5 %collective-permute-start.26 = (bf16[4,4,128,256]{3,2,1,0:T(8,128)(2,1)}, bf16[4,4,128,256]{3,2,1,0:T(8,128)(2,1)}, u32[]{:S(2)}, u32[]{:S(2)}) collective-permute-start(bf16[4,4,128,256]{3,2,1,0:T(8,128)(2,1)} %grad_blocks.12), channel_id=1, source_target_pairs={{0,1},{1,0},{2,3},{3,2},{4,5},{5,4},{6,7},{7,6},{8,9},{9,8},{10,11... | collective-permute-start | bytes 3145736 | tf_op jit(solution)/shard_map/ppermute | solution.py:689
  592.3 10.4 %collective-permute-start.35 = (bf16[256,128]{0,1:T(8,128)(2,1)S(1)}, bf16[256,128]{0,1:T(8,128)(2,1)S(1)}, u32[]{:S(2)}, u32[]{:S(2)}) collective-permute-start(bf16[256,128]{0,1:T(8,128)(2,1)S(1)} %get-tuple-element.169), channel_id=1, source_target_pairs={{0,0},{3,1},{6,2},{1,3},{4,4},{7,5},{2,6},{5,7},{8,8},{11,9},{14,1... | collective-permute-start | bytes 196616 | tf_op jit(solution)/shard_map/ppermute | solution.py:666
  593.0 12.6 %collective-permute-start.36 = (bf16[256,128]{0,1:T(8,128)(2,1)S(1)}, bf16[256,128]{0,1:T(8,128)(2,1)S(1)}, u32[]{:S(2)}, u32[]{:S(2)}) collective-permute-start(bf16[256,128]{0,1:T(8,128)(2,1)S(1)} %get-tuple-element.170), channel_id=1, source_target_pairs={{1,0},{4,1},{7,2},{2,3},{5,4},{0,5},{3,6},{6,7},{9,8},{12,9},{15,1... | collective-permute-start | bytes 196616 | tf_op jit(solution)/shard_map/ppermute | solution.py:666
  593.0 13.6 %collective-permute-start.37 = (bf16[256,128]{0,1:T(8,128)(2,1)S(1)}, bf16[256,128]{0,1:T(8,128)(2,1)S(1)}, u32[]{:S(2)}, u32[]{:S(2)}) collective-permute-start(bf16[256,128]{0,1:T(8,128)(2,1)S(1)} %get-tuple-element.171), channel_id=1, source_target_pairs={{2,0},{5,1},{0,2},{3,3},{6,4},{1,5},{4,6},{7,7},{10,8},{13,9},{8,1... | collective-permute-start | bytes 196616 | tf_op jit(solution)/shard_map/ppermute | solution.py:666
  599.0 17.7 %collective-permute-start.53 = (bf16[128,1024]{1,0:T(8,128)(2,1)}, bf16[128,1024]{1,0:T(8,128)(2,1)}, u32[]{:S(2)}, u32[]{:S(2)}) collective-permute-start(bf16[128,1024]{1,0:T(8,128)(2,1)} %get-tuple-element.150), channel_id=1, source_target_pairs={{0,2},{1,3},{2,4},{3,5},{4,6},{5,7},{6,0},{7,1},{8,10},{9,11},{10,... | collective-permute-start | bytes 786440 | tf_op jit(solution)/shard_map/ppermute | solution.py:689
  602.7 18.0 %collective-permute-start.54 = (bf16[128,1024]{1,0:T(8,128)(2,1)}, bf16[128,1024]{1,0:T(8,128)(2,1)}, u32[]{:S(2)}, u32[]{:S(2)}) collective-permute-start(bf16[128,1024]{1,0:T(8,128)(2,1)} %get-tuple-element.152), channel_id=1, source_target_pairs={{0,4},{1,5},{2,6},{3,7},{4,0},{5,1},{6,2},{7,3},{8,12},{9,13},{10,... | collective-permute-start | bytes 786440 | tf_op jit(solution)/shard_map/ppermute | solution.py:689
  605.5 30.0 %collective-permute-start.55 = (bf16[128,1024]{1,0:T(8,128)(2,1)}, bf16[128,1024]{1,0:T(8,128)(2,1)}, u32[]{:S(2)}, u32[]{:S(2)}) collective-permute-start(bf16[128,1024]{1,0:T(8,128)(2,1)} %get-tuple-element.151), channel_id=1, source_target_pairs={{0,6},{1,7},{2,0},{3,1},{4,2},{5,3},{6,4},{7,5},{8,14},{9,15},{10,... | collective-permute-start | bytes 786440 | tf_op jit(solution)/shard_map/ppermute | solution.py:689
  606.6 31.2 %collective-permute-start.21 = (bf16[2,4,128,256]{3,2,1,0:T(8,128)(2,1)}, bf16[2,4,128,256]{3,2,1,0:T(8,128)(2,1)}, u32[]{:S(2)}, u32[]{:S(2)}) collective-permute-start(bf16[2,4,128,256]{3,2,1,0:T(8,128)(2,1)} %get-tuple-element.93), channel_id=1, source_target_pairs={{0,8},{1,9},{2,10},{3,11},{4,12},{5,13},{6,14},{7,15},{8,0},{9,1},... | collective-permute-start | bytes 1572872 | tf_op jit(solution)/shard_map/ppermute | solution.py:689
  611.1 29.0 %collective-permute-start.47 = (bf16[256,512]{1,0:T(8,128)(2,1)}, bf16[256,512]{1,0:T(8,128)(2,1)S(1)}, u32[]{:S(2)}, u32[]{:S(2)}) collective-permute-start(bf16[256,512]{1,0:T(8,128)(2,1)} %get-tuple-element.153), channel_id=1, source_target_pairs={{0,2},{1,3},{2,4},{3,5},{4,6},{5,7},{6,0},{7,1},{8,10},{9,11},{10,... | collective-permute-start | bytes 786440 | tf_op jit(solution)/shard_map/ppermute | solution.py:689
  616.8 25.3 %collective-permute-start.48 = (bf16[256,512]{1,0:T(8,128)(2,1)S(1)}, bf16[256,512]{1,0:T(8,128)(2,1)S(1)}, u32[]{:S(2)}, u32[]{:S(2)}) collective-permute-start(bf16[256,512]{1,0:T(8,128)(2,1)S(1)} %copy-done.53), channel_id=1, source_target_pairs={{0,4},{1,5},{2,6},{3,7},{4,0},{5,1},{6,2},{7,3},{8,12},{9,13},{10,... | collective-permute-start | bytes 786440 | tf_op jit(solution)/shard_map/ppermute | solution.py:689
  620.7 21.8 %collective-permute-start.49 = (bf16[256,512]{1,0:T(8,128)(2,1)S(1)}, bf16[256,512]{1,0:T(8,128)(2,1)S(1)}, u32[]{:S(2)}, u32[]{:S(2)}) collective-permute-start(bf16[256,512]{1,0:T(8,128)(2,1)S(1)} %copy-done.52), channel_id=1, source_target_pairs={{0,6},{1,7},{2,0},{3,1},{4,2},{5,3},{6,4},{7,5},{8,14},{9,15},{10,... | collective-permute-start | bytes 786440 | tf_op jit(solution)/shard_map/ppermute | solution.py:689
  635.5 10.0 %collective-permute-start.27 = (bf16[2,4,128,256]{3,2,1,0:T(8,128)(2,1)}, bf16[2,4,128,256]{3,2,1,0:T(8,128)(2,1)S(1)}, u32[]{:S(2)}, u32[]{:S(2)}) collective-permute-start(bf16[2,4,128,256]{3,2,1,0:T(8,128)(2,1)} %get-tuple-element.95), channel_id=1, source_target_pairs={{0,16},{1,17},{2,18},{3,19},{4,20},{5,21},{6,22},{7,23},{8,24},{9,... | collective-permute-start | bytes 1572872 | tf_op jit(solution)/shard_map/ppermute | solution.py:689
  638.9 8.8 %collective-permute-start.22 = (bf16[4,128,256]{2,1,0:T(8,128)(2,1)S(1)}, bf16[4,128,256]{2,1,0:T(8,128)(2,1)S(1)}, u32[]{:S(2)}, u32[]{:S(2)}) collective-permute-start(bf16[4,128,256]{2,1,0:T(8,128)(2,1)S(1)} %fusion.12), channel_id=1, source_target_pairs={{0,16},{1,17},{2,18},{3,19},{4,20},{5,21},{6,22},{7,23},{8,24},{9,... | collective-permute-start | bytes 786440 | tf_op jit(solution)/shard_map/ppermute | solution.py:689
  645.5 14.7 %collective-permute-start.28 = (bf16[4,128,256]{2,1,0:T(8,128)(2,1)S(1)}, bf16[4,128,256]{2,1,0:T(8,128)(2,1)S(1)}, u32[]{:S(2)}, u32[]{:S(2)}) collective-permute-start(bf16[4,128,256]{2,1,0:T(8,128)(2,1)S(1)} %fusion.13), channel_id=1, source_target_pairs={{0,8},{1,9},{2,10},{3,11},{4,12},{5,13},{6,14},{7,15},{8,0},{9,1},... | collective-permute-start | bytes 786440 | tf_op jit(solution)/shard_map/ppermute | solution.py:689
  648.8 14.1 %collective-permute-start.23 = (bf16[128,256]{1,0:T(8,128)(2,1)S(1)}, bf16[128,256]{1,0:T(8,128)(2,1)S(1)}, u32[]{:S(2)}, u32[]{:S(2)}) collective-permute-start(bf16[128,256]{1,0:T(8,128)(2,1)S(1)} %get-tuple-element.163), channel_id=1, source_target_pairs={{0,2},{1,3},{2,4},{3,5},{4,6},{5,7},{6,0},{7,1},{8,10},{9,11},{10,... | collective-permute-start | bytes 196616 | tf_op jit(solution)/shard_map/ppermute | solution.py:689
  657.8 7.7 %collective-permute-start.24 = (bf16[128,256]{1,0:T(8,128)(2,1)S(1)}, bf16[128,256]{1,0:T(8,128)(2,1)S(1)}, u32[]{:S(2)}, u32[]{:S(2)}) collective-permute-start(bf16[128,256]{1,0:T(8,128)(2,1)S(1)} %get-tuple-element.165), channel_id=1, source_target_pairs={{0,4},{1,5},{2,6},{3,7},{4,0},{5,1},{6,2},{7,3},{8,12},{9,13},{10,... | collective-permute-start | bytes 196616 | tf_op jit(solution)/shard_map/ppermute | solution.py:689
  657.8 7.7 %collective-permute-start.25 = (bf16[128,256]{1,0:T(8,128)(2,1)S(1)}, bf16[128,256]{1,0:T(8,128)(2,1)S(1)}, u32[]{:S(2)}, u32[]{:S(2)}) collective-permute-start(bf16[128,256]{1,0:T(8,128)(2,1)S(1)} %get-tuple-element.164), channel_id=1, source_target_pairs={{0,6},{1,7},{2,0},{3,1},{4,2},{5,3},{6,4},{7,5},{8,14},{9,15},{10,... | collective-permute-start | bytes 196616 | tf_op jit(solution)/shard_map/ppermute | solution.py:689
  660.3 6.5 collective-permute-start.29
  660.4 8.6 %collective-permute-start.30 = (bf16[128,256]{1,0:T(8,128)(2,1)S(1)}, bf16[128,256]{1,0:T(8,128)(2,1)S(1)}, u32[]{:S(2)}, u32[]{:S(2)}) collective-permute-start(bf16[128,256]{1,0:T(8,128)(2,1)S(1)} %get-tuple-element.168), channel_id=1, source_target_pairs={{0,4},{1,5},{2,6},{3,7},{4,0},{5,1},{6,2},{7,3},{8,12},{9,13},{10,... | collective-permute-start | bytes 196616 | tf_op jit(solution)/shard_map/ppermute | solution.py:689
  662.9 6.1 collective-permute-start.31
  (63 other events, 874.8 us)
Sparse Core Ops, SparseCore 0:
  11.1 66.4 all-gather.11
  112.7 86.4 all-gather.13
  202.2 55.8 all-gather.15
  261.4 100.3 all-gather.17

commit v3 on v2

--- a/solution.py
+++ b/solution.py
@@ -712,132 +712,225 @@
     return jnp.concatenate(parts, axis=1)
 
 
+def stay_order(value, first, second):
+    return (value // second) % 2 + 2 * ((value // first) % 2)
+
+
 def middle_kernel(
-    place_ref, att_ref, stream_ref, low_ref, scale_ref, shift_ref, out_w_ref,
+    place_ref, att_ref, stream_ref, low_ref, turned_low_ref, scale_ref, shift_ref,
     up_0, up_1, up_2, up_3, down_0, down_1, down_2, down_3,
-    layer_ref, hidden_ref, grad_up_ref, grad_mid_ref, grad_low_ref, grad_att_ref, sums_ref, turned_ref,
-    up_w, down_w, normed_ref, middle_ref, out_acc, grad_acc, up_sem, down_sem, *, dp, seq,
+    layer_ref, grad_mid_ref, grad_att_ref, sums_ref, down_own_out, down_other_out, up_own_out, up_other_out,
+    up_w, down_w, out_w, normed_ref, turned_ref, sorted_ref, middle_ref, out_acc,
+    down_own, down_other, up_own, up_other, up_sem, down_sem, out_sem, send_sem, *, dp, seq,
 ):
     dp_at, chip_at, core_at = place_ref[0], place_ref[1], place_ref[2]
     chips = seq // 2
     up_rows, up_cols = up_0.shape[2], up_0.shape[3]
-    down_rows, down_cols = down_0.shape[2], down_0.shape[3]
-
-    def copies():
+    cols = down_0.shape[3]
+    width = stream_ref.shape[1]
+    out_rows = width // dp
+    down_rows = down_0.shape[2] - out_rows
+
+    def copies(name):
         made = []
-        for name, pieces, masks, sems in (
-            ("up", (up_0, up_1, up_2, up_3), (1, 2), up_sem),
-            ("down", (down_0, down_1, down_2, down_3), (2, 1), down_sem),
-        ):
-            for part in range(4):
-                core = core_at if part < 2 else 1 - core_at
-                for step in range(2):
-                    mask = (masks[1] if part % 2 else 0) ^ (masks[0] if step else 0)
-                    row = jnp.bitwise_xor(dp_at, mask)
-                    for back in range(chips):
-                        block = 2 * lax.rem(chip_at + chips - back, chips) + core
-                        if name == "up":
-                            target = up_w.at[block, pl.ds(pl.multiple_of(row * up_rows, up_rows), up_rows), :]
-                        else:
-                            target = down_w.at[
-                                pl.ds(pl.multiple_of(row * down_rows, down_rows), down_rows),
-                                pl.ds(pl.multiple_of(block * down_cols, down_cols), down_cols),
-                            ]
-                        made.append(
-                            pltpu.make_async_copy(
-                                pieces[part].at[step, back], target, sems.at[(part * 2 + step) * chips + back]
-                            )
-                        )
+        pieces, masks = ((up_0, up_1, up_2, up_3), (1, 2)) if name == "up" else ((down_0, down_1, down_2, down_3), (2, 1))
+        for part in range(4):
+            core = core_at if part < 2 else 1 - core_at
+            for step in range(2):
+                mask = (masks[1] if part % 2 else 0) ^ (masks[0] if step else 0)
+                row = jnp.bitwise_xor(dp_at, mask)
+                for back in range(chips):
+                    block = 2 * lax.rem(chip_at + chips - back, chips) + core
+                    column = pl.ds(pl.multiple_of(block * cols, cols), cols)
+                    source, at = pieces[part].at[step, back], (part * 2 + step) * chips + back
+                    if name == "up":
+                        target = up_w.at[block, pl.ds(pl.multiple_of(row * up_rows, up_rows), up_rows), :]
+                        sem = up_sem.at[at]
+                    elif name == "down":
+                        source = source.at[pl.ds(0, down_rows), :]
+                        target = down_w.at[pl.ds(pl.multiple_of(row * down_rows, down_rows), down_rows), column]
+                        sem = down_sem.at[at]
+                    else:
+                        source = source.at[pl.ds(down_rows, out_rows), :]
+                        target = out_w.at[pl.ds(pl.multiple_of(row * out_rows, out_rows), out_rows), column]
+                        sem = out_sem.at[at]
+                    made.append(pltpu.make_async_copy(source, target, sem))
         return made
 
-    for copy in copies():
+    for name in ("out", "up", "down"):
+        for copy in copies(name):
+            copy.start()
+    tiles = [
+        2 * lax.rem(chip_at + ahead, chips) + (1 - core_at if other else core_at)
+        for other in range(2)
+        for ahead in range(chips)
+    ]
+    for at, tile in enumerate(tiles):
+        rows = pl.ds(pl.multiple_of(tile * cols, cols), cols)
+        sorted_ref[at * cols : (at + 1) * cols, :] = turned_low_ref[rows, :]
+    for copy in copies("out"):
+        copy.wait()
+    middle_ref[...] = stream_ref[...] + dot_tn(att_ref[...], out_w[...])
+    grad_acc = grad_mid_ref
+    chunk = 128
+
+    @pl.loop(0, stream_ref.shape[0] // chunk)
+    def _(index):
+        rows = pl.ds(pl.multiple_of(index * chunk, chunk), chunk)
+        middle = middle_ref[rows, :]
+        inverse = lax.rsqrt(jnp.mean(middle * middle, axis=-1, keepdims=True) + epsilon)
+        normed = middle * inverse * (1.0 + scale_ref[...]) + shift_ref[...]
+        normed_ref[rows, :] = normed.astype(jnp.bfloat16)
+        turned = normed.T.astype(jnp.bfloat16)
+        for row in range(dp):
+            place = stay_order(jnp.bitwise_xor(dp_at, row), 2, 1)
+            turned_ref[pl.ds(pl.multiple_of(place * out_rows, out_rows), out_rows), rows] = turned[
+                row * out_rows : (row + 1) * out_rows
+            ]
+        out_acc[rows, :] = jnp.zeros_like(middle)
+        grad_acc[rows, :] = jnp.zeros_like(middle)
+
+    for name in ("up", "down"):
+        for copy in copies(name):
+            copy.wait()
+
+    def hidden_block(other, up_grads):
+        def run(ahead, carry):
+            core = 1 - core_at if other else core_at
+            block = 2 * lax.rem(chip_at + ahead, chips) + core
+            rows = pl.ds(pl.multiple_of(block * up_cols, up_cols), up_cols)
+            up_weight, down_weight = up_w[block], down_w[rows, :]
+            value, derivative = gelu_parts(dot_nn(normed_ref[...], up_weight))
+            hidden = value.astype(jnp.bfloat16)
+            out_acc[...] += dot_nn(hidden, down_weight)
+            grad_up = (dot_nt(low_ref[...], down_weight) * derivative).astype(jnp.bfloat16)
+            grad_acc[...] += dot_nt(grad_up, up_weight)
+            for owner in range(dp):
+                part = dot_nn(turned_ref[owner * up_rows : (owner + 1) * up_rows, :], grad_up)
+                up_grads[owner, ahead] = part.astype(jnp.bfloat16)
+            per_owner = down_rows // up_cols
+            owner = stay_order(jnp.bitwise_xor(dp_at, block // per_owner), 1, 2)
+            at = pl.ds(pl.multiple_of(lax.rem(block, per_owner) * cols, cols), cols)
+            for pair in range(chips):
+                part = dot_nn(sorted_ref[2 * pair * cols : 2 * (pair + 1) * cols, :], hidden).astype(jnp.bfloat16)
+                for tile in range(2):
+                    target, place = (down_own, 2 * pair + tile) if pair < chips // 2 else (down_other, 2 * pair + tile - chips)
+                    target[owner, place, at, :] = part[tile * cols : (tile + 1) * cols]
+            return carry
+
+        lax.fori_loop(0, chips, run, 0)
+
+    hidden_block(1, up_other)
+    send_up_other = pltpu.make_async_copy(up_other, up_other_out, send_sem.at[0])
+    send_up_other.start()
+    hidden_block(0, up_own)
+    packed = down_rows * cols // up_cols
+    sends = [
+        pltpu.make_async_copy(up_own, up_own_out, send_sem.at[1]),
+        pltpu.make_async_copy(
+            down_other.at[:, :, pl.ds(0, packed), :], down_other_out.at[:, :, pl.ds(0, packed), :], send_sem.at[2]
+        ),
+        pltpu.make_async_copy(
+            down_own.at[:, :, pl.ds(0, packed), :], down_own_out.at[:, :, pl.ds(0, packed), :], send_sem.at[3]
+        ),
+    ]
+    for copy in sends:
         copy.start()
-    width = stream_ref.shape[1]
-    tile_rows = width // dp
-    middle_ref[...] = stream_ref[...]
+    sums_ref[...] = jnp.zeros_like(sums_ref)
+
+    @pl.loop(0, stream_ref.shape[0] // chunk)
+    def _(index):
+        rows = pl.ds(pl.multiple_of(index * chunk, chunk), chunk)
+        middle = middle_ref[rows, :]
+        layer_ref[rows, :] = (middle + out_acc[rows, :]).astype(jnp.bfloat16)
+        inverse = lax.rsqrt(jnp.mean(middle * middle, axis=-1, keepdims=True) + epsilon)
+        unit = middle * inverse
+        grad = grad_acc[rows, :]
+        lifted = grad * (1.0 + scale_ref[...])
+        sums_ref[0:1, :] += jnp.sum(grad * unit, axis=0, keepdims=True)
+        sums_ref[1:2, :] += jnp.sum(grad, axis=0, keepdims=True)
+        grad_mid = low_ref[rows, :].astype(jnp.float32) + inverse * (
+            lifted - unit * jnp.mean(lifted * unit, axis=-1, keepdims=True)
+        )
+        grad_mid_ref[rows, :] = grad_mid
+        normed_ref[rows, :] = grad_mid.astype(jnp.bfloat16)
+
+    grad_att_ref[...] = dot_nt(out_w[...], normed_ref[...]).astype(jnp.bfloat16)
+    grads = lanes([normed_ref[:, pl.ds(pl.multiple_of(tile * cols, cols), cols)] for tile in tiles])
+    per_row = up_cols // cols
+    folded = out_rows // per_row
     for row in range(dp):
-        weight = lanes([out_w_ref[row * seq + s] for s in range(seq)])
-        middle_ref[...] += dot_tn(att_ref[row * tile_rows : (row + 1) * tile_rows, :], weight)
-    middle = middle_ref[...]
-    inverse = lax.rsqrt(jnp.mean(middle * middle, axis=-1, keepdims=True) + epsilon)
-    normed = middle * inverse * (1.0 + scale_ref[...]) + shift_ref[...]
-    normed_ref[...] = normed.astype(jnp.bfloat16)
-    turned_ref[...] = normed.T.astype(jnp.bfloat16)
-    for copy in copies():
+        owner = stay_order(jnp.bitwise_xor(dp_at, row), 1, 2)
+        product = dot_nn(att_ref[row * out_rows : (row + 1) * out_rows, :], grads).astype(jnp.bfloat16)
+        for at in range(seq):
+            part = product[:, at * cols : (at + 1) * cols]
+            part = lanes([part[i * folded : (i + 1) * folded] for i in range(per_row)])
+            target = down_own if at < chips else down_other
+            target[owner, at % chips, packed : packed + folded, :] = part
+    last = [
+        pltpu.make_async_copy(
+            down_other.at[:, :, pl.ds(packed, folded), :], down_other_out.at[:, :, pl.ds(packed, folded), :], send_sem.at[4]
+        ),
+        pltpu.make_async_copy(
+            down_own.at[:, :, pl.ds(packed, folded), :], down_own_out.at[:, :, pl.ds(packed, folded), :], send_sem.at[5]
+        ),
+    ]
+    for copy in last:
+        copy.start()
+    for copy in [send_up_other] + sends + last:
         copy.wait()
-    out_acc[...] = jnp.zeros_like(out_acc)
-    grad_acc[...] = jnp.zeros_like(grad_acc)
-
-    @pl.loop(0, seq)
-    def _(block):
-        rows = pl.ds(pl.multiple_of(block * up_cols, up_cols), up_cols)
-        up_weight, down_weight = up_w[block], down_w[rows, :]
-        value, derivative = gelu_parts(dot_nn(normed_ref[...], up_weight))
-        hidden = value.astype(jnp.bfloat16)
-        hidden_ref[:, rows] = hidden
-        out_acc[...] += dot_nn(hidden, down_weight)
-        grad_up = (dot_nt(low_ref[...], down_weight) * derivative).astype(jnp.bfloat16)
-        grad_up_ref[:, rows] = grad_up
-        grad_acc[...] += dot_nt(grad_up, up_weight)
-
-    middle = middle_ref[...]
-    layer_ref[...] = (middle + out_acc[...]).astype(jnp.bfloat16)
-    inverse = lax.rsqrt(jnp.mean(middle * middle, axis=-1, keepdims=True) + epsilon)
-    unit = middle * inverse
-    grad = grad_acc[...]
-    lifted = grad * (1.0 + scale_ref[...])
-    sums_ref[0:1, :] = jnp.sum(grad * unit, axis=0, keepdims=True)
-    sums_ref[1:2, :] = jnp.sum(grad, axis=0, keepdims=True)
-    grad_mid = low_ref[...].astype(jnp.float32) + inverse * (
-        lifted - unit * jnp.mean(lifted * unit, axis=-1, keepdims=True)
-    )
-    grad_mid_ref[...] = grad_mid
-    grad_low_ref[...] = grad_mid.astype(jnp.bfloat16)
-    for row in range(dp):
-        weight = lanes([out_w_ref[row * seq + s] for s in range(seq)])
-        grad_att_ref[row * tile_rows : (row + 1) * tile_rows, :] = dot_nt(weight, grad_low_ref[...]).astype(
-            jnp.bfloat16
-        )
-
-
-def middle_block(place, attended, stream, grad_low, scale, shift, out_tiles, up_pieces, down_pieces, dp, seq):
+
+
+def middle_block(place, attended, stream, grad_low, scale, shift, up_pieces, down_pieces, dp, seq):
     frames, width = stream.shape
-    hidden = up_pieces[0].shape[3] * seq
+    tile_cols = up_pieces[0].shape[3]
+    hidden = tile_cols * seq
+    chips = seq // 2
+    packed = hidden // dp * (width // seq) // tile_cols + width // dp * (width // seq) // tile_cols
     whole = pl.BlockSpec(memory_space=pltpu.VMEM)
     anywhere = pl.BlockSpec(memory_space=pl.ANY)
-    low, wide = jnp.bfloat16, jnp.float32
+    half, full = jnp.bfloat16, jnp.float32
+    down_shape, up_shape = (dp, chips, packed, tile_cols), (dp, chips, width // dp, tile_cols)
     return pl.pallas_call(
         partial(middle_kernel, dp=dp, seq=seq),
         in_specs=[pl.BlockSpec(memory_space=pltpu.SMEM)] + [whole] * 6 + [anywhere] * 8,
-        out_specs=[whole] * 8,
+        out_specs=[whole] * 4 + [anywhere] * 4,
         out_shape=[
-            jax.ShapeDtypeStruct((frames, width), low),
-            jax.ShapeDtypeStruct((frames, hidden), low),
-            jax.ShapeDtypeStruct((frames, hidden), low),
-            jax.ShapeDtypeStruct((frames, width), wide),
-            jax.ShapeDtypeStruct((frames, width), low),
-            jax.ShapeDtypeStruct((width, frames), low),
-            jax.ShapeDtypeStruct((2, width), wide),
-            jax.ShapeDtypeStruct((width, frames), low),
+            jax.ShapeDtypeStruct((frames, width), half),
+            jax.ShapeDtypeStruct((frames, width), full),
+            jax.ShapeDtypeStruct((width, frames), half),
+            jax.ShapeDtypeStruct((2, width), full),
+            jax.ShapeDtypeStruct(down_shape, half),
+            jax.ShapeDtypeStruct(down_shape, half),
+            jax.ShapeDtypeStruct(up_shape, half),
+            jax.ShapeDtypeStruct(up_shape, half),
         ],
         scratch_shapes=[
-            pltpu.VMEM((seq, width, hidden // seq), low),
-            pltpu.VMEM((hidden, width), low),
-            pltpu.VMEM((frames, width), low),
-            pltpu.VMEM((frames, width), wide),
-            pltpu.VMEM((frames, width), wide),
-            pltpu.VMEM((frames, width), wide),
+            pltpu.VMEM((seq, width, tile_cols), half),
+            pltpu.VMEM((hidden, width), half),
+            pltpu.VMEM((width, width), half),
+            pltpu.VMEM((frames, width), half),
+            pltpu.VMEM((width, frames), half),
+            pltpu.VMEM((width, frames), half),
+            pltpu.VMEM((frames, width), full),
+            pltpu.VMEM((frames, width), full),
+            pltpu.VMEM(down_shape, half),
+            pltpu.VMEM(down_shape, half),
+            pltpu.VMEM(up_shape, half),
+            pltpu.VMEM(up_shape, half),
             pltpu.SemaphoreType.DMA((dp * seq,)),
             pltpu.SemaphoreType.DMA((dp * seq,)),
+            pltpu.SemaphoreType.DMA((dp * seq,)),
+            pltpu.SemaphoreType.DMA((6,)),
         ],
-        compiler_params=pltpu.CompilerParams(vmem_limit_bytes=58 << 20),
+        compiler_params=pltpu.CompilerParams(vmem_limit_bytes=62 << 20),
         cost_estimate=pl.CostEstimate(
-            flops=8 * frames * width * hidden + 4 * frames * width * width,
-            bytes_accessed=4 * hidden * width + 24 * frames * width,
+            flops=12 * frames * width * hidden + 6 * frames * width * width,
+            bytes_accessed=8 * hidden * width + 24 * frames * width,
             transcendentals=frames * hidden,
         ),
         name="middle_block",
-    )(place, attended, stream, grad_low, scale, shift, out_tiles, *up_pieces, *down_pieces)
+    )(place, attended, stream, grad_low, grad_low.T, scale, shift, *up_pieces, *down_pieces)
 
 
 def entry_kernel(main_ref, side_ref, weight_ref, scale_ref, shift_ref, stream_ref, normed_ref, *, dp, seq):
@@ -961,79 +1054,117 @@
     )(grad_stream, skip_tiles)
 
 
-def blocks_kernel(place_ref, left_ref, right_ref, *refs, kind, masks, other, chips):
-    chip_at, core_at = place_ref[1], place_ref[2]
-    core = 1 - core_at if other else core_at
+def near_first(place_ref, chips, other, block):
+    core = 1 - place_ref[2] if other else place_ref[2]
+    starts = [(2 * lax.rem(place_ref[1] + ahead, chips) + core) * block for ahead in range(chips)]
+    return [pl.multiple_of(start, block) for start in starts]
+
+
+def turned_parts(place_ref, left_ref, right_ref, chips, seq, other):
+    block = left_ref.shape[0] // seq
+    starts = near_first(place_ref, chips, other, block)
+    left = jnp.concatenate([left_ref[pl.ds(start, block), :] for start in starts], axis=0)
+    product = dot_nn(left, right_ref[...])
+    return [product[ahead * block : (ahead + 1) * block] for ahead in range(chips)]
+
+
+def plain_parts(place_ref, left_ref, right_ref, chips, seq, other):
+    block = right_ref.shape[1] // seq
+    starts = near_first(place_ref, chips, other, block)
+    product = dot_nn(left_ref[...], lanes([right_ref[:, pl.ds(start, block)] for start in starts]))
+    return [product[:, ahead * block : (ahead + 1) * block] for ahead in range(chips)]
+
+
+def fold_columns(part, width):
+    return jnp.concatenate([part[:, at : at + width] for at in range(0, part.shape[1], width)], axis=0)
+
+
+def fold_rows(part, width):
+    rows = part.shape[0] * part.shape[1] // width
+    return lanes([part[at : at + rows] for at in range(0, part.shape[0], rows)])
+
+
+def blocks_kernel(place_ref, *refs, kinds, other, seq, width):
+    chips = seq // 2
     step = pl.program_id(0)
-    out_refs = refs if other else refs[1:]
-    block = out_refs[0].shape[2] if kind == "turned" else out_refs[0].shape[3]
-    starts = [(2 * lax.rem(chip_at + ahead, chips) + core) * block for ahead in range(chips)]
-    starts = [pl.multiple_of(start, block) for start in starts]
-    if kind == "turned":
-        left = jnp.concatenate([left_ref[pl.ds(start, block), :] for start in starts], axis=0)
-        product = dot_nn(left, right_ref[...])
-        parts = [product[ahead * block : (ahead + 1) * block] for ahead in range(chips)]
-    else:
-        right = lanes([right_ref[:, pl.ds(start, block)] for start in starts])
-        product = dot_nn(left_ref[...], right)
-        parts = [product[:, ahead * block : (ahead + 1) * block] for ahead in range(chips)]
-    if other:
+    operands, outs = refs[: 2 * len(kinds)], refs[2 * len(kinds) :]
+    packed = [[] for _ in range(chips)]
+    for at, kind in enumerate(kinds):
+        left_ref, right_ref = operands[2 * at], operands[2 * at + 1]
+        if kind == "turned":
+            parts = [fold_columns(part, width) for part in turned_parts(place_ref, left_ref, right_ref, chips, seq, other)]
+        else:
+            parts = plain_parts(place_ref, left_ref, right_ref, chips, seq, other)
+            parts = [fold_rows(part, width) if part.shape[1] < width else part for part in parts]
         for ahead in range(chips):
-            out_refs[0][0, ahead] = parts[ahead].astype(jnp.bfloat16)
-        return
-    parts = [parts[ahead] + refs[0][0, ahead].astype(jnp.float32) for ahead in range(chips)]
-
-    @pl.when(step < 2)
-    def _():
-        for ahead in range(chips):
-            out_refs[0][0, ahead] = parts[ahead].astype(jnp.bfloat16)
-
-    @pl.when(step >= 2)
-    def _():
-        for ahead in range(chips):
-            out_refs[1][0, ahead] = parts[ahead].astype(jnp.bfloat16)
-
-
-def grad_blocks(place, left, right, kind, masks, seq, arrived=None, part=(0, 1)):
+            packed[ahead].append(parts[ahead])
+    if not other:
+        arrived_ref, outs = outs[0], outs[1:]
+    for ahead in range(chips):
+        row = 0
+        for part in packed[ahead]:
+            rows = slice(row, row + part.shape[0])
+            row += part.shape[0]
+            if other:
+                outs[0][0, ahead, rows, :] = part.astype(jnp.bfloat16)
+            else:
+                low = (part + arrived_ref[0, ahead, rows, :].astype(jnp.float32)).astype(jnp.bfloat16)
+
+                @pl.when(step < 2)
+                def _(low=low, ahead=ahead, rows=rows):
+                    outs[0][0, ahead, rows, :] = low
+
+                @pl.when(step >= 2)
+                def _(low=low, ahead=ahead, rows=rows):
+                    outs[1][0, ahead, rows, :] = low
+
+
+def grad_blocks(place, products, masks, seq, width, arrived=None, part=(0, 1)):
     first, second = masks
     chips, dp = seq // 2, 4
-    depth = left.shape[1]
 
     def owner(i, place):
         return jnp.bitwise_xor(place[0], (i % 2) * second + (i // 2) * first)
 
-    if kind == "turned":
-        columns = right.shape[1] // (dp * part[1])
-        shape = (left.shape[0] // seq, columns)
-        left_spec = pl.BlockSpec(left.shape, lambda i, place: (0, 0))
-        right_spec = pl.BlockSpec((depth, columns), lambda i, place: (0, owner(i, place) * part[1] + part[0]))
+    specs, operands, kinds, rows, flops = [], [], [], 0, 0
+    for kind, left, right in products:
+        depth = left.shape[1]
+        if kind == "turned":
+            columns = right.shape[1] // (dp * part[1])
+            shape = (left.shape[0] // seq, columns)
+            specs += [
+                pl.BlockSpec(left.shape, lambda i, place: (0, 0)),
+                pl.BlockSpec((depth, columns), lambda i, place: (0, owner(i, place) * part[1] + part[0])),
+            ]
+        else:
+            shape = (left.shape[0] // dp, right.shape[1] // seq)
+            specs += [
+                pl.BlockSpec((shape[0], depth), lambda i, place: (owner(i, place), 0)),
+                pl.BlockSpec(right.shape, lambda i, place: (0, 0)),
+            ]
+        operands += [left, right]
+        kinds.append(kind)
+        rows += shape[0] * shape[1] // width
+        flops += 2 * dp * chips * shape[0] * shape[1] * depth
+    other = arrived is None
+    one = (1, chips, rows, width)
+    if other:
+        outs, count = [pl.BlockSpec(one, lambda i, place: (i, 0, 0, 0))], 4
     else:
-        shape = (left.shape[0] // dp, right.shape[1] // seq)
-        left_spec = pl.BlockSpec((shape[0], depth), lambda i, place: (owner(i, place), 0))
-        right_spec = pl.BlockSpec(right.shape, lambda i, place: (0, 0))
-    other = arrived is None
-    one = (1, chips) + shape
-    if other:
-        specs, count = [pl.BlockSpec(one, lambda i, place: (i, 0, 0, 0))], 4
-        extra, operands = [], (left, right)
-    else:
-        specs = [
+        outs = [
             pl.BlockSpec(one, lambda i, place: (jnp.minimum(i, 1), 0, 0, 0)),
             pl.BlockSpec(one, lambda i, place: (jnp.maximum(i - 2, 0), 0, 0, 0)),
         ]
         count = 2
-        extra, operands = [pl.BlockSpec(one, lambda i, place: (i, 0, 0, 0))], (left, right, arrived)
+        specs.append(pl.BlockSpec(one, lambda i, place: (i, 0, 0, 0)))
+        operands.append(arrived)
     return pl.pallas_call(
-        partial(blocks_kernel, kind=kind, masks=masks, other=other, chips=chips),
-        grid_spec=pltpu.PrefetchScalarGridSpec(
-            num_scalar_prefetch=1, grid=(4,), in_specs=[left_spec, right_spec] + extra, out_specs=specs
-        ),
-        out_shape=[jax.ShapeDtypeStruct((count, chips) + shape, jnp.bfloat16)] * len(specs),
-        compiler_params=pltpu.CompilerParams(vmem_limit_bytes=40 << 20),
+        partial(blocks_kernel, kinds=tuple(kinds), other=other, seq=seq, width=width),
+        grid_spec=pltpu.PrefetchScalarGridSpec(num_scalar_prefetch=1, grid=(4,), in_specs=specs, out_specs=outs),
+        out_shape=[jax.ShapeDtypeStruct((count, chips, rows, width), jnp.bfloat16)] * len(outs),
+        compiler_params=pltpu.CompilerParams(vmem_limit_bytes=48 << 20),
         cost_estimate=pl.CostEstimate(
-            flops=2 * dp * chips * shape[0] * shape[1] * depth,
-            bytes_accessed=2 * dp * chips * shape[0] * shape[1] * (1 if other else 2) + 2 * left.size + 2 * right.size,
-            transcendentals=0,
+            flops=flops, bytes_accessed=8 * rows * width * chips * (1 if other else 2) + flops // 512, transcendentals=0
         ),
         name="grad_blocks",
     )(place, *operands)
@@ -1046,37 +1177,14 @@
     return value.astype(jnp.float32)
 
 
-def scatter_first(place, left, right, kind, routes, seq, first, second, part=(0, 1)):
+def low(value):
+    return value.astype(jnp.bfloat16)
+
+
+def pair_sum(place, products, routes, seq, width, first, second, part=(0, 1)):
     masks = (AXIS_MASK[first], AXIS_MASK[second])
-    (outgoing,) = grad_blocks(place, left, right, kind, masks, seq, None, part)
-    arrived = send(outgoing, routes["core"])
-    keep, away = grad_blocks(place, left, right, kind, masks, seq, arrived, part)
-    return keep, send(away, routes[first])
-
-
-def scatter_second(state, routes, second):
-    keep, arrived = state
-    back = send((wide(keep[1]) + wide(arrived[1])).astype(jnp.bfloat16), routes[second])
-    return wide(keep[0]) + wide(arrived[0]), back
-
-
-def scatter_last(state, routes):
-    total = state[0] + wide(state[1])
-    low = total.astype(jnp.bfloat16)
-    got = [send(low[ahead + 1], route) for ahead, route in enumerate(routes["z"])]
-    result = total[0]
-    for piece in got:
-        result = result + wide(piece)
-    return result
-
-
-def dp_sum(value, routes, dp):
-    at = lax.axis_index("dp")
-    result = wide(lax.dynamic_index_in_dim(value, at, 0, keepdims=False))
-    for mask, route in ((1, routes["x"]), (2, routes["y"]), (3, routes["xy"])):
-        piece = lax.dynamic_index_in_dim(value, jnp.bitwise_xor(at, mask), 0, keepdims=False)
-        result = result + wide(send(piece, route))
-    return result
+    (outgoing,) = grad_blocks(place, products, masks, seq, width, None, part)
+    return grad_blocks(place, products, masks, seq, width, send(outgoing, routes["core"]), part)
 
 
 def dp_gather(tile, routes, dp):
@@ -1122,7 +1230,7 @@
     seq_at = lax.axis_index("seq")
     place = jnp.stack([lax.axis_index("dp"), seq_at // 2, seq_at % 2]).astype(jnp.int32)
     up_column = gather_column(up_weight, routes)
-    down_column = gather_column(down_weight, routes)
+    down_column = gather_column(jnp.concatenate([down_weight, out_weight]), routes)
     embed_all = lax.all_gather(time_embed, "dp", axis=0, tiled=True)
     embed_rows = width // dp
     embed_part = lax.dynamic_slice_in_dim(embed_all, lax.axis_index("dp") * embed_rows, embed_rows, 1)
@@ -1137,63 +1245,106 @@
     skip_tiles = lax.all_gather(skip_weight, ("dp", "seq"), axis=0)
     pair_tile = own_pair_columns(qkv_weight, seq)
     pair_weight = dp_gather(pair_tile, routes, dp)
-    skip_tiles, up_column, down_column, pair_weight, cos_all, sin_all, ends, grad_low, place = lax.optimization_barrier(
-        (skip_tiles, up_column, down_column, pair_weight.T, cos_all, sin_all, ends, grad_low, place)
+    skip_tiles, up_column, down_column, cos_all, sin_all, ends, grad_low, place = lax.optimization_barrier(
+        (skip_tiles, up_column, down_column, cos_all, sin_all, ends, grad_low, place)
     )
     stream, normed_one = entry_block(inputs[0], skip_input[0], skip_tiles, scale_one, shift_one, dp, seq)
     normed_all = lax.all_gather(normed_one, "seq", axis=0)
     up_near = gather_near(up_column, routes["x"])
     down_near = gather_near(down_column, routes["y"])
+    normed_all, up_near, down_near, pair_weight = lax.optimization_barrier(
+        (normed_all, up_near, down_near, pair_weight.T)
+    )
     up_far, down_far = send(up_near, routes["y"]), send(down_near, routes["x"])
     up_near_core, down_near_core = send(up_near, routes["core"]), send(down_near, routes["core"])
-    normed_all, up_far, down_far, up_near_core, down_near_core = lax.optimization_barrier(
-        (normed_all, up_far, down_far, up_near_core, down_near_core)
-    )
+    qt, kt, vt, keys, values = project_pair(normed_all, pair_weight, cos_all, sin_all)
+    attended_pair, attended_wide, total = attend_pair(ends, qt, keys, vt)
+    attended_pair, up_far, down_far = lax.optimization_barrier((attended_pair, up_far, down_far))
     up_pieces = (up_near, up_far, up_near_core, send(up_far, routes["core"]))
     down_pieces = (down_near, down_far, down_near_core, send(down_far, routes["core"]))
-    qt, kt, vt, keys, values = project_pair(normed_all, pair_weight, cos_all, sin_all)
-    attended_pair, attended_wide, total = attend_pair(ends, qt, keys, vt)
     attended = lax.all_to_all(attended_pair, "seq", 0, 0).reshape(width, frames)
-    out_tiles = lax.all_gather(out_weight, ("dp", "seq"), axis=0)
-    (
-        layer_output, hidden, grad_up_act, grad_middle, grad_middle_low, grad_attended, sums_two, normed_two_turned,
-    ) = middle_block(
-        place, attended, stream, grad_low, scale_two, shift_two, out_tiles, up_pieces, down_pieces, dp, seq
+    layer_output, grad_middle, grad_attended, sums_two, down_own, down_other, up_own, up_other = middle_block(
+        place, attended, stream, grad_low, scale_two, shift_two, up_pieces, down_pieces, dp, seq
     )
     grad_pair = lax.all_to_all(grad_attended.reshape(seq, PAIR, frames), "seq", 0, 0)
-    down_sum = scatter_first(place, grad_low.T, hidden, "turned", routes, seq, "x", "y")
-    up_sum = scatter_first(place, normed_two_turned, grad_up_act, "plain", routes, seq, "y", "x")
-    out_sum = scatter_first(place, attended, grad_middle_low, "plain", routes, seq, "x", "y")
-
+    down_other, up_other = send(down_other, routes["core"]), send(up_other, routes["core"])
+    down_keep, down_away = low(wide(down_own[:2]) + wide(down_other[:2])), low(wide(down_own[2:]) + wide(down_other[2:]))
+    up_keep, up_away = low(wide(up_own[:2]) + wide(up_other[:2])), low(wide(up_own[2:]) + wide(up_other[2:]))
+    grad_pair, down_away, up_away, down_keep, up_keep = lax.optimization_barrier(
+        (grad_pair, down_away, up_away, down_keep, up_keep)
+    )
+    down_got, up_got = send(down_away, routes["x"]), send(up_away, routes["y"])
     grad_projected = attend_pair_back(ends, qt, grad_pair, attended_wide, total, keys, values, kt, cos_all, sin_all)
+    grad_projected, down_got, up_got = lax.optimization_barrier((grad_projected, down_got, up_got))
     grad_local = lax.all_to_all(grad_projected, "seq", 0, 0)
-    pair_all = lax.all_gather(pair_tile, ("dp", "seq"), axis=0)
-    down_sum = scatter_second(down_sum, routes, "y")
-    up_sum = scatter_second(up_sum, routes, "x")
-    out_sum = scatter_second(out_sum, routes, "y")
+    pair_tiles = lax.all_gather(pair_tile, ("dp", "seq"), axis=0)
+    down_back = send(low(wide(down_keep[1]) + wide(down_got[1])), routes["y"])
+    up_back = send(low(wide(up_keep[1]) + wide(up_got[1])), routes["x"])
     grad_pair_weight = jnp.einsum(
         "icf,ifd->cd", grad_projected, normed_all, preferred_element_type=jnp.float32
     ).astype(jnp.bfloat16)
+    down_total = wide(down_keep[0]) + wide(down_got[0]) + wide(down_back)
+    up_total = wide(up_keep[0]) + wide(up_got[0]) + wide(up_back)
+    mlp_low = [jnp.concatenate([low(down_total[ahead]), low(up_total[ahead])]) for ahead in range(seq // 2)]
+    grad_local, *mlp_low = lax.optimization_barrier((grad_local, *mlp_low))
+    mlp_got = [send(mlp_low[ahead + 1], route) for ahead, route in enumerate(routes["z"])]
+    mlp_own = jnp.concatenate([down_total[0], up_total[0]])
+
     grad_stream, grad_stream_turned, sums_one = exit_block(
-        grad_local.reshape(3 * width, frames), pair_all, stream, grad_middle, scale_one, dp, seq
+        grad_local.reshape(3 * width, frames), pair_tiles, stream, grad_middle, scale_one, dp, seq
     )
     joined = jnp.concatenate([inputs[0], skip_input[0]], axis=-1)
-    skip_sums = [
-        scatter_first(place, grad_stream_turned, joined, "turned", routes, seq, first, second, (part, 2))
-        for part, (first, second) in enumerate((("x", "y"), ("y", "x")))
-    ]
+    half_tile = skip_weight.shape[0] // 2
+    at = lax.axis_index("dp")
+    half_pair = 3 * PAIR // 2
+    wide_tile = up_weight.shape[1]
+    skip_parts = []
+    for part, (first, second) in enumerate((("x", "y"), ("y", "x"))):
+        keep, away = pair_sum(
+            place, [("turned", grad_stream_turned, joined)], routes, seq, half_tile, first, second, (part, 2)
+        )
+        pair_rows = grad_pair_weight[part * half_pair : (part + 1) * half_pair]
+
+        def pair_block(mask):
+            return lax.dynamic_slice_in_dim(pair_rows, jnp.bitwise_xor(at, mask) * half_tile, half_tile, 1)
+
+        near, far = AXIS_MASK[first], AXIS_MASK[second]
+        keep = jnp.concatenate([keep.reshape(2, -1, half_tile), jnp.stack([pair_block(0), pair_block(far)])], axis=1)
+        away = jnp.concatenate(
+            [away.reshape(2, -1, half_tile), jnp.stack([pair_block(near), pair_block(near ^ far)])], axis=1
+        )
+        skip_parts.append((keep, send(away, routes[first]), routes[second]))
     grad_main, grad_side = joined_grads(grad_stream, skip_tiles, dp, seq)
-    sums_one, grad_main, grad_pair_weight = lax.optimization_barrier((sums_one, grad_main, grad_pair_weight))
-    skip_sums = [scatter_second(skip_sums[0], routes, "y"), scatter_second(skip_sums[1], routes, "x")]
-    skip_tile = jnp.concatenate([scatter_last(part, routes) for part in skip_sums], axis=1).T
-    down_tile = scatter_last(down_sum, routes).T
-    up_tile = scatter_last(up_sum, routes)
-    out_tile = scatter_last(out_sum, routes)
-    grad_pair_tile = dp_sum(grad_pair_weight.T.reshape(dp, width // dp, 3 * PAIR), routes, dp)
-    qkv_tile = stored_columns(grad_pair_tile.astype(jnp.bfloat16), seq).astype(jnp.float32)
-    grad_modulation = jnp.concatenate([sums_one[0], sums_one[1], sums_two[0], sums_two[1]])
-    grad_modulation = lax.psum_scatter(grad_modulation, "seq", scatter_dimension=0, tiled=True)
-    grad_modulation = lax.all_gather(grad_modulation[None], "dp", axis=0, tiled=True)
+    skip_own, skip_low, pair_sums = [], [], []
+    skip_rows = seq // 2 * (width // seq)
+    for keep, got, route in skip_parts:
+        back = send(low(wide(keep[1]) + wide(got[1])), route)
+        total_part = wide(keep[0]) + wide(got[0]) + wide(back)
+        pair_sums.append(total_part[skip_rows:])
+        blocks = total_part[:skip_rows].reshape(seq // 2, width // seq, half_tile)
+        skip_own.append(blocks[0])
+        skip_low.append(low(blocks))
+    skip_tile = jnp.concatenate(skip_own, axis=1)
+    skip_low = jnp.concatenate(skip_low, axis=2)
+    for ahead, route in enumerate(routes["z"]):
+        skip_tile = skip_tile + wide(send(skip_low[ahead + 1], route))
+    skip_tile = skip_tile.T
+    qkv_tile = wide(stored_columns(low(jnp.concatenate(pair_sums)).T, seq))
+
+    mlp_tile = mlp_own
+    for piece in mlp_got:
+        mlp_tile = mlp_tile + wide(piece)
+    columns = width // seq
+    fold = down_weight.shape[0] // wide_tile
+    down_tile = lanes([mlp_tile[i * columns : (i + 1) * columns] for i in range(fold)]).T
+    out_tile = mlp_tile[fold * columns : down_total.shape[1]]
+    out_tile = jnp.concatenate([out_tile[:, i * columns : (i + 1) * columns] for i in range(wide_tile // columns)])
+    up_tile = mlp_tile[down_total.shape[1] :]
+    sums_one, grad_main = lax.optimization_barrier((sums_one, grad_main))
+    grad_modulation = jnp.concatenate([sums_one[0], sums_one[1], sums_two[0], sums_two[1]]).reshape(1, seq, -1)
+    grad_modulation = jnp.broadcast_to(grad_modulation, (dp,) + grad_modulation.shape[1:]).reshape(dp * seq, -1)
+    grad_modulation = lax.all_to_all(grad_modulation, ("dp", "seq"), 0, 0, tiled=True)
+    grad_modulation = jnp.sum(grad_modulation.reshape(dp, seq, -1), axis=1)
     ada_tile = lax.dot_general(
         embed_part.astype(jnp.float32), grad_modulation, (((0,), (0,)), ((), ())),
         precision=lax.Precision.HIGHEST,

time: 687 us -> 627 us (0.913)
  starting transfers between devices: 108 us -> 66.7 us
  blocking collectives: 63.7 us -> 38.4 us
  waiting for transfers between devices: 195 us -> 214 us
  local copies, waits for them, and re-layouts: 62.5 us -> 52.1 us
  Pallas kernels: 174 us -> 166 us
  other arithmetic: 43.9 us -> 50.8 us
    ppermute x50 -> x35, starting transfers between devices: 84.4 us -> 39.9 us  [send(): return lax.ppermute(value, ('dp', 'seq'), route)]
    all_to_all x1, waiting for transfers between devices: 31 us -> 2.79 us  [local_paired(): lax.all_to_all(grad_attended.reshape(seq, PAIR, frames), 'seq', 0, 0)]
    all_gather x1, waiting for transfers between devices: 6.93 us -> 35.2 us  [local_paired(): normed_all = lax.all_gather(normed_one, 'seq', axis=0)]
    unnamed x2 -> x1, blocking collectives: 35.1 us -> 9.04 us
    pallas_call x10 -> x4, Pallas kernels: 39 us -> 13.6 us  [grad_blocks(): pl.pallas_call(partial(blocks_kernel, kinds=tuple(kinds), other=other, se...]
    all_to_all x0 -> x1, waiting for transfers between devices: none -> 20.4 us  [local_paired(): lax.all_to_all(grad_modulation, ('dp', 'seq'), 0, 0, tiled=True)]
    ppermute x50 -> x35, waiting for transfers between devices: 128 us -> 109 us  [send(): return lax.ppermute(value, ('dp', 'seq'), route)]
    all_to_all x1, waiting for transfers between devices: 0.01 us -> 18.6 us  [local_paired(): grad_local = lax.all_to_all(grad_projected, 'seq', 0, 0)]
  transfers between devices with their start and end apart: 63 -> 48, of which waited for: 22 -> 20; matrix products, arithmetic and copies ran while one was open for 13% -> 14% of each run, Pallas kernels for 25% -> 26%
where the time goes in v3:
time: 627 us; the launch traced here: 617 us
  waiting for transfers between devices  214 us (34%)
  Pallas kernels  166 us (26%)
  starting transfers between devices  66.7 us (11%)
  local copies, waits for them, and re-layouts  52.1 us (8%)
  other arithmetic  50.8 us (8%)
  blocking collectives  38.4 us (6%)
  between operations  20 us (3%)
  matrix products  9.1 us (1%)
    ppermute x35, waiting for transfers between devices, send(): return lax.ppermute(value, ('dp', 'seq'), route)  109 us
    pallas_call x1, Pallas kernels, middle_block(): pl.pallas_call(partial(middle_kernel, dp=dp, seq=seq), in_specs=[pl.Block...  49 us
    pallas_call x1, Pallas kernels, attend_pair_back(): pl.pallas_call(partial(attend_back_kernel, size=size, length=length, chun...  45.5 us
    ppermute x35, starting transfers between devices, send(): return lax.ppermute(value, ('dp', 'seq'), route)  39.9 us
    all_gather x1, waiting for transfers between devices, local_paired(): normed_all = lax.all_gather(normed_one, 'seq', axis=0)  35.2 us
    pallas_call x1, Pallas kernels, attend_pair(): pl.pallas_call(partial(attend_kernel, size=size, length=length), grid_spe...  34 us
    unnamed x98, local copies, waits for them, and re-layouts  28.5 us
    all_to_all x1, waiting for transfers between devices, local_paired(): attended = lax.all_to_all(attended_pair, 'seq', 0, 0).reshape(width, frames)  26.3 us
  transfers between devices with their start and end apart: 48, of which 20 were waited for; matrix products, arithmetic and copies ran while one was open for 14% of the time, Pallas kernels for 26%

profile of v3, /device:TPU:0, one launch (start us, length us, event | category | flops | bytes accessed | tf_op | source)
XLA Modules:
  0.0 617.0 jit_solution(11870908623413574490)
XLA Ops:
  9.8 3.1 collective-permute-start.3
  12.9 2.6 collective-permute-start.4
  15.6 1.8 collective-permute-start.1
  17.4 1.9 collective-permute-start.2
  20.9 8.2 %all-gather.3 = bf16[4,1,1024]{2,1,0:T(2,128)(2,1)S(1)} all-gather(bf16[1,1,1024]{2,1,0:T(2,128)(2,1)S(1)} %bitcast.168), channel_id=1, replica_groups=mesh['dp'=4,'seq'=8] {'dp'}, dimensions={0}, use_global_device_ids=true | all-gather | bytes 10240 | tf_op jit(solution)/shard_map/all_gather | solution.py:1234
  30.3 3.9 compare_select_fusion.4
  37.5 2.7 multiply_sine_fusion
  42.1 9.0 %all-reduce = f32[4,512]{1,0:T(4,128)S(1)} all-reduce(f32[4,512]{1,0:T(4,128)S(1)} %fusion.14), channel_id=5, replica_groups=mesh['dp'=4,'seq'=8] {'dp'}, use_global_device_ids=true, to_apply=%region_2.3.clone | all-reduce | flops 2048 | bytes 16384
  52.5 21.1 %all_gather.27 = f32[1,4096]{1,0:T(1,128)S(1)} all-gather(f32[1,512]{1,0:T(1,128)S(1)} %constant_dynamic-slice_fusion.3), channel_id=1, replica_groups=mesh['dp'=4,'seq'=8] {'seq'}, dimensions={1}, use_global_device_ids=true | all-gather | bytes 18432 | tf_op jit(solution)/shard_map/all_gather | solution.py:1239
  76.2 2.4 pad_maximum_fusion.4
  78.7 13.1 %collective-permute-done.5 = bf16[1280,128]{1,0:T(8,128)(2,1)S(1)} collective-permute-done((bf16[1280,128]{1,0:T(8,128)(2,1)S(1)}, bf16[1280,128]{1,0:T(8,128)(2,1)S(1)}, u32[]{:S(2)}, u32[]{:S(2)}) %collective-permute-start.5) | collective-permute-done | bytes 327712 | tf_op jit(solution)/shard_map/ppermute | solution.py:689
  91.8 2.2 pad_maximum_fusion.3
  95.3 2.2 copy-done.11
  97.5 4.6 entry_block.1
  105.3 3.0 collective-permute-start.10
  118.5 2.8 collective-permute-start.13
  121.3 19.7 %collective-permute-done.11 = bf16[256,384]{0,1:T(8,128)(2,1)S(1)} collective-permute-done((bf16[256,384]{0,1:T(8,128)(2,1)S(1)}, bf16[256,384]{0,1:T(8,128)(2,1)S(1)}, u32[]{:S(2)}, u32[]{:S(2)}) %collective-permute-start.11) | collective-permute-done | bytes 196640 | tf_op jit(solution)/shard_map/ppermute | solution.py:689
  141.1 3.5 collective-permute-done.13
  144.7 3.2 pad_maximum_fusion.1.up_0
  147.8 3.1 pad_maximum_fusion.down_0
  151.0 35.2 %all-gather.10.cloned.1.call-done = bf16[4096,1024]{1,0:T(8,128)(2,1)} async-done(((bf16[512,1024]{1,0:T(8,128)(2,1)}), bf16[4096,1024]{1,0:T(8,128)(2,1)}) %all-gather.10.cloned.1.call-update) | async-done | bytes 8388624 | tf_op jit(solution)/shard_map/all_gather | solution.py:1252
  188.4 3.4 copy-done.10
  191.8 6.1 project_pair.1
  198.0 34.0 %attend_pair.1 = (bf16[8,128,512]{2,1,0:T(8,128)(2,1)}, f32[8,128,512]{2,1,0:T(8,128)S(1)}, f32[8,2,512]{2,1,0:T(2,128)S(1)}) custom-call(s32[2]{0:T(128)S(1)} %pad_add_fusion.ends_ref, bf16[8,128,512]{2,1,0:T(8,128)(2,1)S(1)} %get-tuple-element.75.qt_ref, bf16[4096,128]{1,0:T(8,128)(2,1)S(1)} %get-tuple-element.76.k_ref, ...), custom_call_target="tpu_custom_call" | custom-call | flops 8589934592 | bytes 7340032 | tf_op jit(solution)/shard_map/attend_pair/pallas_call | solution.py:516
  233.3 2.3 collective-permute-done.14.up_1
  235.6 9.8 %collective-permute-done.15.down_1 = bf16[2,4,1280,128]{3,2,1,0:T(8,128)(2,1)} collective-permute-done((bf16[2,4,1280,128]{3,2,1,0:T(8,128)(2,1)}, bf16[2,4,1280,128]{3,2,1,0:T(8,128)(2,1)}, u32[]{:S(2)}, u32[]{:S(2)}) %collective-permute-start.15) | collective-permute-done | bytes 2621472 | tf_op jit(solution)/shard_map/ppermute | solution.py:689
  246.0 4.2 all-to-all-start
  253.7 26.3 %all-to-all-done = bf16[8,128,512]{2,1,0:T(8,128)(2,1)} async-done(((bf16[8,128,512]{2,1,0:T(8,128)(2,1)}), bf16[8,128,512]{2,1,0:T(8,128)(2,1)}, u32[]{:S(2)}, u32[]{:S(2)}) %all-to-all-start) | async-done | bytes 1048608 | tf_op jit(solution)/shard_map/all_to_all | solution.py:1265
  280.0 49.0 %middle_block.1 = (bf16[512,1024]{1,0:T(8,128)(2,1)}, f32[512,1024]{1,0:T(8,128)}, bf16[1024,512]{1,0:T(8,128)(2,1)}, f32[2,1024]{1,0:T(2,128)}, bf16[4,4,320,51...) custom-call(s32[3]{0:T(128)} %pad_add_fusion.1.place_ref, ...), custom_call_target="tpu_custom_call" | custom-call | flops 28991029248 | bytes 46137344 | tf_op jit(solution)/shard_map/middle_block/pallas_call | solution.py:894
  329.5 4.0 all-to-all-start.1
  333.5 12.3 %collective-permute-done.21 = bf16[4,4,256,512]{3,2,1,0:T(8,128)(2,1)} collective-permute-done((bf16[4,4,256,512]{3,2,1,0:T(8,128)(2,1)}, bf16[4,4,256,512]{3,2,1,0:T(8,128)(2,1)}, u32[]{:S(2)}, u32[]{:S(2)}) %collective-permute-start.21) | collective-permute-done | bytes 4194336 | tf_op jit(solution)/shard_map/ppermute | solution.py:689
  345.8 5.5 add_convert_fusion.2
  352.3 4.9 add_convert_fusion
  357.2 2.8 all-to-all-done.1.gt_ref
  369.9 45.5 %attend_pair_back.1 = bf16[8,384,512]{2,1,0:T(8,128)(2,1)} custom-call(s32[2]{0:T(128)S(1)} %pad_add_fusion.ends_ref, bf16[8,128,512]{2,1,0:T(8,128)(2,1)S(1)} %copy-done.14, bf16[8,128,512]{2,1,0:T(8,128)(2,1)S(1)} %all-to-all-done.1.gt_ref, f32[8,128,512]{2,1,0:T(8,128)S(1)} %copy-done.22, f32[8,2,512]{2,1,0:T(2,128)S(1)} %get-tuple-element.94.total_ref, ...), custom_call_target="tpu_custom_call" | custom-call | flops 21474836480 | bytes 15728640 | tf_op jit(solution)/shard_map/attend_pair_back/pallas_call | solution.py:609
  415.3 3.4 collective-permute-done.22
  418.7 4.6 all-to-all-start.2
  426.1 8.7 %copy.47 = bf16[8192,384]{1,0:T(8,128)(2,1)} copy(bf16[8192,384]{0,1:T(8,128)(2,1)} %all-gather.12.cloned.1.call-done) | data formatting | bytes 12582912 | tf_op jit(solution)/shard_map/all_gather | solution.py:1280
  436.0 2.2 fusion
  438.2 2.1 collective-permute-start.24
  442.2 7.7 %bitcast_convert_fusion = bf16[384,1024]{1,0:T(8,128)(2,1)S(1)} fusion(bf16[8,384,512]{2,1,0:T(8,128)(2,1)} %attend_pair_back.1, bf16[8,512,1024]{2,1,0:T(8,128)(2,1)} %bitcast.144), kind=kOutput, calls=%fused_computation.11 | convolution fusion | flops 3221618688 | bytes 12320768 | tf_op jit(solution)/shard_map/icf,ifd->cd/dot_general | solution.py:1283
  451.5 15.7 %collective-permute-done.25 = bf16[4,256,512]{2,1,0:T(8,128)(2,1)S(1)} collective-permute-done((bf16[4,256,512]{2,1,0:T(8,128)(2,1)S(1)}, bf16[4,256,512]{2,1,0:T(8,128)(2,1)S(1)}, u32[]{:S(2)}, u32[]{:S(2)}) %collective-permute-start.25) | collective-permute-done | bytes 1048608 | tf_op jit(solution)/shard_map/ppermute | solution.py:689
  467.1 1.7 fusion.22
  470.8 3.4 fusion.21
  476.3 18.6 %all-to-all-done.2 = bf16[8,384,512]{2,1,0:T(8,128)(2,1)} async-done(((bf16[8,384,512]{2,1,0:T(8,128)(2,1)}), bf16[8,384,512]{2,1,0:T(8,128)(2,1)}, u32[]{:S(2)}, u32[]{:S(2)}) %all-to-all-start.2) | async-done | bytes 3145760 | tf_op jit(solution)/shard_map/all_to_all | solution.py:1279
  494.9 1.8 collective-permute-start.39
  496.7 2.0 collective-permute-start.40
  501.9 8.2 %exit_block.1 = (bf16[512,1024]{1,0:T(8,128)(2,1)S(1)}, bf16[1024,512]{1,0:T(8,128)(2,1)S(1)}, f32[2,1024]{1,0:T(2,128)S(1)}) custom-call(bf16[3072,512]{1,0:T(8,128)(2,1)} %bitcast.54.projected_ref, bf16[32,256,384]{2,1,0:T(8,128)(2,1)} %bitcast.148, f32[512,1024]{1,0:T(8,128)S(1)} %copy-done.3, f32[512,1024]{1,0:T(8,128)S(1)} %copy-done.4, ...), custom_call_target="tpu_custom_call" | custom-call | flops 3221225472 | bytes 15728640 | tf_op jit(solution)/shard_map/exit_block/pallas_call | solution.py:1002
  510.2 3.0 grad_blocks.4
  513.2 4.8 joined_grads.1
  521.5 4.3 all-to-all-start.3
  525.8 2.0 slice_bitcast_fusion
  527.8 3.0 grad_blocks.6
  531.2 20.4 %all-to-all-done.3 = f32[32,1,512]{2,1,0:T(1,128)} async-done(((f32[32,1,512]{2,1,0:T(1,128)}), f32[32,1,512]{2,1,0:T(1,128)}, u32[]{:S(2)}, u32[]{:S(2)}) %all-to-all-start.3) | async-done | bytes 65568 | tf_op jit(solution)/shard_map/all_to_all | solution.py:1346
  553.6 2.1 fusion.2
  555.7 3.7 grad_blocks.5
  561.2 3.7 grad_blocks.7
  565.7 12.1 %collective-permute-done.27 = bf16[2,704,256]{2,1,0:T(8,128)(2,1)S(1)} collective-permute-done((bf16[2,704,256]{2,1,0:T(8,128)(2,1)S(1)}, bf16[2,704,256]{2,1,0:T(8,128)(2,1)S(1)}, u32[]{:S(2)}, u32[]{:S(2)}) %collective-permute-start.27) | collective-permute-done | bytes 720928 | tf_op jit(solution)/shard_map/ppermute | solution.py:689
  579.2 5.0 collective-permute-done.30
  584.9 5.9 collective-permute-done.28
  593.6 3.6 collective-permute-start.37
  597.6 2.7 collective-permute-start.33
  600.3 2.8 collective-permute-start.34
  606.6 2.7 collective-permute-done.33
  (231 shorter events, 75.3 us)
Async XLA Ops:
  7.2 29.1 %copy-start = (bf16[256,512]{1,0:T(8,128)(2,1)S(1)}, bf16[256,512]{1,0:T(8,128)(2,1)}, u32[]{:S(2)}) copy-start(bf16[256,512]{1,0:T(8,128)(2,1)} %param.23) | copy-start | bytes 786436
  7.2 13.7 %copy-start.40 = (bf16[1,1024]{1,0:T(2,128)(2,1)S(1)}, bf16[1,1024]{1,0:T(2,128)(2,1)}, u32[]{:S(2)}) copy-start(bf16[1,1024]{1,0:T(2,128)(2,1)} %param.17) | copy-start | bytes 6148
  7.2 21.9 %copy-start.38 = (s32[1,3]{1,0:T(1,128)S(1)}, s32[1,3]{1,0:T(1,128)}, u32[]{:S(2)}) copy-start(s32[1,3]{1,0:T(1,128)} %param.19) | copy-start | bytes 40
  7.2 22.5 %copy-start.39 = (s32[1,3]{1,0:T(1,128)S(1)}, s32[1,3]{1,0:T(1,128)}, u32[]{:S(2)}) copy-start(s32[1,3]{1,0:T(1,128)} %param.20) | copy-start | bytes 40
  7.2 23.1 %copy-start.36 = (s32[1,4096]{1,0:T(1,128)S(1)}, s32[1,4096]{1,0:T(1,128)}, u32[]{:S(2)}) copy-start(s32[1,4096]{1,0:T(1,128)} %param.18) | copy-start | bytes 49156
  7.2 88.0 %all-gather.8.cloned.1.call-start = ((), (), s32[]{:S(2)}) async-start(), calls=%async_computation.4 | async-start | bytes 4325376 | tf_op jit(solution)/shard_map/all_gather | solution.py:1245
  8.0 178.1 %all-gather.10.cloned.1.call-start = ((), (), s32[]{:S(2)}) async-start(), calls=%async_computation.5 | async-start | bytes 9437184 | tf_op jit(solution)/shard_map/all_gather | solution.py:1252
  9.8 68.9 %collective-permute-start.3 = (bf16[1280,128]{1,0:T(8,128)(2,1)S(1)}, bf16[1280,128]{1,0:T(8,128)(2,1)S(1)}, u32[]{:S(2)}, u32[]{:S(2)}) collective-permute-start(bf16[1280,128]{1,0:T(8,128)(2,1)S(1)} %constant_dynamic-update-slice_fusion), channel_id=1, source_target_pairs={{0,2},{1,3},{2,4},{3,5},{4,6},{5,7},{6,0},{7,1},{8,10},{9,11},{10,... | collective-permute-start | bytes 983048 | tf_op jit(solution)/shard_map/ppermute | solution.py:689
  12.9 65.8 %collective-permute-start.4 = (bf16[1280,128]{1,0:T(8,128)(2,1)S(1)}, bf16[1280,128]{1,0:T(8,128)(2,1)}, u32[]{:S(2)}, u32[]{:S(2)}) collective-permute-start(bf16[1280,128]{1,0:T(8,128)(2,1)S(1)} %constant_dynamic-update-slice_fusion), channel_id=1, source_target_pairs={{0,4},{1,5},{2,6},{3,7},{4,0},{5,1},{6,2},{7,3},{8,12},{9,13},{10,... | collective-permute-start | bytes 983048 | tf_op jit(solution)/shard_map/ppermute | solution.py:689
  15.5 58.1 %collective-permute-start = (bf16[256,512]{1,0:T(8,128)(2,1)}, bf16[256,512]{1,0:T(8,128)(2,1)S(1)}, u32[]{:S(2)}, u32[]{:S(2)}) collective-permute-start(bf16[256,512]{1,0:T(8,128)(2,1)} %param.26), channel_id=1, source_target_pairs={{0,2},{1,3},{2,4},{3,5},{4,6},{5,7},{6,0},{7,1},{8,10},{9,11},{10,... | collective-permute-start | bytes 786440 | tf_op jit(solution)/shard_map/ppermute | solution.py:689
  15.6 59.9 %collective-permute-start.1 = (bf16[256,512]{1,0:T(8,128)(2,1)}, bf16[256,512]{1,0:T(8,128)(2,1)S(1)}, u32[]{:S(2)}, u32[]{:S(2)}) collective-permute-start(bf16[256,512]{1,0:T(8,128)(2,1)} %param.26), channel_id=1, source_target_pairs={{0,4},{1,5},{2,6},{3,7},{4,0},{5,1},{6,2},{7,3},{8,12},{9,13},{10,... | collective-permute-start | bytes 786440 | tf_op jit(solution)/shard_map/ppermute | solution.py:689
  17.4 58.0 %collective-permute-start.2 = (bf16[256,512]{1,0:T(8,128)(2,1)}, bf16[256,512]{1,0:T(8,128)(2,1)S(1)}, u32[]{:S(2)}, u32[]{:S(2)}) collective-permute-start(bf16[256,512]{1,0:T(8,128)(2,1)} %param.26), channel_id=1, source_target_pairs={{0,6},{1,7},{2,0},{3,1},{4,2},{5,3},{6,4},{7,5},{8,14},{9,15},{10,... | collective-permute-start | bytes 786440 | tf_op jit(solution)/shard_map/ppermute | solution.py:689
  20.8 20.7 %copy-start.41 = (u32[32]{0:T(128)S(1)}, u32[32]{0:T(128)}, u32[]{:S(2)}) copy-start(u32[32]{0:T(128)} %constant.90) | copy-start | bytes 388
  73.6 18.2 %collective-permute-start.5 = (bf16[1280,128]{1,0:T(8,128)(2,1)S(1)}, bf16[1280,128]{1,0:T(8,128)(2,1)S(1)}, u32[]{:S(2)}, u32[]{:S(2)}) collective-permute-start(bf16[1280,128]{1,0:T(8,128)(2,1)S(1)} %constant_dynamic-update-slice_fusion), channel_id=1, source_target_pairs={{0,6},{1,7},{2,0},{3,1},{4,2},{5,3},{6,4},{7,5},{8,14},{9,15},{10,... | collective-permute-start | bytes 983048 | tf_op jit(solution)/shard_map/ppermute | solution.py:689
  76.2 19.0 %copy-start.5 = (bf16[1,512,1024]{2,1,0:T(8,128)(2,1)S(1)}, bf16[1,512,1024]{2,1,0:T(8,128)(2,1)}, u32[]{:S(2)}) copy-start(bf16[1,512,1024]{2,1,0:T(8,128)(2,1)} %param.15) | copy-start | bytes 3145732
  76.2 19.0 %copy-start.6 = (bf16[1,512,1024]{2,1,0:T(8,128)(2,1)S(1)}, bf16[1,512,1024]{2,1,0:T(8,128)(2,1)}, u32[]{:S(2)}) copy-start(bf16[1,512,1024]{2,1,0:T(8,128)(2,1)} %param.16) | copy-start | bytes 3145732
  103.5 44.4 %collective-permute-start.7 = (bf16[4,1280,128]{2,1,0:T(8,128)(2,1)}, bf16[4,1280,128]{2,1,0:T(8,128)(2,1)}, u32[]{:S(2)}, u32[]{:S(2)}) collective-permute-start(bf16[4,1280,128]{2,1,0:T(8,128)(2,1)} %pad_maximum_fusion.3), channel_id=1, source_target_pairs={{0,16},{1,17},{2,18},{3,19},{4,20},{5,21},{6,22},{7,23},{8,24},{9,... | collective-permute-start | bytes 3932168 | tf_op jit(solution)/shard_map/ppermute | solution.py:689
  105.3 12.2 %collective-permute-start.10 = (bf16[256,128]{0,1:T(8,128)(2,1)S(1)}, bf16[256,128]{0,1:T(8,128)(2,1)S(1)}, u32[]{:S(2)}, u32[]{:S(2)}) collective-permute-start(bf16[256,128]{0,1:T(8,128)(2,1)S(1)} %copy.55), channel_id=1, source_target_pairs={{0,2},{1,5},{2,0},{3,3},{4,6},{5,1},{6,4},{7,7},{8,10},{9,13},{10,... | collective-permute-start | bytes 196616 | tf_op jit(solution)/shard_map/ppermute | solution.py:647
  108.4 9.1 %collective-permute-start.8 = (bf16[256,128]{0,1:T(8,128)(2,1)S(1)}, bf16[256,128]{0,1:T(8,128)(2,1)S(1)}, u32[]{:S(2)}, u32[]{:S(2)}) collective-permute-start(bf16[256,128]{0,1:T(8,128)(2,1)S(1)} %copy.53), channel_id=1, source_target_pairs={{0,0},{1,3},{2,6},{3,1},{4,4},{5,7},{6,2},{7,5},{8,8},{9,11},{10,1... | collective-permute-start | bytes 196616 | tf_op jit(solution)/shard_map/ppermute | solution.py:647
  109.2 8.3 %collective-permute-start.9 = (bf16[256,128]{0,1:T(8,128)(2,1)S(1)}, bf16[256,128]{0,1:T(8,128)(2,1)S(1)}, u32[]{:S(2)}, u32[]{:S(2)}) collective-permute-start(bf16[256,128]{0,1:T(8,128)(2,1)S(1)} %copy.54), channel_id=1, source_target_pairs={{0,1},{1,4},{2,7},{3,2},{4,5},{5,0},{6,3},{7,6},{8,9},{9,12},{10,1... | collective-permute-start | bytes 196616 | tf_op jit(solution)/shard_map/ppermute | solution.py:647
  110.6 34.0 %collective-permute-start.6 = (bf16[4,256,512]{2,1,0:T(8,128)(2,1)}, bf16[4,256,512]{2,1,0:T(8,128)(2,1)}, u32[]{:S(2)}, u32[]{:S(2)}) collective-permute-start(bf16[4,256,512]{2,1,0:T(8,128)(2,1)} %pad_maximum_fusion.4), channel_id=1, source_target_pairs={{0,8},{1,9},{2,10},{3,11},{4,12},{5,13},{6,14},{7,15},{8,0},{9,1},... | collective-permute-start | bytes 3145736 | tf_op jit(solution)/shard_map/ppermute | solution.py:689
  117.7 30.1 %copy-start.27 = (bf16[256,384]{0,1:T(8,128)(2,1)}, bf16[256,384]{0,1:T(8,128)(2,1)S(1)}, u32[]{:S(2)}) copy-start(bf16[256,384]{0,1:T(8,128)(2,1)S(1)} %get-tuple-element.196) | copy-start | bytes 589828
  117.8 23.3 %collective-permute-start.11 = (bf16[256,384]{0,1:T(8,128)(2,1)S(1)}, bf16[256,384]{0,1:T(8,128)(2,1)S(1)}, u32[]{:S(2)}, u32[]{:S(2)}) collective-permute-start(bf16[256,384]{0,1:T(8,128)(2,1)S(1)} %get-tuple-element.196), channel_id=1, source_target_pairs={{0,8},{1,9},{2,10},{3,11},{4,12},{5,13},{6,14},{7,15},{8,0},{9,1},... | collective-permute-start | bytes 589832 | tf_op jit(solution)/shard_map/ppermute | solution.py:689
  118.1 22.9 %collective-permute-start.12 = (bf16[256,384]{0,1:T(8,128)(2,1)S(1)}, bf16[256,384]{0,1:T(8,128)(2,1)S(1)}, u32[]{:S(2)}, u32[]{:S(2)}) collective-permute-start(bf16[256,384]{0,1:T(8,128)(2,1)S(1)} %get-tuple-element.196), channel_id=1, source_target_pairs={{0,16},{1,17},{2,18},{3,19},{4,20},{5,21},{6,22},{7,23},{8,24},{9,... | collective-permute-start | bytes 589832 | tf_op jit(solution)/shard_map/ppermute | solution.py:689
  118.5 26.1 %collective-permute-start.13 = (bf16[256,384]{0,1:T(8,128)(2,1)S(1)}, bf16[256,384]{0,1:T(8,128)(2,1)S(1)}, u32[]{:S(2)}, u32[]{:S(2)}) collective-permute-start(bf16[256,384]{0,1:T(8,128)(2,1)S(1)} %get-tuple-element.196), channel_id=1, source_target_pairs={{0,24},{1,25},{2,26},{3,27},{4,28},{5,29},{6,30},{7,31},{8,16},{9,... | collective-permute-start | bytes 589832 | tf_op jit(solution)/shard_map/ppermute | solution.py:689
  147.8 40.6 %copy-start.7 = (f32[32,4096]{1,0:T(8,128)S(1)}, f32[32,4096]{1,0:T(8,128)}, u32[]{:S(2)}) copy-start(f32[32,4096]{1,0:T(8,128)} %get-tuple-element.73.cos_ref) | copy-start | bytes 1572868
  186.1 59.3 %collective-permute-start.15 = (bf16[2,4,1280,128]{3,2,1,0:T(8,128)(2,1)}, bf16[2,4,1280,128]{3,2,1,0:T(8,128)(2,1)}, u32[]{:S(2)}, u32[]{:S(2)}) collective-permute-start(bf16[2,4,1280,128]{3,2,1,0:T(8,128)(2,1)} %pad_maximum_fusion.down_0), channel_id=1, source_target_pairs={{0,8},{1,9},{2,10},{3,11},{4,12},{5,13},{6,14},{7,15},{8,0},{9,1},... | collective-permute-start | bytes 7864328 | tf_op jit(solution)/shard_map/ppermute | solution.py:689
  187.8 47.8 %collective-permute-start.14 = (bf16[2,4,256,512]{3,2,1,0:T(8,128)(2,1)}, bf16[2,4,256,512]{3,2,1,0:T(8,128)(2,1)}, u32[]{:S(2)}, u32[]{:S(2)}) collective-permute-start(bf16[2,4,256,512]{3,2,1,0:T(8,128)(2,1)} %pad_maximum_fusion.1.up_0), channel_id=1, source_target_pairs={{0,16},{1,17},{2,18},{3,19},{4,20},{5,21},{6,22},{7,23},{8,24},{9,... | collective-permute-start | bytes 6291464 | tf_op jit(solution)/shard_map/ppermute | solution.py:689
  188.4 65.3 %collective-permute-start.18 = (bf16[2,4,1280,128]{3,2,1,0:T(8,128)(2,1)}, bf16[2,4,1280,128]{3,2,1,0:T(8,128)(2,1)}, u32[]{:S(2)}, u32[]{:S(2)}) collective-permute-start(bf16[2,4,1280,128]{3,2,1,0:T(8,128)(2,1)} %pad_maximum_fusion.down_0), channel_id=1, source_target_pairs={{0,1},{1,0},{2,3},{3,2},{4,5},{5,4},{6,7},{7,6},{8,9},{9,8},{10,11... | collective-permute-start | bytes 7864328 | tf_op jit(solution)/shard_map/ppermute | solution.py:689
  197.9 34.0 %copy-start.13 = (bf16[8,128,512]{2,1,0:T(8,128)(2,1)}, bf16[8,128,512]{2,1,0:T(8,128)(2,1)S(1)}, u32[]{:S(2)}) copy-start(bf16[8,128,512]{2,1,0:T(8,128)(2,1)S(1)} %get-tuple-element.75.qt_ref) | copy-start | bytes 3145732
  197.9 34.0 %copy-start.15 = (bf16[128,4096]{1,0:T(8,128)(2,1)}, bf16[128,4096]{1,0:T(8,128)(2,1)S(1)}, u32[]{:S(2)}) copy-start(bf16[128,4096]{1,0:T(8,128)(2,1)S(1)} %get-tuple-element.96.kt_ref) | copy-start | bytes 3145732
  197.9 34.0 %copy-start.17 = (bf16[4096,128]{1,0:T(8,128)(2,1)}, bf16[4096,128]{1,0:T(8,128)(2,1)S(1)}, u32[]{:S(2)}) copy-start(bf16[4096,128]{1,0:T(8,128)(2,1)S(1)} %get-tuple-element.76.k_ref) | copy-start | bytes 3145732
  197.9 34.0 %copy-start.19 = (bf16[4096,128]{1,0:T(8,128)(2,1)}, bf16[4096,128]{1,0:T(8,128)(2,1)S(1)}, u32[]{:S(2)}) copy-start(bf16[4096,128]{1,0:T(8,128)(2,1)S(1)} %get-tuple-element.95.v_ref) | copy-start | bytes 3145732
  233.3 17.6 %copy-start.26 = (bf16[512,1024]{0,1:T(8,128)(2,1)S(1)}, bf16[512,1024]{0,1:T(8,128)(2,1)}, u32[]{:S(2)}) copy-start(bf16[512,1024]{0,1:T(8,128)(2,1)} %bitcast_select_fusion) | copy-start | bytes 3145732
  245.4 34.5 %collective-permute-start.19 = (bf16[2,4,1280,128]{3,2,1,0:T(8,128)(2,1)}, bf16[2,4,1280,128]{3,2,1,0:T(8,128)(2,1)}, u32[]{:S(2)}, u32[]{:S(2)}) collective-permute-start(bf16[2,4,1280,128]{3,2,1,0:T(8,128)(2,1)} %collective-permute-done.15.down_1), channel_id=1, source_target_pairs={{0,1},{1,0},{2,3},{3,2},{4,5},{5,4},{6,7},{7,6},{8,9},{9,8},{10,11... | collective-permute-start | bytes 7864328 | tf_op jit(solution)/shard_map/ppermute | solution.py:689
  245.4 8.2 %collective-permute-start.16 = (bf16[2,4,256,512]{3,2,1,0:T(8,128)(2,1)}, bf16[2,4,256,512]{3,2,1,0:T(8,128)(2,1)}, u32[]{:S(2)}, u32[]{:S(2)}) collective-permute-start(bf16[2,4,256,512]{3,2,1,0:T(8,128)(2,1)} %pad_maximum_fusion.1.up_0), channel_id=1, source_target_pairs={{0,1},{1,0},{2,3},{3,2},{4,5},{5,4},{6,7},{7,6},{8,9},{9,8},{10,11... | collective-permute-start | bytes 6291464 | tf_op jit(solution)/shard_map/ppermute | solution.py:689
  246.0 34.0 %collective-permute-start.17 = (bf16[2,4,256,512]{3,2,1,0:T(8,128)(2,1)}, bf16[2,4,256,512]{3,2,1,0:T(8,128)(2,1)}, u32[]{:S(2)}, u32[]{:S(2)}) collective-permute-start(bf16[2,4,256,512]{3,2,1,0:T(8,128)(2,1)} %collective-permute-done.14.up_1), channel_id=1, source_target_pairs={{0,1},{1,0},{2,3},{3,2},{4,5},{5,4},{6,7},{7,6},{8,9},{9,8},{10,11... | collective-permute-start | bytes 6291464 | tf_op jit(solution)/shard_map/ppermute | solution.py:689
  246.0 34.0 %all-to-all-start = ((bf16[8,128,512]{2,1,0:T(8,128)(2,1)}), bf16[8,128,512]{2,1,0:T(8,128)(2,1)}, u32[]{:S(2)}, u32[]{:S(2)}) async-start(bf16[8,128,512]{2,1,0:T(8,128)(2,1)} %get-tuple-element.81), calls=%async_computation | async-start | bytes 2097152 | tf_op jit(solution)/shard_map/all_to_all | solution.py:1265
  250.2 175.9 %all-gather.12.cloned.1.call-start = ((), (), s32[]{:S(2)}) async-start(), calls=%async_computation.6 | async-start | bytes 6488064 | tf_op jit(solution)/shard_map/all_gather | solution.py:1280
  329.0 22.4 %collective-permute-start.20 = (bf16[4,4,320,512]{3,2,1,0:T(8,128)(2,1)}, bf16[4,4,320,512]{3,2,1,0:T(8,128)(2,1)}, u32[]{:S(2)}, u32[]{:S(2)}) collective-permute-start(bf16[4,4,320,512]{3,2,1,0:T(8,128)(2,1)} %get-tuple-element.89), channel_id=1, source_target_pairs={{0,1},{1,0},{2,3},{3,2},{4,5},{5,4},{6,7},{7,6},{8,9},{9,8},{10,11... | collective-permute-start | bytes 15728648 | tf_op jit(solution)/shard_map/ppermute | solution.py:689
  329.0 16.8 %collective-permute-start.21 = (bf16[4,4,256,512]{3,2,1,0:T(8,128)(2,1)}, bf16[4,4,256,512]{3,2,1,0:T(8,128)(2,1)}, u32[]{:S(2)}, u32[]{:S(2)}) collective-permute-start(bf16[4,4,256,512]{3,2,1,0:T(8,128)(2,1)} %get-tuple-element.91), channel_id=1, source_target_pairs={{0,1},{1,0},{2,3},{3,2},{4,5},{5,4},{6,7},{7,6},{8,9},{9,8},{10,11... | collective-permute-start | bytes 12582920 | tf_op jit(solution)/shard_map/ppermute | solution.py:689
  329.5 30.5 %all-to-all-start.1 = ((bf16[8,128,512]{2,1,0:T(8,128)(2,1)}), bf16[8,128,512]{2,1,0:T(8,128)(2,1)S(1)}, u32[]{:S(2)}, u32[]{:S(2)}) async-start(bf16[8,128,512]{2,1,0:T(8,128)(2,1)} %bitcast.157), calls=%async_computation.1 | async-start | bytes 2097152 | tf_op jit(solution)/shard_map/all_to_all | solution.py:1269
  360.0 58.7 %collective-permute-start.22 = (bf16[2,4,320,512]{3,2,1,0:T(8,128)(2,1)}, bf16[2,4,320,512]{3,2,1,0:T(8,128)(2,1)}, u32[]{:S(2)}, u32[]{:S(2)}) collective-permute-start(bf16[2,4,320,512]{3,2,1,0:T(8,128)(2,1)} %get-tuple-element.97), channel_id=1, source_target_pairs={{0,8},{1,9},{2,10},{3,11},{4,12},{5,13},{6,14},{7,15},{8,0},{9,1},... | collective-permute-start | bytes 7864328 | tf_op jit(solution)/shard_map/ppermute | solution.py:689
  361.7 53.6 %collective-permute-start.23 = (bf16[2,4,256,512]{3,2,1,0:T(8,128)(2,1)}, bf16[2,4,256,512]{3,2,1,0:T(8,128)(2,1)}, u32[]{:S(2)}, u32[]{:S(2)}) collective-permute-start(bf16[2,4,256,512]{3,2,1,0:T(8,128)(2,1)} %get-tuple-element.98), channel_id=1, source_target_pairs={{0,16},{1,17},{2,18},{3,19},{4,20},{5,21},{6,22},{7,23},{8,24},{9,... | collective-permute-start | bytes 6291464 | tf_op jit(solution)/shard_map/ppermute | solution.py:689
  418.7 76.2 %all-to-all-start.2 = ((bf16[8,384,512]{2,1,0:T(8,128)(2,1)}), bf16[8,384,512]{2,1,0:T(8,128)(2,1)}, u32[]{:S(2)}, u32[]{:S(2)}) async-start(bf16[8,384,512]{2,1,0:T(8,128)(2,1)} %attend_pair_back.1), calls=%async_computation.2 | async-start | bytes 6291456 | tf_op jit(solution)/shard_map/all_to_all | solution.py:1279
  426.1 8.7 %copy-start.37 = (f32[2,1024]{1,0:T(2,128)S(1)}, f32[2,1024]{1,0:T(2,128)}, u32[]{:S(2)}) copy-start(f32[2,1024]{1,0:T(2,128)} %get-tuple-element.117) | copy-start | bytes 24580
  438.2 31.5 %collective-permute-start.24 = (bf16[4,320,512]{2,1,0:T(8,128)(2,1)S(1)}, bf16[4,320,512]{2,1,0:T(8,128)(2,1)S(1)}, u32[]{:S(2)}, u32[]{:S(2)}) collective-permute-start(bf16[4,320,512]{2,1,0:T(8,128)(2,1)S(1)} %fusion), channel_id=1, source_target_pairs={{0,16},{1,17},{2,18},{3,19},{4,20},{5,21},{6,22},{7,23},{8,24},{9,... | collective-permute-start | bytes 3932168 | tf_op jit(solution)/shard_map/ppermute | solution.py:689
  441.8 25.3 %collective-permute-start.25 = (bf16[4,256,512]{2,1,0:T(8,128)(2,1)S(1)}, bf16[4,256,512]{2,1,0:T(8,128)(2,1)S(1)}, u32[]{:S(2)}, u32[]{:S(2)}) collective-permute-start(bf16[4,256,512]{2,1,0:T(8,128)(2,1)S(1)} %fusion.3), channel_id=1, source_target_pairs={{0,8},{1,9},{2,10},{3,11},{4,12},{5,13},{6,14},{7,15},{8,0},{9,1},... | collective-permute-start | bytes 3145736 | tf_op jit(solution)/shard_map/ppermute | solution.py:689
  494.9 58.7 %collective-permute-start.38 = (bf16[576,512]{1,0:T(8,128)(2,1)}, bf16[576,512]{1,0:T(8,128)(2,1)}, u32[]{:S(2)}, u32[]{:S(2)}) collective-permute-start(bf16[576,512]{1,0:T(8,128)(2,1)} %get-tuple-element.118), channel_id=1, source_target_pairs={{0,2},{1,3},{2,4},{3,5},{4,6},{5,7},{6,0},{7,1},{8,10},{9,11},{10,... | collective-permute-start | bytes 1769480 | tf_op jit(solution)/shard_map/ppermute | solution.py:689
  494.9 58.7 %collective-permute-start.39 = (bf16[576,512]{1,0:T(8,128)(2,1)}, bf16[576,512]{1,0:T(8,128)(2,1)}, u32[]{:S(2)}, u32[]{:S(2)}) collective-permute-start(bf16[576,512]{1,0:T(8,128)(2,1)} %get-tuple-element.119), channel_id=1, source_target_pairs={{0,4},{1,5},{2,6},{3,7},{4,0},{5,1},{6,2},{7,3},{8,12},{9,13},{10,... | collective-permute-start | bytes 1769480 | tf_op jit(solution)/shard_map/ppermute | solution.py:689
  496.7 56.9 %collective-permute-start.40 = (bf16[576,512]{1,0:T(8,128)(2,1)}, bf16[576,512]{1,0:T(8,128)(2,1)}, u32[]{:S(2)}, u32[]{:S(2)}) collective-permute-start(bf16[576,512]{1,0:T(8,128)(2,1)} %pad_maximum_fusion.7), channel_id=1, source_target_pairs={{0,6},{1,7},{2,0},{3,1},{4,2},{5,3},{6,4},{7,5},{8,14},{9,15},{10,... | collective-permute-start | bytes 1769480 | tf_op jit(solution)/shard_map/ppermute | solution.py:689
  513.2 42.5 %collective-permute-start.26 = (bf16[4,4,128,256]{3,2,1,0:T(8,128)(2,1)}, bf16[4,4,128,256]{3,2,1,0:T(8,128)(2,1)}, u32[]{:S(2)}, u32[]{:S(2)}) collective-permute-start(bf16[4,4,128,256]{3,2,1,0:T(8,128)(2,1)} %grad_blocks.4), channel_id=1, source_target_pairs={{0,1},{1,0},{2,3},{3,2},{4,5},{5,4},{6,7},{7,6},{8,9},{9,8},{10,11... | collective-permute-start | bytes 3145736 | tf_op jit(solution)/shard_map/ppermute | solution.py:689
  521.5 30.0 %all-to-all-start.3 = ((f32[32,1,512]{2,1,0:T(1,128)}), f32[32,1,512]{2,1,0:T(1,128)}, u32[]{:S(2)}, u32[]{:S(2)}) async-start(f32[32,1,512]{2,1,0:T(1,128)} %all_to_all.18), calls=%async_computation.3 | async-start | bytes 131072 | tf_op jit(solution)/shard_map/all_to_all | solution.py:1346
  530.8 30.4 %collective-permute-start.29 = (bf16[4,4,128,256]{3,2,1,0:T(8,128)(2,1)}, bf16[4,4,128,256]{3,2,1,0:T(8,128)(2,1)}, u32[]{:S(2)}, u32[]{:S(2)}) collective-permute-start(bf16[4,4,128,256]{3,2,1,0:T(8,128)(2,1)} %grad_blocks.6), channel_id=1, source_target_pairs={{0,1},{1,0},{2,3},{3,2},{4,5},{5,4},{6,7},{7,6},{8,9},{9,8},{10,11... | collective-permute-start | bytes 3145736 | tf_op jit(solution)/shard_map/ppermute | solution.py:689
  559.6 18.3 %collective-permute-start.27 = (bf16[2,704,256]{2,1,0:T(8,128)(2,1)S(1)}, bf16[2,704,256]{2,1,0:T(8,128)(2,1)S(1)}, u32[]{:S(2)}, u32[]{:S(2)}) collective-permute-start(bf16[2,704,256]{2,1,0:T(8,128)(2,1)S(1)} %maximum_maximum_fusion.1), channel_id=1, source_target_pairs={{0,8},{1,9},{2,10},{3,11},{4,12},{5,13},{6,14},{7,15},{8,0},{9,1},... | collective-permute-start | bytes 2162696 | tf_op jit(solution)/shard_map/ppermute | solution.py:689
  565.0 19.1 %collective-permute-start.30 = (bf16[2,704,256]{2,1,0:T(8,128)(2,1)S(1)}, bf16[2,704,256]{2,1,0:T(8,128)(2,1)S(1)}, u32[]{:S(2)}, u32[]{:S(2)}) collective-permute-start(bf16[2,704,256]{2,1,0:T(8,128)(2,1)S(1)} %maximum_maximum_fusion.3), channel_id=1, source_target_pairs={{0,16},{1,17},{2,18},{3,19},{4,20},{5,21},{6,22},{7,23},{8,24},{9,... | collective-permute-start | bytes 2162696 | tf_op jit(solution)/shard_map/ppermute | solution.py:689
  577.9 12.8 %collective-permute-start.28 = (bf16[704,256]{1,0:T(8,128)(2,1)S(1)}, bf16[704,256]{1,0:T(8,128)(2,1)S(1)}, u32[]{:S(2)}, u32[]{:S(2)}) collective-permute-start(bf16[704,256]{1,0:T(8,128)(2,1)S(1)} %fusion.4), channel_id=1, source_target_pairs={{0,16},{1,17},{2,18},{3,19},{4,20},{5,21},{6,22},{7,23},{8,24},{9,... | collective-permute-start | bytes 1081352 | tf_op jit(solution)/shard_map/ppermute | solution.py:689
  584.2 8.3 %collective-permute-start.31 = (bf16[704,256]{1,0:T(8,128)(2,1)S(1)}, bf16[704,256]{1,0:T(8,128)(2,1)S(1)}, u32[]{:S(2)}, u32[]{:S(2)}) collective-permute-start(bf16[704,256]{1,0:T(8,128)(2,1)S(1)} %fusion.5), channel_id=1, source_target_pairs={{0,8},{1,9},{2,10},{3,11},{4,12},{5,13},{6,14},{7,15},{8,0},{9,1},... | collective-permute-start | bytes 1081352 | tf_op jit(solution)/shard_map/ppermute | solution.py:689
  592.8 7.4 %collective-permute-start.35 = (bf16[256,128]{0,1:T(8,128)(2,1)S(1)}, bf16[256,128]{0,1:T(8,128)(2,1)S(1)}, u32[]{:S(2)}, u32[]{:S(2)}) collective-permute-start(bf16[256,128]{0,1:T(8,128)(2,1)S(1)} %get-tuple-element.193), channel_id=1, source_target_pairs={{0,0},{3,1},{6,2},{1,3},{4,4},{7,5},{2,6},{5,7},{8,8},{11,9},{14,1... | collective-permute-start | bytes 196616 | tf_op jit(solution)/shard_map/ppermute | solution.py:666
  593.5 12.1 %collective-permute-start.36 = (bf16[256,128]{0,1:T(8,128)(2,1)S(1)}, bf16[256,128]{0,1:T(8,128)(2,1)S(1)}, u32[]{:S(2)}, u32[]{:S(2)}) collective-permute-start(bf16[256,128]{0,1:T(8,128)(2,1)S(1)} %get-tuple-element.194), channel_id=1, source_target_pairs={{1,0},{4,1},{7,2},{2,3},{5,4},{0,5},{3,6},{6,7},{9,8},{12,9},{15,1... | collective-permute-start | bytes 196616 | tf_op jit(solution)/shard_map/ppermute | solution.py:666
  593.6 12.1 %collective-permute-start.37 = (bf16[256,128]{0,1:T(8,128)(2,1)S(1)}, bf16[256,128]{0,1:T(8,128)(2,1)S(1)}, u32[]{:S(2)}, u32[]{:S(2)}) collective-permute-start(bf16[256,128]{0,1:T(8,128)(2,1)S(1)} %get-tuple-element.195), channel_id=1, source_target_pairs={{2,0},{5,1},{0,2},{3,3},{6,4},{1,5},{4,6},{7,7},{10,8},{13,9},{8,1... | collective-permute-start | bytes 196616 | tf_op jit(solution)/shard_map/ppermute | solution.py:666
  597.2 9.4 %collective-permute-start.32 = (bf16[128,512]{1,0:T(8,128)(2,1)S(1)}, bf16[128,512]{1,0:T(8,128)(2,1)S(1)}, u32[]{:S(2)}, u32[]{:S(2)}) collective-permute-start(bf16[128,512]{1,0:T(8,128)(2,1)S(1)} %get-tuple-element.182), channel_id=1, source_target_pairs={{0,2},{1,3},{2,4},{3,5},{4,6},{5,7},{6,0},{7,1},{8,10},{9,11},{10,... | collective-permute-start | bytes 393224 | tf_op jit(solution)/shard_map/ppermute | solution.py:689
  597.6 11.7 %collective-permute-start.33 = (bf16[128,512]{1,0:T(8,128)(2,1)S(1)}, bf16[128,512]{1,0:T(8,128)(2,1)S(1)}, u32[]{:S(2)}, u32[]{:S(2)}) collective-permute-start(bf16[128,512]{1,0:T(8,128)(2,1)S(1)} %get-tuple-element.183), channel_id=1, source_target_pairs={{0,4},{1,5},{2,6},{3,7},{4,0},{5,1},{6,2},{7,3},{8,12},{9,13},{10,... | collective-permute-start | bytes 393224 | tf_op jit(solution)/shard_map/ppermute | solution.py:689
  600.3 9.1 %collective-permute-start.34 = (bf16[128,512]{1,0:T(8,128)(2,1)S(1)}, bf16[128,512]{1,0:T(8,128)(2,1)S(1)}, u32[]{:S(2)}, u32[]{:S(2)}) collective-permute-start(bf16[128,512]{1,0:T(8,128)(2,1)S(1)} %get-tuple-element.184), channel_id=1, source_target_pairs={{0,6},{1,7},{2,0},{3,1},{4,2},{5,3},{6,4},{7,5},{8,14},{9,15},{10,... | collective-permute-start | bytes 393224 | tf_op jit(solution)/shard_map/ppermute | solution.py:689
  (28 other events, 84.9 us)
Sparse Core Ops, SparseCore 0:
  11.1 84.1 all-gather.7
  103.6 82.4 all-gather.9
  254.5 86.8 all-gather.11

commit v4 on v3

--- a/solution.py
+++ b/solution.py
@@ -409,19 +409,27 @@
 def turn(pair, cosine, sine_part):
     half = HD // 2
     rows = []
-    for head in range(2):
+    for head in range(pair.shape[0] // HD):
         lower = pair[head * HD : head * HD + half]
         upper = pair[head * HD + half : (head + 1) * HD]
         rows += [lower * cosine - upper * sine_part, lower * sine_part + upper * cosine]
     return jnp.concatenate(rows, axis=0)
 
 
-def project_kernel(normed_ref, weight_ref, cos_ref, sin_ref, qt_ref, kt_ref, vt_ref, k_ref, v_ref):
+def head_norms(pair):
+    square = pair * pair
+    return [jnp.sum(square[head * HD : (head + 1) * HD], axis=0, keepdims=True) for head in range(2)]
+
+
+def project_kernel(
+    normed_ref, weight_ref, cos_ref, sin_ref, qt_ref, kt_ref, vt_ref, k_ref, v_ref, norms_ref
+):
     projected = dot_nt(weight_ref[...], normed_ref[0])
     cosine, sine_part = cos_ref[...], sin_ref[...]
     queries = turn(projected[:PAIR], cosine, sine_part).astype(jnp.bfloat16)
     keys = turn(projected[PAIR : 2 * PAIR], cosine, sine_part)
     values = projected[2 * PAIR :]
+    norms_ref[0] = jnp.concatenate(head_norms(queries.astype(jnp.float32) * SCALE) + head_norms(keys), axis=0)
     qt_ref[0] = (queries.astype(jnp.float32) * SCALE).astype(jnp.bfloat16)
     kt_ref[...] = keys.astype(jnp.bfloat16)
     vt_ref[...] = values.astype(jnp.bfloat16)
@@ -447,6 +455,7 @@
             pl.BlockSpec((PAIR, frames), lambda i: (0, i)),
             pl.BlockSpec((frames, PAIR), lambda i: (i, 0)),
             pl.BlockSpec((frames, PAIR), lambda i: (i, 0)),
+            pl.BlockSpec((1, 4, frames), lambda i: (i, 0, 0)),
         ],
         out_shape=[
             jax.ShapeDtypeStruct((chunks, PAIR, frames), jnp.bfloat16),
@@ -454,8 +463,9 @@
             jax.ShapeDtypeStruct((PAIR, length), jnp.bfloat16),
             jax.ShapeDtypeStruct((length, PAIR), jnp.bfloat16),
             jax.ShapeDtypeStruct((length, PAIR), jnp.bfloat16),
+            jax.ShapeDtypeStruct((chunks, 4, frames), jnp.float32),
         ],
-        compiler_params=pltpu.CompilerParams(vmem_limit_bytes=32 << 20),
+        compiler_params=pltpu.CompilerParams(vmem_limit_bytes=60 << 20),
         cost_estimate=pl.CostEstimate(
             flops=6 * length * width * PAIR, bytes_accessed=2 * length * (width + 5 * PAIR), transcendentals=0
         ),
@@ -469,16 +479,23 @@
     return jnp.where(row < HD, block, zero), jnp.where(row < HD, zero, block)
 
 
-def attend_kernel(ends_ref, qt_ref, k_ref, vt_ref, low_ref, full_ref, total_ref, acc_ref, top_ref, *, size, length):
-    start = pl.program_id(0) * size
+SAFE_SCORE = 60.0
+
+
+def attend_kernel(
+    ends_ref, qt_ref, k_ref, vt_ref, norms_ref, low_ref, full_ref, total_ref, acc_ref, top_ref, *, size, length
+):
+    index = pl.program_id(0)
+    start = index * size
     queries = split_heads(qt_ref[0])
     query_segment = segment_of(start + lax.broadcasted_iota(jnp.int32, (1, size), 1), ends_ref)
     first, whole_first, whole_last, last = key_blocks(ends_ref, start, size, length)
     acc_ref[...] = jnp.zeros_like(acc_ref)
-    top_ref[...] = jnp.full_like(top_ref, masked_score)
     ones = jnp.ones((16, size), jnp.bfloat16)
-
-    def step(masked):
+    bound = jnp.max(norms_ref[index, :2, :]) * jnp.max(norms_ref[:, 2:, :])
+    plain = bound < SAFE_SCORE * SAFE_SCORE
+
+    def step(masked, shifted):
         def run(block, carry):
             offset = pl.multiple_of(block * size, size)
             keys = k_ref[pl.ds(offset, size), :]
@@ -487,20 +504,40 @@
                 key_segment = segment_of(offset + lax.broadcasted_iota(jnp.int32, (size, 1), 0), ends_ref)
                 same = key_segment == query_segment
                 scores = [jnp.where(same, part, masked_score) for part in scores]
-            old = [top_ref[head] for head in range(2)]
-            new = [jnp.maximum(old[head], jnp.max(scores[head], axis=0, keepdims=True) * LOG2E) for head in range(2)]
-            weights = [jnp.exp2(scores[head] * LOG2E - new[head]).astype(jnp.bfloat16) for head in range(2)]
+            if shifted:
+                old = [top_ref[head] for head in range(2)]
+                new = [
+                    jnp.maximum(old[head], jnp.max(scores[head], axis=0, keepdims=True) * LOG2E) for head in range(2)
+                ]
+                weights = [jnp.exp2(scores[head] * LOG2E - new[head]).astype(jnp.bfloat16) for head in range(2)]
+            else:
+                weights = [jnp.exp2(scores[head] * LOG2E).astype(jnp.bfloat16) for head in range(2)]
             for head in range(2):
                 values = jnp.concatenate([vt_ref[pl.ds(head * HD, HD), pl.ds(offset, size)], ones], axis=0)
-                acc_ref[head] = acc_ref[head] * jnp.exp2(old[head] - new[head]) + dot_nn(values, weights[head])
-                top_ref[head] = new[head]
+                if shifted:
+                    acc_ref[head] = acc_ref[head] * jnp.exp2(old[head] - new[head]) + dot_nn(values, weights[head])
+                    top_ref[head] = new[head]
+                else:
+                    acc_ref[head] += dot_nn(values, weights[head])
             return carry
 
         return run
 
-    lax.fori_loop(first, whole_first, step(True), 0)
-    lax.fori_loop(whole_first, whole_last, step(False), 0)
-    lax.fori_loop(whole_last, last, step(True), 0)
+    def loops(shifted):
+        lax.fori_loop(first, whole_first, step(True, shifted), 0)
+        lax.fori_loop(whole_first, whole_last, step(False, shifted), 0)
+        lax.fori_loop(whole_last, last, step(True, shifted), 0)
+
+    @pl.when(plain)
+    def _():
+        top_ref[...] = jnp.zeros_like(top_ref)
+        loops(False)
+
+    @pl.when(jnp.logical_not(plain))
+    def _():
+        top_ref[...] = jnp.full_like(top_ref, masked_score)
+        loops(True)
+
     for head in range(2):
         total = acc_ref[head, HD : HD + 1, :]
         attended = acc_ref[head, :HD, :] / total
@@ -509,7 +546,7 @@
         total_ref[0, head : head + 1, :] = jnp.log(total) * LOG2E + top_ref[head]
 
 
-def attend_pair(ends, qt, k, vt):
+def attend_pair(ends, qt, k, vt, norms):
     chunks, _, size = qt.shape
     length = k.shape[0]
     chunk = pl.BlockSpec((1, PAIR, size), lambda i, ends: (i, 0, 0))
@@ -522,6 +559,7 @@
                 chunk,
                 pl.BlockSpec((length, PAIR), lambda i, ends: (0, 0)),
                 pl.BlockSpec((PAIR, length), lambda i, ends: (0, 0)),
+                pl.BlockSpec(norms.shape, lambda i, ends: (0, 0, 0)),
             ],
             out_specs=[chunk, chunk, pl.BlockSpec((1, 2, size), lambda i, ends: (i, 0, 0))],
             scratch_shapes=[pltpu.VMEM((2, HD + 16, size), jnp.float32), pltpu.VMEM((2, 1, size), jnp.float32)],
@@ -536,12 +574,12 @@
             flops=8 * length * length * HD, bytes_accessed=14 * length * PAIR, transcendentals=length * length
         ),
         name="attend_pair",
-    )(ends, qt, k, vt)
+    )(ends, qt, k, vt, norms)
 
 
 def attend_back_kernel(
     ends_ref, qt_ref, gt_ref, full_ref, total_ref, k_ref, v_ref, kt_ref, cos_ref, sin_ref, out_ref,
-    dk_ref, dv_ref, dq_ref, *, size, length, chunks,
+    dk_ref, dv_ref, dq_ref, *, head, size, length, chunks,
 ):
     index = pl.program_id(0)
     start = index * size
@@ -551,34 +589,33 @@
         dk_ref[...] = jnp.zeros_like(dk_ref)
         dv_ref[...] = jnp.zeros_like(dv_ref)
 
-    queries = split_heads(qt_ref[0])
-    grads = split_heads(gt_ref[0])
-    product = gt_ref[0].astype(jnp.float32) * full_ref[0]
-    row_dot = [jnp.sum(product[head * HD : (head + 1) * HD], axis=0, keepdims=True) for head in range(2)]
+    mine = slice(head * HD, (head + 1) * HD)
+    queries = split_heads(qt_ref[0])[head]
+    blank = jnp.zeros_like(gt_ref[0])
+    grads = jnp.concatenate([blank, gt_ref[0]] if head else [gt_ref[0], blank], axis=0)
+    row_dot = jnp.sum(gt_ref[0].astype(jnp.float32) * full_ref[0, mine, :], axis=0, keepdims=True)
+    total = total_ref[0, head : head + 1, :]
     query_segment = segment_of(start + lax.broadcasted_iota(jnp.int32, (1, size), 1), ends_ref)
     first, whole_first, whole_last, last = key_blocks(ends_ref, start, size, length)
     dq_ref[...] = jnp.zeros_like(dq_ref)
-    part = size // 2
+    pieces = 2
+    part = size // pieces
 
     def step(masked):
         def run(block, carry):
-            for piece in range(2):
+            for piece in range(pieces):
                 offset = pl.multiple_of(block * size + piece * part, part)
                 rows = pl.ds(offset, part)
-                keys, values = k_ref[rows, :], v_ref[rows, :]
-                for head in range(2):
-                    scores = dot_nn(keys, queries[head])
-                    if masked:
-                        key_segment = segment_of(offset + lax.broadcasted_iota(jnp.int32, (part, 1), 0), ends_ref)
-                        scores = jnp.where(key_segment == query_segment, scores, masked_score)
-                    weights = jnp.exp2(scores * LOG2E - total_ref[0, head : head + 1, :])
-                    grad_weights = dot_nn(values, grads[head])
-                    grad_scores = (weights * (grad_weights - row_dot[head])).astype(jnp.bfloat16)
-                    dv_ref[rows, :] += dot_nt(weights.astype(jnp.bfloat16), grads[head])
-                    dk_ref[rows, :] += dot_nt(grad_scores, queries[head])
-                    dq_ref[head * HD : (head + 1) * HD, :] += dot_nn(
-                        kt_ref[head * HD : (head + 1) * HD, rows], grad_scores
-                    )
+                scores = dot_nn(k_ref[rows, :], queries)
+                if masked:
+                    key_segment = segment_of(offset + lax.broadcasted_iota(jnp.int32, (part, 1), 0), ends_ref)
+                    scores = jnp.where(key_segment == query_segment, scores, masked_score)
+                weights = jnp.exp2(scores * LOG2E - total)
+                grad_weights = dot_nn(v_ref[rows, :], grads)
+                grad_scores = (weights * (grad_weights - row_dot)).astype(jnp.bfloat16)
+                dv_ref[rows, :] += dot_nt(weights.astype(jnp.bfloat16), grads)
+                dk_ref[rows, :] += dot_nt(grad_scores, queries)
+                dq_ref[...] += dot_nn(kt_ref[mine, rows], grad_scores)
             return carry
 
         return run
@@ -587,18 +624,18 @@
     lax.fori_loop(whole_first, whole_last, step(False), 0)
     lax.fori_loop(whole_last, last, step(True), 0)
     own = pl.ds(pl.multiple_of(start, size), size)
-    out_ref[index, :PAIR, :] = turn(dq_ref[...] * SCALE, cos_ref[:, own], -sin_ref[:, own]).astype(jnp.bfloat16)
+    out_ref[index, :HD, :] = turn(dq_ref[...] * SCALE, cos_ref[:, own], -sin_ref[:, own]).astype(jnp.bfloat16)
 
     @pl.when(index == chunks - 1)
     def _():
         for chunk in range(chunks):
             rows = pl.ds(chunk * size, size)
-            turned = turn(dk_ref[rows, :].T, cos_ref[:, rows], -sin_ref[:, rows])
-            out_ref[chunk, PAIR : 2 * PAIR, :] = turned.astype(jnp.bfloat16)
-            out_ref[chunk, 2 * PAIR :, :] = dv_ref[rows, :].T.astype(jnp.bfloat16)
-
-
-def attend_pair_back(ends, qt, gt, full, total, k, v, kt, cos_all, sin_all):
+            turned = turn(dk_ref[rows, :].T[mine], cos_ref[:, rows], -sin_ref[:, rows])
+            out_ref[chunk, HD : 2 * HD, :] = turned.astype(jnp.bfloat16)
+            out_ref[chunk, 2 * HD :, :] = dv_ref[rows, :].T[mine].astype(jnp.bfloat16)
+
+
+def attend_head_back(head, ends, qt, gt, full, total, k, v, kt, cos_all, sin_all):
     chunks, _, size = qt.shape
     length = k.shape[0]
     chunk = pl.BlockSpec((1, PAIR, size), lambda i, ends: (i, 0, 0))
@@ -607,28 +644,29 @@
         return pl.BlockSpec(shape, lambda i, ends: (0,) * len(shape))
 
     return pl.pallas_call(
-        partial(attend_back_kernel, size=size, length=length, chunks=chunks),
+        partial(attend_back_kernel, head=head, size=size, length=length, chunks=chunks),
         grid_spec=pltpu.PrefetchScalarGridSpec(
             num_scalar_prefetch=1,
             grid=(chunks,),
             in_specs=[
-                chunk, chunk, chunk, pl.BlockSpec((1, 2, size), lambda i, ends: (i, 0, 0)),
+                chunk, pl.BlockSpec((1, HD, size), lambda i, ends: (i, 0, 0)), chunk,
+                pl.BlockSpec((1, 2, size), lambda i, ends: (i, 0, 0)),
                 whole((length, PAIR)), whole((length, PAIR)), whole((PAIR, length)),
                 whole((HD // 2, length)), whole((HD // 2, length)),
             ],
-            out_specs=whole((chunks, 3 * PAIR, size)),
+            out_specs=whole((chunks, 3 * HD, size)),
             scratch_shapes=[
                 pltpu.VMEM((length, PAIR), jnp.float32),
                 pltpu.VMEM((length, PAIR), jnp.float32),
-                pltpu.VMEM((PAIR, size), jnp.float32),
+                pltpu.VMEM((HD, size), jnp.float32),
             ],
         ),
-        out_shape=jax.ShapeDtypeStruct((chunks, 3 * PAIR, size), jnp.bfloat16),
-        compiler_params=pltpu.CompilerParams(vmem_limit_bytes=40 << 20),
+        out_shape=jax.ShapeDtypeStruct((chunks, 3 * HD, size), jnp.bfloat16),
+        compiler_params=pltpu.CompilerParams(vmem_limit_bytes=60 << 20),
         cost_estimate=pl.CostEstimate(
-            flops=20 * length * length * HD, bytes_accessed=30 * length * PAIR, transcendentals=length * length
+            flops=40 * length * length * HD, bytes_accessed=20 * length * PAIR, transcendentals=0
         ),
-        name="attend_pair_back",
+        name="attend_head_back",
     )(ends, qt, gt, full, total, k, v, kt, cos_all, sin_all)
 
 
@@ -641,30 +679,28 @@
     return routes, slots
 
 
-def own_pair_columns(tile, count):
+def own_pair_rows(tile, count):
     routes, slots = pair_routes(count)
-    width = tile.shape[1] // 3
-    got = [lax.ppermute(tile[:, p * width : (p + 1) * width], "seq", routes[p]) for p in range(3)]
+    width = tile.shape[0] // 3
+    got = [lax.ppermute(tile[p * width : (p + 1) * width], "seq", routes[p]) for p in range(3)]
     slot_of = jnp.asarray(slots, jnp.int32)[lax.axis_index("seq")]
-    columns = []
+    rows = []
     for slot in range(3):
-        columns.append(
-            jnp.where(slot_of[0] == slot, got[0], jnp.where(slot_of[1] == slot, got[1], got[2]))
-        )
-    return jnp.concatenate(columns, axis=1)
-
-
-def stored_columns(pair_tile, count):
+        rows.append(jnp.where(slot_of[0] == slot, got[0], jnp.where(slot_of[1] == slot, got[1], got[2])))
+    return jnp.concatenate(rows, axis=0)
+
+
+def stored_rows(pair_tile, count):
     routes, slots = pair_routes(count)
-    width = pair_tile.shape[1] // 3
+    width = pair_tile.shape[0] // 3
     slot_of = jnp.asarray(slots, jnp.int32)[lax.axis_index("seq")]
-    parts = [pair_tile[:, s * width : (s + 1) * width] for s in range(3)]
+    parts = [pair_tile[s * width : (s + 1) * width] for s in range(3)]
     back = []
     for piece in range(3):
         slot = slot_of[piece]
         chosen = jnp.where(slot == 0, parts[0], jnp.where(slot == 1, parts[1], parts[2]))
         back.append(lax.ppermute(chosen, "seq", [(target, source) for source, target in routes[piece]]))
-    return jnp.concatenate(back, axis=1)
+    return jnp.concatenate(back, axis=0)
 
 
 def chip_routes(dp, seq):
@@ -719,7 +755,7 @@
 def middle_kernel(
     place_ref, att_ref, stream_ref, low_ref, turned_low_ref, scale_ref, shift_ref,
     up_0, up_1, up_2, up_3, down_0, down_1, down_2, down_3,
-    layer_ref, grad_mid_ref, grad_att_ref, sums_ref, down_own_out, down_other_out, up_own_out, up_other_out,
+    layer_ref, grad_mid_ref, grad_att_a_ref, grad_att_b_ref, sums_ref, down_own_out, down_other_out, up_own_out, up_other_out,
     up_w, down_w, out_w, normed_ref, turned_ref, sorted_ref, middle_ref, out_acc,
     down_own, down_other, up_own, up_other, up_sem, down_sem, out_sem, send_sem, *, dp, seq,
 ):
@@ -855,7 +891,10 @@
         grad_mid_ref[rows, :] = grad_mid
         normed_ref[rows, :] = grad_mid.astype(jnp.bfloat16)
 
-    grad_att_ref[...] = dot_nt(out_w[...], normed_ref[...]).astype(jnp.bfloat16)
+    grad_att = dot_nt(out_w[...], normed_ref[...]).astype(jnp.bfloat16)
+    for target in range(seq):
+        grad_att_a_ref[target] = grad_att[target * PAIR : target * PAIR + HD]
+        grad_att_b_ref[target] = grad_att[target * PAIR + HD : (target + 1) * PAIR]
     grads = lanes([normed_ref[:, pl.ds(pl.multiple_of(tile * cols, cols), cols)] for tile in tiles])
     per_row = up_cols // cols
     folded = out_rows // per_row
@@ -894,11 +933,12 @@
     return pl.pallas_call(
         partial(middle_kernel, dp=dp, seq=seq),
         in_specs=[pl.BlockSpec(memory_space=pltpu.SMEM)] + [whole] * 6 + [anywhere] * 8,
-        out_specs=[whole] * 4 + [anywhere] * 4,
+        out_specs=[whole] * 5 + [anywhere] * 4,
         out_shape=[
             jax.ShapeDtypeStruct((frames, width), half),
             jax.ShapeDtypeStruct((frames, width), full),
-            jax.ShapeDtypeStruct((width, frames), half),
+            jax.ShapeDtypeStruct((seq, HD, frames), half),
+            jax.ShapeDtypeStruct((seq, HD, frames), half),
             jax.ShapeDtypeStruct((2, width), full),
             jax.ShapeDtypeStruct(down_shape, half),
             jax.ShapeDtypeStruct(down_shape, half),
@@ -978,13 +1018,20 @@
 
 
 def exit_kernel(
-    projected_ref, pair_ref, stream_ref, grad_mid_ref, scale_ref, grad_ref, turned_ref, sums_ref, normed_ref,
+    head_a_ref, head_b_ref, pair_ref, stream_ref, grad_mid_ref, scale_ref, grad_ref, turned_ref, sums_ref, normed_ref,
     *, dp, seq,
 ):
-    rows = pair_ref.shape[1]
+    rows = pair_ref.shape[2]
+    parts = [
+        head_ref[s, piece * HD : (piece + 1) * HD]
+        for s in range(seq)
+        for piece in range(3)
+        for head_ref in (head_a_ref, head_b_ref)
+    ]
+    projected = jnp.concatenate(parts, axis=0).T
     for row in range(dp):
-        weight = lanes([pair_ref[row * seq + s] for s in range(seq)])
-        normed_ref[:, row * rows : (row + 1) * rows] = dot_nn(weight, projected_ref[...]).T
+        weight = pair_ref[row * seq : (row + 1) * seq].reshape(projected.shape[1], rows)
+        normed_ref[:, row * rows : (row + 1) * rows] = dot_nn(projected, weight)
     grad, stream = normed_ref[...], stream_ref[...]
     inverse = lax.rsqrt(jnp.mean(stream * stream, axis=-1, keepdims=True) + epsilon)
     unit = stream * inverse
@@ -996,12 +1043,12 @@
     turned_ref[...] = grad_stream.T.astype(jnp.bfloat16)
 
 
-def exit_block(projected, pair_tiles, stream, grad_mid, scale, dp, seq):
+def exit_block(head_a, head_b, pair_tiles, stream, grad_mid, scale, dp, seq):
     frames, width = stream.shape
     whole = pl.BlockSpec(memory_space=pltpu.VMEM)
     return pl.pallas_call(
         partial(exit_kernel, dp=dp, seq=seq),
-        in_specs=[whole] * 5,
+        in_specs=[whole] * 6,
         out_specs=[whole] * 3,
         out_shape=[
             jax.ShapeDtypeStruct((frames, width), jnp.bfloat16),
@@ -1014,7 +1061,7 @@
             flops=6 * frames * width * width, bytes_accessed=18 * frames * width + 6 * width * width, transcendentals=0
         ),
         name="exit_block",
-    )(projected, pair_tiles, stream, grad_mid, scale)
+    )(head_a, head_b, pair_tiles, stream, grad_mid, scale)
 
 
 def joined_kernel(grad_ref, weight_ref, main_ref, side_ref, *, dp, seq):
@@ -1181,19 +1228,13 @@
     return value.astype(jnp.bfloat16)
 
 
-def pair_sum(place, products, routes, seq, width, first, second, part=(0, 1)):
-    masks = (AXIS_MASK[first], AXIS_MASK[second])
-    (outgoing,) = grad_blocks(place, products, masks, seq, width, None, part)
-    return grad_blocks(place, products, masks, seq, width, send(outgoing, routes["core"]), part)
-
-
 def dp_gather(tile, routes, dp):
     at = lax.axis_index("dp")
-    rows = tile.shape[0]
-    full = jnp.zeros((dp * rows, tile.shape[1]), tile.dtype)
-    full = lax.dynamic_update_slice_in_dim(full, tile, at * rows, 0)
+    columns = tile.shape[1]
+    full = jnp.zeros((tile.shape[0], dp * columns), tile.dtype)
+    full = lax.dynamic_update_slice_in_dim(full, tile, at * columns, 1)
     for mask, route in ((1, routes["x"]), (2, routes["y"]), (3, routes["xy"])):
-        full = lax.dynamic_update_slice_in_dim(full, send(tile, route), jnp.bitwise_xor(at, mask) * rows, 0)
+        full = lax.dynamic_update_slice_in_dim(full, send(tile, route), jnp.bitwise_xor(at, mask) * columns, 1)
     return full
 
 
@@ -1243,8 +1284,7 @@
     shift_two = modulation[:, 3 * width :]
 
     skip_tiles = lax.all_gather(skip_weight, ("dp", "seq"), axis=0)
-    pair_tile = own_pair_columns(qkv_weight, seq)
-    pair_weight = dp_gather(pair_tile, routes, dp)
+    pair_tile = own_pair_rows(qkv_weight.T, seq)
     skip_tiles, up_column, down_column, cos_all, sin_all, ends, grad_low, place = lax.optimization_barrier(
         (skip_tiles, up_column, down_column, cos_all, sin_all, ends, grad_low, place)
     )
@@ -1252,57 +1292,96 @@
     normed_all = lax.all_gather(normed_one, "seq", axis=0)
     up_near = gather_near(up_column, routes["x"])
     down_near = gather_near(down_column, routes["y"])
-    normed_all, up_near, down_near, pair_weight = lax.optimization_barrier(
-        (normed_all, up_near, down_near, pair_weight.T)
-    )
+    pair_weight = dp_gather(pair_tile, routes, dp)
+    up_near, down_near, pair_weight = lax.optimization_barrier((up_near, down_near, pair_weight))
     up_far, down_far = send(up_near, routes["y"]), send(down_near, routes["x"])
+    normed_all, up_near, down_near = lax.optimization_barrier((normed_all, up_near, down_near))
     up_near_core, down_near_core = send(up_near, routes["core"]), send(down_near, routes["core"])
-    qt, kt, vt, keys, values = project_pair(normed_all, pair_weight, cos_all, sin_all)
-    attended_pair, attended_wide, total = attend_pair(ends, qt, keys, vt)
+    qt, kt, vt, keys, values, norms = project_pair(normed_all, pair_weight, cos_all, sin_all)
+    attended_pair, attended_wide, total = attend_pair(ends, qt, keys, vt, norms)
     attended_pair, up_far, down_far = lax.optimization_barrier((attended_pair, up_far, down_far))
     up_pieces = (up_near, up_far, up_near_core, send(up_far, routes["core"]))
     down_pieces = (down_near, down_far, down_near_core, send(down_far, routes["core"]))
     attended = lax.all_to_all(attended_pair, "seq", 0, 0).reshape(width, frames)
-    layer_output, grad_middle, grad_attended, sums_two, down_own, down_other, up_own, up_other = middle_block(
+    attended, pair_tile, far_up, far_down = lax.optimization_barrier(
+        (attended, pair_tile, up_pieces[3], down_pieces[3])
+    )
+    up_pieces, down_pieces = up_pieces[:3] + (far_up,), down_pieces[:3] + (far_down,)
+    pair_tiles = lax.all_gather(pair_tile, ("dp", "seq"), axis=0)
+    layer_output, grad_middle, grad_head_a, grad_head_b, sums_two, down_own, down_other, up_own, up_other = middle_block(
         place, attended, stream, grad_low, scale_two, shift_two, up_pieces, down_pieces, dp, seq
     )
-    grad_pair = lax.all_to_all(grad_attended.reshape(seq, PAIR, frames), "seq", 0, 0)
+    grad_head_a = lax.all_to_all(grad_head_a, "seq", 0, 0)
     down_other, up_other = send(down_other, routes["core"]), send(up_other, routes["core"])
-    down_keep, down_away = low(wide(down_own[:2]) + wide(down_other[:2])), low(wide(down_own[2:]) + wide(down_other[2:]))
-    up_keep, up_away = low(wide(up_own[:2]) + wide(up_other[:2])), low(wide(up_own[2:]) + wide(up_other[2:]))
-    grad_pair, down_away, up_away, down_keep, up_keep = lax.optimization_barrier(
-        (grad_pair, down_away, up_away, down_keep, up_keep)
-    )
-    down_got, up_got = send(down_away, routes["x"]), send(up_away, routes["y"])
-    grad_projected = attend_pair_back(ends, qt, grad_pair, attended_wide, total, keys, values, kt, cos_all, sin_all)
-    grad_projected, down_got, up_got = lax.optimization_barrier((grad_projected, down_got, up_got))
-    grad_local = lax.all_to_all(grad_projected, "seq", 0, 0)
-    pair_tiles = lax.all_gather(pair_tile, ("dp", "seq"), axis=0)
-    down_back = send(low(wide(down_keep[1]) + wide(down_got[1])), routes["y"])
-    up_back = send(low(wide(up_keep[1]) + wide(up_got[1])), routes["x"])
+    down_half, up_half = down_own.shape[2] // 2, up_own.shape[2] // 2
+
+    def leaves(own, other, rows):
+        return low(wide(own[2:, :, rows]) + wide(other[2:, :, rows]))
+
+    away = (
+        leaves(down_own, down_other, slice(0, down_half)),
+        leaves(down_own, down_other, slice(down_half, None)),
+        leaves(up_own, up_other, slice(0, up_half)),
+        leaves(up_own, up_other, slice(up_half, None)),
+    )
+    grad_head_b, *away = lax.optimization_barrier((grad_head_b, *away))
+    grad_head_b = lax.all_to_all(grad_head_b, "seq", 0, 0)
+    saved = (attended_wide, total, keys, values, kt, cos_all, sin_all)
+    grad_head_a, pair_tiles, *away = lax.optimization_barrier((grad_head_a, pair_tiles, *away))
+    down_got = [send(away[0], routes["x"]), send(away[1], routes["x"])]
+    up_got = [send(away[2], routes["y"]), send(away[3], routes["y"])]
+    back_a = attend_head_back(0, ends, qt, grad_head_a, *saved)
+    local_a = lax.all_to_all(back_a, "seq", 0, 0)
+    back_a, grad_head_b, down_got[0], up_got[0] = lax.optimization_barrier(
+        (back_a, grad_head_b, down_got[0], up_got[0])
+    )
+    back_b = attend_head_back(1, ends, qt, grad_head_b, *saved)
+    back_b, local_a = lax.optimization_barrier((back_b, local_a))
+    local_b = lax.all_to_all(back_b, "seq", 0, 0)
+
+    def stays(own, other, got, at):
+        return wide(own[at]) + wide(other[at]) + wide(got[at])
+
+    parts = [part[:, at : at + HD] for at in range(0, 3 * HD, HD) for part in (back_a, back_b)]
+    grad_projected = jnp.concatenate(parts, axis=1)
+    grad_projected, down_got[1], up_got[1] = lax.optimization_barrier((grad_projected, down_got[1], up_got[1]))
+    down_got, up_got = jnp.concatenate(down_got, axis=2), jnp.concatenate(up_got, axis=2)
+    down_back = send(low(stays(down_own, down_other, down_got, 1)), routes["y"])
+    up_back = send(low(stays(up_own, up_other, up_got, 1)), routes["x"])
     grad_pair_weight = jnp.einsum(
         "icf,ifd->cd", grad_projected, normed_all, preferred_element_type=jnp.float32
     ).astype(jnp.bfloat16)
-    down_total = wide(down_keep[0]) + wide(down_got[0]) + wide(down_back)
-    up_total = wide(up_keep[0]) + wide(up_got[0]) + wide(up_back)
-    mlp_low = [jnp.concatenate([low(down_total[ahead]), low(up_total[ahead])]) for ahead in range(seq // 2)]
-    grad_local, *mlp_low = lax.optimization_barrier((grad_local, *mlp_low))
-    mlp_got = [send(mlp_low[ahead + 1], route) for ahead, route in enumerate(routes["z"])]
-    mlp_own = jnp.concatenate([down_total[0], up_total[0]])
-
     grad_stream, grad_stream_turned, sums_one = exit_block(
-        grad_local.reshape(3 * width, frames), pair_tiles, stream, grad_middle, scale_one, dp, seq
+        local_a, local_b, pair_tiles, stream, grad_middle, scale_one, dp, seq
     )
     joined = jnp.concatenate([inputs[0], skip_input[0]], axis=-1)
     half_tile = skip_weight.shape[0] // 2
     at = lax.axis_index("dp")
     half_pair = 3 * PAIR // 2
     wide_tile = up_weight.shape[1]
+    turned = [("turned", grad_stream_turned, joined)]
+    order = (("x", "y"), ("y", "x"))
+
+    def skip_blocks(part, arrived):
+        masks = tuple(AXIS_MASK[axis] for axis in order[part])
+        return grad_blocks(place, turned, masks, seq, half_tile, arrived, (part, 2))
+
+    leaving = [skip_blocks(part, None)[0] for part in range(2)]
+    *leaving, down_back, up_back = lax.optimization_barrier((*leaving, down_back, up_back))
+    arrived = [send(part, routes["core"]) for part in leaving]
+    down_total = stays(down_own, down_other, down_got, 0) + wide(down_back)
+    up_total = stays(up_own, up_other, up_got, 0) + wide(up_back)
+    mlp_low = [jnp.concatenate([low(down_total[ahead]), low(up_total[ahead])]) for ahead in range(seq // 2)]
+    mlp_own = jnp.concatenate([down_total[0], up_total[0]])
+    mlp_got = [send(mlp_low[1], routes["z"][0])]
+    grad_main, grad_side = joined_grads(grad_stream, skip_tiles, dp, seq)
+    arrived[0], arrived[1], grad_main, mlp_got[0], *mlp_low = lax.optimization_barrier(
+        (*arrived, grad_main, mlp_got[0], *mlp_low)
+    )
+    mlp_got.append(send(mlp_low[2], routes["z"][1]))
     skip_parts = []
-    for part, (first, second) in enumerate((("x", "y"), ("y", "x"))):
-        keep, away = pair_sum(
-            place, [("turned", grad_stream_turned, joined)], routes, seq, half_tile, first, second, (part, 2)
-        )
+    for part, (first, second) in enumerate(order):
+        keep, away = skip_blocks(part, arrived[part])
         pair_rows = grad_pair_weight[part * half_pair : (part + 1) * half_pair]
 
         def pair_block(mask):
@@ -1314,7 +1393,12 @@
             [away.reshape(2, -1, half_tile), jnp.stack([pair_block(near), pair_block(near ^ far)])], axis=1
         )
         skip_parts.append((keep, send(away, routes[first]), routes[second]))
-    grad_main, grad_side = joined_grads(grad_stream, skip_tiles, dp, seq)
+    keep_a, keep_b, sums_one = lax.optimization_barrier((skip_parts[0][0], skip_parts[1][0], sums_one))
+    got_a, got_b, mlp_got[1], mlp_low[3] = lax.optimization_barrier(
+        (skip_parts[0][1], skip_parts[1][1], mlp_got[1], mlp_low[3])
+    )
+    mlp_got.append(send(mlp_low[3], routes["z"][2]))
+    skip_parts = [(keep_a, got_a, skip_parts[0][2]), (keep_b, got_b, skip_parts[1][2])]
     skip_own, skip_low, pair_sums = [], [], []
     skip_rows = seq // 2 * (width // seq)
     for keep, got, route in skip_parts:
@@ -1326,10 +1410,11 @@
         skip_low.append(low(blocks))
     skip_tile = jnp.concatenate(skip_own, axis=1)
     skip_low = jnp.concatenate(skip_low, axis=2)
+    skip_low, *mlp_got = lax.optimization_barrier((skip_low, *mlp_got))
     for ahead, route in enumerate(routes["z"]):
         skip_tile = skip_tile + wide(send(skip_low[ahead + 1], route))
     skip_tile = skip_tile.T
-    qkv_tile = wide(stored_columns(low(jnp.concatenate(pair_sums)).T, seq))
+    qkv_tile = wide(stored_rows(low(jnp.concatenate(pair_sums)), seq)).T
 
     mlp_tile = mlp_own
     for piece in mlp_got:
@@ -1340,11 +1425,20 @@
     out_tile = mlp_tile[fold * columns : down_total.shape[1]]
     out_tile = jnp.concatenate([out_tile[:, i * columns : (i + 1) * columns] for i in range(wide_tile // columns)])
     up_tile = mlp_tile[down_total.shape[1] :]
-    sums_one, grad_main = lax.optimization_barrier((sums_one, grad_main))
-    grad_modulation = jnp.concatenate([sums_one[0], sums_one[1], sums_two[0], sums_two[1]]).reshape(1, seq, -1)
-    grad_modulation = jnp.broadcast_to(grad_modulation, (dp,) + grad_modulation.shape[1:]).reshape(dp * seq, -1)
-    grad_modulation = lax.all_to_all(grad_modulation, ("dp", "seq"), 0, 0, tiled=True)
-    grad_modulation = jnp.sum(grad_modulation.reshape(dp, seq, -1), axis=1)
+    grad_modulation = jnp.concatenate([sums_one[0], sums_one[1], sums_two[0], sums_two[1]])
+    chips, chip_at, core_at = seq // 2, seq_at // 2, seq_at % 2
+    grad_modulation = grad_modulation.reshape(chips, 2, -1)
+    kept = lax.dynamic_index_in_dim(grad_modulation, core_at, 1, keepdims=False)
+    kept = kept + send(lax.dynamic_index_in_dim(grad_modulation, 1 - core_at, 1, keepdims=False), routes["core"])
+    column_sum = lax.dynamic_index_in_dim(kept, chip_at, 0)
+    for ahead, route in enumerate(routes["z"]):
+        piece = lax.dynamic_index_in_dim(kept, (chip_at + ahead + 1) % chips, 0)
+        column_sum = column_sum + send(piece, route)
+    column_sum = jnp.concatenate([column_sum, send(column_sum, routes["x"])])
+    grad_modulation = jnp.concatenate([column_sum, send(column_sum, routes["y"])])
+    embed_part = jnp.concatenate(
+        [lax.dynamic_index_in_dim(embed_part, jnp.bitwise_xor(at, mask), 0) for mask in range(dp)]
+    )
     ada_tile = lax.dot_general(
         embed_part.astype(jnp.float32), grad_modulation, (((0,), (0,)), ((), ())),
         precision=lax.Precision.HIGHEST,

time: 627 us -> 597 us (0.952)
  waiting for transfers between devices: 214 us -> 142 us
  blocking collectives: 38.4 us -> 68.4 us
  starting transfers between devices: 66.7 us -> 83.3 us
    all_to_all x4, waiting for transfers between devices: 68 us -> 11.2 us  [the longest x1 8.12 us: local_paired(): local_b = lax.all_to_all(back_b, 'seq', 0, 0)]
    all_to_all x0 -> x1, blocking collectives: none -> 30.1 us  [local_paired(): attended = lax.all_to_all(attended_pair, 'seq', 0, 0).reshape(width, frames)]
    ppermute x35 -> x43, waiting for transfers between devices: 109 us -> 89.7 us  [send(): return lax.ppermute(value, ('dp', 'seq'), route)]
    ppermute x35 -> x43, starting transfers between devices: 39.9 us -> 56.7 us  [send(): return lax.ppermute(value, ('dp', 'seq'), route)]
    pallas_call x1, Pallas kernels: 34 us -> 19.9 us  [attend_pair(): pl.pallas_call(partial(attend_kernel, size=size, length=length), grid_spe...]
    pallas_call x2 -> x3, Pallas kernels: 53.7 us -> 64.2 us  [the longest x2 56.2 us: attend_head_back(): pl.pallas_call(partial(attend_back_kernel, head=head, size=size, length=l...]
    all_gather x1 -> x0, local copies, waits for them, and re-layouts: 8.66 us -> none  [local_paired(): pair_tiles = lax.all_gather(pair_tile, ('dp', 'seq'), axis=0)]
    unnamed x98 -> x121, local copies, waits for them, and re-layouts: 28.5 us -> 36.2 us
  transfers between devices with their start and end apart: 48 -> 56, of which waited for: 20 -> 21; matrix products, arithmetic and copies ran while one was open for 14% -> 16% of each run, Pallas kernels for 26% -> 26%
where the time goes in v4:
time: 597 us; the launch traced here: 589 us
  Pallas kernels  162 us (27%)
  waiting for transfers between devices  142 us (24%)
  starting transfers between devices  83.3 us (14%)
  blocking collectives  68.4 us (11%)
  local copies, waits for them, and re-layouts  54.6 us (9%)
  other arithmetic  50.9 us (9%)
  between operations  20.3 us (3%)
  matrix products  8.31 us (1%)
    ppermute x43, waiting for transfers between devices, send(): return lax.ppermute(value, ('dp', 'seq'), route)  89.7 us
    ppermute x43, starting transfers between devices, send(): return lax.ppermute(value, ('dp', 'seq'), route)  56.7 us
    pallas_call x2, Pallas kernels, attend_head_back(): pl.pallas_call(partial(attend_back_kernel, head=head, size=size, length=l...  56.2 us
    pallas_call x1, Pallas kernels, middle_block(): pl.pallas_call(partial(middle_kernel, dp=dp, seq=seq), in_specs=[pl.Block...  49.1 us
    unnamed x121, local copies, waits for them, and re-layouts  36.2 us
    all_gather x1, waiting for transfers between devices, local_paired(): normed_all = lax.all_gather(normed_one, 'seq', axis=0)  32 us
    all_to_all x1, blocking collectives, local_paired(): attended = lax.all_to_all(attended_pair, 'seq', 0, 0).reshape(width, frames)  30.1 us
    all_gather x1, blocking collectives, local_paired(): modulation = lax.all_gather(modulation_part, 'seq', axis=1, tiled=True)  21 us
  transfers between devices with their start and end apart: 56, of which 21 were waited for; matrix products, arithmetic and copies ran while one was open for 16% of the time, Pallas kernels for 26%

profile of v4, /device:TPU:0, one launch (start us, length us, event | category | flops | bytes accessed | tf_op | source)
XLA Modules:
  0.0 589.2 jit_solution(2234186098793339459)
XLA Ops:
  9.8 3.1 collective-permute-start.3
  12.9 2.6 collective-permute-start.4
  20.9 8.2 %all-gather.3 = bf16[4,1,1024]{2,1,0:T(2,128)(2,1)S(1)} all-gather(bf16[1,1,1024]{2,1,0:T(2,128)(2,1)S(1)} %bitcast.173), channel_id=1, replica_groups=mesh['dp'=4,'seq'=8] {'dp'}, dimensions={0}, use_global_device_ids=true | all-gather | bytes 10240 | tf_op jit(solution)/shard_map/all_gather | solution.py:1275
  30.3 3.9 compare_select_fusion.4
  37.5 2.8 multiply_sine_fusion
  42.2 9.0 %all-reduce = f32[4,512]{1,0:T(4,128)S(1)} all-reduce(f32[4,512]{1,0:T(4,128)S(1)} %fusion.27), channel_id=5, replica_groups=mesh['dp'=4,'seq'=8] {'dp'}, use_global_device_ids=true, to_apply=%region_2.3.clone | all-reduce | flops 2048 | bytes 16384
  52.5 21.0 %all_gather.27 = f32[1,4096]{1,0:T(1,128)S(1)} all-gather(f32[1,512]{1,0:T(1,128)S(1)} %constant_dynamic-slice_fusion.13), channel_id=1, replica_groups=mesh['dp'=4,'seq'=8] {'seq'}, dimensions={1}, use_global_device_ids=true | all-gather | bytes 18432 | tf_op jit(solution)/shard_map/all_gather | solution.py:1280
  76.2 2.4 pad_maximum_fusion.4
  78.7 13.1 %collective-permute-done.5 = bf16[1280,128]{1,0:T(8,128)(2,1)S(1)} collective-permute-done((bf16[1280,128]{1,0:T(8,128)(2,1)S(1)}, bf16[1280,128]{1,0:T(8,128)(2,1)S(1)}, u32[]{:S(2)}, u32[]{:S(2)}) %collective-permute-start.5) | collective-permute-done | bytes 327712 | tf_op jit(solution)/shard_map/ppermute | solution.py:725
  93.1 2.2 all-gather.8.cloned.1.call-done
  95.3 2.2 copy-done.10
  97.5 4.6 entry_block.1
  107.0 3.0 collective-permute-start.10
  121.7 2.8 collective-permute-start.13
  124.5 18.3 %collective-permute-done.11 = bf16[384,256]{1,0:T(8,128)(2,1)} collective-permute-done((bf16[384,256]{1,0:T(8,128)(2,1)S(1)}, bf16[384,256]{1,0:T(8,128)(2,1)}, u32[]{:S(2)}, u32[]{:S(2)}) %collective-permute-start.11) | collective-permute-done | bytes 196640 | tf_op jit(solution)/shard_map/ppermute | solution.py:725
  148.8 3.1 pad_maximum_fusion.down_0
  154.9 32.0 %all-gather.10.cloned.1.call-done = bf16[4096,1024]{1,0:T(8,128)(2,1)} async-done(((bf16[512,1024]{1,0:T(8,128)(2,1)}), bf16[4096,1024]{1,0:T(8,128)(2,1)}) %all-gather.10.cloned.1.call-update) | async-done | bytes 8388624 | tf_op jit(solution)/shard_map/all_gather | solution.py:1292
  186.8 10.5 %project_pair.1 = (bf16[8,128,512]{2,1,0:T(8,128)(2,1)}, bf16[128,4096]{1,0:T(8,128)(2,1)}, bf16[128,4096]{1,0:T(8,128)(2,1)}, bf16[4096,128]{1,0:T(8,128)(2,1)}...) custom-call(bf16[8,512,1024]{2,1,0:T(8,128)(2,1)} %bitcast.174, ...), custom_call_target="tpu_custom_call" | custom-call | flops 3221225472 | bytes 13631488 | tf_op jit(solution)/shard_map/project_pair/pallas_call | solution.py:443
  201.8 19.9 %attend_pair.1 = (bf16[8,128,512]{2,1,0:T(8,128)(2,1)S(1)}, f32[8,128,512]{2,1,0:T(8,128)S(1)}, f32[8,2,512]{2,1,0:T(2,128)S(1)}) custom-call(s32[2]{0:T(128)S(1)} %pad_add_fusion.ends_ref, bf16[8,128,512]{2,1,0:T(8,128)(2,1)S(1)} %copy-done.13, bf16[4096,128]{1,0:T(8,128)(2,1)S(1)} %copy-done.14, bf16[128,4096]{1,0:T(8,128)(2,1)S(1)} %copy-done.15, ...), custom_call_target="tpu_custom_call" | custom-call | flops 8589934592 | bytes 7340032 | tf_op jit(solution)/shard_map/attend_pair/pallas_call | solution.py:553
  222.4 30.1 %all_to_all.25 = bf16[8,128,512]{2,1,0:T(8,128)(2,1)} all-to-all(bf16[8,128,512]{2,1,0:T(8,128)(2,1)S(1)} %get-tuple-element.117), channel_id=1, replica_groups=mesh['dp'=4,'seq'=8] {'seq'}, dimensions={0} | all-to-all | bytes 2097152 | tf_op jit(solution)/shard_map/all_to_all | solution.py:1305
  255.8 6.4 %collective-permute-done.18.up_2 = bf16[2,4,256,512]{3,2,1,0:T(8,128)(2,1)} collective-permute-done((bf16[2,4,256,512]{3,2,1,0:T(8,128)(2,1)}, bf16[2,4,256,512]{3,2,1,0:T(8,128)(2,1)}, u32[]{:S(2)}, u32[]{:S(2)}) %collective-permute-start.18) | collective-permute-done | bytes 2097184 | tf_op jit(solution)/shard_map/ppermute | solution.py:725
  262.2 49.1 %middle_block.1 = (bf16[512,1024]{1,0:T(8,128)(2,1)}, f32[512,1024]{1,0:T(8,128)}, bf16[8,64,512]{2,1,0:T(8,128)(2,1)}, bf16[8,64,512]{2,1,0:T(8,128)(2,1)}, f32...) custom-call(s32[3]{0:T(128)} %pad_add_fusion.1.place_ref, ...), custom_call_target="tpu_custom_call" | custom-call | flops 28991029248 | bytes 46137344 | tf_op jit(solution)/shard_map/middle_block/pallas_call | solution.py:933
  311.8 4.6 all-to-all-start.1
  319.4 9.1 %collective-permute-done.21 = bf16[4,4,256,512]{3,2,1,0:T(8,128)(2,1)} collective-permute-done((bf16[4,4,256,512]{3,2,1,0:T(8,128)(2,1)}, bf16[4,4,256,512]{3,2,1,0:T(8,128)(2,1)}, u32[]{:S(2)}, u32[]{:S(2)}) %collective-permute-start.21) | collective-permute-done | bytes 4194336 | tf_op jit(solution)/shard_map/ppermute | solution.py:725
  328.5 4.4 add_convert_fusion.4
  332.9 4.1 add_convert_fusion.1
  337.0 4.1 all-to-all-start.2
  341.1 3.8 collective-permute-start.22
  345.0 1.9 collective-permute-start.24
  347.1 28.1 %attend_head_back.2 = bf16[8,192,512]{2,1,0:T(8,128)(2,1)} custom-call(s32[2]{0:T(128)} %copy-done.12, bf16[8,128,512]{2,1,0:T(8,128)(2,1)} %get-tuple-element.112.qt_ref, bf16[8,64,512]{2,1,0:T(8,128)(2,1)} %all-to-all-done.1.gt_ref, f32[8,128,512]{2,1,0:T(8,128)} %copy-done.17, f32[8,2,512]{2,1,0:T(2,128)} %copy-done.18, ...), custom_call_target="tpu_custom_call" | custom-call | flops 42949672960 | bytes 10485760 | tf_op jit(solution)/shard_map/attend_head_back/pallas_call | solution.py:646
  375.2 4.9 all-to-all-start.3
  380.1 1.9 slice_dynamic-update-slice_fusion.5
  382.0 2.5 constant_dynamic-update-slice_fusion.3
  384.5 28.1 %attend_head_back.3 = bf16[8,192,512]{2,1,0:T(8,128)(2,1)} custom-call(s32[2]{0:T(128)} %copy-done.12, bf16[8,128,512]{2,1,0:T(8,128)(2,1)} %get-tuple-element.112.qt_ref, bf16[8,64,512]{2,1,0:T(8,128)(2,1)} %all-to-all-done.2.gt_ref, f32[8,128,512]{2,1,0:T(8,128)} %copy-done.17, f32[8,2,512]{2,1,0:T(2,128)} %copy-done.18, ...), custom_call_target="tpu_custom_call" | custom-call | flops 42949672960 | bytes 10485760 | tf_op jit(solution)/shard_map/attend_head_back/pallas_call | solution.py:646
  412.7 2.3 constant_dynamic-update-slice_fusion.5
  414.9 3.1 all-to-all-done.3.head_a_ref
  418.0 4.5 all-to-all-start.4
  422.5 2.0 slice_dynamic-update-slice_fusion.4
  424.6 2.1 slice_dynamic-update-slice_fusion.3
  427.5 1.9 slice_dynamic-update-slice_fusion.1
  430.4 3.7 fusion.3
  434.2 5.2 collective-permute-start.27
  440.8 4.3 fusion
  445.3 7.0 %bitcast_convert_fusion = bf16[384,1024]{1,0:T(8,128)(2,1)} fusion(bf16[8,384,512]{2,1,0:T(8,128)(2,1)S(1)} %copy-done.43, bf16[8,512,1024]{2,1,0:T(8,128)(2,1)} %bitcast.175), kind=kOutput, calls=%fused_computation.11 | convolution fusion | flops 3221618688 | bytes 12320768 | tf_op jit(solution)/shard_map/icf,ifd->cd/dot_general | solution.py:1351
  452.2 8.1 %all-to-all-done.4.head_b_ref = bf16[8,192,512]{2,1,0:T(8,128)(2,1)} async-done(((bf16[8,192,512]{2,1,0:T(8,128)(2,1)}), bf16[8,192,512]{2,1,0:T(8,128)(2,1)}, u32[]{:S(2)}, u32[]{:S(2)}) %all-to-all-start.4) | async-done | bytes 1572896 | tf_op jit(solution)/shard_map/all_to_all | solution.py:1340
  463.6 8.0 %exit_block.1 = (bf16[512,1024]{1,0:T(8,128)(2,1)S(1)}, bf16[1024,512]{1,0:T(8,128)(2,1)S(1)}, f32[2,1024]{1,0:T(2,128)S(1)}) custom-call(bf16[8,192,512]{2,1,0:T(8,128)(2,1)} %all-to-all-done.3.head_a_ref, bf16[8,192,512]{2,1,0:T(8,128)(2,1)} %all-to-all-done.4.head_b_ref, bf16[32,384,256]{2,1,0:T(8,128)(2,1)} %bitcast.151, f32[512,1024]{1,0:T(8,128)S(1)} %copy-done.3, ...), custom_call_target="tpu_custom_call" | custom-call | flops 3221225472 | bytes 15728640 | tf_op jit(solution)/shard_map/exit_block/pallas_call | solution.py:1049
  471.5 2.0 grad_blocks.5
  473.6 2.0 grad_blocks.4
  476.3 4.6 fusion.39
  481.6 3.5 fusion.40
  489.6 4.7 joined_grads.1
  494.3 8.0 %collective-permute-done.30 = bf16[576,512]{1,0:T(8,128)(2,1)S(1)} collective-permute-done((bf16[576,512]{1,0:T(8,128)(2,1)S(1)}, bf16[576,512]{1,0:T(8,128)(2,1)S(1)}, u32[]{:S(2)}, u32[]{:S(2)}) %collective-permute-start.30) | collective-permute-done | bytes 589856 | tf_op jit(solution)/shard_map/ppermute | solution.py:725
  502.3 2.2 grad_blocks.7
  504.6 2.2 grad_blocks.6
  507.8 4.9 collective-permute-start.32
  513.3 2.8 collective-permute-start.42
  516.1 2.1 collective-permute-done.41
  521.3 21.0 %collective-permute-done.42 = f32[1,512]{1,0:T(1,128)S(1)} collective-permute-done((f32[1,512]{1,0:T(1,128)S(1)}, f32[1,512]{1,0:T(1,128)S(1)}, u32[]{:S(2)}, u32[]{:S(2)}) %collective-permute-start.42) | collective-permute-done | bytes 2080 | tf_op jit(solution)/shard_map/ppermute | solution.py:725
  552.1 3.2 collective-permute-done.34
  556.4 2.3 collective-permute-start.48
  560.2 5.0 collective-permute-done.47
  568.9 2.1 collective-permute-start.37
  571.0 2.3 collective-permute-start.38
  577.2 4.3 collective-permute-done.38
  (276 shorter events, 89.6 us)
Async XLA Ops:
  7.2 29.1 %copy-start = (bf16[256,512]{1,0:T(8,128)(2,1)S(1)}, bf16[256,512]{1,0:T(8,128)(2,1)}, u32[]{:S(2)}) copy-start(bf16[256,512]{1,0:T(8,128)(2,1)} %param.23) | copy-start | bytes 786436
  7.2 23.1 %copy-start.44 = (s32[1,4096]{1,0:T(1,128)S(1)}, s32[1,4096]{1,0:T(1,128)}, u32[]{:S(2)}) copy-start(s32[1,4096]{1,0:T(1,128)} %param.18) | copy-start | bytes 49156
  7.2 88.0 %all-gather.8.cloned.1.call-start = ((), (), s32[]{:S(2)}) async-start(), calls=%async_computation.5 | async-start | bytes 4325376 | tf_op jit(solution)/shard_map/all_gather | solution.py:1286
  8.0 178.8 %all-gather.10.cloned.1.call-start = ((), (), s32[]{:S(2)}) async-start(), calls=%async_computation.6 | async-start | bytes 9437184 | tf_op jit(solution)/shard_map/all_gather | solution.py:1292
  9.8 68.8 %collective-permute-start.3 = (bf16[1280,128]{1,0:T(8,128)(2,1)S(1)}, bf16[1280,128]{1,0:T(8,128)(2,1)S(1)}, u32[]{:S(2)}, u32[]{:S(2)}) collective-permute-start(bf16[1280,128]{1,0:T(8,128)(2,1)S(1)} %constant_dynamic-update-slice_fusion), channel_id=1, source_target_pairs={{0,2},{1,3},{2,4},{3,5},{4,6},{5,7},{6,0},{7,1},{8,10},{9,11},{10,... | collective-permute-start | bytes 983048 | tf_op jit(solution)/shard_map/ppermute | solution.py:725
  12.9 65.8 %collective-permute-start.4 = (bf16[1280,128]{1,0:T(8,128)(2,1)S(1)}, bf16[1280,128]{1,0:T(8,128)(2,1)S(1)}, u32[]{:S(2)}, u32[]{:S(2)}) collective-permute-start(bf16[1280,128]{1,0:T(8,128)(2,1)S(1)} %constant_dynamic-update-slice_fusion), channel_id=1, source_target_pairs={{0,4},{1,5},{2,6},{3,7},{4,0},{5,1},{6,2},{7,3},{8,12},{9,13},{10,... | collective-permute-start | bytes 983048 | tf_op jit(solution)/shard_map/ppermute | solution.py:725
  15.5 58.1 %collective-permute-start = (bf16[256,512]{1,0:T(8,128)(2,1)}, bf16[256,512]{1,0:T(8,128)(2,1)S(1)}, u32[]{:S(2)}, u32[]{:S(2)}) collective-permute-start(bf16[256,512]{1,0:T(8,128)(2,1)} %param.26), channel_id=1, source_target_pairs={{0,2},{1,3},{2,4},{3,5},{4,6},{5,7},{6,0},{7,1},{8,10},{9,11},{10,... | collective-permute-start | bytes 786440 | tf_op jit(solution)/shard_map/ppermute | solution.py:725
  15.6 59.9 %collective-permute-start.1 = (bf16[256,512]{1,0:T(8,128)(2,1)}, bf16[256,512]{1,0:T(8,128)(2,1)S(1)}, u32[]{:S(2)}, u32[]{:S(2)}) collective-permute-start(bf16[256,512]{1,0:T(8,128)(2,1)} %param.26), channel_id=1, source_target_pairs={{0,4},{1,5},{2,6},{3,7},{4,0},{5,1},{6,2},{7,3},{8,12},{9,13},{10,... | collective-permute-start | bytes 786440 | tf_op jit(solution)/shard_map/ppermute | solution.py:725
  17.4 58.0 %collective-permute-start.2 = (bf16[256,512]{1,0:T(8,128)(2,1)}, bf16[256,512]{1,0:T(8,128)(2,1)S(1)}, u32[]{:S(2)}, u32[]{:S(2)}) collective-permute-start(bf16[256,512]{1,0:T(8,128)(2,1)} %param.26), channel_id=1, source_target_pairs={{0,6},{1,7},{2,0},{3,1},{4,2},{5,3},{6,4},{7,5},{8,14},{9,15},{10,... | collective-permute-start | bytes 786440 | tf_op jit(solution)/shard_map/ppermute | solution.py:725
  41.6 155.7 %copy-start.12 = (s32[2]{0:T(128)}, s32[2]{0:T(128)S(1)}, u32[]{:S(2)}) copy-start(s32[2]{0:T(128)S(1)} %pad_add_fusion.ends_ref) | copy-start | bytes 28
  73.6 18.2 %collective-permute-start.5 = (bf16[1280,128]{1,0:T(8,128)(2,1)S(1)}, bf16[1280,128]{1,0:T(8,128)(2,1)S(1)}, u32[]{:S(2)}, u32[]{:S(2)}) collective-permute-start(bf16[1280,128]{1,0:T(8,128)(2,1)S(1)} %constant_dynamic-update-slice_fusion), channel_id=1, source_target_pairs={{0,6},{1,7},{2,0},{3,1},{4,2},{5,3},{6,4},{7,5},{8,14},{9,15},{10,... | collective-permute-start | bytes 983048 | tf_op jit(solution)/shard_map/ppermute | solution.py:725
  103.4 43.6 %copy-start.29 = (bf16[4,256,512]{2,1,0:T(8,128)(2,1)S(1)}, bf16[4,256,512]{2,1,0:T(8,128)(2,1)}, u32[]{:S(2)}) copy-start(bf16[4,256,512]{2,1,0:T(8,128)(2,1)} %pad_maximum_fusion.4) | copy-start | bytes 3145732
  103.4 237.7 %all-gather.12.cloned.1.call-start = ((), (), s32[]{:S(2)}) async-start(), calls=%async_computation.7 | async-start | bytes 6488064 | tf_op jit(solution)/shard_map/all_gather | solution.py:1310
  104.6 43.9 %collective-permute-start.7 = (bf16[4,1280,128]{2,1,0:T(8,128)(2,1)}, bf16[4,1280,128]{2,1,0:T(8,128)(2,1)}, u32[]{:S(2)}, u32[]{:S(2)}) collective-permute-start(bf16[4,1280,128]{2,1,0:T(8,128)(2,1)} %pad_maximum_fusion.3), channel_id=1, source_target_pairs={{0,16},{1,17},{2,18},{3,19},{4,20},{5,21},{6,22},{7,23},{8,24},{9,... | collective-permute-start | bytes 3932168 | tf_op jit(solution)/shard_map/ppermute | solution.py:725
  107.0 12.2 %collective-permute-start.10 = (bf16[128,256]{1,0:T(8,128)(2,1)}, bf16[128,256]{1,0:T(8,128)(2,1)S(1)}, u32[]{:S(2)}, u32[]{:S(2)}) collective-permute-start(bf16[128,256]{1,0:T(8,128)(2,1)} %get-tuple-element.272), channel_id=1, source_target_pairs={{0,2},{1,5},{2,0},{3,3},{4,6},{5,1},{6,4},{7,7},{8,10},{9,13},{10,... | collective-permute-start | bytes 196616 | tf_op jit(solution)/shard_map/ppermute | solution.py:685
  110.0 9.3 %collective-permute-start.8 = (bf16[128,256]{1,0:T(8,128)(2,1)S(1)}, bf16[128,256]{1,0:T(8,128)(2,1)S(1)}, u32[]{:S(2)}, u32[]{:S(2)}) collective-permute-start(bf16[128,256]{1,0:T(8,128)(2,1)S(1)} %get-tuple-element.274), channel_id=1, source_target_pairs={{0,0},{1,3},{2,6},{3,1},{4,4},{5,7},{6,2},{7,5},{8,8},{9,11},{10,1... | collective-permute-start | bytes 196616 | tf_op jit(solution)/shard_map/ppermute | solution.py:685
  110.6 8.6 %collective-permute-start.9 = (bf16[128,256]{1,0:T(8,128)(2,1)S(1)}, bf16[128,256]{1,0:T(8,128)(2,1)S(1)}, u32[]{:S(2)}, u32[]{:S(2)}) collective-permute-start(bf16[128,256]{1,0:T(8,128)(2,1)S(1)} %get-tuple-element.273), channel_id=1, source_target_pairs={{0,1},{1,4},{2,7},{3,2},{4,5},{5,0},{6,3},{7,6},{8,9},{9,12},{10,1... | collective-permute-start | bytes 196616 | tf_op jit(solution)/shard_map/ppermute | solution.py:685
  112.3 34.7 %collective-permute-start.6 = (bf16[4,256,512]{2,1,0:T(8,128)(2,1)}, bf16[4,256,512]{2,1,0:T(8,128)(2,1)S(1)}, u32[]{:S(2)}, u32[]{:S(2)}) collective-permute-start(bf16[4,256,512]{2,1,0:T(8,128)(2,1)} %pad_maximum_fusion.4), channel_id=1, source_target_pairs={{0,8},{1,9},{2,10},{3,11},{4,12},{5,13},{6,14},{7,15},{8,0},{9,1},... | collective-permute-start | bytes 3145736 | tf_op jit(solution)/shard_map/ppermute | solution.py:725
  121.0 27.5 %copy-start.31 = (bf16[384,256]{1,0:T(8,128)(2,1)}, bf16[384,256]{1,0:T(8,128)(2,1)S(1)}, u32[]{:S(2)}) copy-start(bf16[384,256]{1,0:T(8,128)(2,1)S(1)} %get-tuple-element.129) | copy-start | bytes 589828
  121.0 21.8 %collective-permute-start.11 = (bf16[384,256]{1,0:T(8,128)(2,1)S(1)}, bf16[384,256]{1,0:T(8,128)(2,1)}, u32[]{:S(2)}, u32[]{:S(2)}) collective-permute-start(bf16[384,256]{1,0:T(8,128)(2,1)S(1)} %get-tuple-element.129), channel_id=1, source_target_pairs={{0,8},{1,9},{2,10},{3,11},{4,12},{5,13},{6,14},{7,15},{8,0},{9,1},... | collective-permute-start | bytes 589832 | tf_op jit(solution)/shard_map/ppermute | solution.py:725
  121.3 23.1 %collective-permute-start.12 = (bf16[384,256]{1,0:T(8,128)(2,1)S(1)}, bf16[384,256]{1,0:T(8,128)(2,1)}, u32[]{:S(2)}, u32[]{:S(2)}) collective-permute-start(bf16[384,256]{1,0:T(8,128)(2,1)S(1)} %get-tuple-element.129), channel_id=1, source_target_pairs={{0,16},{1,17},{2,18},{3,19},{4,20},{5,21},{6,22},{7,23},{8,24},{9,... | collective-permute-start | bytes 589832 | tf_op jit(solution)/shard_map/ppermute | solution.py:725
  121.7 24.5 %collective-permute-start.13 = (bf16[384,256]{1,0:T(8,128)(2,1)S(1)}, bf16[384,256]{1,0:T(8,128)(2,1)S(1)}, u32[]{:S(2)}, u32[]{:S(2)}) collective-permute-start(bf16[384,256]{1,0:T(8,128)(2,1)S(1)} %get-tuple-element.129), channel_id=1, source_target_pairs={{0,24},{1,25},{2,26},{3,27},{4,28},{5,29},{6,30},{7,31},{8,16},{9,... | collective-permute-start | bytes 589832 | tf_op jit(solution)/shard_map/ppermute | solution.py:725
  151.9 69.9 %collective-permute-start.15 = (bf16[2,4,1280,128]{3,2,1,0:T(8,128)(2,1)}, bf16[2,4,1280,128]{3,2,1,0:T(8,128)(2,1)}, u32[]{:S(2)}, u32[]{:S(2)}) collective-permute-start(bf16[2,4,1280,128]{3,2,1,0:T(8,128)(2,1)} %pad_maximum_fusion.down_0), channel_id=1, source_target_pairs={{0,8},{1,9},{2,10},{3,11},{4,12},{5,13},{6,14},{7,15},{8,0},{9,1},... | collective-permute-start | bytes 7864328 | tf_op jit(solution)/shard_map/ppermute | solution.py:725
  153.4 68.3 %collective-permute-start.14 = (bf16[2,4,256,512]{3,2,1,0:T(8,128)(2,1)}, bf16[2,4,256,512]{3,2,1,0:T(8,128)(2,1)}, u32[]{:S(2)}, u32[]{:S(2)}) collective-permute-start(bf16[2,4,256,512]{3,2,1,0:T(8,128)(2,1)} %pad_maximum_fusion.1.up_0), channel_id=1, source_target_pairs={{0,16},{1,17},{2,18},{3,19},{4,20},{5,21},{6,22},{7,23},{8,24},{9,... | collective-permute-start | bytes 6291464 | tf_op jit(solution)/shard_map/ppermute | solution.py:725
  221.8 30.7 %copy-start.17 = (f32[8,128,512]{2,1,0:T(8,128)}, f32[8,128,512]{2,1,0:T(8,128)S(1)}, u32[]{:S(2)}) copy-start(f32[8,128,512]{2,1,0:T(8,128)S(1)} %get-tuple-element.140.full_ref) | copy-start | bytes 6291460
  221.8 34.0 %copy-start.18 = (f32[8,2,512]{2,1,0:T(2,128)}, f32[8,2,512]{2,1,0:T(2,128)S(1)}, u32[]{:S(2)}) copy-start(f32[8,2,512]{2,1,0:T(2,128)S(1)} %get-tuple-element.141.total_ref) | copy-start | bytes 98308
  221.8 32.6 %copy-start.28 = (bf16[512,1024]{0,1:T(8,128)(2,1)S(1)}, bf16[512,1024]{0,1:T(8,128)(2,1)}, u32[]{:S(2)}) copy-start(bf16[512,1024]{0,1:T(8,128)(2,1)} %bitcast_select_fusion) | copy-start | bytes 3145732
  221.8 32.0 %collective-permute-start.17 = (bf16[2,4,1280,128]{3,2,1,0:T(8,128)(2,1)}, bf16[2,4,1280,128]{3,2,1,0:T(8,128)(2,1)}, u32[]{:S(2)}, u32[]{:S(2)}) collective-permute-start(bf16[2,4,1280,128]{3,2,1,0:T(8,128)(2,1)} %collective-permute-done.15.down_1), channel_id=1, source_target_pairs={{0,1},{1,0},{2,3},{3,2},{4,5},{5,4},{6,7},{7,6},{8,9},{9,8},{10,11... | collective-permute-start | bytes 7864328 | tf_op jit(solution)/shard_map/ppermute | solution.py:725
  222.1 30.4 %collective-permute-start.16 = (bf16[2,4,256,512]{3,2,1,0:T(8,128)(2,1)}, bf16[2,4,256,512]{3,2,1,0:T(8,128)(2,1)S(1)}, u32[]{:S(2)}, u32[]{:S(2)}) collective-permute-start(bf16[2,4,256,512]{3,2,1,0:T(8,128)(2,1)} %collective-permute-done.14.up_1), channel_id=1, source_target_pairs={{0,1},{1,0},{2,3},{3,2},{4,5},{5,4},{6,7},{7,6},{8,9},{9,8},{10,11... | collective-permute-start | bytes 6291464 | tf_op jit(solution)/shard_map/ppermute | solution.py:725
  253.8 8.3 %collective-permute-start.19 = (bf16[2,4,1280,128]{3,2,1,0:T(8,128)(2,1)}, bf16[2,4,1280,128]{3,2,1,0:T(8,128)(2,1)}, u32[]{:S(2)}, u32[]{:S(2)}) collective-permute-start(bf16[2,4,1280,128]{3,2,1,0:T(8,128)(2,1)} %pad_maximum_fusion.down_0), channel_id=1, source_target_pairs={{0,1},{1,0},{2,3},{3,2},{4,5},{5,4},{6,7},{7,6},{8,9},{9,8},{10,11... | collective-permute-start | bytes 7864328 | tf_op jit(solution)/shard_map/ppermute | solution.py:725
  253.9 8.2 %collective-permute-start.18 = (bf16[2,4,256,512]{3,2,1,0:T(8,128)(2,1)}, bf16[2,4,256,512]{3,2,1,0:T(8,128)(2,1)}, u32[]{:S(2)}, u32[]{:S(2)}) collective-permute-start(bf16[2,4,256,512]{3,2,1,0:T(8,128)(2,1)} %pad_maximum_fusion.1.up_0), channel_id=1, source_target_pairs={{0,1},{1,0},{2,3},{3,2},{4,5},{5,4},{6,7},{7,6},{8,9},{9,8},{10,11... | collective-permute-start | bytes 6291464 | tf_op jit(solution)/shard_map/ppermute | solution.py:725
  311.2 21.7 %collective-permute-start.20 = (bf16[4,4,320,512]{3,2,1,0:T(8,128)(2,1)}, bf16[4,4,320,512]{3,2,1,0:T(8,128)(2,1)}, u32[]{:S(2)}, u32[]{:S(2)}) collective-permute-start(bf16[4,4,320,512]{3,2,1,0:T(8,128)(2,1)} %get-tuple-element.132), channel_id=1, source_target_pairs={{0,1},{1,0},{2,3},{3,2},{4,5},{5,4},{6,7},{7,6},{8,9},{9,8},{10,11... | collective-permute-start | bytes 15728648 | tf_op jit(solution)/shard_map/ppermute | solution.py:725
  311.4 17.1 %collective-permute-start.21 = (bf16[4,4,256,512]{3,2,1,0:T(8,128)(2,1)}, bf16[4,4,256,512]{3,2,1,0:T(8,128)(2,1)}, u32[]{:S(2)}, u32[]{:S(2)}) collective-permute-start(bf16[4,4,256,512]{3,2,1,0:T(8,128)(2,1)} %get-tuple-element.134), channel_id=1, source_target_pairs={{0,1},{1,0},{2,3},{3,2},{4,5},{5,4},{6,7},{7,6},{8,9},{9,8},{10,11... | collective-permute-start | bytes 12582920 | tf_op jit(solution)/shard_map/ppermute | solution.py:725
  311.8 25.2 %all-to-all-start.1 = ((bf16[8,64,512]{2,1,0:T(8,128)(2,1)}), bf16[8,64,512]{2,1,0:T(8,128)(2,1)}, u32[]{:S(2)}, u32[]{:S(2)}) async-start(bf16[8,64,512]{2,1,0:T(8,128)(2,1)} %get-tuple-element.128), calls=%async_computation.1 | async-start | bytes 1048576 | tf_op jit(solution)/shard_map/all_to_all | solution.py:1314
  337.0 38.2 %all-to-all-start.2 = ((bf16[8,64,512]{2,1,0:T(8,128)(2,1)}), bf16[8,64,512]{2,1,0:T(8,128)(2,1)}, u32[]{:S(2)}, u32[]{:S(2)}) async-start(bf16[8,64,512]{2,1,0:T(8,128)(2,1)} %get-tuple-element.144), calls=%async_computation.2 | async-start | bytes 1048576 | tf_op jit(solution)/shard_map/all_to_all | solution.py:1328
  341.1 39.0 %collective-permute-start.22 = (bf16[2,4,160,512]{3,2,1,0:T(8,128)(2,1)}, bf16[2,4,160,512]{3,2,1,0:T(8,128)(2,1)}, u32[]{:S(2)}, u32[]{:S(2)}) collective-permute-start(bf16[2,4,160,512]{3,2,1,0:T(8,128)(2,1)} %get-tuple-element.145), channel_id=1, source_target_pairs={{0,8},{1,9},{2,10},{3,11},{4,12},{5,13},{6,14},{7,15},{8,0},{9,1},... | collective-permute-start | bytes 3932168 | tf_op jit(solution)/shard_map/ppermute | solution.py:725
  345.0 35.1 %collective-permute-start.23 = (bf16[2,4,128,512]{3,2,1,0:T(8,128)(2,1)}, bf16[2,4,128,512]{3,2,1,0:T(8,128)(2,1)}, u32[]{:S(2)}, u32[]{:S(2)}) collective-permute-start(bf16[2,4,128,512]{3,2,1,0:T(8,128)(2,1)} %get-tuple-element.146), channel_id=1, source_target_pairs={{0,16},{1,17},{2,18},{3,19},{4,20},{5,21},{6,22},{7,23},{8,24},{9,... | collective-permute-start | bytes 3145736 | tf_op jit(solution)/shard_map/ppermute | solution.py:725
  345.0 85.3 %collective-permute-start.24 = (bf16[2,4,160,512]{3,2,1,0:T(8,128)(2,1)}, bf16[2,4,160,512]{3,2,1,0:T(8,128)(2,1)}, u32[]{:S(2)}, u32[]{:S(2)}) collective-permute-start(bf16[2,4,160,512]{3,2,1,0:T(8,128)(2,1)} %get-tuple-element.155), channel_id=1, source_target_pairs={{0,8},{1,9},{2,10},{3,11},{4,12},{5,13},{6,14},{7,15},{8,0},{9,1},... | collective-permute-start | bytes 3932168 | tf_op jit(solution)/shard_map/ppermute | solution.py:725
  346.9 83.3 %collective-permute-start.25 = (bf16[2,4,128,512]{3,2,1,0:T(8,128)(2,1)}, bf16[2,4,128,512]{3,2,1,0:T(8,128)(2,1)S(1)}, u32[]{:S(2)}, u32[]{:S(2)}) collective-permute-start(bf16[2,4,128,512]{3,2,1,0:T(8,128)(2,1)} %get-tuple-element.156), channel_id=1, source_target_pairs={{0,16},{1,17},{2,18},{3,19},{4,20},{5,21},{6,22},{7,23},{8,24},{9,... | collective-permute-start | bytes 3145736 | tf_op jit(solution)/shard_map/ppermute | solution.py:725
  375.2 42.8 %all-to-all-start.3 = ((bf16[8,192,512]{2,1,0:T(8,128)(2,1)}), bf16[8,192,512]{2,1,0:T(8,128)(2,1)}, u32[]{:S(2)}, u32[]{:S(2)}) async-start(bf16[8,192,512]{2,1,0:T(8,128)(2,1)} %attend_head_back.2), calls=%async_computation.3 | async-start | bytes 3145728 | tf_op jit(solution)/shard_map/all_to_all | solution.py:1334
  418.0 42.3 %all-to-all-start.4 = ((bf16[8,192,512]{2,1,0:T(8,128)(2,1)}), bf16[8,192,512]{2,1,0:T(8,128)(2,1)}, u32[]{:S(2)}, u32[]{:S(2)}) async-start(bf16[8,192,512]{2,1,0:T(8,128)(2,1)} %attend_head_back.3), calls=%async_computation.4 | async-start | bytes 3145728 | tf_op jit(solution)/shard_map/all_to_all | solution.py:1340
  434.2 41.5 %collective-permute-start.27 = (bf16[4,256,512]{2,1,0:T(8,128)(2,1)}, bf16[4,256,512]{2,1,0:T(8,128)(2,1)S(1)}, u32[]{:S(2)}, u32[]{:S(2)}) collective-permute-start(bf16[4,256,512]{2,1,0:T(8,128)(2,1)} %fusion.3), channel_id=1, source_target_pairs={{0,8},{1,9},{2,10},{3,11},{4,12},{5,13},{6,14},{7,15},{8,0},{9,1},... | collective-permute-start | bytes 3145736 | tf_op jit(solution)/shard_map/ppermute | solution.py:725
  445.1 31.2 %collective-permute-start.26 = (bf16[4,320,512]{2,1,0:T(8,128)(2,1)}, bf16[4,320,512]{2,1,0:T(8,128)(2,1)}, u32[]{:S(2)}, u32[]{:S(2)}) collective-permute-start(bf16[4,320,512]{2,1,0:T(8,128)(2,1)} %fusion), channel_id=1, source_target_pairs={{0,16},{1,17},{2,18},{3,19},{4,20},{5,21},{6,22},{7,23},{8,24},{9,... | collective-permute-start | bytes 3932168 | tf_op jit(solution)/shard_map/ppermute | solution.py:725
  481.0 21.3 %collective-permute-start.28 = (bf16[4,4,128,256]{3,2,1,0:T(8,128)(2,1)S(1)}, bf16[4,4,128,256]{3,2,1,0:T(8,128)(2,1)S(1)}, u32[]{:S(2)}, u32[]{:S(2)}) collective-permute-start(bf16[4,4,128,256]{3,2,1,0:T(8,128)(2,1)S(1)} %grad_blocks.4), channel_id=1, source_target_pairs={{0,1},{1,0},{2,3},{3,2},{4,5},{5,4},{6,7},{7,6},{8,9},{9,8},{10,11... | collective-permute-start | bytes 3145736 | tf_op jit(solution)/shard_map/ppermute | solution.py:725
  481.1 21.3 %collective-permute-start.29 = (bf16[4,4,128,256]{3,2,1,0:T(8,128)(2,1)S(1)}, bf16[4,4,128,256]{3,2,1,0:T(8,128)(2,1)S(1)}, u32[]{:S(2)}, u32[]{:S(2)}) collective-permute-start(bf16[4,4,128,256]{3,2,1,0:T(8,128)(2,1)S(1)} %grad_blocks.5), channel_id=1, source_target_pairs={{0,1},{1,0},{2,3},{3,2},{4,5},{5,4},{6,7},{7,6},{8,9},{9,8},{10,11... | collective-permute-start | bytes 3145736 | tf_op jit(solution)/shard_map/ppermute | solution.py:725
  485.2 17.2 %collective-permute-start.30 = (bf16[576,512]{1,0:T(8,128)(2,1)S(1)}, bf16[576,512]{1,0:T(8,128)(2,1)S(1)}, u32[]{:S(2)}, u32[]{:S(2)}) collective-permute-start(bf16[576,512]{1,0:T(8,128)(2,1)S(1)} %pad_maximum_fusion.5), channel_id=1, source_target_pairs={{0,2},{1,3},{2,4},{3,5},{4,6},{5,7},{6,0},{7,1},{8,10},{9,11},{10,... | collective-permute-start | bytes 1769480 | tf_op jit(solution)/shard_map/ppermute | solution.py:725
  507.2 5.5 collective-permute-start.40
  507.8 39.2 %collective-permute-start.32 = (bf16[2,704,256]{2,1,0:T(8,128)(2,1)S(1)}, bf16[2,704,256]{2,1,0:T(8,128)(2,1)S(1)}, u32[]{:S(2)}, u32[]{:S(2)}) collective-permute-start(bf16[2,704,256]{2,1,0:T(8,128)(2,1)S(1)} %maximum_maximum_fusion.3), channel_id=1, source_target_pairs={{0,16},{1,17},{2,18},{3,19},{4,20},{5,21},{6,22},{7,23},{8,24},{9,... | collective-permute-start | bytes 2162696 | tf_op jit(solution)/shard_map/ppermute | solution.py:725
  512.7 5.5 collective-permute-start.41
  512.9 34.2 %collective-permute-start.31 = (bf16[2,704,256]{2,1,0:T(8,128)(2,1)S(1)}, bf16[2,704,256]{2,1,0:T(8,128)(2,1)S(1)}, u32[]{:S(2)}, u32[]{:S(2)}) collective-permute-start(bf16[2,704,256]{2,1,0:T(8,128)(2,1)S(1)} %maximum_maximum_fusion.2), channel_id=1, source_target_pairs={{0,8},{1,9},{2,10},{3,11},{4,12},{5,13},{6,14},{7,15},{8,0},{9,1},... | collective-permute-start | bytes 2162696 | tf_op jit(solution)/shard_map/ppermute | solution.py:725
  513.2 33.8 %collective-permute-start.33 = (bf16[576,512]{1,0:T(8,128)(2,1)}, bf16[576,512]{1,0:T(8,128)(2,1)S(1)}, u32[]{:S(2)}, u32[]{:S(2)}) collective-permute-start(bf16[576,512]{1,0:T(8,128)(2,1)} %get-tuple-element.177), channel_id=1, source_target_pairs={{0,4},{1,5},{2,6},{3,7},{4,0},{5,1},{6,2},{7,3},{8,12},{9,13},{10,... | collective-permute-start | bytes 1769480 | tf_op jit(solution)/shard_map/ppermute | solution.py:725
  513.3 28.9 %collective-permute-start.42 = (f32[1,512]{1,0:T(1,128)S(1)}, f32[1,512]{1,0:T(1,128)S(1)}, u32[]{:S(2)}, u32[]{:S(2)}) collective-permute-start(f32[1,512]{1,0:T(1,128)S(1)} %get-tuple-element.291), channel_id=1, source_target_pairs={{0,4},{1,5},{2,6},{3,7},{4,0},{5,1},{6,2},{7,3},{8,12},{9,13},{10,... | collective-permute-start | bytes 6152 | tf_op jit(solution)/shard_map/ppermute | solution.py:725
  518.3 24.0 %collective-permute-start.43 = (f32[1,512]{1,0:T(1,128)S(1)}, f32[1,512]{1,0:T(1,128)S(1)}, u32[]{:S(2)}, u32[]{:S(2)}) collective-permute-start(f32[1,512]{1,0:T(1,128)S(1)} %get-tuple-element.290), channel_id=1, source_target_pairs={{0,6},{1,7},{2,0},{3,1},{4,2},{5,3},{6,4},{7,5},{8,14},{9,15},{10,... | collective-permute-start | bytes 6152 | tf_op jit(solution)/shard_map/ppermute | solution.py:725
  542.3 3.7 collective-permute-start.44
  545.9 3.8 collective-permute-start.45
  547.1 8.1 %collective-permute-start.34 = (bf16[704,256]{1,0:T(8,128)(2,1)S(1)}, bf16[704,256]{1,0:T(8,128)(2,1)S(1)}, u32[]{:S(2)}, u32[]{:S(2)}) collective-permute-start(bf16[704,256]{1,0:T(8,128)(2,1)S(1)} %fusion.4), channel_id=1, source_target_pairs={{0,16},{1,17},{2,18},{3,19},{4,20},{5,21},{6,22},{7,23},{8,24},{9,... | collective-permute-start | bytes 1081352 | tf_op jit(solution)/shard_map/ppermute | solution.py:725
  548.3 7.8 %collective-permute-start.35 = (bf16[704,256]{1,0:T(8,128)(2,1)S(1)}, bf16[704,256]{1,0:T(8,128)(2,1)S(1)}, u32[]{:S(2)}, u32[]{:S(2)}) collective-permute-start(bf16[704,256]{1,0:T(8,128)(2,1)S(1)} %fusion.5), channel_id=1, source_target_pairs={{0,8},{1,9},{2,10},{3,11},{4,12},{5,13},{6,14},{7,15},{8,0},{9,1},... | collective-permute-start | bytes 1081352 | tf_op jit(solution)/shard_map/ppermute | solution.py:725
  550.9 16.3 %collective-permute-start.36 = (bf16[576,512]{1,0:T(8,128)(2,1)}, bf16[576,512]{1,0:T(8,128)(2,1)}, u32[]{:S(2)}, u32[]{:S(2)}) collective-permute-start(bf16[576,512]{1,0:T(8,128)(2,1)} %get-tuple-element.184), channel_id=1, source_target_pairs={{0,6},{1,7},{2,0},{3,1},{4,2},{5,3},{6,4},{7,5},{8,14},{9,15},{10,... | collective-permute-start | bytes 1769480 | tf_op jit(solution)/shard_map/ppermute | solution.py:725
  556.4 8.8 %collective-permute-start.47 = (bf16[128,256]{1,0:T(8,128)(2,1)S(1)}, bf16[128,256]{1,0:T(8,128)(2,1)S(1)}, u32[]{:S(2)}, u32[]{:S(2)}) collective-permute-start(bf16[128,256]{1,0:T(8,128)(2,1)S(1)} %get-tuple-element.252), channel_id=1, source_target_pairs={{1,0},{4,1},{7,2},{2,3},{5,4},{0,5},{3,6},{6,7},{9,8},{12,9},{15,1... | collective-permute-start | bytes 196616 | tf_op jit(solution)/shard_map/ppermute | solution.py:702
  556.4 9.8 %collective-permute-start.48 = (bf16[128,256]{1,0:T(8,128)(2,1)S(1)}, bf16[128,256]{1,0:T(8,128)(2,1)S(1)}, u32[]{:S(2)}, u32[]{:S(2)}) collective-permute-start(bf16[128,256]{1,0:T(8,128)(2,1)S(1)} %get-tuple-element.253), channel_id=1, source_target_pairs={{2,0},{5,1},{0,2},{3,3},{6,4},{1,5},{4,6},{7,7},{10,8},{13,9},{8,1... | collective-permute-start | bytes 196616 | tf_op jit(solution)/shard_map/ppermute | solution.py:702
  558.8 7.5 %collective-permute-start.46 = (bf16[128,256]{1,0:T(8,128)(2,1)S(1)}, bf16[128,256]{1,0:T(8,128)(2,1)S(1)}, u32[]{:S(2)}, u32[]{:S(2)}) collective-permute-start(bf16[128,256]{1,0:T(8,128)(2,1)S(1)} %get-tuple-element.224), channel_id=1, source_target_pairs={{0,0},{3,1},{6,2},{1,3},{4,4},{7,5},{2,6},{5,7},{8,8},{11,9},{14,1... | collective-permute-start | bytes 196616 | tf_op jit(solution)/shard_map/ppermute | solution.py:702
  568.9 8.4 %collective-permute-start.37 = (bf16[128,512]{1,0:T(8,128)(2,1)S(1)}, bf16[128,512]{1,0:T(8,128)(2,1)S(1)}, u32[]{:S(2)}, u32[]{:S(2)}) collective-permute-start(bf16[128,512]{1,0:T(8,128)(2,1)S(1)} %get-tuple-element.256), channel_id=1, source_target_pairs={{0,2},{1,3},{2,4},{3,5},{4,6},{5,7},{6,0},{7,1},{8,10},{9,11},{10,... | collective-permute-start | bytes 393224 | tf_op jit(solution)/shard_map/ppermute | solution.py:725
  571.0 10.6 %collective-permute-start.38 = (bf16[128,512]{1,0:T(8,128)(2,1)S(1)}, bf16[128,512]{1,0:T(8,128)(2,1)S(1)}, u32[]{:S(2)}, u32[]{:S(2)}) collective-permute-start(bf16[128,512]{1,0:T(8,128)(2,1)S(1)} %get-tuple-element.258), channel_id=1, source_target_pairs={{0,4},{1,5},{2,6},{3,7},{4,0},{5,1},{6,2},{7,3},{8,12},{9,13},{10,... | collective-permute-start | bytes 393224 | tf_op jit(solution)/shard_map/ppermute | solution.py:725
  573.3 8.3 %collective-permute-start.39 = (bf16[128,512]{1,0:T(8,128)(2,1)S(1)}, bf16[128,512]{1,0:T(8,128)(2,1)S(1)}, u32[]{:S(2)}, u32[]{:S(2)}) collective-permute-start(bf16[128,512]{1,0:T(8,128)(2,1)S(1)} %get-tuple-element.257), channel_id=1, source_target_pairs={{0,6},{1,7},{2,0},{3,1},{4,2},{5,3},{6,4},{7,5},{8,14},{9,15},{10,... | collective-permute-start | bytes 393224 | tf_op jit(solution)/shard_map/ppermute | solution.py:725
  (43 other events, 276.9 us)
Sparse Core Ops, SparseCore 0:
  11.1 84.1 all-gather.7
  103.5 83.2 all-gather.9
  254.0 74.3 all-gather.11

commit v5 on v4

--- a/solution.py
+++ b/solution.py
@@ -797,7 +797,7 @@
         for copy in copies(name):
             copy.start()
     tiles = [
-        2 * lax.rem(chip_at + ahead, chips) + (1 - core_at if other else core_at)
+        2 * ahead + (1 - core_at if other else core_at)
         for other in range(2)
         for ahead in range(chips)
     ]
@@ -833,7 +833,7 @@
     def hidden_block(other, up_grads):
         def run(ahead, carry):
             core = 1 - core_at if other else core_at
-            block = 2 * lax.rem(chip_at + ahead, chips) + core
+            block = 2 * ahead + core
             rows = pl.ds(pl.multiple_of(block * up_cols, up_cols), up_cols)
             up_weight, down_weight = up_w[block], down_w[rows, :]
             value, derivative = gelu_parts(dot_nn(normed_ref[...], up_weight))
@@ -854,7 +854,7 @@
                     target[owner, place, at, :] = part[tile * cols : (tile + 1) * cols]
             return carry
 
-        lax.fori_loop(0, chips, run, 0)
+        lax.fori_loop(0, chips, run, 0, unroll=2)
 
     hidden_block(1, up_other)
     send_up_other = pltpu.make_async_copy(up_other, up_other_out, send_sem.at[0])
@@ -1017,33 +1017,71 @@
     )(main, side, skip_tiles, scale, shift)
 
 
+def head_product(head, head_ref, pair_ref, dp, seq):
+    parts = [head_ref[s, piece * HD : (piece + 1) * HD] for s in range(seq) for piece in range(3)]
+    projected = jnp.concatenate(parts, axis=0).T
+    for row in range(dp):
+        weight = jnp.concatenate(
+            [
+                pair_ref[row * seq + s, piece * PAIR + head * HD : piece * PAIR + (head + 1) * HD]
+                for s in range(seq)
+                for piece in range(3)
+            ],
+            axis=0,
+        )
+        yield row, dot_nn(projected, weight)
+
+
+def first_head_kernel(head_ref, pair_ref, out_ref, *, dp, seq):
+    rows = pair_ref.shape[2]
+    for row, product in head_product(0, head_ref, pair_ref, dp, seq):
+        out_ref[:, row * rows : (row + 1) * rows] = product
+
+
+def first_head(head_a, pair_tiles, dp, seq):
+    frames, width = head_a.shape[2], pair_tiles.shape[2] * dp
+    whole = pl.BlockSpec(memory_space=pltpu.VMEM)
+    return pl.pallas_call(
+        partial(first_head_kernel, dp=dp, seq=seq),
+        in_specs=[whole] * 2,
+        out_specs=whole,
+        out_shape=jax.ShapeDtypeStruct((frames, width), jnp.float32),
+        compiler_params=pltpu.CompilerParams(vmem_limit_bytes=32 << 20),
+        cost_estimate=pl.CostEstimate(
+            flops=3 * frames * width * width, bytes_accessed=7 * frames * width + 6 * width * width, transcendentals=0
+        ),
+        name="first_head",
+    )(head_a, pair_tiles)
+
+
 def exit_kernel(
-    head_a_ref, head_b_ref, pair_ref, stream_ref, grad_mid_ref, scale_ref, grad_ref, turned_ref, sums_ref, normed_ref,
+    partial_ref, head_ref, pair_ref, stream_ref, grad_mid_ref, scale_ref, grad_ref, turned_ref, sums_ref, normed_ref,
     *, dp, seq,
 ):
     rows = pair_ref.shape[2]
-    parts = [
-        head_ref[s, piece * HD : (piece + 1) * HD]
-        for s in range(seq)
-        for piece in range(3)
-        for head_ref in (head_a_ref, head_b_ref)
-    ]
-    projected = jnp.concatenate(parts, axis=0).T
-    for row in range(dp):
-        weight = pair_ref[row * seq : (row + 1) * seq].reshape(projected.shape[1], rows)
-        normed_ref[:, row * rows : (row + 1) * rows] = dot_nn(projected, weight)
-    grad, stream = normed_ref[...], stream_ref[...]
-    inverse = lax.rsqrt(jnp.mean(stream * stream, axis=-1, keepdims=True) + epsilon)
-    unit = stream * inverse
-    lifted = grad * (1.0 + scale_ref[...])
-    sums_ref[0:1, :] = jnp.sum(grad * unit, axis=0, keepdims=True)
-    sums_ref[1:2, :] = jnp.sum(grad, axis=0, keepdims=True)
-    grad_stream = grad_mid_ref[...] + inverse * (lifted - unit * jnp.mean(lifted * unit, axis=-1, keepdims=True))
-    grad_ref[...] = grad_stream.astype(jnp.bfloat16)
-    turned_ref[...] = grad_stream.T.astype(jnp.bfloat16)
-
-
-def exit_block(head_a, head_b, pair_tiles, stream, grad_mid, scale, dp, seq):
+    for row, product in head_product(1, head_ref, pair_ref, dp, seq):
+        columns = slice(row * rows, (row + 1) * rows)
+        normed_ref[:, columns] = product + partial_ref[:, columns]
+    sums_ref[...] = jnp.zeros_like(sums_ref)
+    chunk = 128
+
+    @pl.loop(0, stream_ref.shape[0] // chunk)
+    def _(index):
+        at = pl.ds(pl.multiple_of(index * chunk, chunk), chunk)
+        grad, stream = normed_ref[at, :], stream_ref[at, :]
+        inverse = lax.rsqrt(jnp.mean(stream * stream, axis=-1, keepdims=True) + epsilon)
+        unit = stream * inverse
+        lifted = grad * (1.0 + scale_ref[...])
+        sums_ref[0:1, :] += jnp.sum(grad * unit, axis=0, keepdims=True)
+        sums_ref[1:2, :] += jnp.sum(grad, axis=0, keepdims=True)
+        grad_stream = grad_mid_ref[at, :] + inverse * (
+            lifted - unit * jnp.mean(lifted * unit, axis=-1, keepdims=True)
+        )
+        grad_ref[at, :] = grad_stream.astype(jnp.bfloat16)
+        turned_ref[:, at] = grad_stream.T.astype(jnp.bfloat16)
+
+
+def exit_block(first, head_b, pair_tiles, stream, grad_mid, scale, dp, seq):
     frames, width = stream.shape
     whole = pl.BlockSpec(memory_space=pltpu.VMEM)
     return pl.pallas_call(
@@ -1058,10 +1096,10 @@
         scratch_shapes=[pltpu.VMEM((frames, width), jnp.float32)],
         compiler_params=pltpu.CompilerParams(vmem_limit_bytes=40 << 20),
         cost_estimate=pl.CostEstimate(
-            flops=6 * frames * width * width, bytes_accessed=18 * frames * width + 6 * width * width, transcendentals=0
+            flops=3 * frames * width * width, bytes_accessed=18 * frames * width + 6 * width * width, transcendentals=0
         ),
         name="exit_block",
-    )(head_a, head_b, pair_tiles, stream, grad_mid, scale)
+    )(first, head_b, pair_tiles, stream, grad_mid, scale)
 
 
 def joined_kernel(grad_ref, weight_ref, main_ref, side_ref, *, dp, seq):
@@ -1101,15 +1139,14 @@
     )(grad_stream, skip_tiles)
 
 
-def near_first(place_ref, chips, other, block):
+def along_chips(place_ref, chips, other, block):
     core = 1 - place_ref[2] if other else place_ref[2]
-    starts = [(2 * lax.rem(place_ref[1] + ahead, chips) + core) * block for ahead in range(chips)]
-    return [pl.multiple_of(start, block) for start in starts]
+    return [pl.multiple_of((2 * chip + core) * block, block) for chip in range(chips)]
 
 
 def turned_parts(place_ref, left_ref, right_ref, chips, seq, other):
     block = left_ref.shape[0] // seq
-    starts = near_first(place_ref, chips, other, block)
+    starts = along_chips(place_ref, chips, other, block)
     left = jnp.concatenate([left_ref[pl.ds(start, block), :] for start in starts], axis=0)
     product = dot_nn(left, right_ref[...])
     return [product[ahead * block : (ahead + 1) * block] for ahead in range(chips)]
@@ -1117,7 +1154,7 @@
 
 def plain_parts(place_ref, left_ref, right_ref, chips, seq, other):
     block = right_ref.shape[1] // seq
-    starts = near_first(place_ref, chips, other, block)
+    starts = along_chips(place_ref, chips, other, block)
     product = dot_nn(left_ref[...], lanes([right_ref[:, pl.ds(start, block)] for start in starts]))
     return [product[:, ahead * block : (ahead + 1) * block] for ahead in range(chips)]
 
@@ -1238,6 +1275,11 @@
     return full
 
 
+def chips_exchange(value, seq):
+    groups = [[core + 2 * chip for chip in range(seq // 2)] for core in range(2)]
+    return lax.all_to_all(value, "seq", 0, 0, axis_index_groups=groups)
+
+
 def local_paired(
     inputs, skip_input, time_embed, segment_ids, span_start, span_length, cotangent,
     skip_weight, ada_weight, qkv_weight, out_weight, up_weight, down_weight,
@@ -1342,19 +1384,29 @@
     def stays(own, other, got, at):
         return wide(own[at]) + wide(other[at]) + wide(got[at])
 
+    back_a, back_b, down_got[1], up_got[1] = lax.optimization_barrier((back_a, back_b, down_got[1], up_got[1]))
+    down_got, up_got = jnp.concatenate(down_got, axis=2), jnp.concatenate(up_got, axis=2)
+    down_low, up_low = low(stays(down_own, down_other, down_got, 1)), low(stays(up_own, up_other, up_got, 1))
+    down_low, up_low, back_a, back_b = lax.optimization_barrier((down_low, up_low, back_a, back_b))
+    down_back, up_back = send(down_low, routes["y"]), send(up_low, routes["x"])
     parts = [part[:, at : at + HD] for at in range(0, 3 * HD, HD) for part in (back_a, back_b)]
     grad_projected = jnp.concatenate(parts, axis=1)
-    grad_projected, down_got[1], up_got[1] = lax.optimization_barrier((grad_projected, down_got[1], up_got[1]))
-    down_got, up_got = jnp.concatenate(down_got, axis=2), jnp.concatenate(up_got, axis=2)
-    down_back = send(low(stays(down_own, down_other, down_got, 1)), routes["y"])
-    up_back = send(low(stays(up_own, up_other, up_got, 1)), routes["x"])
     grad_pair_weight = jnp.einsum(
         "icf,ifd->cd", grad_projected, normed_all, preferred_element_type=jnp.float32
     ).astype(jnp.bfloat16)
+    local_b, grad_pair_weight = lax.optimization_barrier((local_b, grad_pair_weight))
     grad_stream, grad_stream_turned, sums_one = exit_block(
-        local_a, local_b, pair_tiles, stream, grad_middle, scale_one, dp, seq
+        first_head(local_a, pair_tiles, dp, seq), local_b, pair_tiles, stream, grad_middle, scale_one, dp, seq
     )
     joined = jnp.concatenate([inputs[0], skip_input[0]], axis=-1)
+    chips, chip_at, core_at = seq // 2, seq_at // 2, seq_at % 2
+    grad_modulation = jnp.concatenate([sums_one[0], sums_one[1], sums_two[0], sums_two[1]]).reshape(chips, 2, -1)
+    kept = lax.dynamic_index_in_dim(grad_modulation, core_at, 1, keepdims=False)
+    kept = kept + send(lax.dynamic_index_in_dim(grad_modulation, 1 - core_at, 1, keepdims=False), routes["core"])
+    column_sum = lax.dynamic_index_in_dim(kept, chip_at, 0)
+    for ahead, route in enumerate(routes["z"]):
+        piece = lax.dynamic_index_in_dim(kept, (chip_at + ahead + 1) % chips, 0)
+        column_sum = column_sum + send(piece, route)
     half_tile = skip_weight.shape[0] // 2
     at = lax.axis_index("dp")
     half_pair = 3 * PAIR // 2
@@ -1371,14 +1423,9 @@
     arrived = [send(part, routes["core"]) for part in leaving]
     down_total = stays(down_own, down_other, down_got, 0) + wide(down_back)
     up_total = stays(up_own, up_other, up_got, 0) + wide(up_back)
-    mlp_low = [jnp.concatenate([low(down_total[ahead]), low(up_total[ahead])]) for ahead in range(seq // 2)]
-    mlp_own = jnp.concatenate([down_total[0], up_total[0]])
-    mlp_got = [send(mlp_low[1], routes["z"][0])]
-    grad_main, grad_side = joined_grads(grad_stream, skip_tiles, dp, seq)
-    arrived[0], arrived[1], grad_main, mlp_got[0], *mlp_low = lax.optimization_barrier(
-        (*arrived, grad_main, mlp_got[0], *mlp_low)
-    )
-    mlp_got.append(send(mlp_low[2], routes["z"][1]))
+    mlp_low = jnp.concatenate([low(down_total), low(up_total)], axis=1)
+    column_sum, mlp_low = lax.optimization_barrier((column_sum, mlp_low))
+    mlp_got = chips_exchange(mlp_low, seq)
     skip_parts = []
     for part, (first, second) in enumerate(order):
         keep, away = skip_blocks(part, arrived[part])
@@ -1392,50 +1439,37 @@
         away = jnp.concatenate(
             [away.reshape(2, -1, half_tile), jnp.stack([pair_block(near), pair_block(near ^ far)])], axis=1
         )
-        skip_parts.append((keep, send(away, routes[first]), routes[second]))
-    keep_a, keep_b, sums_one = lax.optimization_barrier((skip_parts[0][0], skip_parts[1][0], sums_one))
-    got_a, got_b, mlp_got[1], mlp_low[3] = lax.optimization_barrier(
-        (skip_parts[0][1], skip_parts[1][1], mlp_got[1], mlp_low[3])
-    )
-    mlp_got.append(send(mlp_low[3], routes["z"][2]))
-    skip_parts = [(keep_a, got_a, skip_parts[0][2]), (keep_b, got_b, skip_parts[1][2])]
-    skip_own, skip_low, pair_sums = [], [], []
-    skip_rows = seq // 2 * (width // seq)
+        skip_parts.append([keep, away, first, second])
+    skip_parts[0][1], skip_parts[1][1], grad_stream, column_sum = lax.optimization_barrier(
+        (skip_parts[0][1], skip_parts[1][1], grad_stream, column_sum)
+    )
+    skip_parts = [(keep, send(away, routes[first]), routes[second]) for keep, away, first, second in skip_parts]
+    grad_main, grad_side = joined_grads(grad_stream, skip_tiles, dp, seq)
+    got_a, got_b, grad_main, column_sum = lax.optimization_barrier(
+        (skip_parts[0][1], skip_parts[1][1], grad_main, column_sum)
+    )
+    skip_parts = [(skip_parts[0][0], got_a, skip_parts[0][2]), (skip_parts[1][0], got_b, skip_parts[1][2])]
+    grad_modulation = jnp.concatenate([column_sum, send(column_sum, routes["x"])])
+    grad_modulation = jnp.concatenate([grad_modulation, send(grad_modulation, routes["y"])])
+    skip_low, pair_sums = [], []
+    skip_rows = chips * (width // seq)
     for keep, got, route in skip_parts:
         back = send(low(wide(keep[1]) + wide(got[1])), route)
         total_part = wide(keep[0]) + wide(got[0]) + wide(back)
         pair_sums.append(total_part[skip_rows:])
-        blocks = total_part[:skip_rows].reshape(seq // 2, width // seq, half_tile)
-        skip_own.append(blocks[0])
-        skip_low.append(low(blocks))
-    skip_tile = jnp.concatenate(skip_own, axis=1)
+        skip_low.append(low(total_part[:skip_rows].reshape(chips, width // seq, half_tile)))
     skip_low = jnp.concatenate(skip_low, axis=2)
-    skip_low, *mlp_got = lax.optimization_barrier((skip_low, *mlp_got))
-    for ahead, route in enumerate(routes["z"]):
-        skip_tile = skip_tile + wide(send(skip_low[ahead + 1], route))
-    skip_tile = skip_tile.T
+    skip_low, mlp_got = lax.optimization_barrier((skip_low, mlp_got))
+    skip_tile = jnp.sum(wide(chips_exchange(skip_low, seq)), axis=0).T
     qkv_tile = wide(stored_rows(low(jnp.concatenate(pair_sums)), seq)).T
 
-    mlp_tile = mlp_own
-    for piece in mlp_got:
-        mlp_tile = mlp_tile + wide(piece)
+    mlp_tile = jnp.sum(wide(mlp_got), axis=0)
     columns = width // seq
     fold = down_weight.shape[0] // wide_tile
     down_tile = lanes([mlp_tile[i * columns : (i + 1) * columns] for i in range(fold)]).T
     out_tile = mlp_tile[fold * columns : down_total.shape[1]]
     out_tile = jnp.concatenate([out_tile[:, i * columns : (i + 1) * columns] for i in range(wide_tile // columns)])
     up_tile = mlp_tile[down_total.shape[1] :]
-    grad_modulation = jnp.concatenate([sums_one[0], sums_one[1], sums_two[0], sums_two[1]])
-    chips, chip_at, core_at = seq // 2, seq_at // 2, seq_at % 2
-    grad_modulation = grad_modulation.reshape(chips, 2, -1)
-    kept = lax.dynamic_index_in_dim(grad_modulation, core_at, 1, keepdims=False)
-    kept = kept + send(lax.dynamic_index_in_dim(grad_modulation, 1 - core_at, 1, keepdims=False), routes["core"])
-    column_sum = lax.dynamic_index_in_dim(kept, chip_at, 0)
-    for ahead, route in enumerate(routes["z"]):
-        piece = lax.dynamic_index_in_dim(kept, (chip_at + ahead + 1) % chips, 0)
-        column_sum = column_sum + send(piece, route)
-    column_sum = jnp.concatenate([column_sum, send(column_sum, routes["x"])])
-    grad_modulation = jnp.concatenate([column_sum, send(column_sum, routes["y"])])
     embed_part = jnp.concatenate(
         [lax.dynamic_index_in_dim(embed_part, jnp.bitwise_xor(at, mask), 0) for mask in range(dp)]
     )

time: 597 us -> 589 us (0.987)
  waiting for transfers between devices: 142 us -> 128 us
    ppermute x43 -> x37, waiting for transfers between devices: 89.7 us -> 62.5 us  [send(): return lax.ppermute(value, ('dp', 'seq'), route)]
    all_to_all x0 -> x2, starting transfers between devices: none -> 10.4 us  [chips_exchange(): return lax.all_to_all(value, 'seq', 0, 0, axis_index_groups=groups)]
    ppermute x43 -> x37, starting transfers between devices: 56.7 us -> 47.1 us  [send(): return lax.ppermute(value, ('dp', 'seq'), route)]
    all_to_all x0 -> x2, waiting for transfers between devices: none -> 9.08 us  [chips_exchange(): return lax.all_to_all(value, 'seq', 0, 0, axis_index_groups=groups)]
    another operation x4 -> x2, other arithmetic: 8.37 us -> 1.25 us
    convert_element_type x6 -> x8, other arithmetic: 16.6 us -> 22.3 us  [low(): return value.astype(jnp.bfloat16)]
    unnamed x121 -> x129, local copies, waits for them, and re-layouts: 36.2 us -> 35 us
  transfers between devices with their start and end apart: 56 -> 52, of which waited for: 21 -> 16; matrix products, arithmetic and copies ran while one was open for 16% -> 15% of each run, Pallas kernels for 26% -> 28%
where the time goes in v5:
time: 589 us; the launch traced here: 581 us
  Pallas kernels  167 us (28%)
  waiting for transfers between devices  128 us (22%)
  starting transfers between devices  85 us (14%)
  blocking collectives  68.3 us (12%)
  local copies, waits for them, and re-layouts  54.2 us (9%)
  other arithmetic  52.6 us (9%)
  between operations  20.1 us (3%)
    ppermute x37, waiting for transfers between devices, send(): return lax.ppermute(value, ('dp', 'seq'), route)  62.5 us
    pallas_call x2, Pallas kernels, attend_head_back(): pl.pallas_call(partial(attend_back_kernel, head=head, size=size, length=l...  56.2 us
    pallas_call x1, Pallas kernels, middle_block(): pl.pallas_call(partial(middle_kernel, dp=dp, seq=seq), in_specs=[pl.Block...  48.7 us
    ppermute x37, starting transfers between devices, send(): return lax.ppermute(value, ('dp', 'seq'), route)  47.1 us
    unnamed x129, local copies, waits for them, and re-layouts  35 us
    all_gather x1, waiting for transfers between devices, local_paired(): normed_all = lax.all_gather(normed_one, 'seq', axis=0)  31.8 us
    all_to_all x1, blocking collectives, local_paired(): attended = lax.all_to_all(attended_pair, 'seq', 0, 0).reshape(width, frames)  30.2 us
    convert_element_type x8, other arithmetic, low(): return value.astype(jnp.bfloat16)  22.3 us
  transfers between devices with their start and end apart: 52, of which 16 were waited for; matrix products, arithmetic and copies ran while one was open for 15% of the time, Pallas kernels for 28%

profile of v5, /device:TPU:0, one launch (start us, length us, event | category | flops | bytes accessed | tf_op | source)
XLA Modules:
  0.0 580.8 jit_solution(12374205663487483404)
XLA Ops:
  9.8 3.1 collective-permute-start.3
  12.9 2.6 collective-permute-start.4
  15.6 1.8 collective-permute-start.1
  17.4 1.9 collective-permute-start.2
  20.9 8.2 %all-gather.3 = bf16[4,1,1024]{2,1,0:T(2,128)(2,1)S(1)} all-gather(bf16[1,1,1024]{2,1,0:T(2,128)(2,1)S(1)} %bitcast.158), channel_id=1, replica_groups=mesh['dp'=4,'seq'=8] {'dp'}, dimensions={0}, use_global_device_ids=true | all-gather | bytes 10240 | tf_op jit(solution)/shard_map/all_gather | solution.py:1317
  30.3 3.9 compare_select_fusion.4
  37.5 2.8 multiply_sine_fusion
  42.2 9.0 %all-reduce = f32[4,512]{1,0:T(4,128)S(1)} all-reduce(f32[4,512]{1,0:T(4,128)S(1)} %fusion.26), channel_id=5, replica_groups=mesh['dp'=4,'seq'=8] {'dp'}, use_global_device_ids=true, to_apply=%region_2.3.clone | all-reduce | flops 2048 | bytes 16384
  52.6 20.9 %all_gather.27 = f32[1,4096]{1,0:T(1,128)S(1)} all-gather(f32[1,512]{1,0:T(1,128)S(1)} %constant_dynamic-slice_fusion.13), channel_id=1, replica_groups=mesh['dp'=4,'seq'=8] {'seq'}, dimensions={1}, use_global_device_ids=true | all-gather | bytes 18432 | tf_op jit(solution)/shard_map/all_gather | solution.py:1322
  76.3 2.4 pad_maximum_fusion.5
  78.7 13.1 %collective-permute-done.5 = bf16[1280,128]{1,0:T(8,128)(2,1)S(1)} collective-permute-done((bf16[1280,128]{1,0:T(8,128)(2,1)S(1)}, bf16[1280,128]{1,0:T(8,128)(2,1)S(1)}, u32[]{:S(2)}, u32[]{:S(2)}) %collective-permute-start.5) | collective-permute-done | bytes 327712 | tf_op jit(solution)/shard_map/ppermute | solution.py:725
  93.1 2.2 all-gather.8.cloned.1.call-done
  95.3 2.2 copy-done.17
  97.5 4.6 entry_block.1
  107.0 3.0 collective-permute-start.10
  121.7 2.8 collective-permute-start.13
  124.5 18.4 %collective-permute-done.11 = bf16[384,256]{1,0:T(8,128)(2,1)} collective-permute-done((bf16[384,256]{1,0:T(8,128)(2,1)S(1)}, bf16[384,256]{1,0:T(8,128)(2,1)}, u32[]{:S(2)}, u32[]{:S(2)}) %collective-permute-start.11) | collective-permute-done | bytes 196640 | tf_op jit(solution)/shard_map/ppermute | solution.py:725
  148.9 3.1 pad_maximum_fusion.down_0
  155.0 31.8 %all-gather.10.cloned.1.call-done = bf16[4096,1024]{1,0:T(8,128)(2,1)} async-done(((bf16[512,1024]{1,0:T(8,128)(2,1)}), bf16[4096,1024]{1,0:T(8,128)(2,1)}) %all-gather.10.cloned.1.call-update) | async-done | bytes 8388624 | tf_op jit(solution)/shard_map/all_gather | solution.py:1334
  186.8 10.5 %project_pair.1 = (bf16[8,128,512]{2,1,0:T(8,128)(2,1)}, bf16[128,4096]{1,0:T(8,128)(2,1)}, bf16[128,4096]{1,0:T(8,128)(2,1)}, bf16[4096,128]{1,0:T(8,128)(2,1)}...) custom-call(bf16[8,512,1024]{2,1,0:T(8,128)(2,1)} %bitcast.159, ...), custom_call_target="tpu_custom_call" | custom-call | flops 3221225472 | bytes 13631488 | tf_op jit(solution)/shard_map/project_pair/pallas_call | solution.py:443
  201.8 19.9 %attend_pair.1 = (bf16[8,128,512]{2,1,0:T(8,128)(2,1)S(1)}, f32[8,128,512]{2,1,0:T(8,128)S(1)}, f32[8,2,512]{2,1,0:T(2,128)S(1)}) custom-call(s32[2]{0:T(128)S(1)} %pad_add_fusion.ends_ref, bf16[8,128,512]{2,1,0:T(8,128)(2,1)S(1)} %copy-done.22, bf16[4096,128]{1,0:T(8,128)(2,1)S(1)} %copy-done.23, bf16[128,4096]{1,0:T(8,128)(2,1)S(1)} %copy-done.24, ...), custom_call_target="tpu_custom_call" | custom-call | flops 8589934592 | bytes 7340032 | tf_op jit(solution)/shard_map/attend_pair/pallas_call | solution.py:553
  222.4 30.2 %all_to_all.35 = bf16[8,128,512]{2,1,0:T(8,128)(2,1)} all-to-all(bf16[8,128,512]{2,1,0:T(8,128)(2,1)S(1)} %get-tuple-element.119), channel_id=1, replica_groups=mesh['dp'=4,'seq'=8] {'seq'}, dimensions={0} | all-to-all | bytes 2097152 | tf_op jit(solution)/shard_map/all_to_all | solution.py:1347
  255.8 6.4 %collective-permute-done.18.up_2 = bf16[2,4,256,512]{3,2,1,0:T(8,128)(2,1)} collective-permute-done((bf16[2,4,256,512]{3,2,1,0:T(8,128)(2,1)}, bf16[2,4,256,512]{3,2,1,0:T(8,128)(2,1)}, u32[]{:S(2)}, u32[]{:S(2)}) %collective-permute-start.18) | collective-permute-done | bytes 2097184 | tf_op jit(solution)/shard_map/ppermute | solution.py:725
  262.2 48.7 %middle_block.1 = (bf16[512,1024]{1,0:T(8,128)(2,1)}, f32[512,1024]{1,0:T(8,128)}, bf16[8,64,512]{2,1,0:T(8,128)(2,1)}, bf16[8,64,512]{2,1,0:T(8,128)(2,1)}, f32...) custom-call(s32[3]{0:T(128)} %pad_add_fusion.1.place_ref, ...), custom_call_target="tpu_custom_call" | custom-call | flops 28991029248 | bytes 46137344 | tf_op jit(solution)/shard_map/middle_block/pallas_call | solution.py:933
  311.6 4.1 all-to-all-start.1
  317.3 11.0 %collective-permute-done.21 = bf16[4,4,256,512]{3,2,1,0:T(8,128)(2,1)} collective-permute-done((bf16[4,4,256,512]{3,2,1,0:T(8,128)(2,1)}, bf16[4,4,256,512]{3,2,1,0:T(8,128)(2,1)}, u32[]{:S(2)}, u32[]{:S(2)}) %collective-permute-start.21) | collective-permute-done | bytes 4194336 | tf_op jit(solution)/shard_map/ppermute | solution.py:725
  328.3 4.4 add_convert_fusion.4
  332.7 4.1 add_convert_fusion.1
  336.8 4.3 all-to-all-start.2
  341.2 4.0 collective-permute-start.22
  345.2 1.9 collective-permute-start.24
  347.2 28.1 %attend_head_back.2 = bf16[8,192,512]{2,1,0:T(8,128)(2,1)} custom-call(s32[2]{0:T(128)} %copy-done.21, bf16[8,128,512]{2,1,0:T(8,128)(2,1)} %get-tuple-element.114.qt_ref, bf16[8,64,512]{2,1,0:T(8,128)(2,1)} %all-to-all-done.1.gt_ref, f32[8,128,512]{2,1,0:T(8,128)} %copy-done.26, f32[8,2,512]{2,1,0:T(2,128)} %copy-done.27, ...), custom_call_target="tpu_custom_call" | custom-call | flops 42949672960 | bytes 10485760 | tf_op jit(solution)/shard_map/attend_head_back/pallas_call | solution.py:646
  375.3 5.1 all-to-all-start.3
  380.4 28.2 %attend_head_back.3 = bf16[8,192,512]{2,1,0:T(8,128)(2,1)} custom-call(s32[2]{0:T(128)} %copy-done.21, bf16[8,128,512]{2,1,0:T(8,128)(2,1)} %get-tuple-element.114.qt_ref, bf16[8,64,512]{2,1,0:T(8,128)(2,1)} %all-to-all-done.2.gt_ref, f32[8,128,512]{2,1,0:T(8,128)} %copy-done.26, f32[8,2,512]{2,1,0:T(2,128)} %copy-done.27, ...), custom_call_target="tpu_custom_call" | custom-call | flops 42949672960 | bytes 10485760 | tf_op jit(solution)/shard_map/attend_head_back/pallas_call | solution.py:646
  408.6 2.3 constant_dynamic-update-slice_fusion.5
  410.9 2.5 constant_dynamic-update-slice_fusion.3
  413.4 5.0 all-to-all-done.3.head_ref
  418.3 4.5 all-to-all-start.4
  424.0 2.6 constant_dynamic-update-slice_fusion.2
  426.6 3.9 fusion.2
  430.5 3.1 fusion.3
  433.7 4.8 collective-permute-start.26
  438.8 3.4 first_head.1.partial_ref
  443.6 4.3 bitcast_convert_fusion
  447.9 12.8 %all-to-all-done.4.head_ref = bf16[8,192,512]{2,1,0:T(8,128)(2,1)} async-done(((bf16[8,192,512]{2,1,0:T(8,128)(2,1)}), bf16[8,192,512]{2,1,0:T(8,128)(2,1)}, u32[]{:S(2)}, u32[]{:S(2)}) %all-to-all-start.4) | async-done | bytes 1572896 | tf_op jit(solution)/shard_map/all_to_all | solution.py:1382
  465.5 6.7 %exit_block.1 = (bf16[512,1024]{1,0:T(8,128)(2,1)S(1)}, bf16[1024,512]{1,0:T(8,128)(2,1)S(1)}, f32[2,1024]{1,0:T(2,128)S(1)}) custom-call(f32[512,1024]{1,0:T(8,128)S(1)} %copy-done.3, bf16[8,192,512]{2,1,0:T(8,128)(2,1)} %all-to-all-done.4.head_ref, bf16[32,384,256]{2,1,0:T(8,128)(2,1)} %bitcast.122, f32[512,1024]{1,0:T(8,128)S(1)} %copy-done.5, ...), custom_call_target="tpu_custom_call" | custom-call | flops 1610612736 | bytes 15728640 | tf_op jit(solution)/shard_map/exit_block/pallas_call | solution.py:1087
  473.1 2.0 grad_blocks.5
  476.1 3.1 grad_blocks.4
  480.0 3.2 fusion
  483.2 2.4 fusion.1
  487.5 2.0 collective-permute-start.33
  491.7 4.8 all-to-all-start.5
  499.1 3.7 grad_blocks.6
  503.6 3.7 grad_blocks.7
  509.4 4.7 collective-permute-start.34
  516.3 2.2 copy-done.18
  518.5 4.7 joined_grads.1
  523.2 6.9 %collective-permute-done.34 = bf16[2,704,256]{2,1,0:T(8,128)(2,1)} collective-permute-done((bf16[2,704,256]{2,1,0:T(8,128)(2,1)}, bf16[2,704,256]{2,1,0:T(8,128)(2,1)}, u32[]{:S(2)}, u32[]{:S(2)}) %collective-permute-start.34) | collective-permute-done | bytes 720928 | tf_op jit(solution)/shard_map/ppermute | solution.py:725
  537.4 4.3 collective-permute-done.39
  544.4 3.3 collective-permute-start.42
  549.2 3.6 collective-permute-done.42
  553.8 5.6 all-to-all-start.6
  559.3 2.1 convert_reduce_fusion
  564.0 9.1 %all-to-all-done.6 = bf16[4,128,512]{2,1,0:T(8,128)(2,1)S(1)} async-done(((bf16[4,128,512]{2,1,0:T(8,128)(2,1)}), bf16[4,128,512]{2,1,0:T(8,128)(2,1)S(1)}, u32[]{:S(2)}, u32[]{:S(2)}) %all-to-all-start.6) | async-done | bytes 524320 | tf_op jit(solution)/shard_map/all_to_all | solution.py:1280
  (271 shorter events, 84.7 us)
Async XLA Ops:
  7.2 29.1 %copy-start = (bf16[256,512]{1,0:T(8,128)(2,1)S(1)}, bf16[256,512]{1,0:T(8,128)(2,1)}, u32[]{:S(2)}) copy-start(bf16[256,512]{1,0:T(8,128)(2,1)} %param.23) | copy-start | bytes 786436
  7.2 21.9 %copy-start.46 = (s32[1,3]{1,0:T(1,128)S(1)}, s32[1,3]{1,0:T(1,128)}, u32[]{:S(2)}) copy-start(s32[1,3]{1,0:T(1,128)} %param.19) | copy-start | bytes 40
  7.2 22.5 %copy-start.47 = (s32[1,3]{1,0:T(1,128)S(1)}, s32[1,3]{1,0:T(1,128)}, u32[]{:S(2)}) copy-start(s32[1,3]{1,0:T(1,128)} %param.20) | copy-start | bytes 40
  7.2 23.1 %copy-start.43 = (s32[1,4096]{1,0:T(1,128)S(1)}, s32[1,4096]{1,0:T(1,128)}, u32[]{:S(2)}) copy-start(s32[1,4096]{1,0:T(1,128)} %param.18) | copy-start | bytes 49156
  7.2 88.0 %all-gather.8.cloned.1.call-start = ((), (), s32[]{:S(2)}) async-start(), calls=%async_computation.7 | async-start | bytes 4325376 | tf_op jit(solution)/shard_map/all_gather | solution.py:1328
  8.0 178.8 %all-gather.10.cloned.1.call-start = ((), (), s32[]{:S(2)}) async-start(), calls=%async_computation.8 | async-start | bytes 9437184 | tf_op jit(solution)/shard_map/all_gather | solution.py:1334
  9.8 68.9 %collective-permute-start.3 = (bf16[1280,128]{1,0:T(8,128)(2,1)S(1)}, bf16[1280,128]{1,0:T(8,128)(2,1)S(1)}, u32[]{:S(2)}, u32[]{:S(2)}) collective-permute-start(bf16[1280,128]{1,0:T(8,128)(2,1)S(1)} %constant_dynamic-update-slice_fusion), channel_id=1, source_target_pairs={{0,2},{1,3},{2,4},{3,5},{4,6},{5,7},{6,0},{7,1},{8,10},{9,11},{10,... | collective-permute-start | bytes 983048 | tf_op jit(solution)/shard_map/ppermute | solution.py:725
  12.9 65.8 %collective-permute-start.4 = (bf16[1280,128]{1,0:T(8,128)(2,1)S(1)}, bf16[1280,128]{1,0:T(8,128)(2,1)S(1)}, u32[]{:S(2)}, u32[]{:S(2)}) collective-permute-start(bf16[1280,128]{1,0:T(8,128)(2,1)S(1)} %constant_dynamic-update-slice_fusion), channel_id=1, source_target_pairs={{0,4},{1,5},{2,6},{3,7},{4,0},{5,1},{6,2},{7,3},{8,12},{9,13},{10,... | collective-permute-start | bytes 983048 | tf_op jit(solution)/shard_map/ppermute | solution.py:725
  15.5 58.0 %collective-permute-start = (bf16[256,512]{1,0:T(8,128)(2,1)}, bf16[256,512]{1,0:T(8,128)(2,1)S(1)}, u32[]{:S(2)}, u32[]{:S(2)}) collective-permute-start(bf16[256,512]{1,0:T(8,128)(2,1)} %param.26), channel_id=1, source_target_pairs={{0,2},{1,3},{2,4},{3,5},{4,6},{5,7},{6,0},{7,1},{8,10},{9,11},{10,... | collective-permute-start | bytes 786440 | tf_op jit(solution)/shard_map/ppermute | solution.py:725
  15.6 59.8 %collective-permute-start.1 = (bf16[256,512]{1,0:T(8,128)(2,1)}, bf16[256,512]{1,0:T(8,128)(2,1)S(1)}, u32[]{:S(2)}, u32[]{:S(2)}) collective-permute-start(bf16[256,512]{1,0:T(8,128)(2,1)} %param.26), channel_id=1, source_target_pairs={{0,4},{1,5},{2,6},{3,7},{4,0},{5,1},{6,2},{7,3},{8,12},{9,13},{10,... | collective-permute-start | bytes 786440 | tf_op jit(solution)/shard_map/ppermute | solution.py:725
  17.4 58.0 %collective-permute-start.2 = (bf16[256,512]{1,0:T(8,128)(2,1)}, bf16[256,512]{1,0:T(8,128)(2,1)S(1)}, u32[]{:S(2)}, u32[]{:S(2)}) collective-permute-start(bf16[256,512]{1,0:T(8,128)(2,1)} %param.26), channel_id=1, source_target_pairs={{0,6},{1,7},{2,0},{3,1},{4,2},{5,3},{6,4},{7,5},{8,14},{9,15},{10,... | collective-permute-start | bytes 786440 | tf_op jit(solution)/shard_map/ppermute | solution.py:725
  20.8 20.8 %copy-start.50 = (u32[32]{0:T(128)S(1)}, u32[32]{0:T(128)}, u32[]{:S(2)}) copy-start(u32[32]{0:T(128)} %constant.185) | copy-start | bytes 388
  41.6 155.7 %copy-start.21 = (s32[2]{0:T(128)}, s32[2]{0:T(128)S(1)}, u32[]{:S(2)}) copy-start(s32[2]{0:T(128)S(1)} %pad_add_fusion.ends_ref) | copy-start | bytes 28
  73.5 18.3 %collective-permute-start.5 = (bf16[1280,128]{1,0:T(8,128)(2,1)S(1)}, bf16[1280,128]{1,0:T(8,128)(2,1)S(1)}, u32[]{:S(2)}, u32[]{:S(2)}) collective-permute-start(bf16[1280,128]{1,0:T(8,128)(2,1)S(1)} %constant_dynamic-update-slice_fusion), channel_id=1, source_target_pairs={{0,6},{1,7},{2,0},{3,1},{4,2},{5,3},{6,4},{7,5},{8,14},{9,15},{10,... | collective-permute-start | bytes 983048 | tf_op jit(solution)/shard_map/ppermute | solution.py:725
  75.4 19.8 %copy-start.14 = (f32[1,1024]{1,0:T(1,128)}, f32[1,1024]{1,0:T(1,128)S(1)}, u32[]{:S(2)}) copy-start(f32[1,1024]{1,0:T(1,128)S(1)} %get-tuple-element.273.scale_ref) | copy-start | bytes 12292
  103.4 43.7 %copy-start.35 = (bf16[4,256,512]{2,1,0:T(8,128)(2,1)S(1)}, bf16[4,256,512]{2,1,0:T(8,128)(2,1)}, u32[]{:S(2)}) copy-start(bf16[4,256,512]{2,1,0:T(8,128)(2,1)} %pad_maximum_fusion.5) | copy-start | bytes 3145732
  103.4 237.7 %all-gather.12.cloned.1.call-start = ((), (), s32[]{:S(2)}) async-start(), calls=%async_computation.9 | async-start | bytes 6488064 | tf_op jit(solution)/shard_map/all_gather | solution.py:1352
  104.6 44.0 %collective-permute-start.7 = (bf16[4,1280,128]{2,1,0:T(8,128)(2,1)}, bf16[4,1280,128]{2,1,0:T(8,128)(2,1)}, u32[]{:S(2)}, u32[]{:S(2)}) collective-permute-start(bf16[4,1280,128]{2,1,0:T(8,128)(2,1)} %pad_maximum_fusion.4), channel_id=1, source_target_pairs={{0,16},{1,17},{2,18},{3,19},{4,20},{5,21},{6,22},{7,23},{8,24},{9,... | collective-permute-start | bytes 3932168 | tf_op jit(solution)/shard_map/ppermute | solution.py:725
  107.0 12.2 %collective-permute-start.10 = (bf16[128,256]{1,0:T(8,128)(2,1)}, bf16[128,256]{1,0:T(8,128)(2,1)S(1)}, u32[]{:S(2)}, u32[]{:S(2)}) collective-permute-start(bf16[128,256]{1,0:T(8,128)(2,1)} %get-tuple-element.259), channel_id=1, source_target_pairs={{0,2},{1,5},{2,0},{3,3},{4,6},{5,1},{6,4},{7,7},{8,10},{9,13},{10,... | collective-permute-start | bytes 196616 | tf_op jit(solution)/shard_map/ppermute | solution.py:685
  110.0 9.3 %collective-permute-start.8 = (bf16[128,256]{1,0:T(8,128)(2,1)S(1)}, bf16[128,256]{1,0:T(8,128)(2,1)S(1)}, u32[]{:S(2)}, u32[]{:S(2)}) collective-permute-start(bf16[128,256]{1,0:T(8,128)(2,1)S(1)} %get-tuple-element.261), channel_id=1, source_target_pairs={{0,0},{1,3},{2,6},{3,1},{4,4},{5,7},{6,2},{7,5},{8,8},{9,11},{10,1... | collective-permute-start | bytes 196616 | tf_op jit(solution)/shard_map/ppermute | solution.py:685
  110.6 8.6 %collective-permute-start.9 = (bf16[128,256]{1,0:T(8,128)(2,1)S(1)}, bf16[128,256]{1,0:T(8,128)(2,1)S(1)}, u32[]{:S(2)}, u32[]{:S(2)}) collective-permute-start(bf16[128,256]{1,0:T(8,128)(2,1)S(1)} %get-tuple-element.260), channel_id=1, source_target_pairs={{0,1},{1,4},{2,7},{3,2},{4,5},{5,0},{6,3},{7,6},{8,9},{9,12},{10,1... | collective-permute-start | bytes 196616 | tf_op jit(solution)/shard_map/ppermute | solution.py:685
  112.4 34.7 %collective-permute-start.6 = (bf16[4,256,512]{2,1,0:T(8,128)(2,1)}, bf16[4,256,512]{2,1,0:T(8,128)(2,1)S(1)}, u32[]{:S(2)}, u32[]{:S(2)}) collective-permute-start(bf16[4,256,512]{2,1,0:T(8,128)(2,1)} %pad_maximum_fusion.5), channel_id=1, source_target_pairs={{0,8},{1,9},{2,10},{3,11},{4,12},{5,13},{6,14},{7,15},{8,0},{9,1},... | collective-permute-start | bytes 3145736 | tf_op jit(solution)/shard_map/ppermute | solution.py:725
  121.0 27.5 %copy-start.36 = (bf16[384,256]{1,0:T(8,128)(2,1)}, bf16[384,256]{1,0:T(8,128)(2,1)S(1)}, u32[]{:S(2)}) copy-start(bf16[384,256]{1,0:T(8,128)(2,1)S(1)} %get-tuple-element.131) | copy-start | bytes 589828
  121.0 21.8 %collective-permute-start.11 = (bf16[384,256]{1,0:T(8,128)(2,1)S(1)}, bf16[384,256]{1,0:T(8,128)(2,1)}, u32[]{:S(2)}, u32[]{:S(2)}) collective-permute-start(bf16[384,256]{1,0:T(8,128)(2,1)S(1)} %get-tuple-element.131), channel_id=1, source_target_pairs={{0,8},{1,9},{2,10},{3,11},{4,12},{5,13},{6,14},{7,15},{8,0},{9,1},... | collective-permute-start | bytes 589832 | tf_op jit(solution)/shard_map/ppermute | solution.py:725
  121.3 23.2 %collective-permute-start.12 = (bf16[384,256]{1,0:T(8,128)(2,1)S(1)}, bf16[384,256]{1,0:T(8,128)(2,1)}, u32[]{:S(2)}, u32[]{:S(2)}) collective-permute-start(bf16[384,256]{1,0:T(8,128)(2,1)S(1)} %get-tuple-element.131), channel_id=1, source_target_pairs={{0,16},{1,17},{2,18},{3,19},{4,20},{5,21},{6,22},{7,23},{8,24},{9,... | collective-permute-start | bytes 589832 | tf_op jit(solution)/shard_map/ppermute | solution.py:725
  121.7 24.6 %collective-permute-start.13 = (bf16[384,256]{1,0:T(8,128)(2,1)S(1)}, bf16[384,256]{1,0:T(8,128)(2,1)S(1)}, u32[]{:S(2)}, u32[]{:S(2)}) collective-permute-start(bf16[384,256]{1,0:T(8,128)(2,1)S(1)} %get-tuple-element.131), channel_id=1, source_target_pairs={{0,24},{1,25},{2,26},{3,27},{4,28},{5,29},{6,30},{7,31},{8,16},{9,... | collective-permute-start | bytes 589832 | tf_op jit(solution)/shard_map/ppermute | solution.py:725
  152.0 69.8 %collective-permute-start.15 = (bf16[2,4,1280,128]{3,2,1,0:T(8,128)(2,1)}, bf16[2,4,1280,128]{3,2,1,0:T(8,128)(2,1)}, u32[]{:S(2)}, u32[]{:S(2)}) collective-permute-start(bf16[2,4,1280,128]{3,2,1,0:T(8,128)(2,1)} %pad_maximum_fusion.down_0), channel_id=1, source_target_pairs={{0,8},{1,9},{2,10},{3,11},{4,12},{5,13},{6,14},{7,15},{8,0},{9,1},... | collective-permute-start | bytes 7864328 | tf_op jit(solution)/shard_map/ppermute | solution.py:725
  153.6 68.2 %collective-permute-start.14 = (bf16[2,4,256,512]{3,2,1,0:T(8,128)(2,1)}, bf16[2,4,256,512]{3,2,1,0:T(8,128)(2,1)}, u32[]{:S(2)}, u32[]{:S(2)}) collective-permute-start(bf16[2,4,256,512]{3,2,1,0:T(8,128)(2,1)} %pad_maximum_fusion.2.up_0), channel_id=1, source_target_pairs={{0,16},{1,17},{2,18},{3,19},{4,20},{5,21},{6,22},{7,23},{8,24},{9,... | collective-permute-start | bytes 6291464 | tf_op jit(solution)/shard_map/ppermute | solution.py:725
  221.7 30.8 %copy-start.26 = (f32[8,128,512]{2,1,0:T(8,128)}, f32[8,128,512]{2,1,0:T(8,128)S(1)}, u32[]{:S(2)}) copy-start(f32[8,128,512]{2,1,0:T(8,128)S(1)} %get-tuple-element.142.full_ref) | copy-start | bytes 6291460
  221.8 34.1 %copy-start.27 = (f32[8,2,512]{2,1,0:T(2,128)}, f32[8,2,512]{2,1,0:T(2,128)S(1)}, u32[]{:S(2)}) copy-start(f32[8,2,512]{2,1,0:T(2,128)S(1)} %get-tuple-element.143.total_ref) | copy-start | bytes 98308
  221.8 32.7 %copy-start.34 = (bf16[512,1024]{0,1:T(8,128)(2,1)S(1)}, bf16[512,1024]{0,1:T(8,128)(2,1)}, u32[]{:S(2)}) copy-start(bf16[512,1024]{0,1:T(8,128)(2,1)} %bitcast_select_fusion) | copy-start | bytes 3145732
  221.8 32.1 %collective-permute-start.17 = (bf16[2,4,1280,128]{3,2,1,0:T(8,128)(2,1)}, bf16[2,4,1280,128]{3,2,1,0:T(8,128)(2,1)}, u32[]{:S(2)}, u32[]{:S(2)}) collective-permute-start(bf16[2,4,1280,128]{3,2,1,0:T(8,128)(2,1)} %collective-permute-done.15.down_1), channel_id=1, source_target_pairs={{0,1},{1,0},{2,3},{3,2},{4,5},{5,4},{6,7},{7,6},{8,9},{9,8},{10,11... | collective-permute-start | bytes 7864328 | tf_op jit(solution)/shard_map/ppermute | solution.py:725
  222.1 30.5 %collective-permute-start.16 = (bf16[2,4,256,512]{3,2,1,0:T(8,128)(2,1)}, bf16[2,4,256,512]{3,2,1,0:T(8,128)(2,1)S(1)}, u32[]{:S(2)}, u32[]{:S(2)}) collective-permute-start(bf16[2,4,256,512]{3,2,1,0:T(8,128)(2,1)} %collective-permute-done.14.up_1), channel_id=1, source_target_pairs={{0,1},{1,0},{2,3},{3,2},{4,5},{5,4},{6,7},{7,6},{8,9},{9,8},{10,11... | collective-permute-start | bytes 6291464 | tf_op jit(solution)/shard_map/ppermute | solution.py:725
  253.9 8.3 %collective-permute-start.19 = (bf16[2,4,1280,128]{3,2,1,0:T(8,128)(2,1)}, bf16[2,4,1280,128]{3,2,1,0:T(8,128)(2,1)}, u32[]{:S(2)}, u32[]{:S(2)}) collective-permute-start(bf16[2,4,1280,128]{3,2,1,0:T(8,128)(2,1)} %pad_maximum_fusion.down_0), channel_id=1, source_target_pairs={{0,1},{1,0},{2,3},{3,2},{4,5},{5,4},{6,7},{7,6},{8,9},{9,8},{10,11... | collective-permute-start | bytes 7864328 | tf_op jit(solution)/shard_map/ppermute | solution.py:725
  254.0 8.2 %collective-permute-start.18 = (bf16[2,4,256,512]{3,2,1,0:T(8,128)(2,1)}, bf16[2,4,256,512]{3,2,1,0:T(8,128)(2,1)}, u32[]{:S(2)}, u32[]{:S(2)}) collective-permute-start(bf16[2,4,256,512]{3,2,1,0:T(8,128)(2,1)} %pad_maximum_fusion.2.up_0), channel_id=1, source_target_pairs={{0,1},{1,0},{2,3},{3,2},{4,5},{5,4},{6,7},{7,6},{8,9},{9,8},{10,11... | collective-permute-start | bytes 6291464 | tf_op jit(solution)/shard_map/ppermute | solution.py:725
  311.0 21.7 %collective-permute-start.20 = (bf16[4,4,320,512]{3,2,1,0:T(8,128)(2,1)}, bf16[4,4,320,512]{3,2,1,0:T(8,128)(2,1)}, u32[]{:S(2)}, u32[]{:S(2)}) collective-permute-start(bf16[4,4,320,512]{3,2,1,0:T(8,128)(2,1)} %get-tuple-element.134), channel_id=1, source_target_pairs={{0,1},{1,0},{2,3},{3,2},{4,5},{5,4},{6,7},{7,6},{8,9},{9,8},{10,11... | collective-permute-start | bytes 15728648 | tf_op jit(solution)/shard_map/ppermute | solution.py:725
  311.2 17.1 %collective-permute-start.21 = (bf16[4,4,256,512]{3,2,1,0:T(8,128)(2,1)}, bf16[4,4,256,512]{3,2,1,0:T(8,128)(2,1)}, u32[]{:S(2)}, u32[]{:S(2)}) collective-permute-start(bf16[4,4,256,512]{3,2,1,0:T(8,128)(2,1)} %get-tuple-element.136), channel_id=1, source_target_pairs={{0,1},{1,0},{2,3},{3,2},{4,5},{5,4},{6,7},{7,6},{8,9},{9,8},{10,11... | collective-permute-start | bytes 12582920 | tf_op jit(solution)/shard_map/ppermute | solution.py:725
  311.6 25.2 %all-to-all-start.1 = ((bf16[8,64,512]{2,1,0:T(8,128)(2,1)}), bf16[8,64,512]{2,1,0:T(8,128)(2,1)}, u32[]{:S(2)}, u32[]{:S(2)}) async-start(bf16[8,64,512]{2,1,0:T(8,128)(2,1)} %get-tuple-element.130), calls=%async_computation.1 | async-start | bytes 1048576 | tf_op jit(solution)/shard_map/all_to_all | solution.py:1356
  336.8 38.5 %all-to-all-start.2 = ((bf16[8,64,512]{2,1,0:T(8,128)(2,1)}), bf16[8,64,512]{2,1,0:T(8,128)(2,1)}, u32[]{:S(2)}, u32[]{:S(2)}) async-start(bf16[8,64,512]{2,1,0:T(8,128)(2,1)} %get-tuple-element.146), calls=%async_computation.2 | async-start | bytes 1048576 | tf_op jit(solution)/shard_map/all_to_all | solution.py:1370
  341.2 39.3 %collective-permute-start.22 = (bf16[2,4,160,512]{3,2,1,0:T(8,128)(2,1)}, bf16[2,4,160,512]{3,2,1,0:T(8,128)(2,1)}, u32[]{:S(2)}, u32[]{:S(2)}) collective-permute-start(bf16[2,4,160,512]{3,2,1,0:T(8,128)(2,1)} %get-tuple-element.147), channel_id=1, source_target_pairs={{0,8},{1,9},{2,10},{3,11},{4,12},{5,13},{6,14},{7,15},{8,0},{9,1},... | collective-permute-start | bytes 3932168 | tf_op jit(solution)/shard_map/ppermute | solution.py:725
  345.1 35.3 %collective-permute-start.23 = (bf16[2,4,128,512]{3,2,1,0:T(8,128)(2,1)}, bf16[2,4,128,512]{3,2,1,0:T(8,128)(2,1)}, u32[]{:S(2)}, u32[]{:S(2)}) collective-permute-start(bf16[2,4,128,512]{3,2,1,0:T(8,128)(2,1)} %get-tuple-element.148), channel_id=1, source_target_pairs={{0,16},{1,17},{2,18},{3,19},{4,20},{5,21},{6,22},{7,23},{8,24},{9,... | collective-permute-start | bytes 3145736 | tf_op jit(solution)/shard_map/ppermute | solution.py:725
  345.2 77.7 %collective-permute-start.24 = (bf16[2,4,160,512]{3,2,1,0:T(8,128)(2,1)}, bf16[2,4,160,512]{3,2,1,0:T(8,128)(2,1)}, u32[]{:S(2)}, u32[]{:S(2)}) collective-permute-start(bf16[2,4,160,512]{3,2,1,0:T(8,128)(2,1)} %get-tuple-element.155), channel_id=1, source_target_pairs={{0,8},{1,9},{2,10},{3,11},{4,12},{5,13},{6,14},{7,15},{8,0},{9,1},... | collective-permute-start | bytes 3932168 | tf_op jit(solution)/shard_map/ppermute | solution.py:725
  347.1 75.7 %collective-permute-start.25 = (bf16[2,4,128,512]{3,2,1,0:T(8,128)(2,1)}, bf16[2,4,128,512]{3,2,1,0:T(8,128)(2,1)S(1)}, u32[]{:S(2)}, u32[]{:S(2)}) collective-permute-start(bf16[2,4,128,512]{3,2,1,0:T(8,128)(2,1)} %get-tuple-element.156), channel_id=1, source_target_pairs={{0,16},{1,17},{2,18},{3,19},{4,20},{5,21},{6,22},{7,23},{8,24},{9,... | collective-permute-start | bytes 3145736 | tf_op jit(solution)/shard_map/ppermute | solution.py:725
  375.3 43.0 %all-to-all-start.3 = ((bf16[8,192,512]{2,1,0:T(8,128)(2,1)}), bf16[8,192,512]{2,1,0:T(8,128)(2,1)}, u32[]{:S(2)}, u32[]{:S(2)}) async-start(bf16[8,192,512]{2,1,0:T(8,128)(2,1)} %attend_head_back.2), calls=%async_computation.3 | async-start | bytes 3145728 | tf_op jit(solution)/shard_map/all_to_all | solution.py:1376
  418.3 42.3 %all-to-all-start.4 = ((bf16[8,192,512]{2,1,0:T(8,128)(2,1)}), bf16[8,192,512]{2,1,0:T(8,128)(2,1)}, u32[]{:S(2)}, u32[]{:S(2)}) async-start(bf16[8,192,512]{2,1,0:T(8,128)(2,1)} %attend_head_back.3), calls=%async_computation.4 | async-start | bytes 3145728 | tf_op jit(solution)/shard_map/all_to_all | solution.py:1382
  433.7 45.5 %collective-permute-start.26 = (bf16[4,320,512]{2,1,0:T(8,128)(2,1)}, bf16[4,320,512]{2,1,0:T(8,128)(2,1)}, u32[]{:S(2)}, u32[]{:S(2)}) collective-permute-start(bf16[4,320,512]{2,1,0:T(8,128)(2,1)} %fusion.2), channel_id=1, source_target_pairs={{0,16},{1,17},{2,18},{3,19},{4,20},{5,21},{6,22},{7,23},{8,24},{9,... | collective-permute-start | bytes 3932168 | tf_op jit(solution)/shard_map/ppermute | solution.py:725
  438.5 40.7 %collective-permute-start.27 = (bf16[4,256,512]{2,1,0:T(8,128)(2,1)}, bf16[4,256,512]{2,1,0:T(8,128)(2,1)}, u32[]{:S(2)}, u32[]{:S(2)}) collective-permute-start(bf16[4,256,512]{2,1,0:T(8,128)(2,1)} %fusion.3), channel_id=1, source_target_pairs={{0,8},{1,9},{2,10},{3,11},{4,12},{5,13},{6,14},{7,15},{8,0},{9,1},... | collective-permute-start | bytes 3145736 | tf_op jit(solution)/shard_map/ppermute | solution.py:725
  479.2 19.9 %collective-permute-start.28 = (bf16[4,4,128,256]{3,2,1,0:T(8,128)(2,1)}, bf16[4,4,128,256]{3,2,1,0:T(8,128)(2,1)}, u32[]{:S(2)}, u32[]{:S(2)}) collective-permute-start(bf16[4,4,128,256]{3,2,1,0:T(8,128)(2,1)} %grad_blocks.4), channel_id=1, source_target_pairs={{0,1},{1,0},{2,3},{3,2},{4,5},{5,4},{6,7},{7,6},{8,9},{9,8},{10,11... | collective-permute-start | bytes 3145736 | tf_op jit(solution)/shard_map/ppermute | solution.py:725
  479.3 6.3 %collective-permute-start.30 = (f32[4,512]{1,0:T(4,128)S(1)}, f32[4,512]{1,0:T(4,128)S(1)}, u32[]{:S(2)}, u32[]{:S(2)}) collective-permute-start(f32[4,512]{1,0:T(4,128)S(1)} %bitcast.155), channel_id=1, source_target_pairs={{0,1},{1,0},{2,3},{3,2},{4,5},{5,4},{6,7},{7,6},{8,9},{9,8},{10,11... | collective-permute-start | bytes 24584 | tf_op jit(solution)/shard_map/ppermute | solution.py:725
  479.9 23.7 %collective-permute-start.29 = (bf16[4,4,128,256]{3,2,1,0:T(8,128)(2,1)}, bf16[4,4,128,256]{3,2,1,0:T(8,128)(2,1)}, u32[]{:S(2)}, u32[]{:S(2)}) collective-permute-start(bf16[4,4,128,256]{3,2,1,0:T(8,128)(2,1)} %copy-done.7), channel_id=1, source_target_pairs={{0,1},{1,0},{2,3},{3,2},{4,5},{5,4},{6,7},{7,6},{8,9},{9,8},{10,11... | collective-permute-start | bytes 3145736 | tf_op jit(solution)/shard_map/ppermute | solution.py:725
  485.6 5.5 collective-permute-start.31
  485.7 5.4 collective-permute-start.32
  487.5 4.1 collective-permute-start.33
  491.7 62.1 %all-to-all-start.5 = ((bf16[4,576,512]{2,1,0:T(8,128)(2,1)}), bf16[4,576,512]{2,1,0:T(8,128)(2,1)}, u32[]{:S(2)}, u32[]{:S(2)}) async-start(bf16[4,576,512]{2,1,0:T(8,128)(2,1)} %pad_maximum_fusion.1), calls=%async_computation.5 | async-start | bytes 4718592 | tf_op jit(solution)/shard_map/all_to_all | solution.py:1280
  509.4 20.7 %collective-permute-start.34 = (bf16[2,704,256]{2,1,0:T(8,128)(2,1)}, bf16[2,704,256]{2,1,0:T(8,128)(2,1)}, u32[]{:S(2)}, u32[]{:S(2)}) collective-permute-start(bf16[2,704,256]{2,1,0:T(8,128)(2,1)} %get-tuple-element.180), channel_id=1, source_target_pairs={{0,8},{1,9},{2,10},{3,11},{4,12},{5,13},{6,14},{7,15},{8,0},{9,1},... | collective-permute-start | bytes 2162696 | tf_op jit(solution)/shard_map/ppermute | solution.py:725
  514.1 17.4 %collective-permute-start.35 = (bf16[2,704,256]{2,1,0:T(8,128)(2,1)}, bf16[2,704,256]{2,1,0:T(8,128)(2,1)S(1)}, u32[]{:S(2)}, u32[]{:S(2)}) collective-permute-start(bf16[2,704,256]{2,1,0:T(8,128)(2,1)} %get-tuple-element.181), channel_id=1, source_target_pairs={{0,16},{1,17},{2,18},{3,19},{4,20},{5,21},{6,22},{7,23},{8,24},{9,... | collective-permute-start | bytes 2162696 | tf_op jit(solution)/shard_map/ppermute | solution.py:725
  531.5 3.6 collective-permute-start.38
  532.9 10.0 %collective-permute-start.36 = (bf16[704,256]{1,0:T(8,128)(2,1)S(1)}, bf16[704,256]{1,0:T(8,128)(2,1)S(1)}, u32[]{:S(2)}, u32[]{:S(2)}) collective-permute-start(bf16[704,256]{1,0:T(8,128)(2,1)S(1)} %fusion.6), channel_id=1, source_target_pairs={{0,16},{1,17},{2,18},{3,19},{4,20},{5,21},{6,22},{7,23},{8,24},{9,... | collective-permute-start | bytes 1081352 | tf_op jit(solution)/shard_map/ppermute | solution.py:725
  535.0 6.6 %collective-permute-start.39 = (f32[2,512]{1,0:T(2,128)S(1)}, f32[2,512]{1,0:T(2,128)S(1)}, u32[]{:S(2)}, u32[]{:S(2)}) collective-permute-start(f32[2,512]{1,0:T(2,128)S(1)} %pad_maximum_fusion.10), channel_id=1, source_target_pairs={{0,16},{1,17},{2,18},{3,19},{4,20},{5,21},{6,22},{7,23},{8,24},{9,... | collective-permute-start | bytes 12296 | tf_op jit(solution)/shard_map/ppermute | solution.py:725
  535.7 8.4 %collective-permute-start.37 = (bf16[704,256]{1,0:T(8,128)(2,1)S(1)}, bf16[704,256]{1,0:T(8,128)(2,1)S(1)}, u32[]{:S(2)}, u32[]{:S(2)}) collective-permute-start(bf16[704,256]{1,0:T(8,128)(2,1)S(1)} %fusion.7), channel_id=1, source_target_pairs={{0,8},{1,9},{2,10},{3,11},{4,12},{5,13},{6,14},{7,15},{8,0},{9,1},... | collective-permute-start | bytes 1081352 | tf_op jit(solution)/shard_map/ppermute | solution.py:725
  544.3 4.9 collective-permute-start.41
  544.4 8.4 %collective-permute-start.42 = (bf16[128,256]{1,0:T(8,128)(2,1)S(1)}, bf16[128,256]{1,0:T(8,128)(2,1)S(1)}, u32[]{:S(2)}, u32[]{:S(2)}) collective-permute-start(bf16[128,256]{1,0:T(8,128)(2,1)S(1)} %get-tuple-element.243), channel_id=1, source_target_pairs={{2,0},{5,1},{0,2},{3,3},{6,4},{1,5},{4,6},{7,7},{10,8},{13,9},{8,1... | collective-permute-start | bytes 196616 | tf_op jit(solution)/shard_map/ppermute | solution.py:702
  547.7 5.1 collective-permute-start.40
  553.8 19.4 %all-to-all-start.6 = ((bf16[4,128,512]{2,1,0:T(8,128)(2,1)}), bf16[4,128,512]{2,1,0:T(8,128)(2,1)S(1)}, u32[]{:S(2)}, u32[]{:S(2)}) async-start(bf16[4,128,512]{2,1,0:T(8,128)(2,1)} %pad_maximum_fusion.6), calls=%async_computation.6 | async-start | bytes 1048576 | tf_op jit(solution)/shard_map/all_to_all | solution.py:1280
  (43 other events, 231.2 us)
Sparse Core Ops, SparseCore 0:
  11.1 84.1 all-gather.7
  103.5 83.2 all-gather.9
  254.0 74.1 all-gather.11

commit v6 on v5

--- a/solution.py
+++ b/solution.py
@@ -569,7 +569,7 @@
             jax.ShapeDtypeStruct((chunks, PAIR, size), jnp.float32),
             jax.ShapeDtypeStruct((chunks, 2, size), jnp.float32),
         ],
-        compiler_params=pltpu.CompilerParams(vmem_limit_bytes=32 << 20),
+        compiler_params=pltpu.CompilerParams(vmem_limit_bytes=60 << 20),
         cost_estimate=pl.CostEstimate(
             flops=8 * length * length * HD, bytes_accessed=14 * length * PAIR, transcendentals=length * length
         ),
@@ -920,7 +920,7 @@
         copy.wait()
 
 
-def middle_block(place, attended, stream, grad_low, scale, shift, up_pieces, down_pieces, dp, seq):
+def middle_block(place, attended, stream, grad_low, grad_low_turned, scale, shift, up_pieces, down_pieces, dp, seq):
     frames, width = stream.shape
     tile_cols = up_pieces[0].shape[3]
     hidden = tile_cols * seq
@@ -970,7 +970,7 @@
             transcendentals=frames * hidden,
         ),
         name="middle_block",
-    )(place, attended, stream, grad_low, grad_low.T, scale, shift, *up_pieces, *down_pieces)
+    )(place, attended, stream, grad_low, grad_low_turned, scale, shift, *up_pieces, *down_pieces)
 
 
 def entry_kernel(main_ref, side_ref, weight_ref, scale_ref, shift_ref, stream_ref, normed_ref, *, dp, seq):
@@ -1094,7 +1094,7 @@
             jax.ShapeDtypeStruct((2, width), jnp.float32),
         ],
         scratch_shapes=[pltpu.VMEM((frames, width), jnp.float32)],
-        compiler_params=pltpu.CompilerParams(vmem_limit_bytes=40 << 20),
+        compiler_params=pltpu.CompilerParams(vmem_limit_bytes=60 << 20),
         cost_estimate=pl.CostEstimate(
             flops=3 * frames * width * width, bytes_accessed=18 * frames * width + 6 * width * width, transcendentals=0
         ),
@@ -1327,8 +1327,8 @@
 
     skip_tiles = lax.all_gather(skip_weight, ("dp", "seq"), axis=0)
     pair_tile = own_pair_rows(qkv_weight.T, seq)
-    skip_tiles, up_column, down_column, cos_all, sin_all, ends, grad_low, place = lax.optimization_barrier(
-        (skip_tiles, up_column, down_column, cos_all, sin_all, ends, grad_low, place)
+    skip_tiles, up_column, down_column, cos_all, sin_all, ends, grad_low, grad_low_turned, place = lax.optimization_barrier(
+        (skip_tiles, up_column, down_column, cos_all, sin_all, ends, grad_low, grad_low.T, place)
     )
     stream, normed_one = entry_block(inputs[0], skip_input[0], skip_tiles, scale_one, shift_one, dp, seq)
     normed_all = lax.all_gather(normed_one, "seq", axis=0)
@@ -1351,7 +1351,7 @@
     up_pieces, down_pieces = up_pieces[:3] + (far_up,), down_pieces[:3] + (far_down,)
     pair_tiles = lax.all_gather(pair_tile, ("dp", "seq"), axis=0)
     layer_output, grad_middle, grad_head_a, grad_head_b, sums_two, down_own, down_other, up_own, up_other = middle_block(
-        place, attended, stream, grad_low, scale_two, shift_two, up_pieces, down_pieces, dp, seq
+        place, attended, stream, grad_low, grad_low_turned, scale_two, shift_two, up_pieces, down_pieces, dp, seq
     )
     grad_head_a = lax.all_to_all(grad_head_a, "seq", 0, 0)
     down_other, up_other = send(down_other, routes["core"]), send(up_other, routes["core"])

time: 589 us -> 584 us (level)
  local copies, waits for them, and re-layouts: 54.2 us -> 41.5 us
  Pallas kernels: 167 us -> 174 us
    unnamed x129 -> x103, local copies, waits for them, and re-layouts: 35 us -> 23 us
  transfers between devices with their start and end apart: 52 -> 52, of which waited for: 16 -> 16; matrix products, arithmetic and copies ran while one was open for 15% -> 16% of each run, Pallas kernels for 28% -> 29%
where the time goes in v6:
time: 584 us; the launch traced here: 577 us
  Pallas kernels  174 us (30%)
  waiting for transfers between devices  128 us (22%)
  starting transfers between devices  85.2 us (15%)
  blocking collectives  67.9 us (12%)
  other arithmetic  55.9 us (10%)
  local copies, waits for them, and re-layouts  41.5 us (7%)
  between operations  20.2 us (3%)
    ppermute x37, waiting for transfers between devices, send(): return lax.ppermute(value, ('dp', 'seq'), route)  62.9 us
    pallas_call x2, Pallas kernels, attend_head_back(): pl.pallas_call(partial(attend_back_kernel, head=head, size=size, length=l...  56.2 us
    pallas_call x1, Pallas kernels, middle_block(): pl.pallas_call(partial(middle_kernel, dp=dp, seq=seq), in_specs=[pl.Block...  48.7 us
    ppermute x37, starting transfers between devices, send(): return lax.ppermute(value, ('dp', 'seq'), route)  45.9 us
    all_gather x1, waiting for transfers between devices, local_paired(): normed_all = lax.all_gather(normed_one, 'seq', axis=0)  32.5 us
    all_to_all x1, blocking collectives, local_paired(): attended = lax.all_to_all(attended_pair, 'seq', 0, 0).reshape(width, frames)  31.1 us
    convert_element_type x8, other arithmetic, low(): return value.astype(jnp.bfloat16)  23.1 us
    pallas_call x1, Pallas kernels, attend_pair(): pl.pallas_call(partial(attend_kernel, size=size, length=length), grid_spe...  23.1 us
  transfers between devices with their start and end apart: 52, of which 16 were waited for; matrix products, arithmetic and copies ran while one was open for 16% of the time, Pallas kernels for 29%

profile of v6, /device:TPU:0, one launch (start us, length us, event | category | flops | bytes accessed | tf_op | source)
XLA Modules:
  0.0 577.5 jit_solution(1264706908295404586)
XLA Ops:
  9.8 3.1 collective-permute-start.3
  12.9 2.6 collective-permute-start.4
  15.6 1.8 collective-permute-start.1
  17.4 1.9 collective-permute-start.2
  20.8 8.2 %all-gather.3 = bf16[4,1,1024]{2,1,0:T(2,128)(2,1)S(1)} all-gather(bf16[1,1,1024]{2,1,0:T(2,128)(2,1)S(1)} %bitcast.160), channel_id=1, replica_groups=mesh['dp'=4,'seq'=8] {'dp'}, dimensions={0}, use_global_device_ids=true | all-gather | bytes 10240 | tf_op jit(solution)/shard_map/all_gather | solution.py:1317
  30.3 3.9 compare_select_fusion.4
  38.6 2.8 multiply_sine_fusion
  41.4 1.9 pad_add_fusion.ends_ref
  43.9 9.0 %all-reduce = f32[4,512]{1,0:T(4,128)S(1)} all-reduce(f32[4,512]{1,0:T(4,128)S(1)} %fusion.26), channel_id=5, replica_groups=mesh['dp'=4,'seq'=8] {'dp'}, use_global_device_ids=true, to_apply=%region_2.3.clone | all-reduce | flops 2048 | bytes 16384
  54.2 19.5 %all_gather.27 = f32[1,4096]{1,0:T(1,128)S(1)} all-gather(f32[1,512]{1,0:T(1,128)S(1)} %constant_dynamic-slice_fusion.13), channel_id=1, replica_groups=mesh['dp'=4,'seq'=8] {'seq'}, dimensions={1}, use_global_device_ids=true | all-gather | bytes 18432 | tf_op jit(solution)/shard_map/all_gather | solution.py:1322
  76.5 2.4 pad_maximum_fusion.5
  78.9 13.1 %collective-permute-done.5 = bf16[1280,128]{1,0:T(8,128)(2,1)S(1)} collective-permute-done((bf16[1280,128]{1,0:T(8,128)(2,1)S(1)}, bf16[1280,128]{1,0:T(8,128)(2,1)S(1)}, u32[]{:S(2)}, u32[]{:S(2)}) %collective-permute-start.5) | collective-permute-done | bytes 327712 | tf_op jit(solution)/shard_map/ppermute | solution.py:725
  93.2 2.2 all-gather.8.cloned.1.call-done
  95.4 2.2 copy-done.12
  97.6 4.6 entry_block.1
  106.5 3.0 collective-permute-start.10
  121.4 2.6 collective-permute-start.13
  124.0 18.4 %collective-permute-done.11 = bf16[384,256]{1,0:T(8,128)(2,1)} collective-permute-done((bf16[384,256]{1,0:T(8,128)(2,1)S(1)}, bf16[384,256]{1,0:T(8,128)(2,1)}, u32[]{:S(2)}, u32[]{:S(2)}) %collective-permute-start.11) | collective-permute-done | bytes 196640 | tf_op jit(solution)/shard_map/ppermute | solution.py:725
  148.3 3.1 pad_maximum_fusion.down_0
  154.3 32.5 %all-gather.10.cloned.1.call-done = bf16[4096,1024]{1,0:T(8,128)(2,1)} async-done(((bf16[512,1024]{1,0:T(8,128)(2,1)}), bf16[4096,1024]{1,0:T(8,128)(2,1)}) %all-gather.10.cloned.1.call-update) | async-done | bytes 8388624 | tf_op jit(solution)/shard_map/all_gather | solution.py:1334
  186.8 10.5 %project_pair.1 = (bf16[8,128,512]{2,1,0:T(8,128)(2,1)}, bf16[128,4096]{1,0:T(8,128)(2,1)}, bf16[128,4096]{1,0:T(8,128)(2,1)}, bf16[4096,128]{1,0:T(8,128)(2,1)}...) custom-call(bf16[8,512,1024]{2,1,0:T(8,128)(2,1)} %bitcast.161, ...), custom_call_target="tpu_custom_call" | custom-call | flops 3221225472 | bytes 13631488 | tf_op jit(solution)/shard_map/project_pair/pallas_call | solution.py:443
  197.3 23.1 %attend_pair.1 = (bf16[8,128,512]{2,1,0:T(8,128)(2,1)}, f32[8,128,512]{2,1,0:T(8,128)}, f32[8,2,512]{2,1,0:T(2,128)}) custom-call(s32[2]{0:T(128)} %pad_add_fusion.ends_ref, bf16[8,128,512]{2,1,0:T(8,128)(2,1)} %get-tuple-element.115.qt_ref, bf16[4096,128]{1,0:T(8,128)(2,1)} %get-tuple-element.116.k_ref, bf16[128,4096]{1,0:T(8,128)(2,1)} %get-tuple-element.117.vt_ref, ...), custom_call_target="tpu_custom_call" | custom-call | flops 8589934592 | bytes 7340032 | tf_op jit(solution)/shard_map/attend_pair/pallas_call | solution.py:553
  221.0 31.1 %all_to_all.35 = bf16[8,128,512]{2,1,0:T(8,128)(2,1)} all-to-all(bf16[8,128,512]{2,1,0:T(8,128)(2,1)} %get-tuple-element.120), channel_id=1, replica_groups=mesh['dp'=4,'seq'=8] {'seq'}, dimensions={0} | all-to-all | bytes 2097152 | tf_op jit(solution)/shard_map/all_to_all | solution.py:1347
  254.0 6.4 %collective-permute-done.18.up_2 = bf16[2,4,256,512]{3,2,1,0:T(8,128)(2,1)} collective-permute-done((bf16[2,4,256,512]{3,2,1,0:T(8,128)(2,1)}, bf16[2,4,256,512]{3,2,1,0:T(8,128)(2,1)}, u32[]{:S(2)}, u32[]{:S(2)}) %collective-permute-start.18) | collective-permute-done | bytes 2097184 | tf_op jit(solution)/shard_map/ppermute | solution.py:725
  260.5 48.7 %middle_block.1 = (bf16[512,1024]{1,0:T(8,128)(2,1)}, f32[512,1024]{1,0:T(8,128)}, bf16[8,64,512]{2,1,0:T(8,128)(2,1)}, bf16[8,64,512]{2,1,0:T(8,128)(2,1)}, f32...) custom-call(s32[3]{0:T(128)} %pad_add_fusion.1.place_ref, ...), custom_call_target="tpu_custom_call" | custom-call | flops 28991029248 | bytes 46137344 | tf_op jit(solution)/shard_map/middle_block/pallas_call | solution.py:933
  309.8 4.1 all-to-all-start.1
  315.5 11.0 %collective-permute-done.21 = bf16[4,4,256,512]{3,2,1,0:T(8,128)(2,1)} collective-permute-done((bf16[4,4,256,512]{3,2,1,0:T(8,128)(2,1)}, bf16[4,4,256,512]{3,2,1,0:T(8,128)(2,1)}, u32[]{:S(2)}, u32[]{:S(2)}) %collective-permute-start.21) | collective-permute-done | bytes 4194336 | tf_op jit(solution)/shard_map/ppermute | solution.py:725
  326.5 4.3 add_convert_fusion.4
  330.8 4.0 add_convert_fusion.1
  334.9 4.3 all-to-all-start.2
  339.2 4.1 collective-permute-start.22
  345.4 28.1 %attend_head_back.2 = bf16[8,192,512]{2,1,0:T(8,128)(2,1)} custom-call(s32[2]{0:T(128)} %pad_add_fusion.ends_ref, bf16[8,128,512]{2,1,0:T(8,128)(2,1)} %get-tuple-element.115.qt_ref, bf16[8,64,512]{2,1,0:T(8,128)(2,1)} %all-to-all-done.1.gt_ref, f32[8,128,512]{2,1,0:T(8,128)} %get-tuple-element.144.full_ref, f32[8,2,512]{2,1,0:T(2,128)} %get-tuple-element.145.total_ref, ...), custom_call_target="tpu_custom_call" | custom-call | flops 42949672960 | bytes 10485760 | tf_op jit(solution)/shard_map/attend_head_back/pallas_call | solution.py:646
  373.5 5.1 all-to-all-start.3
  378.6 28.1 %attend_head_back.3 = bf16[8,192,512]{2,1,0:T(8,128)(2,1)} custom-call(s32[2]{0:T(128)} %pad_add_fusion.ends_ref, bf16[8,128,512]{2,1,0:T(8,128)(2,1)} %get-tuple-element.115.qt_ref, bf16[8,64,512]{2,1,0:T(8,128)(2,1)} %all-to-all-done.2.gt_ref, f32[8,128,512]{2,1,0:T(8,128)} %get-tuple-element.144.full_ref, f32[8,2,512]{2,1,0:T(2,128)} %get-tuple-element.145.total_ref, ...), custom_call_target="tpu_custom_call" | custom-call | flops 42949672960 | bytes 10485760 | tf_op jit(solution)/shard_map/attend_head_back/pallas_call | solution.py:646
  406.7 2.3 constant_dynamic-update-slice_fusion.5
  408.9 2.5 constant_dynamic-update-slice_fusion.3
  411.4 5.1 all-to-all-done.3.head_ref
  416.5 4.5 all-to-all-start.4
  422.1 2.6 constant_dynamic-update-slice_fusion.2
  424.8 3.9 fusion.2
  428.7 3.1 fusion.3
  431.7 4.1 collective-permute-start.26
  437.0 3.4 first_head.1.partial_ref
  441.7 4.3 bitcast_convert_fusion
  446.0 12.8 %all-to-all-done.4.head_ref = bf16[8,192,512]{2,1,0:T(8,128)(2,1)} async-done(((bf16[8,192,512]{2,1,0:T(8,128)(2,1)}), bf16[8,192,512]{2,1,0:T(8,128)(2,1)}, u32[]{:S(2)}, u32[]{:S(2)}) %all-to-all-start.4) | async-done | bytes 1572896 | tf_op jit(solution)/shard_map/all_to_all | solution.py:1382
  458.8 9.8 %exit_block.1 = (bf16[512,1024]{1,0:T(8,128)(2,1)}, bf16[1024,512]{1,0:T(8,128)(2,1)}, f32[2,1024]{1,0:T(2,128)}) custom-call(f32[512,1024]{1,0:T(8,128)} %copy-done.4, bf16[8,192,512]{2,1,0:T(8,128)(2,1)} %all-to-all-done.4.head_ref, bf16[32,384,256]{2,1,0:T(8,128)(2,1)} %bitcast.125, f32[512,1024]{1,0:T(8,128)} %copy-done.5, ...), custom_call_target="tpu_custom_call" | custom-call | flops 1610612736 | bytes 15728640 | tf_op jit(solution)/shard_map/exit_block/pallas_call | solution.py:1087
  469.9 2.0 grad_blocks.5
  471.9 3.0 grad_blocks.4
  475.8 3.2 fusion
  479.0 2.4 fusion.1
  483.3 2.0 collective-permute-start.33
  487.5 4.8 all-to-all-start.5
  495.0 3.7 grad_blocks.6
  499.5 3.7 grad_blocks.7
  504.6 4.9 collective-permute-start.34
  511.7 2.2 copy-done.13
  513.9 4.7 joined_grads.1
  518.6 6.8 %collective-permute-done.34 = bf16[2,704,256]{2,1,0:T(8,128)(2,1)} collective-permute-done((bf16[2,704,256]{2,1,0:T(8,128)(2,1)}, bf16[2,704,256]{2,1,0:T(8,128)(2,1)}, u32[]{:S(2)}, u32[]{:S(2)}) %collective-permute-start.34) | collective-permute-done | bytes 720928 | tf_op jit(solution)/shard_map/ppermute | solution.py:725
  533.3 3.6 collective-permute-done.39
  540.8 3.6 collective-permute-start.42
  545.9 2.5 collective-permute-done.42
  549.3 6.7 %all-to-all-start.6 = ((bf16[4,128,512]{2,1,0:T(8,128)(2,1)}), bf16[4,128,512]{2,1,0:T(8,128)(2,1)S(1)}, u32[]{:S(2)}, u32[]{:S(2)}) async-start(bf16[4,128,512]{2,1,0:T(8,128)(2,1)} %pad_maximum_fusion.6), calls=%async_computation.6 | async-start | bytes 1048576 | tf_op jit(solution)/shard_map/all_to_all | solution.py:1280
  556.0 2.1 convert_reduce_fusion
  560.7 9.1 %all-to-all-done.6 = bf16[4,128,512]{2,1,0:T(8,128)(2,1)S(1)} async-done(((bf16[4,128,512]{2,1,0:T(8,128)(2,1)}), bf16[4,128,512]{2,1,0:T(8,128)(2,1)S(1)}, u32[]{:S(2)}, u32[]{:S(2)}) %all-to-all-start.6) | async-done | bytes 524320 | tf_op jit(solution)/shard_map/all_to_all | solution.py:1280
  (246 shorter events, 76.1 us)
Async XLA Ops:
  7.2 29.1 %copy-start = (bf16[256,512]{1,0:T(8,128)(2,1)S(1)}, bf16[256,512]{1,0:T(8,128)(2,1)}, u32[]{:S(2)}) copy-start(bf16[256,512]{1,0:T(8,128)(2,1)} %param.23) | copy-start | bytes 786436
  7.2 13.6 %copy-start.36 = (bf16[1,1024]{1,0:T(2,128)(2,1)S(1)}, bf16[1,1024]{1,0:T(2,128)(2,1)}, u32[]{:S(2)}) copy-start(bf16[1,1024]{1,0:T(2,128)(2,1)} %param.17) | copy-start | bytes 6148
  7.2 21.9 %copy-start.34 = (s32[1,3]{1,0:T(1,128)S(1)}, s32[1,3]{1,0:T(1,128)}, u32[]{:S(2)}) copy-start(s32[1,3]{1,0:T(1,128)} %param.19) | copy-start | bytes 40
  7.2 22.5 %copy-start.35 = (s32[1,3]{1,0:T(1,128)S(1)}, s32[1,3]{1,0:T(1,128)}, u32[]{:S(2)}) copy-start(s32[1,3]{1,0:T(1,128)} %param.20) | copy-start | bytes 40
  7.2 23.1 %copy-start.30 = (s32[1,4096]{1,0:T(1,128)S(1)}, s32[1,4096]{1,0:T(1,128)}, u32[]{:S(2)}) copy-start(s32[1,4096]{1,0:T(1,128)} %param.18) | copy-start | bytes 49156
  7.2 88.2 %all-gather.8.cloned.1.call-start = ((), (), s32[]{:S(2)}) async-start(), calls=%async_computation.7 | async-start | bytes 4325376 | tf_op jit(solution)/shard_map/all_gather | solution.py:1328
  8.0 178.8 %all-gather.10.cloned.1.call-start = ((), (), s32[]{:S(2)}) async-start(), calls=%async_computation.8 | async-start | bytes 9437184 | tf_op jit(solution)/shard_map/all_gather | solution.py:1334
  9.8 69.1 %collective-permute-start.3 = (bf16[1280,128]{1,0:T(8,128)(2,1)S(1)}, bf16[1280,128]{1,0:T(8,128)(2,1)S(1)}, u32[]{:S(2)}, u32[]{:S(2)}) collective-permute-start(bf16[1280,128]{1,0:T(8,128)(2,1)S(1)} %constant_dynamic-update-slice_fusion), channel_id=1, source_target_pairs={{0,2},{1,3},{2,4},{3,5},{4,6},{5,7},{6,0},{7,1},{8,10},{9,11},{10,... | collective-permute-start | bytes 983048 | tf_op jit(solution)/shard_map/ppermute | solution.py:725
  12.9 66.0 %collective-permute-start.4 = (bf16[1280,128]{1,0:T(8,128)(2,1)S(1)}, bf16[1280,128]{1,0:T(8,128)(2,1)S(1)}, u32[]{:S(2)}, u32[]{:S(2)}) collective-permute-start(bf16[1280,128]{1,0:T(8,128)(2,1)S(1)} %constant_dynamic-update-slice_fusion), channel_id=1, source_target_pairs={{0,4},{1,5},{2,6},{3,7},{4,0},{5,1},{6,2},{7,3},{8,12},{9,13},{10,... | collective-permute-start | bytes 983048 | tf_op jit(solution)/shard_map/ppermute | solution.py:725
  15.5 58.1 %collective-permute-start = (bf16[256,512]{1,0:T(8,128)(2,1)}, bf16[256,512]{1,0:T(8,128)(2,1)S(1)}, u32[]{:S(2)}, u32[]{:S(2)}) collective-permute-start(bf16[256,512]{1,0:T(8,128)(2,1)} %param.26), channel_id=1, source_target_pairs={{0,2},{1,3},{2,4},{3,5},{4,6},{5,7},{6,0},{7,1},{8,10},{9,11},{10,... | collective-permute-start | bytes 786440 | tf_op jit(solution)/shard_map/ppermute | solution.py:725
  15.6 60.0 %collective-permute-start.1 = (bf16[256,512]{1,0:T(8,128)(2,1)}, bf16[256,512]{1,0:T(8,128)(2,1)S(1)}, u32[]{:S(2)}, u32[]{:S(2)}) collective-permute-start(bf16[256,512]{1,0:T(8,128)(2,1)} %param.26), channel_id=1, source_target_pairs={{0,4},{1,5},{2,6},{3,7},{4,0},{5,1},{6,2},{7,3},{8,12},{9,13},{10,... | collective-permute-start | bytes 786440 | tf_op jit(solution)/shard_map/ppermute | solution.py:725
  17.4 58.2 %collective-permute-start.2 = (bf16[256,512]{1,0:T(8,128)(2,1)}, bf16[256,512]{1,0:T(8,128)(2,1)S(1)}, u32[]{:S(2)}, u32[]{:S(2)}) collective-permute-start(bf16[256,512]{1,0:T(8,128)(2,1)} %param.26), channel_id=1, source_target_pairs={{0,6},{1,7},{2,0},{3,1},{4,2},{5,3},{6,4},{7,5},{8,14},{9,15},{10,... | collective-permute-start | bytes 786440 | tf_op jit(solution)/shard_map/ppermute | solution.py:725
  73.6 18.4 %collective-permute-start.5 = (bf16[1280,128]{1,0:T(8,128)(2,1)S(1)}, bf16[1280,128]{1,0:T(8,128)(2,1)S(1)}, u32[]{:S(2)}, u32[]{:S(2)}) collective-permute-start(bf16[1280,128]{1,0:T(8,128)(2,1)S(1)} %constant_dynamic-update-slice_fusion), channel_id=1, source_target_pairs={{0,6},{1,7},{2,0},{3,1},{4,2},{5,3},{6,4},{7,5},{8,14},{9,15},{10,... | collective-permute-start | bytes 983048 | tf_op jit(solution)/shard_map/ppermute | solution.py:725
  75.6 19.8 %copy-start.10 = (f32[1,1024]{1,0:T(1,128)}, f32[1,1024]{1,0:T(1,128)S(1)}, u32[]{:S(2)}) copy-start(f32[1,1024]{1,0:T(1,128)S(1)} %get-tuple-element.275.scale_ref) | copy-start | bytes 12292
  76.5 19.0 %copy-start.6 = (bf16[1,512,1024]{2,1,0:T(8,128)(2,1)S(1)}, bf16[1,512,1024]{2,1,0:T(8,128)(2,1)}, u32[]{:S(2)}) copy-start(bf16[1,512,1024]{2,1,0:T(8,128)(2,1)} %param.15) | copy-start | bytes 3145732
  76.5 19.0 %copy-start.7 = (bf16[1,512,1024]{2,1,0:T(8,128)(2,1)S(1)}, bf16[1,512,1024]{2,1,0:T(8,128)(2,1)}, u32[]{:S(2)}) copy-start(bf16[1,512,1024]{2,1,0:T(8,128)(2,1)} %param.16) | copy-start | bytes 3145732
  103.6 42.8 %copy-start.22 = (bf16[4,256,512]{2,1,0:T(8,128)(2,1)S(1)}, bf16[4,256,512]{2,1,0:T(8,128)(2,1)}, u32[]{:S(2)}) copy-start(bf16[4,256,512]{2,1,0:T(8,128)(2,1)} %pad_maximum_fusion.5) | copy-start | bytes 3145732
  103.6 235.6 %all-gather.12.cloned.1.call-start = ((), (), s32[]{:S(2)}) async-start(), calls=%async_computation.9 | async-start | bytes 6488064 | tf_op jit(solution)/shard_map/all_gather | solution.py:1352
  104.8 43.1 %collective-permute-start.7 = (bf16[4,1280,128]{2,1,0:T(8,128)(2,1)}, bf16[4,1280,128]{2,1,0:T(8,128)(2,1)}, u32[]{:S(2)}, u32[]{:S(2)}) collective-permute-start(bf16[4,1280,128]{2,1,0:T(8,128)(2,1)} %pad_maximum_fusion.4), channel_id=1, source_target_pairs={{0,16},{1,17},{2,18},{3,19},{4,20},{5,21},{6,22},{7,23},{8,24},{9,... | collective-permute-start | bytes 3932168 | tf_op jit(solution)/shard_map/ppermute | solution.py:725
  106.5 12.2 %collective-permute-start.10 = (bf16[128,256]{1,0:T(8,128)(2,1)S(1)}, bf16[128,256]{1,0:T(8,128)(2,1)S(1)}, u32[]{:S(2)}, u32[]{:S(2)}) collective-permute-start(bf16[128,256]{1,0:T(8,128)(2,1)S(1)} %get-tuple-element.261), channel_id=1, source_target_pairs={{0,2},{1,5},{2,0},{3,3},{4,6},{5,1},{6,4},{7,7},{8,10},{9,13},{10,... | collective-permute-start | bytes 196616 | tf_op jit(solution)/shard_map/ppermute | solution.py:685
  109.5 9.2 %collective-permute-start.8 = (bf16[128,256]{1,0:T(8,128)(2,1)S(1)}, bf16[128,256]{1,0:T(8,128)(2,1)S(1)}, u32[]{:S(2)}, u32[]{:S(2)}) collective-permute-start(bf16[128,256]{1,0:T(8,128)(2,1)S(1)} %get-tuple-element.263), channel_id=1, source_target_pairs={{0,0},{1,3},{2,6},{3,1},{4,4},{5,7},{6,2},{7,5},{8,8},{9,11},{10,1... | collective-permute-start | bytes 196616 | tf_op jit(solution)/shard_map/ppermute | solution.py:685
  110.1 8.6 %collective-permute-start.9 = (bf16[128,256]{1,0:T(8,128)(2,1)S(1)}, bf16[128,256]{1,0:T(8,128)(2,1)S(1)}, u32[]{:S(2)}, u32[]{:S(2)}) collective-permute-start(bf16[128,256]{1,0:T(8,128)(2,1)S(1)} %get-tuple-element.262), channel_id=1, source_target_pairs={{0,1},{1,4},{2,7},{3,2},{4,5},{5,0},{6,3},{7,6},{8,9},{9,12},{10,1... | collective-permute-start | bytes 196616 | tf_op jit(solution)/shard_map/ppermute | solution.py:685
  111.9 34.5 %collective-permute-start.6 = (bf16[4,256,512]{2,1,0:T(8,128)(2,1)}, bf16[4,256,512]{2,1,0:T(8,128)(2,1)S(1)}, u32[]{:S(2)}, u32[]{:S(2)}) collective-permute-start(bf16[4,256,512]{2,1,0:T(8,128)(2,1)} %pad_maximum_fusion.5), channel_id=1, source_target_pairs={{0,8},{1,9},{2,10},{3,11},{4,12},{5,13},{6,14},{7,15},{8,0},{9,1},... | collective-permute-start | bytes 3145736 | tf_op jit(solution)/shard_map/ppermute | solution.py:725
  120.5 27.4 %copy-start.23 = (bf16[384,256]{1,0:T(8,128)(2,1)}, bf16[384,256]{1,0:T(8,128)(2,1)S(1)}, u32[]{:S(2)}) copy-start(bf16[384,256]{1,0:T(8,128)(2,1)S(1)} %get-tuple-element.133) | copy-start | bytes 589828
  120.5 21.9 %collective-permute-start.11 = (bf16[384,256]{1,0:T(8,128)(2,1)S(1)}, bf16[384,256]{1,0:T(8,128)(2,1)}, u32[]{:S(2)}, u32[]{:S(2)}) collective-permute-start(bf16[384,256]{1,0:T(8,128)(2,1)S(1)} %get-tuple-element.133), channel_id=1, source_target_pairs={{0,8},{1,9},{2,10},{3,11},{4,12},{5,13},{6,14},{7,15},{8,0},{9,1},... | collective-permute-start | bytes 589832 | tf_op jit(solution)/shard_map/ppermute | solution.py:725
  120.9 23.1 %collective-permute-start.12 = (bf16[384,256]{1,0:T(8,128)(2,1)S(1)}, bf16[384,256]{1,0:T(8,128)(2,1)}, u32[]{:S(2)}, u32[]{:S(2)}) collective-permute-start(bf16[384,256]{1,0:T(8,128)(2,1)S(1)} %get-tuple-element.133), channel_id=1, source_target_pairs={{0,16},{1,17},{2,18},{3,19},{4,20},{5,21},{6,22},{7,23},{8,24},{9,... | collective-permute-start | bytes 589832 | tf_op jit(solution)/shard_map/ppermute | solution.py:725
  121.4 24.3 %collective-permute-start.13 = (bf16[384,256]{1,0:T(8,128)(2,1)S(1)}, bf16[384,256]{1,0:T(8,128)(2,1)S(1)}, u32[]{:S(2)}, u32[]{:S(2)}) collective-permute-start(bf16[384,256]{1,0:T(8,128)(2,1)S(1)} %get-tuple-element.133), channel_id=1, source_target_pairs={{0,24},{1,25},{2,26},{3,27},{4,28},{5,29},{6,30},{7,31},{8,16},{9,... | collective-permute-start | bytes 589832 | tf_op jit(solution)/shard_map/ppermute | solution.py:725
  151.4 69.0 %collective-permute-start.15 = (bf16[2,4,1280,128]{3,2,1,0:T(8,128)(2,1)}, bf16[2,4,1280,128]{3,2,1,0:T(8,128)(2,1)}, u32[]{:S(2)}, u32[]{:S(2)}) collective-permute-start(bf16[2,4,1280,128]{3,2,1,0:T(8,128)(2,1)} %pad_maximum_fusion.down_0), channel_id=1, source_target_pairs={{0,8},{1,9},{2,10},{3,11},{4,12},{5,13},{6,14},{7,15},{8,0},{9,1},... | collective-permute-start | bytes 7864328 | tf_op jit(solution)/shard_map/ppermute | solution.py:725
  152.9 67.5 %collective-permute-start.14 = (bf16[2,4,256,512]{3,2,1,0:T(8,128)(2,1)}, bf16[2,4,256,512]{3,2,1,0:T(8,128)(2,1)}, u32[]{:S(2)}, u32[]{:S(2)}) collective-permute-start(bf16[2,4,256,512]{3,2,1,0:T(8,128)(2,1)} %pad_maximum_fusion.2.up_0), channel_id=1, source_target_pairs={{0,16},{1,17},{2,18},{3,19},{4,20},{5,21},{6,22},{7,23},{8,24},{9,... | collective-permute-start | bytes 6291464 | tf_op jit(solution)/shard_map/ppermute | solution.py:725
  220.4 32.4 %copy-start.21 = (bf16[512,1024]{0,1:T(8,128)(2,1)S(1)}, bf16[512,1024]{0,1:T(8,128)(2,1)}, u32[]{:S(2)}) copy-start(bf16[512,1024]{0,1:T(8,128)(2,1)} %bitcast_select_fusion) | copy-start | bytes 3145732
  220.4 31.7 %collective-permute-start.17 = (bf16[2,4,1280,128]{3,2,1,0:T(8,128)(2,1)}, bf16[2,4,1280,128]{3,2,1,0:T(8,128)(2,1)}, u32[]{:S(2)}, u32[]{:S(2)}) collective-permute-start(bf16[2,4,1280,128]{3,2,1,0:T(8,128)(2,1)} %collective-permute-done.15.down_1), channel_id=1, source_target_pairs={{0,1},{1,0},{2,3},{3,2},{4,5},{5,4},{6,7},{7,6},{8,9},{9,8},{10,11... | collective-permute-start | bytes 7864328 | tf_op jit(solution)/shard_map/ppermute | solution.py:725
  220.7 31.4 %collective-permute-start.16 = (bf16[2,4,256,512]{3,2,1,0:T(8,128)(2,1)}, bf16[2,4,256,512]{3,2,1,0:T(8,128)(2,1)}, u32[]{:S(2)}, u32[]{:S(2)}) collective-permute-start(bf16[2,4,256,512]{3,2,1,0:T(8,128)(2,1)} %collective-permute-done.14.up_1), channel_id=1, source_target_pairs={{0,1},{1,0},{2,3},{3,2},{4,5},{5,4},{6,7},{7,6},{8,9},{9,8},{10,11... | collective-permute-start | bytes 6291464 | tf_op jit(solution)/shard_map/ppermute | solution.py:725
  252.1 8.3 %collective-permute-start.19 = (bf16[2,4,1280,128]{3,2,1,0:T(8,128)(2,1)}, bf16[2,4,1280,128]{3,2,1,0:T(8,128)(2,1)}, u32[]{:S(2)}, u32[]{:S(2)}) collective-permute-start(bf16[2,4,1280,128]{3,2,1,0:T(8,128)(2,1)} %pad_maximum_fusion.down_0), channel_id=1, source_target_pairs={{0,1},{1,0},{2,3},{3,2},{4,5},{5,4},{6,7},{7,6},{8,9},{9,8},{10,11... | collective-permute-start | bytes 7864328 | tf_op jit(solution)/shard_map/ppermute | solution.py:725
  252.2 8.2 %collective-permute-start.18 = (bf16[2,4,256,512]{3,2,1,0:T(8,128)(2,1)}, bf16[2,4,256,512]{3,2,1,0:T(8,128)(2,1)}, u32[]{:S(2)}, u32[]{:S(2)}) collective-permute-start(bf16[2,4,256,512]{3,2,1,0:T(8,128)(2,1)} %pad_maximum_fusion.2.up_0), channel_id=1, source_target_pairs={{0,1},{1,0},{2,3},{3,2},{4,5},{5,4},{6,7},{7,6},{8,9},{9,8},{10,11... | collective-permute-start | bytes 6291464 | tf_op jit(solution)/shard_map/ppermute | solution.py:725
  309.2 21.6 %collective-permute-start.20 = (bf16[4,4,320,512]{3,2,1,0:T(8,128)(2,1)}, bf16[4,4,320,512]{3,2,1,0:T(8,128)(2,1)}, u32[]{:S(2)}, u32[]{:S(2)}) collective-permute-start(bf16[4,4,320,512]{3,2,1,0:T(8,128)(2,1)} %get-tuple-element.136), channel_id=1, source_target_pairs={{0,1},{1,0},{2,3},{3,2},{4,5},{5,4},{6,7},{7,6},{8,9},{9,8},{10,11... | collective-permute-start | bytes 15728648 | tf_op jit(solution)/shard_map/ppermute | solution.py:725
  309.4 17.1 %collective-permute-start.21 = (bf16[4,4,256,512]{3,2,1,0:T(8,128)(2,1)}, bf16[4,4,256,512]{3,2,1,0:T(8,128)(2,1)}, u32[]{:S(2)}, u32[]{:S(2)}) collective-permute-start(bf16[4,4,256,512]{3,2,1,0:T(8,128)(2,1)} %get-tuple-element.138), channel_id=1, source_target_pairs={{0,1},{1,0},{2,3},{3,2},{4,5},{5,4},{6,7},{7,6},{8,9},{9,8},{10,11... | collective-permute-start | bytes 12582920 | tf_op jit(solution)/shard_map/ppermute | solution.py:725
  309.8 25.1 %all-to-all-start.1 = ((bf16[8,64,512]{2,1,0:T(8,128)(2,1)}), bf16[8,64,512]{2,1,0:T(8,128)(2,1)}, u32[]{:S(2)}, u32[]{:S(2)}) async-start(bf16[8,64,512]{2,1,0:T(8,128)(2,1)} %get-tuple-element.132), calls=%async_computation.1 | async-start | bytes 1048576 | tf_op jit(solution)/shard_map/all_to_all | solution.py:1356
  334.9 38.6 %all-to-all-start.2 = ((bf16[8,64,512]{2,1,0:T(8,128)(2,1)}), bf16[8,64,512]{2,1,0:T(8,128)(2,1)}, u32[]{:S(2)}, u32[]{:S(2)}) async-start(bf16[8,64,512]{2,1,0:T(8,128)(2,1)} %get-tuple-element.148), calls=%async_computation.2 | async-start | bytes 1048576 | tf_op jit(solution)/shard_map/all_to_all | solution.py:1370
  339.2 39.3 %collective-permute-start.22 = (bf16[2,4,160,512]{3,2,1,0:T(8,128)(2,1)}, bf16[2,4,160,512]{3,2,1,0:T(8,128)(2,1)}, u32[]{:S(2)}, u32[]{:S(2)}) collective-permute-start(bf16[2,4,160,512]{3,2,1,0:T(8,128)(2,1)} %get-tuple-element.149), channel_id=1, source_target_pairs={{0,8},{1,9},{2,10},{3,11},{4,12},{5,13},{6,14},{7,15},{8,0},{9,1},... | collective-permute-start | bytes 3932168 | tf_op jit(solution)/shard_map/ppermute | solution.py:725
  343.3 35.3 %collective-permute-start.23 = (bf16[2,4,128,512]{3,2,1,0:T(8,128)(2,1)}, bf16[2,4,128,512]{3,2,1,0:T(8,128)(2,1)}, u32[]{:S(2)}, u32[]{:S(2)}) collective-permute-start(bf16[2,4,128,512]{3,2,1,0:T(8,128)(2,1)} %get-tuple-element.150), channel_id=1, source_target_pairs={{0,16},{1,17},{2,18},{3,19},{4,20},{5,21},{6,22},{7,23},{8,24},{9,... | collective-permute-start | bytes 3145736 | tf_op jit(solution)/shard_map/ppermute | solution.py:725
  343.3 77.7 %collective-permute-start.24 = (bf16[2,4,160,512]{3,2,1,0:T(8,128)(2,1)}, bf16[2,4,160,512]{3,2,1,0:T(8,128)(2,1)}, u32[]{:S(2)}, u32[]{:S(2)}) collective-permute-start(bf16[2,4,160,512]{3,2,1,0:T(8,128)(2,1)} %get-tuple-element.157), channel_id=1, source_target_pairs={{0,8},{1,9},{2,10},{3,11},{4,12},{5,13},{6,14},{7,15},{8,0},{9,1},... | collective-permute-start | bytes 3932168 | tf_op jit(solution)/shard_map/ppermute | solution.py:725
  344.7 76.3 %collective-permute-start.25 = (bf16[2,4,128,512]{3,2,1,0:T(8,128)(2,1)}, bf16[2,4,128,512]{3,2,1,0:T(8,128)(2,1)S(1)}, u32[]{:S(2)}, u32[]{:S(2)}) collective-permute-start(bf16[2,4,128,512]{3,2,1,0:T(8,128)(2,1)} %get-tuple-element.158), channel_id=1, source_target_pairs={{0,16},{1,17},{2,18},{3,19},{4,20},{5,21},{6,22},{7,23},{8,24},{9,... | collective-permute-start | bytes 3145736 | tf_op jit(solution)/shard_map/ppermute | solution.py:725
  373.5 43.0 %all-to-all-start.3 = ((bf16[8,192,512]{2,1,0:T(8,128)(2,1)}), bf16[8,192,512]{2,1,0:T(8,128)(2,1)}, u32[]{:S(2)}, u32[]{:S(2)}) async-start(bf16[8,192,512]{2,1,0:T(8,128)(2,1)} %attend_head_back.2), calls=%async_computation.3 | async-start | bytes 3145728 | tf_op jit(solution)/shard_map/all_to_all | solution.py:1376
  416.5 42.3 %all-to-all-start.4 = ((bf16[8,192,512]{2,1,0:T(8,128)(2,1)}), bf16[8,192,512]{2,1,0:T(8,128)(2,1)}, u32[]{:S(2)}, u32[]{:S(2)}) async-start(bf16[8,192,512]{2,1,0:T(8,128)(2,1)} %attend_head_back.3), calls=%async_computation.4 | async-start | bytes 3145728 | tf_op jit(solution)/shard_map/all_to_all | solution.py:1382
  424.8 12.2 %slice-start = ((s8[6291456]{0:T(1024)(128)(4,1)}), s8[4194304]{0:T(1024)(128)(4,1)S(1)}, s32[]{:S(2)}) async-start(s8[6291456]{0:T(1024)(128)(4,1)} %bitcast.126), calls=%async_computation.10 | async-start | bytes 8388608
  431.7 43.2 %collective-permute-start.26 = (bf16[4,320,512]{2,1,0:T(8,128)(2,1)}, bf16[4,320,512]{2,1,0:T(8,128)(2,1)}, u32[]{:S(2)}, u32[]{:S(2)}) collective-permute-start(bf16[4,320,512]{2,1,0:T(8,128)(2,1)} %fusion.2), channel_id=1, source_target_pairs={{0,16},{1,17},{2,18},{3,19},{4,20},{5,21},{6,22},{7,23},{8,24},{9,... | collective-permute-start | bytes 3932168 | tf_op jit(solution)/shard_map/ppermute | solution.py:725
  435.9 39.1 %collective-permute-start.27 = (bf16[4,256,512]{2,1,0:T(8,128)(2,1)}, bf16[4,256,512]{2,1,0:T(8,128)(2,1)}, u32[]{:S(2)}, u32[]{:S(2)}) collective-permute-start(bf16[4,256,512]{2,1,0:T(8,128)(2,1)} %fusion.3), channel_id=1, source_target_pairs={{0,8},{1,9},{2,10},{3,11},{4,12},{5,13},{6,14},{7,15},{8,0},{9,1},... | collective-permute-start | bytes 3145736 | tf_op jit(solution)/shard_map/ppermute | solution.py:725
  474.9 20.0 %collective-permute-start.28 = (bf16[4,4,128,256]{3,2,1,0:T(8,128)(2,1)}, bf16[4,4,128,256]{3,2,1,0:T(8,128)(2,1)}, u32[]{:S(2)}, u32[]{:S(2)}) collective-permute-start(bf16[4,4,128,256]{3,2,1,0:T(8,128)(2,1)} %grad_blocks.4), channel_id=1, source_target_pairs={{0,1},{1,0},{2,3},{3,2},{4,5},{5,4},{6,7},{7,6},{8,9},{9,8},{10,11... | collective-permute-start | bytes 3145736 | tf_op jit(solution)/shard_map/ppermute | solution.py:725
  475.1 6.3 %collective-permute-start.30 = (f32[4,512]{1,0:T(4,128)S(1)}, f32[4,512]{1,0:T(4,128)S(1)}, u32[]{:S(2)}, u32[]{:S(2)}) collective-permute-start(f32[4,512]{1,0:T(4,128)S(1)} %bitcast.157), channel_id=1, source_target_pairs={{0,1},{1,0},{2,3},{3,2},{4,5},{5,4},{6,7},{7,6},{8,9},{9,8},{10,11... | collective-permute-start | bytes 24584 | tf_op jit(solution)/shard_map/ppermute | solution.py:725
  475.7 23.8 %collective-permute-start.29 = (bf16[4,4,128,256]{3,2,1,0:T(8,128)(2,1)S(1)}, bf16[4,4,128,256]{3,2,1,0:T(8,128)(2,1)}, u32[]{:S(2)}, u32[]{:S(2)}) collective-permute-start(bf16[4,4,128,256]{3,2,1,0:T(8,128)(2,1)S(1)} %grad_blocks.5), channel_id=1, source_target_pairs={{0,1},{1,0},{2,3},{3,2},{4,5},{5,4},{6,7},{7,6},{8,9},{9,8},{10,11... | collective-permute-start | bytes 3145736 | tf_op jit(solution)/shard_map/ppermute | solution.py:725
  481.4 5.5 collective-permute-start.31
  481.5 5.4 collective-permute-start.32
  483.3 4.1 collective-permute-start.33
  487.5 61.8 %all-to-all-start.5 = ((bf16[4,576,512]{2,1,0:T(8,128)(2,1)}), bf16[4,576,512]{2,1,0:T(8,128)(2,1)}, u32[]{:S(2)}, u32[]{:S(2)}) async-start(bf16[4,576,512]{2,1,0:T(8,128)(2,1)} %pad_maximum_fusion.1), calls=%async_computation.5 | async-start | bytes 4718592 | tf_op jit(solution)/shard_map/all_to_all | solution.py:1280
  504.6 20.8 %collective-permute-start.34 = (bf16[2,704,256]{2,1,0:T(8,128)(2,1)}, bf16[2,704,256]{2,1,0:T(8,128)(2,1)}, u32[]{:S(2)}, u32[]{:S(2)}) collective-permute-start(bf16[2,704,256]{2,1,0:T(8,128)(2,1)} %get-tuple-element.182), channel_id=1, source_target_pairs={{0,8},{1,9},{2,10},{3,11},{4,12},{5,13},{6,14},{7,15},{8,0},{9,1},... | collective-permute-start | bytes 2162696 | tf_op jit(solution)/shard_map/ppermute | solution.py:725
  509.5 17.4 %collective-permute-start.35 = (bf16[2,704,256]{2,1,0:T(8,128)(2,1)}, bf16[2,704,256]{2,1,0:T(8,128)(2,1)}, u32[]{:S(2)}, u32[]{:S(2)}) collective-permute-start(bf16[2,704,256]{2,1,0:T(8,128)(2,1)} %get-tuple-element.183), channel_id=1, source_target_pairs={{0,16},{1,17},{2,18},{3,19},{4,20},{5,21},{6,22},{7,23},{8,24},{9,... | collective-permute-start | bytes 2162696 | tf_op jit(solution)/shard_map/ppermute | solution.py:725
  526.9 3.6 collective-permute-start.38
  528.3 9.8 %collective-permute-start.36 = (bf16[704,256]{1,0:T(8,128)(2,1)S(1)}, bf16[704,256]{1,0:T(8,128)(2,1)S(1)}, u32[]{:S(2)}, u32[]{:S(2)}) collective-permute-start(bf16[704,256]{1,0:T(8,128)(2,1)S(1)} %fusion.6), channel_id=1, source_target_pairs={{0,16},{1,17},{2,18},{3,19},{4,20},{5,21},{6,22},{7,23},{8,24},{9,... | collective-permute-start | bytes 1081352 | tf_op jit(solution)/shard_map/ppermute | solution.py:725
  530.5 6.4 %collective-permute-start.39 = (f32[2,512]{1,0:T(2,128)S(1)}, f32[2,512]{1,0:T(2,128)S(1)}, u32[]{:S(2)}, u32[]{:S(2)}) collective-permute-start(f32[2,512]{1,0:T(2,128)S(1)} %pad_maximum_fusion.10), channel_id=1, source_target_pairs={{0,16},{1,17},{2,18},{3,19},{4,20},{5,21},{6,22},{7,23},{8,24},{9,... | collective-permute-start | bytes 12296 | tf_op jit(solution)/shard_map/ppermute | solution.py:725
  531.9 7.6 %collective-permute-start.37 = (bf16[704,256]{1,0:T(8,128)(2,1)S(1)}, bf16[704,256]{1,0:T(8,128)(2,1)S(1)}, u32[]{:S(2)}, u32[]{:S(2)}) collective-permute-start(bf16[704,256]{1,0:T(8,128)(2,1)S(1)} %fusion.7), channel_id=1, source_target_pairs={{0,8},{1,9},{2,10},{3,11},{4,12},{5,13},{6,14},{7,15},{8,0},{9,1},... | collective-permute-start | bytes 1081352 | tf_op jit(solution)/shard_map/ppermute | solution.py:725
  540.7 5.1 collective-permute-start.41
  540.8 7.5 %collective-permute-start.42 = (bf16[128,256]{1,0:T(8,128)(2,1)S(1)}, bf16[128,256]{1,0:T(8,128)(2,1)S(1)}, u32[]{:S(2)}, u32[]{:S(2)}) collective-permute-start(bf16[128,256]{1,0:T(8,128)(2,1)S(1)} %get-tuple-element.245), channel_id=1, source_target_pairs={{2,0},{5,1},{0,2},{3,3},{6,4},{1,5},{4,6},{7,7},{10,8},{13,9},{8,1... | collective-permute-start | bytes 196616 | tf_op jit(solution)/shard_map/ppermute | solution.py:702
  544.3 4.0 collective-permute-start.40
  549.3 20.5 %all-to-all-start.6 = ((bf16[4,128,512]{2,1,0:T(8,128)(2,1)}), bf16[4,128,512]{2,1,0:T(8,128)(2,1)S(1)}, u32[]{:S(2)}, u32[]{:S(2)}) async-start(bf16[4,128,512]{2,1,0:T(8,128)(2,1)} %pad_maximum_fusion.6), calls=%async_computation.6 | async-start | bytes 1048576 | tf_op jit(solution)/shard_map/all_to_all | solution.py:1280
  (30 other events, 145.4 us)
Sparse Core Ops, SparseCore 0:
  11.1 84.3 all-gather.7
  103.7 83.0 all-gather.9
  252.3 74.1 all-gather.11

commit v7 on v6

--- a/solution.py
+++ b/solution.py
@@ -1046,7 +1046,7 @@
         in_specs=[whole] * 2,
         out_specs=whole,
         out_shape=jax.ShapeDtypeStruct((frames, width), jnp.float32),
-        compiler_params=pltpu.CompilerParams(vmem_limit_bytes=32 << 20),
+        compiler_params=pltpu.CompilerParams(vmem_limit_bytes=60 << 20),
         cost_estimate=pl.CostEstimate(
             flops=3 * frames * width * width, bytes_accessed=7 * frames * width + 6 * width * width, transcendentals=0
         ),

time: 584 us -> 584 us (level)
  waiting for transfers between devices: 128 us -> 116 us
    all_to_all x1, waiting for transfers between devices: 12.8 us -> 2.12 us  [local_paired(): local_b = lax.all_to_all(back_b, 'seq', 0, 0)]
    unnamed x103 -> x93, local copies, waits for them, and re-layouts: 23 us -> 25.6 us
  transfers between devices with their start and end apart: 52 -> 52, of which waited for: 16 -> 16; matrix products, arithmetic and copies ran while one was open for 16% -> 18% of each run, Pallas kernels for 29% -> 30%
where the time goes in v7:
time: 584 us; the launch traced here: 577 us
  Pallas kernels  176 us (30%)
  waiting for transfers between devices  116 us (20%)
  starting transfers between devices  85.4 us (15%)
  blocking collectives  67.7 us (12%)
  other arithmetic  56.2 us (10%)
  local copies, waits for them, and re-layouts  45 us (8%)
  between operations  20.2 us (3%)
  matrix products  10 us (2%)
    ppermute x37, waiting for transfers between devices, send(): return lax.ppermute(value, ('dp', 'seq'), route)  61.9 us
    pallas_call x2, Pallas kernels, attend_head_back(): pl.pallas_call(partial(attend_back_kernel, head=head, size=size, length=l...  56.2 us
    pallas_call x1, Pallas kernels, middle_block(): pl.pallas_call(partial(middle_kernel, dp=dp, seq=seq), in_specs=[pl.Block...  48.7 us
    ppermute x37, starting transfers between devices, send(): return lax.ppermute(value, ('dp', 'seq'), route)  46.3 us
    all_gather x1, waiting for transfers between devices, local_paired(): normed_all = lax.all_gather(normed_one, 'seq', axis=0)  32.5 us
    all_to_all x1, blocking collectives, local_paired(): attended = lax.all_to_all(attended_pair, 'seq', 0, 0).reshape(width, frames)  31.2 us
    unnamed x93, local copies, waits for them, and re-layouts  25.6 us
    convert_element_type x8, other arithmetic, low(): return value.astype(jnp.bfloat16)  23.3 us
  transfers between devices with their start and end apart: 52, of which 16 were waited for; matrix products, arithmetic and copies ran while one was open for 18% of the time, Pallas kernels for 30%

profile of v7, /device:TPU:0, one launch (start us, length us, event | category | flops | bytes accessed | tf_op | source)
XLA Modules:
  0.0 577.2 jit_solution(9811268710185199923)
XLA Ops:
  9.8 3.1 collective-permute-start.3
  12.9 2.6 collective-permute-start.4
  15.6 1.8 collective-permute-start.1
  17.4 1.9 collective-permute-start.2
  20.8 8.2 %all-gather.3 = bf16[4,1,1024]{2,1,0:T(2,128)(2,1)S(1)} all-gather(bf16[1,1,1024]{2,1,0:T(2,128)(2,1)S(1)} %bitcast.158), channel_id=1, replica_groups=mesh['dp'=4,'seq'=8] {'dp'}, dimensions={0}, use_global_device_ids=true | all-gather | bytes 10240 | tf_op jit(solution)/shard_map/all_gather | solution.py:1317
  30.3 3.9 compare_select_fusion.4
  38.7 2.8 multiply_sine_fusion
  41.4 1.9 pad_add_fusion.ends_ref
  43.9 9.0 %all-reduce = f32[4,512]{1,0:T(4,128)S(1)} all-reduce(f32[4,512]{1,0:T(4,128)S(1)} %fusion.26), channel_id=5, replica_groups=mesh['dp'=4,'seq'=8] {'dp'}, use_global_device_ids=true, to_apply=%region_2.3.clone | all-reduce | flops 2048 | bytes 16384
  54.3 19.3 %all_gather.27 = f32[1,4096]{1,0:T(1,128)S(1)} all-gather(f32[1,512]{1,0:T(1,128)S(1)} %constant_dynamic-slice_fusion.13), channel_id=1, replica_groups=mesh['dp'=4,'seq'=8] {'seq'}, dimensions={1}, use_global_device_ids=true | all-gather | bytes 18432 | tf_op jit(solution)/shard_map/all_gather | solution.py:1322
  76.4 2.4 pad_maximum_fusion.5
  78.8 13.2 %collective-permute-done.5 = bf16[1280,128]{1,0:T(8,128)(2,1)S(1)} collective-permute-done((bf16[1280,128]{1,0:T(8,128)(2,1)S(1)}, bf16[1280,128]{1,0:T(8,128)(2,1)S(1)}, u32[]{:S(2)}, u32[]{:S(2)}) %collective-permute-start.5) | collective-permute-done | bytes 327712 | tf_op jit(solution)/shard_map/ppermute | solution.py:725
  93.2 2.2 all-gather.8.cloned.1.call-done
  95.4 2.2 copy-done.11
  97.6 4.6 entry_block.1
  106.5 3.0 collective-permute-start.10
  121.3 2.7 collective-permute-start.13
  124.0 18.4 %collective-permute-done.11 = bf16[384,256]{1,0:T(8,128)(2,1)} collective-permute-done((bf16[384,256]{1,0:T(8,128)(2,1)S(1)}, bf16[384,256]{1,0:T(8,128)(2,1)}, u32[]{:S(2)}, u32[]{:S(2)}) %collective-permute-start.11) | collective-permute-done | bytes 196640 | tf_op jit(solution)/shard_map/ppermute | solution.py:725
  148.3 3.1 pad_maximum_fusion.down_0
  154.3 32.5 %all-gather.10.cloned.1.call-done = bf16[4096,1024]{1,0:T(8,128)(2,1)} async-done(((bf16[512,1024]{1,0:T(8,128)(2,1)}), bf16[4096,1024]{1,0:T(8,128)(2,1)}) %all-gather.10.cloned.1.call-update) | async-done | bytes 8388624 | tf_op jit(solution)/shard_map/all_gather | solution.py:1334
  186.8 10.5 %project_pair.1 = (bf16[8,128,512]{2,1,0:T(8,128)(2,1)}, bf16[128,4096]{1,0:T(8,128)(2,1)}, bf16[128,4096]{1,0:T(8,128)(2,1)}, bf16[4096,128]{1,0:T(8,128)(2,1)}...) custom-call(bf16[8,512,1024]{2,1,0:T(8,128)(2,1)} %bitcast.159, ...), custom_call_target="tpu_custom_call" | custom-call | flops 3221225472 | bytes 13631488 | tf_op jit(solution)/shard_map/project_pair/pallas_call | solution.py:443
  197.3 23.0 %attend_pair.1 = (bf16[8,128,512]{2,1,0:T(8,128)(2,1)}, f32[8,128,512]{2,1,0:T(8,128)}, f32[8,2,512]{2,1,0:T(2,128)}) custom-call(s32[2]{0:T(128)} %pad_add_fusion.ends_ref, bf16[8,128,512]{2,1,0:T(8,128)(2,1)} %get-tuple-element.115.qt_ref, bf16[4096,128]{1,0:T(8,128)(2,1)} %get-tuple-element.116.k_ref, bf16[128,4096]{1,0:T(8,128)(2,1)} %get-tuple-element.117.vt_ref, ...), custom_call_target="tpu_custom_call" | custom-call | flops 8589934592 | bytes 7340032 | tf_op jit(solution)/shard_map/attend_pair/pallas_call | solution.py:553
  220.9 31.2 %all_to_all.35 = bf16[8,128,512]{2,1,0:T(8,128)(2,1)} all-to-all(bf16[8,128,512]{2,1,0:T(8,128)(2,1)} %get-tuple-element.120), channel_id=1, replica_groups=mesh['dp'=4,'seq'=8] {'seq'}, dimensions={0} | all-to-all | bytes 2097152 | tf_op jit(solution)/shard_map/all_to_all | solution.py:1347
  254.0 6.4 %collective-permute-done.18.up_2 = bf16[2,4,256,512]{3,2,1,0:T(8,128)(2,1)} collective-permute-done((bf16[2,4,256,512]{3,2,1,0:T(8,128)(2,1)}, bf16[2,4,256,512]{3,2,1,0:T(8,128)(2,1)}, u32[]{:S(2)}, u32[]{:S(2)}) %collective-permute-start.18) | collective-permute-done | bytes 2097184 | tf_op jit(solution)/shard_map/ppermute | solution.py:725
  260.5 48.7 %middle_block.1 = (bf16[512,1024]{1,0:T(8,128)(2,1)}, f32[512,1024]{1,0:T(8,128)}, bf16[8,64,512]{2,1,0:T(8,128)(2,1)}, bf16[8,64,512]{2,1,0:T(8,128)(2,1)}, f32...) custom-call(s32[3]{0:T(128)} %pad_add_fusion.1.place_ref, ...), custom_call_target="tpu_custom_call" | custom-call | flops 28991029248 | bytes 46137344 | tf_op jit(solution)/shard_map/middle_block/pallas_call | solution.py:933
  309.8 4.2 all-to-all-start.1
  315.5 11.0 %collective-permute-done.21 = bf16[4,4,256,512]{3,2,1,0:T(8,128)(2,1)} collective-permute-done((bf16[4,4,256,512]{3,2,1,0:T(8,128)(2,1)}, bf16[4,4,256,512]{3,2,1,0:T(8,128)(2,1)}, u32[]{:S(2)}, u32[]{:S(2)}) %collective-permute-start.21) | collective-permute-done | bytes 4194336 | tf_op jit(solution)/shard_map/ppermute | solution.py:725
  326.5 4.4 add_convert_fusion.4
  330.9 4.1 add_convert_fusion.1
  335.0 4.3 all-to-all-start.2
  339.4 3.9 collective-permute-start.22
  345.4 28.1 %attend_head_back.2 = bf16[8,192,512]{2,1,0:T(8,128)(2,1)} custom-call(s32[2]{0:T(128)} %pad_add_fusion.ends_ref, bf16[8,128,512]{2,1,0:T(8,128)(2,1)} %get-tuple-element.115.qt_ref, bf16[8,64,512]{2,1,0:T(8,128)(2,1)} %all-to-all-done.1.gt_ref, f32[8,128,512]{2,1,0:T(8,128)} %get-tuple-element.144.full_ref, f32[8,2,512]{2,1,0:T(2,128)} %get-tuple-element.145.total_ref, ...), custom_call_target="tpu_custom_call" | custom-call | flops 42949672960 | bytes 10485760 | tf_op jit(solution)/shard_map/attend_head_back/pallas_call | solution.py:646
  373.5 5.1 all-to-all-start.3
  378.6 28.1 %attend_head_back.3 = bf16[8,192,512]{2,1,0:T(8,128)(2,1)} custom-call(s32[2]{0:T(128)} %pad_add_fusion.ends_ref, bf16[8,128,512]{2,1,0:T(8,128)(2,1)} %get-tuple-element.115.qt_ref, bf16[8,64,512]{2,1,0:T(8,128)(2,1)} %all-to-all-done.2.gt_ref, f32[8,128,512]{2,1,0:T(8,128)} %get-tuple-element.144.full_ref, f32[8,2,512]{2,1,0:T(2,128)} %get-tuple-element.145.total_ref, ...), custom_call_target="tpu_custom_call" | custom-call | flops 42949672960 | bytes 10485760 | tf_op jit(solution)/shard_map/attend_head_back/pallas_call | solution.py:646
  406.7 2.3 constant_dynamic-update-slice_fusion.5
  409.0 2.5 constant_dynamic-update-slice_fusion.3
  411.4 5.1 all-to-all-done.3.head_ref
  416.5 4.5 all-to-all-start.4
  422.2 2.5 constant_dynamic-update-slice_fusion.2
  424.6 3.9 fusion.2
  428.5 3.1 fusion.3
  431.7 4.6 collective-permute-start.26
  441.7 6.4 %first_head.1.partial_ref = f32[512,1024]{1,0:T(8,128)} custom-call(bf16[8,192,512]{2,1,0:T(8,128)(2,1)} %all-to-all-done.3.head_ref, bf16[32,384,256]{2,1,0:T(8,128)(2,1)} %bitcast.135), custom_call_target="tpu_custom_call" | custom-call | flops 1610612736 | bytes 9961472 | tf_op jit(solution)/shard_map/first_head/pallas_call | solution.py:1044
  448.1 8.7 %bitcast_convert_fusion = bf16[384,1024]{1,0:T(8,128)(2,1)} fusion(bf16[8,384,512]{2,1,0:T(8,128)(2,1)} %slice_dynamic-update-slice_fusion, bf16[8,512,1024]{2,1,0:T(8,128)(2,1)} %bitcast.160), kind=kOutput, calls=%fused_computation.15 | convolution fusion | flops 3221618688 | bytes 12320768 | tf_op jit(solution)/shard_map/icf,ifd->cd/dot_general | solution.py:1394
  456.7 2.1 all-to-all-done.4.head_ref
  458.8 9.7 %exit_block.1 = (bf16[512,1024]{1,0:T(8,128)(2,1)}, bf16[1024,512]{1,0:T(8,128)(2,1)}, f32[2,1024]{1,0:T(2,128)}) custom-call(f32[512,1024]{1,0:T(8,128)} %first_head.1.partial_ref, bf16[8,192,512]{2,1,0:T(8,128)(2,1)} %all-to-all-done.4.head_ref, bf16[32,384,256]{2,1,0:T(8,128)(2,1)} %bitcast.136, f32[512,1024]{1,0:T(8,128)} %copy-done.4, ...), custom_call_target="tpu_custom_call" | custom-call | flops 1610612736 | bytes 15728640 | tf_op jit(solution)/shard_map/exit_block/pallas_call | solution.py:1087
  469.8 2.0 grad_blocks.5
  471.9 3.0 grad_blocks.4
  475.7 3.2 fusion
  478.9 2.4 fusion.1
  481.5 2.2 collective-permute-start.32
  487.4 4.8 all-to-all-start.5
  494.9 3.7 grad_blocks.6
  499.5 3.8 grad_blocks.7
  504.5 4.7 collective-permute-start.34
  511.5 2.2 copy-done.12
  513.7 4.7 joined_grads.1
  518.4 6.7 %collective-permute-done.34 = bf16[2,704,256]{2,1,0:T(8,128)(2,1)} collective-permute-done((bf16[2,704,256]{2,1,0:T(8,128)(2,1)}, bf16[2,704,256]{2,1,0:T(8,128)(2,1)}, u32[]{:S(2)}, u32[]{:S(2)}) %collective-permute-start.34) | collective-permute-done | bytes 720928 | tf_op jit(solution)/shard_map/ppermute | solution.py:725
  533.3 3.3 collective-permute-done.39
  540.4 3.6 collective-permute-start.42
  545.6 2.7 collective-permute-done.42
  549.2 6.5 %all-to-all-start.6 = ((bf16[4,128,512]{2,1,0:T(8,128)(2,1)}), bf16[4,128,512]{2,1,0:T(8,128)(2,1)S(1)}, u32[]{:S(2)}, u32[]{:S(2)}) async-start(bf16[4,128,512]{2,1,0:T(8,128)(2,1)} %pad_maximum_fusion.6), calls=%async_computation.6 | async-start | bytes 1048576 | tf_op jit(solution)/shard_map/all_to_all | solution.py:1280
  555.7 2.1 convert_reduce_fusion
  560.4 9.1 %all-to-all-done.6 = bf16[4,128,512]{2,1,0:T(8,128)(2,1)S(1)} async-done(((bf16[4,128,512]{2,1,0:T(8,128)(2,1)}), bf16[4,128,512]{2,1,0:T(8,128)(2,1)S(1)}, u32[]{:S(2)}, u32[]{:S(2)}) %all-to-all-start.6) | async-done | bytes 524320 | tf_op jit(solution)/shard_map/all_to_all | solution.py:1280
  (234 shorter events, 79.2 us)
Async XLA Ops:
  7.2 29.1 %copy-start = (bf16[256,512]{1,0:T(8,128)(2,1)S(1)}, bf16[256,512]{1,0:T(8,128)(2,1)}, u32[]{:S(2)}) copy-start(bf16[256,512]{1,0:T(8,128)(2,1)} %param.23) | copy-start | bytes 786436
  7.2 13.6 %copy-start.35 = (bf16[1,1024]{1,0:T(2,128)(2,1)S(1)}, bf16[1,1024]{1,0:T(2,128)(2,1)}, u32[]{:S(2)}) copy-start(bf16[1,1024]{1,0:T(2,128)(2,1)} %param.17) | copy-start | bytes 6148
  7.2 21.9 %copy-start.33 = (s32[1,3]{1,0:T(1,128)S(1)}, s32[1,3]{1,0:T(1,128)}, u32[]{:S(2)}) copy-start(s32[1,3]{1,0:T(1,128)} %param.19) | copy-start | bytes 40
  7.2 22.5 %copy-start.34 = (s32[1,3]{1,0:T(1,128)S(1)}, s32[1,3]{1,0:T(1,128)}, u32[]{:S(2)}) copy-start(s32[1,3]{1,0:T(1,128)} %param.20) | copy-start | bytes 40
  7.2 23.1 %copy-start.29 = (s32[1,4096]{1,0:T(1,128)S(1)}, s32[1,4096]{1,0:T(1,128)}, u32[]{:S(2)}) copy-start(s32[1,4096]{1,0:T(1,128)} %param.18) | copy-start | bytes 49156
  7.2 88.2 %all-gather.8.cloned.1.call-start = ((), (), s32[]{:S(2)}) async-start(), calls=%async_computation.7 | async-start | bytes 4325376 | tf_op jit(solution)/shard_map/all_gather | solution.py:1328
  8.0 178.8 %all-gather.10.cloned.1.call-start = ((), (), s32[]{:S(2)}) async-start(), calls=%async_computation.8 | async-start | bytes 9437184 | tf_op jit(solution)/shard_map/all_gather | solution.py:1334
  9.8 69.0 %collective-permute-start.3 = (bf16[1280,128]{1,0:T(8,128)(2,1)S(1)}, bf16[1280,128]{1,0:T(8,128)(2,1)S(1)}, u32[]{:S(2)}, u32[]{:S(2)}) collective-permute-start(bf16[1280,128]{1,0:T(8,128)(2,1)S(1)} %constant_dynamic-update-slice_fusion), channel_id=1, source_target_pairs={{0,2},{1,3},{2,4},{3,5},{4,6},{5,7},{6,0},{7,1},{8,10},{9,11},{10,... | collective-permute-start | bytes 983048 | tf_op jit(solution)/shard_map/ppermute | solution.py:725
  12.9 65.9 %collective-permute-start.4 = (bf16[1280,128]{1,0:T(8,128)(2,1)S(1)}, bf16[1280,128]{1,0:T(8,128)(2,1)S(1)}, u32[]{:S(2)}, u32[]{:S(2)}) collective-permute-start(bf16[1280,128]{1,0:T(8,128)(2,1)S(1)} %constant_dynamic-update-slice_fusion), channel_id=1, source_target_pairs={{0,4},{1,5},{2,6},{3,7},{4,0},{5,1},{6,2},{7,3},{8,12},{9,13},{10,... | collective-permute-start | bytes 983048 | tf_op jit(solution)/shard_map/ppermute | solution.py:725
  15.5 58.1 %collective-permute-start = (bf16[256,512]{1,0:T(8,128)(2,1)}, bf16[256,512]{1,0:T(8,128)(2,1)S(1)}, u32[]{:S(2)}, u32[]{:S(2)}) collective-permute-start(bf16[256,512]{1,0:T(8,128)(2,1)} %param.26), channel_id=1, source_target_pairs={{0,2},{1,3},{2,4},{3,5},{4,6},{5,7},{6,0},{7,1},{8,10},{9,11},{10,... | collective-permute-start | bytes 786440 | tf_op jit(solution)/shard_map/ppermute | solution.py:725
  15.6 60.0 %collective-permute-start.1 = (bf16[256,512]{1,0:T(8,128)(2,1)}, bf16[256,512]{1,0:T(8,128)(2,1)S(1)}, u32[]{:S(2)}, u32[]{:S(2)}) collective-permute-start(bf16[256,512]{1,0:T(8,128)(2,1)} %param.26), channel_id=1, source_target_pairs={{0,4},{1,5},{2,6},{3,7},{4,0},{5,1},{6,2},{7,3},{8,12},{9,13},{10,... | collective-permute-start | bytes 786440 | tf_op jit(solution)/shard_map/ppermute | solution.py:725
  17.4 58.2 %collective-permute-start.2 = (bf16[256,512]{1,0:T(8,128)(2,1)}, bf16[256,512]{1,0:T(8,128)(2,1)S(1)}, u32[]{:S(2)}, u32[]{:S(2)}) collective-permute-start(bf16[256,512]{1,0:T(8,128)(2,1)} %param.26), channel_id=1, source_target_pairs={{0,6},{1,7},{2,0},{3,1},{4,2},{5,3},{6,4},{7,5},{8,14},{9,15},{10,... | collective-permute-start | bytes 786440 | tf_op jit(solution)/shard_map/ppermute | solution.py:725
  73.6 18.4 %collective-permute-start.5 = (bf16[1280,128]{1,0:T(8,128)(2,1)S(1)}, bf16[1280,128]{1,0:T(8,128)(2,1)S(1)}, u32[]{:S(2)}, u32[]{:S(2)}) collective-permute-start(bf16[1280,128]{1,0:T(8,128)(2,1)S(1)} %constant_dynamic-update-slice_fusion), channel_id=1, source_target_pairs={{0,6},{1,7},{2,0},{3,1},{4,2},{5,3},{6,4},{7,5},{8,14},{9,15},{10,... | collective-permute-start | bytes 983048 | tf_op jit(solution)/shard_map/ppermute | solution.py:725
  75.6 19.8 %copy-start.9 = (f32[1,1024]{1,0:T(1,128)}, f32[1,1024]{1,0:T(1,128)S(1)}, u32[]{:S(2)}) copy-start(f32[1,1024]{1,0:T(1,128)S(1)} %get-tuple-element.275.scale_ref) | copy-start | bytes 12292
  76.4 19.0 %copy-start.5 = (bf16[1,512,1024]{2,1,0:T(8,128)(2,1)S(1)}, bf16[1,512,1024]{2,1,0:T(8,128)(2,1)}, u32[]{:S(2)}) copy-start(bf16[1,512,1024]{2,1,0:T(8,128)(2,1)} %param.15) | copy-start | bytes 3145732
  76.4 19.0 %copy-start.6 = (bf16[1,512,1024]{2,1,0:T(8,128)(2,1)S(1)}, bf16[1,512,1024]{2,1,0:T(8,128)(2,1)}, u32[]{:S(2)}) copy-start(bf16[1,512,1024]{2,1,0:T(8,128)(2,1)} %param.16) | copy-start | bytes 3145732
  103.5 42.9 %copy-start.21 = (bf16[4,256,512]{2,1,0:T(8,128)(2,1)S(1)}, bf16[4,256,512]{2,1,0:T(8,128)(2,1)}, u32[]{:S(2)}) copy-start(bf16[4,256,512]{2,1,0:T(8,128)(2,1)} %pad_maximum_fusion.5) | copy-start | bytes 3145732
  103.6 235.8 %all-gather.12.cloned.1.call-start = ((), (), s32[]{:S(2)}) async-start(), calls=%async_computation.9 | async-start | bytes 6488064 | tf_op jit(solution)/shard_map/all_gather | solution.py:1352
  104.7 43.2 %collective-permute-start.7 = (bf16[4,1280,128]{2,1,0:T(8,128)(2,1)}, bf16[4,1280,128]{2,1,0:T(8,128)(2,1)}, u32[]{:S(2)}, u32[]{:S(2)}) collective-permute-start(bf16[4,1280,128]{2,1,0:T(8,128)(2,1)} %pad_maximum_fusion.4), channel_id=1, source_target_pairs={{0,16},{1,17},{2,18},{3,19},{4,20},{5,21},{6,22},{7,23},{8,24},{9,... | collective-permute-start | bytes 3932168 | tf_op jit(solution)/shard_map/ppermute | solution.py:725
  106.5 12.2 %collective-permute-start.10 = (bf16[128,256]{1,0:T(8,128)(2,1)S(1)}, bf16[128,256]{1,0:T(8,128)(2,1)S(1)}, u32[]{:S(2)}, u32[]{:S(2)}) collective-permute-start(bf16[128,256]{1,0:T(8,128)(2,1)S(1)} %get-tuple-element.261), channel_id=1, source_target_pairs={{0,2},{1,5},{2,0},{3,3},{4,6},{5,1},{6,4},{7,7},{8,10},{9,13},{10,... | collective-permute-start | bytes 196616 | tf_op jit(solution)/shard_map/ppermute | solution.py:685
  109.5 9.2 %collective-permute-start.8 = (bf16[128,256]{1,0:T(8,128)(2,1)S(1)}, bf16[128,256]{1,0:T(8,128)(2,1)S(1)}, u32[]{:S(2)}, u32[]{:S(2)}) collective-permute-start(bf16[128,256]{1,0:T(8,128)(2,1)S(1)} %get-tuple-element.263), channel_id=1, source_target_pairs={{0,0},{1,3},{2,6},{3,1},{4,4},{5,7},{6,2},{7,5},{8,8},{9,11},{10,1... | collective-permute-start | bytes 196616 | tf_op jit(solution)/shard_map/ppermute | solution.py:685
  110.1 8.6 %collective-permute-start.9 = (bf16[128,256]{1,0:T(8,128)(2,1)S(1)}, bf16[128,256]{1,0:T(8,128)(2,1)S(1)}, u32[]{:S(2)}, u32[]{:S(2)}) collective-permute-start(bf16[128,256]{1,0:T(8,128)(2,1)S(1)} %get-tuple-element.262), channel_id=1, source_target_pairs={{0,1},{1,4},{2,7},{3,2},{4,5},{5,0},{6,3},{7,6},{8,9},{9,12},{10,1... | collective-permute-start | bytes 196616 | tf_op jit(solution)/shard_map/ppermute | solution.py:685
  111.9 34.6 %collective-permute-start.6 = (bf16[4,256,512]{2,1,0:T(8,128)(2,1)}, bf16[4,256,512]{2,1,0:T(8,128)(2,1)S(1)}, u32[]{:S(2)}, u32[]{:S(2)}) collective-permute-start(bf16[4,256,512]{2,1,0:T(8,128)(2,1)} %pad_maximum_fusion.5), channel_id=1, source_target_pairs={{0,8},{1,9},{2,10},{3,11},{4,12},{5,13},{6,14},{7,15},{8,0},{9,1},... | collective-permute-start | bytes 3145736 | tf_op jit(solution)/shard_map/ppermute | solution.py:725
  120.5 27.5 %copy-start.22 = (bf16[384,256]{1,0:T(8,128)(2,1)}, bf16[384,256]{1,0:T(8,128)(2,1)S(1)}, u32[]{:S(2)}) copy-start(bf16[384,256]{1,0:T(8,128)(2,1)S(1)} %get-tuple-element.133) | copy-start | bytes 589828
  120.5 21.9 %collective-permute-start.11 = (bf16[384,256]{1,0:T(8,128)(2,1)S(1)}, bf16[384,256]{1,0:T(8,128)(2,1)}, u32[]{:S(2)}, u32[]{:S(2)}) collective-permute-start(bf16[384,256]{1,0:T(8,128)(2,1)S(1)} %get-tuple-element.133), channel_id=1, source_target_pairs={{0,8},{1,9},{2,10},{3,11},{4,12},{5,13},{6,14},{7,15},{8,0},{9,1},... | collective-permute-start | bytes 589832 | tf_op jit(solution)/shard_map/ppermute | solution.py:725
  120.9 23.1 %collective-permute-start.12 = (bf16[384,256]{1,0:T(8,128)(2,1)S(1)}, bf16[384,256]{1,0:T(8,128)(2,1)}, u32[]{:S(2)}, u32[]{:S(2)}) collective-permute-start(bf16[384,256]{1,0:T(8,128)(2,1)S(1)} %get-tuple-element.133), channel_id=1, source_target_pairs={{0,16},{1,17},{2,18},{3,19},{4,20},{5,21},{6,22},{7,23},{8,24},{9,... | collective-permute-start | bytes 589832 | tf_op jit(solution)/shard_map/ppermute | solution.py:725
  121.3 24.4 %collective-permute-start.13 = (bf16[384,256]{1,0:T(8,128)(2,1)S(1)}, bf16[384,256]{1,0:T(8,128)(2,1)S(1)}, u32[]{:S(2)}, u32[]{:S(2)}) collective-permute-start(bf16[384,256]{1,0:T(8,128)(2,1)S(1)} %get-tuple-element.133), channel_id=1, source_target_pairs={{0,24},{1,25},{2,26},{3,27},{4,28},{5,29},{6,30},{7,31},{8,16},{9,... | collective-permute-start | bytes 589832 | tf_op jit(solution)/shard_map/ppermute | solution.py:725
  151.4 69.0 %collective-permute-start.15 = (bf16[2,4,1280,128]{3,2,1,0:T(8,128)(2,1)}, bf16[2,4,1280,128]{3,2,1,0:T(8,128)(2,1)}, u32[]{:S(2)}, u32[]{:S(2)}) collective-permute-start(bf16[2,4,1280,128]{3,2,1,0:T(8,128)(2,1)} %pad_maximum_fusion.down_0), channel_id=1, source_target_pairs={{0,8},{1,9},{2,10},{3,11},{4,12},{5,13},{6,14},{7,15},{8,0},{9,1},... | collective-permute-start | bytes 7864328 | tf_op jit(solution)/shard_map/ppermute | solution.py:725
  152.9 67.4 %collective-permute-start.14 = (bf16[2,4,256,512]{3,2,1,0:T(8,128)(2,1)}, bf16[2,4,256,512]{3,2,1,0:T(8,128)(2,1)}, u32[]{:S(2)}, u32[]{:S(2)}) collective-permute-start(bf16[2,4,256,512]{3,2,1,0:T(8,128)(2,1)} %pad_maximum_fusion.2.up_0), channel_id=1, source_target_pairs={{0,16},{1,17},{2,18},{3,19},{4,20},{5,21},{6,22},{7,23},{8,24},{9,... | collective-permute-start | bytes 6291464 | tf_op jit(solution)/shard_map/ppermute | solution.py:725
  220.3 32.4 %copy-start.20 = (bf16[512,1024]{0,1:T(8,128)(2,1)S(1)}, bf16[512,1024]{0,1:T(8,128)(2,1)}, u32[]{:S(2)}) copy-start(bf16[512,1024]{0,1:T(8,128)(2,1)} %bitcast_select_fusion) | copy-start | bytes 3145732
  220.4 31.7 %collective-permute-start.17 = (bf16[2,4,1280,128]{3,2,1,0:T(8,128)(2,1)}, bf16[2,4,1280,128]{3,2,1,0:T(8,128)(2,1)}, u32[]{:S(2)}, u32[]{:S(2)}) collective-permute-start(bf16[2,4,1280,128]{3,2,1,0:T(8,128)(2,1)} %collective-permute-done.15.down_1), channel_id=1, source_target_pairs={{0,1},{1,0},{2,3},{3,2},{4,5},{5,4},{6,7},{7,6},{8,9},{9,8},{10,11... | collective-permute-start | bytes 7864328 | tf_op jit(solution)/shard_map/ppermute | solution.py:725
  220.7 31.4 %collective-permute-start.16 = (bf16[2,4,256,512]{3,2,1,0:T(8,128)(2,1)}, bf16[2,4,256,512]{3,2,1,0:T(8,128)(2,1)}, u32[]{:S(2)}, u32[]{:S(2)}) collective-permute-start(bf16[2,4,256,512]{3,2,1,0:T(8,128)(2,1)} %collective-permute-done.14.up_1), channel_id=1, source_target_pairs={{0,1},{1,0},{2,3},{3,2},{4,5},{5,4},{6,7},{7,6},{8,9},{9,8},{10,11... | collective-permute-start | bytes 6291464 | tf_op jit(solution)/shard_map/ppermute | solution.py:725
  252.1 8.3 %collective-permute-start.19 = (bf16[2,4,1280,128]{3,2,1,0:T(8,128)(2,1)}, bf16[2,4,1280,128]{3,2,1,0:T(8,128)(2,1)}, u32[]{:S(2)}, u32[]{:S(2)}) collective-permute-start(bf16[2,4,1280,128]{3,2,1,0:T(8,128)(2,1)} %pad_maximum_fusion.down_0), channel_id=1, source_target_pairs={{0,1},{1,0},{2,3},{3,2},{4,5},{5,4},{6,7},{7,6},{8,9},{9,8},{10,11... | collective-permute-start | bytes 7864328 | tf_op jit(solution)/shard_map/ppermute | solution.py:725
  252.2 8.2 %collective-permute-start.18 = (bf16[2,4,256,512]{3,2,1,0:T(8,128)(2,1)}, bf16[2,4,256,512]{3,2,1,0:T(8,128)(2,1)}, u32[]{:S(2)}, u32[]{:S(2)}) collective-permute-start(bf16[2,4,256,512]{3,2,1,0:T(8,128)(2,1)} %pad_maximum_fusion.2.up_0), channel_id=1, source_target_pairs={{0,1},{1,0},{2,3},{3,2},{4,5},{5,4},{6,7},{7,6},{8,9},{9,8},{10,11... | collective-permute-start | bytes 6291464 | tf_op jit(solution)/shard_map/ppermute | solution.py:725
  309.2 21.7 %collective-permute-start.20 = (bf16[4,4,320,512]{3,2,1,0:T(8,128)(2,1)}, bf16[4,4,320,512]{3,2,1,0:T(8,128)(2,1)}, u32[]{:S(2)}, u32[]{:S(2)}) collective-permute-start(bf16[4,4,320,512]{3,2,1,0:T(8,128)(2,1)} %get-tuple-element.136), channel_id=1, source_target_pairs={{0,1},{1,0},{2,3},{3,2},{4,5},{5,4},{6,7},{7,6},{8,9},{9,8},{10,11... | collective-permute-start | bytes 15728648 | tf_op jit(solution)/shard_map/ppermute | solution.py:725
  309.4 17.1 %collective-permute-start.21 = (bf16[4,4,256,512]{3,2,1,0:T(8,128)(2,1)}, bf16[4,4,256,512]{3,2,1,0:T(8,128)(2,1)}, u32[]{:S(2)}, u32[]{:S(2)}) collective-permute-start(bf16[4,4,256,512]{3,2,1,0:T(8,128)(2,1)} %get-tuple-element.138), channel_id=1, source_target_pairs={{0,1},{1,0},{2,3},{3,2},{4,5},{5,4},{6,7},{7,6},{8,9},{9,8},{10,11... | collective-permute-start | bytes 12582920 | tf_op jit(solution)/shard_map/ppermute | solution.py:725
  309.8 25.3 %all-to-all-start.1 = ((bf16[8,64,512]{2,1,0:T(8,128)(2,1)}), bf16[8,64,512]{2,1,0:T(8,128)(2,1)}, u32[]{:S(2)}, u32[]{:S(2)}) async-start(bf16[8,64,512]{2,1,0:T(8,128)(2,1)} %get-tuple-element.132), calls=%async_computation.1 | async-start | bytes 1048576 | tf_op jit(solution)/shard_map/all_to_all | solution.py:1356
  335.0 38.5 %all-to-all-start.2 = ((bf16[8,64,512]{2,1,0:T(8,128)(2,1)}), bf16[8,64,512]{2,1,0:T(8,128)(2,1)}, u32[]{:S(2)}, u32[]{:S(2)}) async-start(bf16[8,64,512]{2,1,0:T(8,128)(2,1)} %get-tuple-element.148), calls=%async_computation.2 | async-start | bytes 1048576 | tf_op jit(solution)/shard_map/all_to_all | solution.py:1370
  339.4 39.2 %collective-permute-start.22 = (bf16[2,4,160,512]{3,2,1,0:T(8,128)(2,1)}, bf16[2,4,160,512]{3,2,1,0:T(8,128)(2,1)}, u32[]{:S(2)}, u32[]{:S(2)}) collective-permute-start(bf16[2,4,160,512]{3,2,1,0:T(8,128)(2,1)} %get-tuple-element.149), channel_id=1, source_target_pairs={{0,8},{1,9},{2,10},{3,11},{4,12},{5,13},{6,14},{7,15},{8,0},{9,1},... | collective-permute-start | bytes 3932168 | tf_op jit(solution)/shard_map/ppermute | solution.py:725
  343.3 35.3 %collective-permute-start.23 = (bf16[2,4,128,512]{3,2,1,0:T(8,128)(2,1)}, bf16[2,4,128,512]{3,2,1,0:T(8,128)(2,1)}, u32[]{:S(2)}, u32[]{:S(2)}) collective-permute-start(bf16[2,4,128,512]{3,2,1,0:T(8,128)(2,1)} %get-tuple-element.150), channel_id=1, source_target_pairs={{0,16},{1,17},{2,18},{3,19},{4,20},{5,21},{6,22},{7,23},{8,24},{9,... | collective-permute-start | bytes 3145736 | tf_op jit(solution)/shard_map/ppermute | solution.py:725
  343.3 77.7 %collective-permute-start.24 = (bf16[2,4,160,512]{3,2,1,0:T(8,128)(2,1)}, bf16[2,4,160,512]{3,2,1,0:T(8,128)(2,1)}, u32[]{:S(2)}, u32[]{:S(2)}) collective-permute-start(bf16[2,4,160,512]{3,2,1,0:T(8,128)(2,1)} %get-tuple-element.157), channel_id=1, source_target_pairs={{0,8},{1,9},{2,10},{3,11},{4,12},{5,13},{6,14},{7,15},{8,0},{9,1},... | collective-permute-start | bytes 3932168 | tf_op jit(solution)/shard_map/ppermute | solution.py:725
  345.0 76.0 %collective-permute-start.25 = (bf16[2,4,128,512]{3,2,1,0:T(8,128)(2,1)}, bf16[2,4,128,512]{3,2,1,0:T(8,128)(2,1)S(1)}, u32[]{:S(2)}, u32[]{:S(2)}) collective-permute-start(bf16[2,4,128,512]{3,2,1,0:T(8,128)(2,1)} %get-tuple-element.158), channel_id=1, source_target_pairs={{0,16},{1,17},{2,18},{3,19},{4,20},{5,21},{6,22},{7,23},{8,24},{9,... | collective-permute-start | bytes 3145736 | tf_op jit(solution)/shard_map/ppermute | solution.py:725
  373.5 43.0 %all-to-all-start.3 = ((bf16[8,192,512]{2,1,0:T(8,128)(2,1)}), bf16[8,192,512]{2,1,0:T(8,128)(2,1)}, u32[]{:S(2)}, u32[]{:S(2)}) async-start(bf16[8,192,512]{2,1,0:T(8,128)(2,1)} %attend_head_back.2), calls=%async_computation.3 | async-start | bytes 3145728 | tf_op jit(solution)/shard_map/all_to_all | solution.py:1376
  416.5 42.3 %all-to-all-start.4 = ((bf16[8,192,512]{2,1,0:T(8,128)(2,1)}), bf16[8,192,512]{2,1,0:T(8,128)(2,1)}, u32[]{:S(2)}, u32[]{:S(2)}) async-start(bf16[8,192,512]{2,1,0:T(8,128)(2,1)} %attend_head_back.3), calls=%async_computation.4 | async-start | bytes 3145728 | tf_op jit(solution)/shard_map/all_to_all | solution.py:1382
  431.7 43.2 %collective-permute-start.26 = (bf16[4,320,512]{2,1,0:T(8,128)(2,1)}, bf16[4,320,512]{2,1,0:T(8,128)(2,1)}, u32[]{:S(2)}, u32[]{:S(2)}) collective-permute-start(bf16[4,320,512]{2,1,0:T(8,128)(2,1)} %fusion.2), channel_id=1, source_target_pairs={{0,16},{1,17},{2,18},{3,19},{4,20},{5,21},{6,22},{7,23},{8,24},{9,... | collective-permute-start | bytes 3932168 | tf_op jit(solution)/shard_map/ppermute | solution.py:725
  436.2 38.7 %collective-permute-start.27 = (bf16[4,256,512]{2,1,0:T(8,128)(2,1)}, bf16[4,256,512]{2,1,0:T(8,128)(2,1)}, u32[]{:S(2)}, u32[]{:S(2)}) collective-permute-start(bf16[4,256,512]{2,1,0:T(8,128)(2,1)} %fusion.3), channel_id=1, source_target_pairs={{0,8},{1,9},{2,10},{3,11},{4,12},{5,13},{6,14},{7,15},{8,0},{9,1},... | collective-permute-start | bytes 3145736 | tf_op jit(solution)/shard_map/ppermute | solution.py:725
  474.9 20.0 %collective-permute-start.28 = (bf16[4,4,128,256]{3,2,1,0:T(8,128)(2,1)}, bf16[4,4,128,256]{3,2,1,0:T(8,128)(2,1)}, u32[]{:S(2)}, u32[]{:S(2)}) collective-permute-start(bf16[4,4,128,256]{3,2,1,0:T(8,128)(2,1)} %grad_blocks.4), channel_id=1, source_target_pairs={{0,1},{1,0},{2,3},{3,2},{4,5},{5,4},{6,7},{7,6},{8,9},{9,8},{10,11... | collective-permute-start | bytes 3145736 | tf_op jit(solution)/shard_map/ppermute | solution.py:725
  475.1 6.3 %collective-permute-start.30 = (f32[4,512]{1,0:T(4,128)S(1)}, f32[4,512]{1,0:T(4,128)S(1)}, u32[]{:S(2)}, u32[]{:S(2)}) collective-permute-start(f32[4,512]{1,0:T(4,128)S(1)} %bitcast.155), channel_id=1, source_target_pairs={{0,1},{1,0},{2,3},{3,2},{4,5},{5,4},{6,7},{7,6},{8,9},{9,8},{10,11... | collective-permute-start | bytes 24584 | tf_op jit(solution)/shard_map/ppermute | solution.py:725
  475.6 23.8 %collective-permute-start.29 = (bf16[4,4,128,256]{3,2,1,0:T(8,128)(2,1)S(1)}, bf16[4,4,128,256]{3,2,1,0:T(8,128)(2,1)}, u32[]{:S(2)}, u32[]{:S(2)}) collective-permute-start(bf16[4,4,128,256]{3,2,1,0:T(8,128)(2,1)S(1)} %grad_blocks.5), channel_id=1, source_target_pairs={{0,1},{1,0},{2,3},{3,2},{4,5},{5,4},{6,7},{7,6},{8,9},{9,8},{10,11... | collective-permute-start | bytes 3145736 | tf_op jit(solution)/shard_map/ppermute | solution.py:725
  481.4 5.4 collective-permute-start.31
  481.5 5.4 collective-permute-start.32
  483.7 3.7 collective-permute-start.33
  487.4 61.8 %all-to-all-start.5 = ((bf16[4,576,512]{2,1,0:T(8,128)(2,1)}), bf16[4,576,512]{2,1,0:T(8,128)(2,1)}, u32[]{:S(2)}, u32[]{:S(2)}) async-start(bf16[4,576,512]{2,1,0:T(8,128)(2,1)} %pad_maximum_fusion.1), calls=%async_computation.5 | async-start | bytes 4718592 | tf_op jit(solution)/shard_map/all_to_all | solution.py:1280
  504.5 20.7 %collective-permute-start.34 = (bf16[2,704,256]{2,1,0:T(8,128)(2,1)}, bf16[2,704,256]{2,1,0:T(8,128)(2,1)}, u32[]{:S(2)}, u32[]{:S(2)}) collective-permute-start(bf16[2,704,256]{2,1,0:T(8,128)(2,1)} %get-tuple-element.182), channel_id=1, source_target_pairs={{0,8},{1,9},{2,10},{3,11},{4,12},{5,13},{6,14},{7,15},{8,0},{9,1},... | collective-permute-start | bytes 2162696 | tf_op jit(solution)/shard_map/ppermute | solution.py:725
  509.2 17.4 %collective-permute-start.35 = (bf16[2,704,256]{2,1,0:T(8,128)(2,1)}, bf16[2,704,256]{2,1,0:T(8,128)(2,1)}, u32[]{:S(2)}, u32[]{:S(2)}) collective-permute-start(bf16[2,704,256]{2,1,0:T(8,128)(2,1)} %get-tuple-element.183), channel_id=1, source_target_pairs={{0,16},{1,17},{2,18},{3,19},{4,20},{5,21},{6,22},{7,23},{8,24},{9,... | collective-permute-start | bytes 2162696 | tf_op jit(solution)/shard_map/ppermute | solution.py:725
  526.6 3.6 collective-permute-start.38
  528.0 9.8 %collective-permute-start.36 = (bf16[704,256]{1,0:T(8,128)(2,1)S(1)}, bf16[704,256]{1,0:T(8,128)(2,1)S(1)}, u32[]{:S(2)}, u32[]{:S(2)}) collective-permute-start(bf16[704,256]{1,0:T(8,128)(2,1)S(1)} %fusion.6), channel_id=1, source_target_pairs={{0,16},{1,17},{2,18},{3,19},{4,20},{5,21},{6,22},{7,23},{8,24},{9,... | collective-permute-start | bytes 1081352 | tf_op jit(solution)/shard_map/ppermute | solution.py:725
  530.2 6.4 %collective-permute-start.39 = (f32[2,512]{1,0:T(2,128)S(1)}, f32[2,512]{1,0:T(2,128)S(1)}, u32[]{:S(2)}, u32[]{:S(2)}) collective-permute-start(f32[2,512]{1,0:T(2,128)S(1)} %pad_maximum_fusion.10), channel_id=1, source_target_pairs={{0,16},{1,17},{2,18},{3,19},{4,20},{5,21},{6,22},{7,23},{8,24},{9,... | collective-permute-start | bytes 12296 | tf_op jit(solution)/shard_map/ppermute | solution.py:725
  531.6 7.5 %collective-permute-start.37 = (bf16[704,256]{1,0:T(8,128)(2,1)S(1)}, bf16[704,256]{1,0:T(8,128)(2,1)S(1)}, u32[]{:S(2)}, u32[]{:S(2)}) collective-permute-start(bf16[704,256]{1,0:T(8,128)(2,1)S(1)} %fusion.7), channel_id=1, source_target_pairs={{0,8},{1,9},{2,10},{3,11},{4,12},{5,13},{6,14},{7,15},{8,0},{9,1},... | collective-permute-start | bytes 1081352 | tf_op jit(solution)/shard_map/ppermute | solution.py:725
  540.4 5.2 collective-permute-start.41
  540.4 7.8 %collective-permute-start.42 = (bf16[128,256]{1,0:T(8,128)(2,1)S(1)}, bf16[128,256]{1,0:T(8,128)(2,1)S(1)}, u32[]{:S(2)}, u32[]{:S(2)}) collective-permute-start(bf16[128,256]{1,0:T(8,128)(2,1)S(1)} %get-tuple-element.245), channel_id=1, source_target_pairs={{2,0},{5,1},{0,2},{3,3},{6,4},{1,5},{4,6},{7,7},{10,8},{13,9},{8,1... | collective-permute-start | bytes 196616 | tf_op jit(solution)/shard_map/ppermute | solution.py:702
  544.0 4.2 collective-permute-start.40
  549.2 20.3 %all-to-all-start.6 = ((bf16[4,128,512]{2,1,0:T(8,128)(2,1)}), bf16[4,128,512]{2,1,0:T(8,128)(2,1)S(1)}, u32[]{:S(2)}, u32[]{:S(2)}) async-start(bf16[4,128,512]{2,1,0:T(8,128)(2,1)} %pad_maximum_fusion.6), calls=%async_computation.6 | async-start | bytes 1048576 | tf_op jit(solution)/shard_map/all_to_all | solution.py:1280
  558.6 11.7 %copy-start.1 = (bf16[256,512]{1,0:T(8,128)(2,1)S(1)}, bf16[256,512]{1,0:T(8,128)(2,1)}, u32[]{:S(2)}) copy-start(bf16[256,512]{1,0:T(8,128)(2,1)} %param.23) | copy-start | bytes 786436
  (25 other events, 111.5 us)
Sparse Core Ops, SparseCore 0:
  11.1 84.2 all-gather.7
  103.7 83.1 all-gather.9
  252.3 74.1 all-gather.11
